TPU v7x, 32 devices: a whole 2x2x4 slice. The times are simulated.
32 devices in a mesh: ctx: 8 (over y, x, core), mp: 4 (over z).
Axes of the slice: x: 2, y: 2, z: 4, core: 2. Of those that a mesh axis runs over, the one named last changes fastest.
Arguments:
- tile_embeds: bfloat16 [4, 2048, 768], P('mp', 'ctx'), may hold values from -10 to 10
- norm_gain: float32 [768], replicated, may hold values from 0.1 to 1.9
- norm_bias: float32 [768], replicated, may hold values from -3 to 3
- w_qkv: bfloat16 [768, 2304], P('mp'), may hold values from -1.5 to 1.5
- w_out: bfloat16 [768, 768], P('mp'), may hold values from -0.21875 to 0.21875
- valid_count: int32 [4], P('mp'), may hold values from 256 to 2048
Outputs:
- encoded: bfloat16 [4, 2048, 768], P('mp', 'ctx')
All inputs are finite; a program needn't handle non-finite values.
Results may differ from a plain program's by a relative error of at most 0.008.
The roundings to bfloat16 on the way count: a program that leaves them out, or rounds other values in their place, can miss the bound.
Values may be sent and summed in bfloat16 or wider, within the bound.
No kernel may reach another device: no remote copies, remote signals or barrier semaphores. Data moves between devices by JAX's collectives and lax.ppermute only.
A program may use at most 64 MiB of HBM per device.

v0:
```python
from functools import reduce
import math

import jax
import jax.numpy as jnp
from jax import lax
from jax.sharding import PartitionSpec as P

HEADS = 12
HEAD_DIM = 64
MIDDLE_DILATION = 4
SLIDE_DILATION = 16
SHARDS_PER_SEG = 4


NEG_FILL = -1e30


def as_sent(x):

    def short(part):
        return part.astype(jnp.bfloat16) if part.dtype == jnp.float32 else part

    return jax.tree.map(short, x)


def swapped(value, axis, apart):
    mask = 2**apart
    pairs = [(source, source ^ mask) for source in range(lax.axis_size(axis))]
    return lax.ppermute(value, axis, pairs)


def layer_norm(row_data, norm_gain, norm_bias):
    floats = row_data.astype(jnp.float32)
    centre = jnp.mean(floats, axis=-1, keepdims=True)
    spread = jnp.mean((floats - centre) ** 2, axis=-1, keepdims=True)
    return ((floats - centre) * lax.rsqrt(spread + 1e-05) * norm_gain + norm_bias).astype(
        jnp.bfloat16
    )


def select_rows(head_rows, dilation_rate):
    return jnp.stack(
        [
            head_rows[head_number].reshape(-1, dilation_rate, head_rows.shape[-1])[
                :, head_number % dilation_rate
            ]
            for head_number in range(head_rows.shape[0])
        ]
    )


def build_step(query_block, offsets, dilation_rate, total_valid):
    rescale_factor = 1.0 / math.sqrt(query_block.shape[-1])

    def compute(running, shard_part, first):
        running_max, running_sum, running_num = running
        key_matrix, value_matrix = shard_part
        count_here = key_matrix.shape[1]
        dilated_index = first + jnp.arange(count_here, dtype=jnp.int32)
        key_position = dilated_index[None, :] * dilation_rate + offsets[:, None]
        allowed = key_position < total_valid
        logit_matrix = (
            jnp.einsum("hqe,hke->hqk", query_block, key_matrix, preferred_element_type=jnp.float32)
            * rescale_factor
        )
        logit_matrix = jnp.where(allowed[:, None, :], logit_matrix, NEG_FILL)
        new_max = jnp.maximum(running_max, jnp.max(logit_matrix, axis=-1))
        rescale = jnp.exp(running_max - new_max)
        weights = jnp.where(allowed[:, None, :], jnp.exp(logit_matrix - new_max[..., None]), 0.0)
        running_sum = jnp.sum(weights, axis=-1)
        running_num = jnp.einsum(
            "hqk,hke->hqe",
            weights.astype(jnp.bfloat16),
            value_matrix,
            preferred_element_type=jnp.float32,
        )
        return (new_max, running_sum, running_num)

    return compute


def initial_stats(head_count, query_count, head_dim):
    return (
        jnp.full((head_count, query_count), NEG_FILL, jnp.float32),
        jnp.zeros((head_count, query_count), jnp.float32),
        jnp.zeros((head_count, query_count, head_dim), jnp.float32),
    )


def widen_rows(values, offsets, dilation_rate, fill_value):
    picked = jnp.arange(dilation_rate)[None, :] == offsets[:, None]
    if values.ndim == 2:
        return jnp.where(picked[:, None, :], values[:, :, None], fill_value).reshape(
            values.shape[0], -1
        )
    return jnp.where(picked[:, None, :, None], values[:, :, None, :], fill_value).reshape(
        values.shape[0], -1, values.shape[-1]
    )


def local(tile_embeds, norm_gain, norm_bias, w_qkv, w_out, valid_count):
    tile_rows = tile_embeds[0]
    local_rows = tile_rows.shape[0]
    model_width = tile_rows.shape[1]
    head_count = HEADS
    head_dim = HEAD_DIM
    total_valid = valid_count[0]
    device_index = lax.axis_index("ctx")
    first_row = device_index * local_rows
    normed = layer_norm(tile_rows, norm_gain, norm_bias)
    whole_qkv, whole_out = (
        lax.all_gather(w_qkv, "mp", axis=0, tiled=True),
        lax.all_gather(w_out, "mp", axis=0, tiled=True),
    )
    projected = jnp.dot(normed, whole_qkv, preferred_element_type=jnp.float32).astype(jnp.bfloat16)
    gathered_queries = (
        projected[:, :model_width].reshape(local_rows, head_count, head_dim).transpose(1, 0, 2)
    )
    gathered_keys = (
        projected[:, model_width : 2 * model_width]
        .reshape(local_rows, head_count, head_dim)
        .transpose(1, 0, 2)
    )
    gathered_values = (
        projected[:, 2 * model_width :].reshape(local_rows, head_count, head_dim).transpose(1, 0, 2)
    )
    position = first_row + jnp.arange(local_rows, dtype=jnp.int32)
    key_valid = position < total_valid
    head_shifts = jnp.arange(head_count, dtype=jnp.int32)
    local_step = build_step(gathered_queries, head_shifts * 0, 1, total_valid)
    local_stats = local_step(
        initial_stats(head_count, local_rows, head_dim), (gathered_keys, gathered_values), first_row
    )
    middle_shifts = head_shifts % MIDDLE_DILATION
    middle_queries = select_rows(gathered_queries, MIDDLE_DILATION)
    middle_keys = select_rows(gathered_keys, MIDDLE_DILATION)
    middle_values = select_rows(gathered_values, MIDDLE_DILATION)
    grouped_rows = SHARDS_PER_SEG * local_rows // MIDDLE_DILATION
    mid_step = build_step(middle_queries, middle_shifts, MIDDLE_DILATION, total_valid)
    mid_initial = initial_stats(head_count, middle_queries.shape[1], head_dim)
    gathered = (middle_keys, middle_values)
    for bit_number in range(SHARDS_PER_SEG.bit_length() - 1):
        partner = jax.tree.map(
            lambda part, own: part.astype(own.dtype),
            swapped(as_sent(gathered), "ctx", bit_number),
            gathered,
        )
        lower_half = device_index // (1 << bit_number) % 2 == 0
        gathered = tuple(
            (
                jnp.where(
                    lower_half,
                    jnp.concatenate([own_part, other_part], 1),
                    jnp.concatenate([other_part, own_part], 1),
                )
                for own_part, other_part in zip(gathered, partner)
            )
        )
    middle_state = mid_step(mid_initial, gathered, device_index // SHARDS_PER_SEG * grouped_rows)
    slide_shifts = head_shifts % SLIDE_DILATION
    slide_queries = select_rows(gathered_queries, SLIDE_DILATION)
    slide_keys = select_rows(gathered_keys, SLIDE_DILATION)
    slide_values = select_rows(gathered_values, SLIDE_DILATION)
    slide_step = build_step(slide_queries, slide_shifts, SLIDE_DILATION, total_valid)
    slide_state = slide_step(
        initial_stats(head_count, slide_queries.shape[1], head_dim),
        (
            lax.all_gather(slide_keys, "ctx", axis=1, tiled=True),
            lax.all_gather(slide_values, "ctx", axis=1, tiled=True),
        ),
        jnp.int32(0),
    )
    branches = [local_stats]
    for branch_stats, offsets, dilation_rate in (
        (middle_state, middle_shifts, MIDDLE_DILATION),
        (slide_state, slide_shifts, SLIDE_DILATION),
    ):
        branches.append(
            (
                widen_rows(branch_stats[0], offsets, dilation_rate, NEG_FILL),
                widen_rows(branch_stats[1], offsets, dilation_rate, 0.0),
                widen_rows(branch_stats[2], offsets, dilation_rate, 0.0),
            )
        )
    top_score = reduce(jnp.maximum, [entry[0] for entry in branches])
    denominator = sum((jnp.exp(entry[0] - top_score) * entry[1] for entry in branches))
    weighted_sum = sum((jnp.exp(entry[0] - top_score)[..., None] * entry[2] for entry in branches))
    head_result = jnp.where(key_valid[None, :, None], weighted_sum / denominator[..., None], 0.0)
    attention = head_result.astype(jnp.bfloat16).transpose(1, 0, 2).reshape(local_rows, model_width)
    projection = jnp.dot(attention, whole_out, preferred_element_type=jnp.float32)
    return (tile_rows.astype(jnp.float32) + projection).astype(jnp.bfloat16)[None]


def solution(mesh):
    placed = (P("mp", "ctx", None), P(), P(), P("mp", None), P("mp", None), P("mp"))
    return jax.shard_map(
        local, mesh=mesh, in_specs=placed, out_specs=P("mp", "ctx", None), check_vma=False
    )
```

profile of v0, /device:TPU:0, one launch (start us, length us, event | category | flops | bytes accessed | tf_op | source)
XLA Modules:
  0.0 249.5 jit_solution(8458888001286115925)
XLA Ops:
  13.9 67.7 %all-gather.3.cloned.1.call-done = bf16[768,2304]{1,0:T(8,128)(2,1)} async-done(((bf16[192,2304]{1,0:T(8,128)(2,1)}), bf16[768,2304]{1,0:T(8,128)(2,1)}) %all-gather.3.cloned.1.call-update) | async-done | bytes 3538960 | tf_op jit(solution)/shard_map/all_gather | solution.py:113
  81.7 3.3 %convolution_convert_fusion = bf16[256,2304]{1,0:T(8,128)(2,1)S(1)} fusion(bf16[768,2304]{1,0:T(8,128)(2,1)} %all-gather.3.cloned.1.call-done, bf16[1,256,768]{2,1,0:T(8,128)(2,1)} %param.6, f32[768]{0:T(1024)} %param.8, f32[768]{0:T(1024)} %param.7, f32[256]{0:T(256)S(1)} %add_rsqrt_fusion, f32[256]{0:T(256)S(1)} %broadcast_multiply_fusion), kind=kOutput, calls=%fused_computation | convolution fusion | flops 907739136 | bytes 5120000 | tf_op jit(solution)/shard_map/dot_general | solution.py:116
  104.9 10.6 %all_gather.13 = bf16[12,128,64]{2,1,0:T(8,128)(2,1)S(1)} all-gather(bf16[12,16,64]{2,1,0:T(8,128)(2,1)S(1)} %constant_dynamic-update-slice_fusion.36), channel_id=1, replica_groups=mesh['ctx'=8,'mp'=4] {'ctx'}, dimensions={1}, use_global_device_ids=true | all-gather | bytes 221184 | tf_op jit(solution)/shard_map/all_gather | solution.py:169
  117.5 1.8 fusion
  121.8 1.5 copy.509
  124.8 1.5 copy.511
  126.2 1.5 slice.558
  127.7 1.5 copy.513
  129.2 1.5 slice.560
  130.7 1.5 copy.515
  132.1 1.5 slice.562
  133.6 1.5 copy.517
  136.6 1.5 copy.519
  139.5 1.5 copy.521
  142.5 1.5 copy.523
  144.0 1.5 slice.570
  145.4 1.5 copy.525
  149.9 1.5 slice.574
  151.3 1.5 copy.529
  152.8 1.5 slice.576
  154.3 1.5 copy.531
  180.7 10.5 %all_gather.14 = bf16[12,128,64]{2,1,0:T(8,128)(2,1)S(1)} all-gather(bf16[12,16,64]{2,1,0:T(8,128)(2,1)S(1)} %constant_dynamic-update-slice_fusion.60), channel_id=1, replica_groups=mesh['ctx'=8,'mp'=4] {'ctx'}, dimensions={1}, use_global_device_ids=true | all-gather | bytes 221184 | tf_op jit(solution)/shard_map/all_gather | solution.py:170
  204.8 2.1 fusion.1
  207.8 2.1 maximum_select_fusion.4
  214.2 2.7 %copy.559 = f32[12,256,64]{1,2,0:T(8,128)} copy(f32[12,256,64]{2,1,0:T(8,128)} %bitcast.410) | data formatting | bytes 1572864 | tf_op jit(solution)/shard_map/jit(_where)/broadcast_in_dim | solution.py:97
  217.0 1.9 maximum_select_fusion.5
  221.6 2.8 %fusion.78 = (f32[12,64]{1,0:T(8,128)S(1)}, f32[12,64,256]{2,1,0:T(8,128)}) fusion(bf16[12,64,64]{2,1,0:T(8,128)(2,1)} %constant_dynamic-update-slice_fusion, bf16[12,128,64]{2,1,0:T(8,128)(2,1)} %collective-permute-done.1, bf16[12,128,64]{2,1,0:T(8,128)(2,1)} %maximum_select_fusion.4, pred[]{:T(512)S(6)} %eq.109, pred[12,256]{1,0:T(8,128)(4,1)S(1)} %copy-done.12), kind=kOutput, calls=%fused_computation.238 | convolution fusion | flops 27524352 | bytes 1284097 | tf_op jit(solution)/shard_map/hqe,hke->hqk/dot_general | solution.py:64
  226.3 3.9 %collective-permute-done.3 = bf16[12,128,64]{2,1,0:T(8,128)(2,1)} collective-permute-done((bf16[12,128,64]{2,1,0:T(8,128)(2,1)}, bf16[12,128,64]{2,1,0:T(8,128)(2,1)}, u32[]{:S(2)}, u32[]{:S(2)}) %collective-permute-start.3) | collective-permute-done | bytes 196640 | tf_op jit(solution)/shard_map/ppermute | solution.py:30
  230.3 2.1 fusion.40
  233.9 2.7 %copy.534 = f32[12,256,64]{1,2,0:T(8,128)} copy(f32[12,256,64]{2,1,0:T(8,128)} %bitcast.411) | data formatting | bytes 1572864 | tf_op jit(solution)/shard_map/jit(_where)/broadcast_in_dim | solution.py:97
  236.7 3.3 %fusion.26 = bf16[12,256,64]{1,2,0:T(8,128)(2,1)} fusion(bf16[12,256,64]{1,2,0:T(8,128)(2,1)} %bitcast.417, f32[12,256,256]{1,2,0:T(8,128)S(1)} %get-tuple-element.49, f32[12,256]{1,0:T(8,128)} %broadcast_maximum_fusion, pred[256]{0:T(512)(128)(4,1)} %add_compare_fusion.2, f32[12,256,64]{1,2,0:T(8,128)} %copy.559, f32[12,256,64]{1,2,0:T(8,128)} %copy.534, ...), kind=kOutput, calls=%fused_computation.23 | convolution fusion | flops 106561536 | bytes 5572864 | tf_op jit(solution)/shard_map/hqk,hke->hqe/dot_general | solution.py:72
  240.0 2.7 %fusion.17 = bf16[1,256,768]{2,1,0:T(8,128)(2,1)} fusion(bf16[256,768]{0,1:T(8,128)(2,1)} %bitcast.420, bf16[768,768]{1,0:T(8,128)(2,1)} %all-gather.5.cloned.1.call-done, bf16[1,256,768]{2,1,0:T(8,128)(2,1)S(1)} %copy-done), kind=kOutput, calls=%fused_computation.15 | convolution fusion | flops 302579712 | bytes 2359296 | tf_op jit(solution)/shard_map/dot_general | solution.py:191
  (249 shorter events, 89.1 us)
Async XLA Ops:
  6.5 75.1 %all-gather.3.cloned.1.call-start = ((), (), s32[]{:S(2)}) async-start(), calls=%async_computation | async-start | bytes 4423680 | tf_op jit(solution)/shard_map/all_gather | solution.py:113
  7.3 232.8 %all-gather.5.cloned.1.call-start = ((), (), s32[]{:S(2)}) async-start(), calls=%async_computation.1 | async-start | bytes 1474560 | tf_op jit(solution)/shard_map/all_gather | solution.py:114
  13.4 102.5 %copy-start.10 = (pred[12,128]{1,0:T(8,128)(4,1)}, pred[12,128]{1,0:T(8,128)(4,1)S(1)}, u32[]{:S(2)}) copy-start(pred[12,128]{1,0:T(8,128)(4,1)S(1)} %add_compare_fusion.1) | copy-start | bytes 4612
  95.2 112.6 %collective-permute-start = (bf16[12,64,64]{2,1,0:T(8,128)(2,1)}, bf16[12,64,64]{2,1,0:T(8,128)(2,1)}, u32[]{:S(2)}, u32[]{:S(2)}) collective-permute-start(bf16[12,64,64]{2,1,0:T(8,128)(2,1)} %constant_dynamic-update-slice_fusion.12), channel_id=1, source_target_pairs={{0,4},{4,0},{8,12},{12,8},{16,20},{20,16},{24,28},{28,24},{1,5},{5... | collective-permute-start | bytes 294920 | tf_op jit(solution)/shard_map/ppermute | solution.py:30
  95.4 21.5 %copy-start.1 = (bf16[256,768]{0,1:T(8,128)(2,1)}, bf16[256,768]{0,1:T(8,128)(2,1)S(1)}, u32[]{:S(2)}) copy-start(bf16[256,768]{0,1:T(8,128)(2,1)S(1)} %copy.405) | copy-start | bytes 1179652
  121.0 85.9 %copy-start.2 = (bf16[256,768]{0,1:T(8,128)(2,1)}, bf16[256,768]{0,1:T(8,128)(2,1)S(1)}, u32[]{:S(2)}) copy-start(bf16[256,768]{0,1:T(8,128)(2,1)S(1)} %copy.506) | copy-start | bytes 1179652
  155.8 51.1 %copy-start.3 = (f32[12,16,128]{2,1,0:T(8,128)S(1)}, f32[12,16,128]{2,1,0:T(8,128)}, u32[]{:S(2)}) copy-start(f32[12,16,128]{2,1,0:T(8,128)} %get-tuple-element.51) | copy-start | bytes 294916
  155.8 51.1 %copy-start.5 = (f32[12,16]{1,0:T(8,128)S(1)}, f32[12,16]{1,0:T(8,128)}, u32[]{:S(2)}) copy-start(f32[12,16]{1,0:T(8,128)} %broadcast_maximum_fusion.1) | copy-start | bytes 2308
  155.8 51.1 %copy-start.11 = (pred[12,128]{1,0:T(8,128)(4,1)S(1)}, pred[12,128]{1,0:T(8,128)(4,1)}, u32[]{:S(2)}) copy-start(pred[12,128]{1,0:T(8,128)(4,1)} %copy-done.10) | copy-start | bytes 4612
  155.8 51.4 %copy-start.6 = (bf16[64,1,64]{2,1,0:T(2,128)(2,1)S(1)}, bf16[64,1,64]{2,1,0:T(2,128)(2,1)}, u32[]{:S(2)}) copy-start(bf16[64,1,64]{2,1,0:T(2,128)(2,1)} %slice.505) | copy-start | bytes 24580
  170.9 46.1 %collective-permute-start.2 = (bf16[12,64,64]{2,1,0:T(8,128)(2,1)}, bf16[12,64,64]{2,1,0:T(8,128)(2,1)}, u32[]{:S(2)}, u32[]{:S(2)}) collective-permute-start(bf16[12,64,64]{2,1,0:T(8,128)(2,1)} %constant_dynamic-update-slice_fusion.48), channel_id=1, source_target_pairs={{0,4},{4,0},{8,12},{12,8},{16,20},{20,16},{24,28},{28,24},{1,5},{5... | collective-permute-start | bytes 294920 | tf_op jit(solution)/shard_map/ppermute | solution.py:30
  206.9 10.1 %copy-start.4 = (bf16[12,64,64]{2,1,0:T(8,128)(2,1)S(1)}, bf16[12,64,64]{2,1,0:T(8,128)(2,1)}, u32[]{:S(2)}) copy-start(bf16[12,64,64]{2,1,0:T(8,128)(2,1)} %constant_dynamic-update-slice_fusion.48) | copy-start | bytes 294916
  209.9 11.7 %collective-permute-start.1 = (bf16[12,128,64]{2,1,0:T(8,128)(2,1)}, bf16[12,128,64]{2,1,0:T(8,128)(2,1)}, u32[]{:S(2)}, u32[]{:S(2)}) collective-permute-start(bf16[12,128,64]{2,1,0:T(8,128)(2,1)} %maximum_select_fusion.4), channel_id=1, source_target_pairs={{0,8},{4,12},{8,0},{12,4},{16,24},{20,28},{24,16},{28,20},{1,9},{5... | collective-permute-start | bytes 589832 | tf_op jit(solution)/shard_map/ppermute | solution.py:30
  213.0 8.7 %copy-start.12 = (pred[12,256]{1,0:T(8,128)(4,1)S(1)}, pred[12,256]{1,0:T(8,128)(4,1)}, u32[]{:S(2)}) copy-start(pred[12,256]{1,0:T(8,128)(4,1)} %add_compare_fusion) | copy-start | bytes 9220
  218.9 11.4 %collective-permute-start.3 = (bf16[12,128,64]{2,1,0:T(8,128)(2,1)}, bf16[12,128,64]{2,1,0:T(8,128)(2,1)}, u32[]{:S(2)}, u32[]{:S(2)}) collective-permute-start(bf16[12,128,64]{2,1,0:T(8,128)(2,1)} %maximum_select_fusion.5), channel_id=1, source_target_pairs={{0,8},{4,12},{8,0},{12,4},{16,24},{20,28},{24,16},{28,20},{1,9},{5... | collective-permute-start | bytes 589832 | tf_op jit(solution)/shard_map/ppermute | solution.py:30
  232.4 4.2 %copy-start.7 = (f32[12,256]{1,0:T(8,128)S(1)}, f32[12,256]{1,0:T(8,128)}, u32[]{:S(2)}) copy-start(f32[12,256]{1,0:T(8,128)} %fusion.1) | copy-start | bytes 36868
  232.4 4.2 %copy-start.8 = (f32[12,256]{1,0:T(8,128)S(1)}, f32[12,256]{1,0:T(8,128)}, u32[]{:S(2)}) copy-start(f32[12,256]{1,0:T(8,128)} %broadcast_in_dim.281) | copy-start | bytes 36868
  232.4 4.2 %copy-start.9 = (f32[12,256]{1,0:T(8,128)S(1)}, f32[12,256]{1,0:T(8,128)}, u32[]{:S(2)}) copy-start(f32[12,256]{1,0:T(8,128)} %broadcast_in_dim.266) | copy-start | bytes 36868
  232.4 4.2 %copy-start.13 = (pred[12,256]{1,0:T(8,128)(4,1)S(1)}, pred[12,256]{1,0:T(8,128)(4,1)}, u32[]{:S(2)}) copy-start(pred[12,256]{1,0:T(8,128)(4,1)} %copy.456) | copy-start | bytes 9220
  232.4 4.2 %copy-start.14 = (pred[12,256]{1,0:T(8,128)(4,1)S(1)}, pred[12,256]{1,0:T(8,128)(4,1)}, u32[]{:S(2)}) copy-start(pred[12,256]{1,0:T(8,128)(4,1)} %broadcast_in_dim.261) | copy-start | bytes 9220
  236.7 3.3 %copy-start = (bf16[1,256,768]{2,1,0:T(8,128)(2,1)S(1)}, bf16[1,256,768]{2,1,0:T(8,128)(2,1)}, u32[]{:S(2)}) copy-start(bf16[1,256,768]{2,1,0:T(8,128)(2,1)} %param.6) | copy-start | bytes 1179652
Sparse Core Ops, SparseCore 0:
  8.9 72.6 all-gather.2
  83.2 28.6 all-gather.4
where the time goes:
time: 254 us; the launch traced here: 250 us
  local copies, waits for them, and re-layouts  107 us (42%)
  waiting for transfers between devices  74.3 us (29%)
  blocking collectives  21.1 us (8%)
  matrix products  17.2 us (7%)
  between operations  14.9 us (6%)
  other arithmetic  12.8 us (5%)
    all_gather x1, waiting for transfers between devices, local(): lax.all_gather(w_qkv, 'mp', axis=0, tiled=True)  67.7 us
    slice x111, local copies, waits for them, and re-layouts, select_rows(): head_rows[head_number].reshape(-1, dilation_rate, head_rows.shape[-1])  54.9 us
    unnamed x96, local copies, waits for them, and re-layouts  35.4 us
    all_gather x1, blocking collectives, local(): lax.all_gather(slide_keys, 'ctx', axis=1, tiled=True)  10.6 us
    all_gather x1, blocking collectives, local(): lax.all_gather(slide_values, 'ctx', axis=1, tiled=True)  10.5 us
    broadcast_in_dim x4, local copies, waits for them, and re-layouts, widen_rows(): jnp.where(picked[:, None, :, None], values[:, :, None, :], fill_value)  8.16 us
    dot_general x3, matrix products, compute(): jnp.einsum('hqk,hke->hqe', weights.astype(jnp.bfloat16), value_matrix, pr...  5.71 us
    dot_general x3, matrix products, compute(): jnp.einsum('hqe,hke->hqk', query_block, key_matrix, preferred_element_typ...  5.55 us
  transfers between devices with their start and end apart: 6, of which 3 were waited for; matrix products, arithmetic and copies ran while one was open for 54% of the time, Pallas kernels for 0%

commit v1 on v0

v1 whole, which is shorter than its diff:
```python
import math

import jax
import jax.numpy as jnp
from jax import lax
from jax.experimental import pallas as pl
from jax.experimental.pallas import tpu as pltpu
from jax.sharding import PartitionSpec as P

HEADS = 12
HEAD_DIM = 64
MID = 4
WIDE = 16
SHARDS = 4
STEPS = WIDE // MID
GROUP_HEADS = HEADS // SHARDS
GROUP_WIDTH = GROUP_HEADS * HEAD_DIM
NEG_FILL = -1e30
SCALE = math.log2(math.e) / math.sqrt(HEAD_DIM)
VMEM_LIMIT = 56 * 1024 * 1024


def call(body, out_shape, scratch=(), n_scalar=0, n_in=0, aliases=None):
    specs = [pl.BlockSpec(memory_space=pltpu.SMEM)] * n_scalar + [
        pl.BlockSpec(memory_space=pltpu.VMEM)
    ] * n_in
    outs = jax.tree.map(lambda _: pl.BlockSpec(memory_space=pltpu.VMEM), out_shape)
    return pl.pallas_call(
        body,
        out_shape=out_shape,
        in_specs=specs,
        out_specs=outs,
        scratch_shapes=list(scratch),
        input_output_aliases=aliases or {},
        compiler_params=pltpu.CompilerParams(vmem_limit_bytes=VMEM_LIMIT),
    )


def flip(value, axis, mask):
    pairs = [(source, source ^ mask) for source in range(lax.axis_size(axis))]
    return lax.ppermute(value, axis, pairs)


def residue_order(rows):
    depth = rows // WIDE
    new = lax.broadcasted_iota(jnp.int32, (rows, rows), 0)
    old = lax.broadcasted_iota(jnp.int32, (rows, rows), 1)
    return (old == (new % depth) * WIDE + new // depth).astype(jnp.bfloat16)


def position_order(rows):
    depth = rows // WIDE
    new = lax.broadcasted_iota(jnp.int32, (rows, rows), 0)
    old = lax.broadcasted_iota(jnp.int32, (rows, rows), 1)
    return (old == (new % WIDE) * depth + new // WIDE).astype(jnp.bfloat16)


def matmul(left, right):
    return jnp.dot(left, right, preferred_element_type=jnp.float32)


def matmul_t(left, right):
    return lax.dot_general(
        left, right, (((1,), (1,)), ((), ())), preferred_element_type=jnp.float32
    )


def norm_body(*refs):
    x_refs, gain_ref, bias_ref, out_refs = refs[:SHARDS], refs[SHARDS], refs[SHARDS + 1], refs[SHARDS + 2 :]
    order = residue_order(x_refs[0].shape[0])
    for x_ref, out_ref in zip(x_refs, out_refs):
        floats = x_ref[...].astype(jnp.float32)
        centred = floats - jnp.mean(floats, axis=-1, keepdims=True)
        spread = jnp.mean(centred * centred, axis=-1, keepdims=True)
        normed = (centred * lax.rsqrt(spread + 1e-05) * gain_ref[...] + bias_ref[...]).astype(
            jnp.bfloat16
        )
        out_ref[...] = matmul(order, normed).astype(jnp.bfloat16)


def group_indices():
    shard = lax.axis_index("ctx")
    return shard % SHARDS, shard // SHARDS


def qkv_body(n_mp, shared, *refs):
    normed_refs, refs = refs[:SHARDS], refs[SHARDS:]
    n_weights = 1 + (2 if shared else 1) * (n_mp - 1)
    weight_refs, refs = refs[:n_weights], refs[n_weights:]
    out_refs, sent_ref, whole_ref = refs[:SHARDS], refs[SHARDS], refs[SHARDS + 1]
    member, group = group_indices()
    mp_index = lax.axis_index("mp")
    rows = weight_refs[0].shape[0]

    def put(ref, source, offset):
        start = pl.multiple_of(source * rows + offset, 16)
        whole_ref[pl.ds(start, ref.shape[0]), :] = ref[...]

    put(weight_refs[0], mp_index, 0)
    for apart in range(1, n_mp):
        if shared:
            half = group % 2
            put(weight_refs[2 * apart - 1], mp_index ^ apart, half * (rows // 2))
            put(weight_refs[2 * apart], mp_index ^ apart, (1 - half) * (rows // 2))
        else:
            put(weight_refs[apart], mp_index ^ apart, 0)
    for normed_ref, out_ref in zip(normed_refs, out_refs):
        projected = matmul(normed_ref[...], whole_ref[...]).astype(jnp.bfloat16)
        out_ref[...] = projected.reshape(out_ref.shape)
    depth = out_refs[0].shape[2]
    for index in range(GROUP_HEADS):
        head = member * GROUP_HEADS + index
        low = index * HEAD_DIM
        for shard, out_ref in enumerate(out_refs):
            block = out_ref[head // MID, head % MID]
            key = block[:, GROUP_WIDTH + low : GROUP_WIDTH + low + HEAD_DIM]
            value = block[:, 2 * GROUP_WIDTH + low : 2 * GROUP_WIDTH + low + HEAD_DIM]
            sent_ref[index, shard * depth : (shard + 1) * depth, :] = jnp.concatenate(
                [key, value], axis=1
            )


def branch(query, key, value, allowed):
    score = matmul_t(query, key) * SCALE
    score = jnp.where(allowed, score, NEG_FILL)
    largest = jnp.max(score, axis=-1, keepdims=True)
    weight = jnp.exp2(score - largest)
    total = jnp.sum(weight, axis=-1, keepdims=True)
    return largest, total, matmul(weight.astype(jnp.bfloat16), value)


def merge(one, two):
    top = jnp.maximum(one[0], two[0])
    left = jnp.exp2(one[0] - top)
    right = jnp.exp2(two[0] - top)
    return top, left * one[1] + right * two[1], left * one[2] + right * two[2]


def near_body(valid_ref, *refs):
    qkv_refs, refs = refs[:SHARDS], refs[SHARDS:]
    out_refs, refs = refs[:SHARDS], refs[SHARDS:]
    kept_max, kept_sum, kept_num, all_max, all_sum, all_num = refs
    member, group = group_indices()
    valid = valid_ref[0]
    depth = qkv_refs[0].shape[2]
    rows = WIDE * depth
    key_at = lax.broadcasted_iota(jnp.int32, (1, rows), 1)
    row_at = lax.broadcasted_iota(jnp.int32, (rows, 1), 0)
    bases = [(group * SHARDS + (member ^ apart)) * rows for apart in range(SHARDS)]

    def part(ref, low):
        return ref[...].reshape(rows, -1)[:, low : low + HEAD_DIM]

    for index in range(GROUP_HEADS):
        head = member * GROUP_HEADS + index
        low = index * HEAD_DIM
        offset = head % MID
        for shard, ref in enumerate(qkv_refs):
            block = ref[...].reshape(rows, 3 * GROUP_WIDTH)
            allowed = bases[shard] + (key_at % depth) * WIDE + key_at // depth < valid
            largest, total, number = branch(
                block[:, low : low + HEAD_DIM],
                block[:, GROUP_WIDTH + low : GROUP_WIDTH + low + HEAD_DIM],
                block[:, 2 * GROUP_WIDTH + low : 2 * GROUP_WIDTH + low + HEAD_DIM],
                allowed,
            )
            all_max[shard] = largest.reshape(STEPS, MID, depth, 1)
            all_sum[shard] = total.reshape(STEPS, MID, depth, 1)
            all_num[shard] = number.reshape(STEPS, MID, depth, HEAD_DIM)
        taken = jnp.concatenate(
            [ref[:, offset].reshape(STEPS * depth, 3 * GROUP_WIDTH) for ref in qkv_refs], axis=0
        )
        count = STEPS * depth
        mid_at = lax.broadcasted_iota(jnp.int32, (1, count), 1)
        mid_position = (mid_at % depth) * WIDE + (mid_at // depth) * MID + offset
        allowed = jnp.concatenate([base + mid_position for base in bases], axis=1) < valid
        middle = branch(
            taken[:, low : low + HEAD_DIM],
            taken[:, GROUP_WIDTH + low : GROUP_WIDTH + low + HEAD_DIM],
            taken[:, 2 * GROUP_WIDTH + low : 2 * GROUP_WIDTH + low + HEAD_DIM],
            allowed,
        )
        here = (
            all_max[:, :, offset].reshape(SHARDS * count, 1),
            all_sum[:, :, offset].reshape(SHARDS * count, 1),
            all_num[:, :, offset].reshape(SHARDS * count, HEAD_DIM),
        )
        top, total, number = merge(here, middle)
        all_max[:, :, offset] = top.reshape(SHARDS, STEPS, depth, 1)
        all_sum[:, :, offset] = total.reshape(SHARDS, STEPS, depth, 1)
        all_num[:, :, offset] = number.reshape(SHARDS, STEPS, depth, HEAD_DIM)
        kept_max[index] = all_max[:, head // MID, offset].reshape(SHARDS * depth, 1)
        kept_sum[index] = all_sum[:, head // MID, offset].reshape(SHARDS * depth, 1)
        kept_num[index] = all_num[:, head // MID, offset].reshape(SHARDS * depth, HEAD_DIM)
        for shard, ref in enumerate(out_refs):
            position = bases[shard] + (row_at % depth) * WIDE + row_at // depth
            number = all_num[shard].reshape(rows, HEAD_DIM)
            total = all_sum[shard].reshape(rows, 1)
            attention = jnp.where(position < valid, number / total, 0.0).astype(jnp.bfloat16)
            ref[:, :, :, low : low + HEAD_DIM] = attention.reshape(STEPS, MID, depth, HEAD_DIM)


def far_body(n_groups, valid_ref, *refs):
    qkv_refs, refs = refs[:SHARDS], refs[SHARDS:]
    sent_refs, refs = refs[:n_groups], refs[n_groups:]
    kept_max, kept_sum, kept_num = refs[:3]
    in_refs, out_refs = refs[3 : 3 + SHARDS], refs[3 + SHARDS :]
    member, group = group_indices()
    valid = valid_ref[0]
    depth = qkv_refs[0].shape[2]
    count = SHARDS * depth
    for ref, out_ref in zip(in_refs, out_refs):
        out_ref[...] = ref[...]

    def positions(at, head, apart):
        block = at // depth
        shard = (group ^ apart) * SHARDS + (member ^ block)
        return (shard * depth + at % depth) * WIDE + head

    key_at = lax.broadcasted_iota(jnp.int32, (1, count), 1)
    row_at = lax.broadcasted_iota(jnp.int32, (count, 1), 0)
    for index in range(GROUP_HEADS):
        head = member * GROUP_HEADS + index
        low = index * HEAD_DIM
        query = jnp.concatenate(
            [ref[head // MID, head % MID][:, low : low + HEAD_DIM] for ref in qkv_refs], axis=0
        )
        allowed = (
            jnp.concatenate([positions(key_at, head, apart) for apart in range(n_groups)], axis=1)
            < valid
        )
        both = jnp.concatenate([ref[index] for ref in sent_refs], axis=0)
        slide = branch(query, both[:, :HEAD_DIM], both[:, HEAD_DIM:], allowed)
        _, total, number = merge((kept_max[index], kept_sum[index], kept_num[index]), slide)
        inside = positions(row_at, head, 0) < valid
        attention = jnp.where(inside, number / total, 0.0).astype(jnp.bfloat16)
        for shard, ref in enumerate(out_refs):
            ref[head // MID, head % MID, :, low : low + HEAD_DIM] = attention[
                shard * depth : (shard + 1) * depth
            ]


def gather_body(n_mp, *refs):
    own_ref, pair_refs, out_ref = refs[0], refs[1:-1], refs[-1]
    mp_index = lax.axis_index("mp")
    rows = own_ref.shape[0]
    out_ref[pl.ds(pl.multiple_of(mp_index * rows, 16), rows), :] = own_ref[...]
    for apart in range(1, n_mp):
        if len(pair_refs) == n_mp - 1:
            start = pl.multiple_of((mp_index ^ apart) * rows, 16)
            out_ref[pl.ds(start, rows), :] = pair_refs[apart - 1][...]
        else:
            core = lax.axis_index("ctx") % 2
            half = rows // 2
            for turn in range(2):
                start = (mp_index ^ apart) * rows + (core ^ turn) * half
                out_ref[pl.ds(pl.multiple_of(start, 16), half), :] = pair_refs[
                    2 * (apart - 1) + turn
                ][...]


def out_body(x_ref, *refs):
    part_refs, weight_ref, out_ref = refs[:SHARDS], refs[SHARDS], refs[SHARDS + 1]
    rows = x_ref.shape[0]
    member, _ = group_indices()
    order = position_order(rows)
    total = x_ref[...].astype(jnp.float32)
    update = jnp.zeros(total.shape, jnp.float32)
    for apart, ref in enumerate(part_refs):
        part = matmul(order, ref[...].reshape(rows, GROUP_WIDTH)).astype(jnp.bfloat16)
        start = pl.multiple_of((member ^ apart) * GROUP_WIDTH, GROUP_WIDTH)
        update = update + matmul(part, weight_ref[pl.ds(start, GROUP_WIDTH), :])
    out_ref[...] = (total + update).astype(jnp.bfloat16)


def local(tile_embeds, norm_gain, norm_bias, w_qkv, w_out, valid_count):
    x = tile_embeds[0]
    rows, width = x.shape
    n_mp = lax.axis_size("mp")
    n_groups = lax.axis_size("ctx") // SHARDS
    depth = rows // WIDE
    weight_rows = w_qkv.shape[0]
    member, group = group_indices()
    bf16 = jnp.bfloat16

    def shape(*dims, kind=bf16):
        return jax.ShapeDtypeStruct(dims, kind)

    x_far = flip(x, "ctx", 2)
    chunks = [x, flip(x, "ctx", 1), x_far, flip(x_far, "ctx", 1)]

    mine = jnp.concatenate(
        [
            lax.dynamic_slice(
                w_qkv, (0, part * width + member * GROUP_WIDTH), (weight_rows, GROUP_WIDTH)
            )
            for part in range(3)
        ],
        axis=1,
    )
    shared = n_groups % 2 == 0 and weight_rows % 32 == 0
    weights = [mine]
    if shared:
        half = weight_rows // 2
        piece = lax.dynamic_slice(mine, (group % 2 * half, 0), (half, 3 * GROUP_WIDTH))
        for apart in range(1, n_mp):
            direct = flip(piece, "mp", apart)
            weights += [direct, flip(direct, "ctx", SHARDS)]
    else:
        weights += [flip(mine, "mp", apart) for apart in range(1, n_mp)]

    out_parts = [w_out]
    if weight_rows % 32 == 0:
        half = weight_rows // 2
        piece = lax.dynamic_slice(w_out, (member % 2 * half, 0), (half, width))
        for apart in range(1, n_mp):
            direct = flip(piece, "mp", apart)
            out_parts += [direct, flip(direct, "ctx", 1)]
    else:
        out_parts += [flip(w_out, "mp", apart) for apart in range(1, n_mp)]

    normed = call(norm_body, [shape(rows, width)] * SHARDS, n_in=SHARDS + 2)(
        *chunks, norm_gain.reshape(1, width), norm_bias.reshape(1, width)
    )
    block = shape(STEPS, MID, depth, 3 * GROUP_WIDTH)
    *qkv, sent = call(
        lambda *refs: qkv_body(n_mp, shared, *refs),
        [block] * SHARDS + [shape(GROUP_HEADS, SHARDS * depth, 2 * HEAD_DIM)],
        scratch=[pltpu.VMEM((n_mp * weight_rows, 3 * GROUP_WIDTH), bf16)],
        n_in=SHARDS + len(weights),
    )(*normed, *weights)
    others = [sent] + [flip(sent, "ctx", SHARDS * apart) for apart in range(1, n_groups)]

    f32 = jnp.float32
    part = shape(STEPS, MID, depth, GROUP_WIDTH)
    stats = [
        shape(GROUP_HEADS, SHARDS * depth, 1, kind=f32),
        shape(GROUP_HEADS, SHARDS * depth, 1, kind=f32),
        shape(GROUP_HEADS, SHARDS * depth, HEAD_DIM, kind=f32),
    ]
    near = call(
        near_body,
        [part] * SHARDS + stats,
        scratch=[
            pltpu.VMEM((SHARDS, STEPS, MID, depth, 1), f32),
            pltpu.VMEM((SHARDS, STEPS, MID, depth, 1), f32),
            pltpu.VMEM((SHARDS, STEPS, MID, depth, HEAD_DIM), f32),
        ],
        n_scalar=1,
        n_in=SHARDS,
    )(valid_count, *qkv)
    attention = call(
        lambda *refs: far_body(n_groups, *refs),
        [part] * SHARDS,
        n_scalar=1,
        n_in=SHARDS + n_groups + 3 + SHARDS,
        aliases={1 + SHARDS + n_groups + 3 + shard: shard for shard in range(SHARDS)},
    )(valid_count, *qkv, *others, *near[SHARDS:], *near[:SHARDS])
    received = [attention[0]] + [flip(attention[apart], "ctx", apart) for apart in range(1, SHARDS)]
    whole_out = call(
        lambda *refs: gather_body(n_mp, *refs), shape(width, width), n_in=len(out_parts)
    )(*out_parts)
    return call(out_body, shape(rows, width), n_in=SHARDS + 2)(x, *received, whole_out)[None]


def solution(mesh):
    placed = (P("mp", "ctx", None), P(), P(), P("mp", None), P("mp", None), P("mp"))
    return jax.shard_map(
        local, mesh=mesh, in_specs=placed, out_specs=P("mp", "ctx", None), check_vma=False
    )
```

time: 254 us -> 69.1 us (0.27); the launches traced: 250 us -> 68.7 us
  local copies, waits for them, and re-layouts: 107 us -> 5.72 us
  waiting for transfers between devices: 74.3 us -> 17.6 us
  Pallas kernels: 0 us -> 24.2 us
  blocking collectives: 21.1 us -> 0 us
  starting transfers between devices: 2.43 us -> 20.3 us
  matrix products: 17.2 us -> 0 us
  between operations: 14.9 us -> 0.82 us
  other arithmetic: 12.8 us -> 0.11 us
    all_gather x2 -> x0, waiting for transfers between devices: 67.7 us -> none  [the longest x1 67.7 us: local(): lax.all_gather(w_qkv, 'mp', axis=0, tiled=True)]
    slice x115 -> x0, local copies, waits for them, and re-layouts: 57.2 us -> none  [the longest x111 54.9 us: select_rows(): head_rows[head_number].reshape(-1, dilation_rate, head_rows.shape[-1])]
    unnamed x96 -> x46, local copies, waits for them, and re-layouts: 35.4 us -> 3.28 us
    pallas_call x0 -> x6, Pallas kernels: none -> 24.2 us  [the longest x1 7.58 us: local(): call(near_body, [part] * SHARDS + stats, scratch=[pltpu.VMEM((SHARDS, STE...]
    all_gather x2 -> x0, blocking collectives: 21.1 us -> none  [the longest x1 10.6 us: local(): lax.all_gather(slide_keys, 'ctx', axis=1, tiled=True)]
    ppermute x4 -> x19, starting transfers between devices: 2.39 us -> 20.3 us  [flip(): return lax.ppermute(value, axis, pairs)]
    dot_general x8 -> x0, matrix products: 17.2 us -> none  [the longest x3 5.71 us: compute(): jnp.einsum('hqk,hke->hqe', weights.astype(jnp.bfloat16), value_matrix, pr...]
    ppermute x4 -> x19, waiting for transfers between devices: 5.21 us -> 17.6 us  [flip(): return lax.ppermute(value, axis, pairs)]
  transfers between devices with their start and end apart: 6 -> 19, of which waited for: 3 -> 5; matrix products, arithmetic and copies ran while one was open for 54% -> 4% of each run, Pallas kernels for 0% -> 30%
where the time goes in v1:
time: 69.1 us; the launch traced here: 68.7 us
  Pallas kernels  24.2 us (35%)
  starting transfers between devices  20.3 us (29%)
  waiting for transfers between devices  17.6 us (25%)
  local copies, waits for them, and re-layouts  5.72 us (8%)
  between operations  0.82 us (1%)
    ppermute x19, starting transfers between devices, flip(): return lax.ppermute(value, axis, pairs)  20.3 us
    ppermute x19, waiting for transfers between devices, flip(): return lax.ppermute(value, axis, pairs)  17.6 us
    pallas_call x1, Pallas kernels, local(): call(near_body, [part] * SHARDS + stats, scratch=[pltpu.VMEM((SHARDS, STE...  7.58 us
    pallas_call x1, Pallas kernels, local(): call(lambda *refs: qkv_body(n_mp, shared, *refs), [block] * SHARDS + [sha...  3.86 us
    pallas_call x1, Pallas kernels, local(): call(norm_body, [shape(rows, width)] * SHARDS, n_in=SHARDS + 2)  3.74 us
    pallas_call x1, Pallas kernels, local(): call(out_body, shape(rows, width), n_in=SHARDS + 2)(x, *received, whole_out)  3.33 us
    unnamed x46, local copies, waits for them, and re-layouts  3.28 us
    pallas_call x1, Pallas kernels, local(): call(lambda *refs: far_body(n_groups, *refs), [part] * SHARDS, n_scalar=1...  3.23 us
  transfers between devices with their start and end apart: 19, of which 5 were waited for; matrix products, arithmetic and copies ran while one was open for 4% of the time, Pallas kernels for 30%

profile of v1, /device:TPU:0, one launch (start us, length us, event | category | flops | bytes accessed | tf_op | source)
XLA Modules:
  0.0 68.7 jit_solution(13821260832782239790)
XLA Ops:
  0.0 3.0 %collective-permute-start.1 = (bf16[256,768]{1,0:T(8,128)(2,1)}, bf16[256,768]{1,0:T(8,128)(2,1)S(1)}, u32[]{:S(2)}, u32[]{:S(2)}) collective-permute-start(bf16[256,768]{1,0:T(8,128)(2,1)} %bitcast.2), channel_id=1, source_target_pairs={{0,8},{4,12},{8,0},{12,4},{16,24},{20,28},{24,16},{28,20},{1,9},{5... | collective-permute-start | bytes 1179656 | tf_op jit(solution)/shard_map/ppermute | solution.py:41
  3.0 1.2 %constant_dynamic-slice_fusion.4 = (bf16[192,192]{1,0:T(8,128)(2,1)S(1)}, bf16[192,192]{1,0:T(8,128)(2,1)S(1)}, bf16[192,192]{1,0:T(8,128)(2,1)S(1)}) fusion(bf16[192,2304]{1,0:T(8,128)(2,1)} %param.9, s32[]{:T(128)S(6)} %select_n.35, s32[]{:T(128)S(6)} %select_n.37, s32[]{:T(128)S(6)} %select_n.36), kind=kLoop, calls=%fused_computation.5 | loop fusion | bytes 442380 | tf_op jit(solution)/shard_map/dynamic_slice | solution.py:294
  4.4 8.0 %collective-permute-done.1.refs_2_ = bf16[256,768]{1,0:T(8,128)(2,1)S(1)} collective-permute-done((bf16[256,768]{1,0:T(8,128)(2,1)}, bf16[256,768]{1,0:T(8,128)(2,1)S(1)}, u32[]{:S(2)}, u32[]{:S(2)}) %collective-permute-start.1) | collective-permute-done | bytes 393248 | tf_op jit(solution)/shard_map/ppermute | solution.py:41
  12.4 1.9 %collective-permute-start.3 = (bf16[96,576]{1,0:T(8,128)(2,1)S(1)}, bf16[96,576]{1,0:T(8,128)(2,1)S(1)}, u32[]{:S(2)}, u32[]{:S(2)}) collective-permute-start(bf16[96,576]{1,0:T(8,128)(2,1)S(1)} %constant_dynamic-slice_fusion.1), channel_id=1, source_target_pairs={{0,1},{1,0},{2,3},{3,2},{4,5},{5,4},{6,7},{7,6},{8,9},{9,8},{10,11... | collective-permute-start | bytes 331784 | tf_op jit(solution)/shard_map/ppermute | solution.py:41
  14.3 2.6 %collective-permute-start.5 = (bf16[96,576]{1,0:T(8,128)(2,1)S(1)}, bf16[96,576]{1,0:T(8,128)(2,1)S(1)}, u32[]{:S(2)}, u32[]{:S(2)}) collective-permute-start(bf16[96,576]{1,0:T(8,128)(2,1)S(1)} %constant_dynamic-slice_fusion.1), channel_id=1, source_target_pairs={{0,2},{1,3},{2,0},{3,1},{4,6},{5,7},{6,4},{7,5},{8,10},{9,11},{10,... | collective-permute-start | bytes 331784 | tf_op jit(solution)/shard_map/ppermute | solution.py:41
  16.9 0.5 collective-permute-start.13
  17.4 3.3 %collective-permute-done.3.refs_5_ = bf16[96,576]{1,0:T(8,128)(2,1)S(1)} collective-permute-done((bf16[96,576]{1,0:T(8,128)(2,1)S(1)}, bf16[96,576]{1,0:T(8,128)(2,1)S(1)}, u32[]{:S(2)}, u32[]{:S(2)}) %collective-permute-start.3) | collective-permute-done | bytes 110624 | tf_op jit(solution)/shard_map/ppermute | solution.py:41
  20.7 3.1 %collective-permute-start.7 = (bf16[96,576]{1,0:T(8,128)(2,1)S(1)}, bf16[96,576]{1,0:T(8,128)(2,1)S(1)}, u32[]{:S(2)}, u32[]{:S(2)}) collective-permute-start(bf16[96,576]{1,0:T(8,128)(2,1)S(1)} %constant_dynamic-slice_fusion.1), channel_id=1, source_target_pairs={{0,3},{1,2},{2,1},{3,0},{4,7},{5,6},{6,5},{7,4},{8,11},{9,10},{10,... | collective-permute-start | bytes 331784 | tf_op jit(solution)/shard_map/ppermute | solution.py:41
  23.8 1.5 %collective-permute-start.4 = (bf16[96,576]{1,0:T(8,128)(2,1)S(1)}, bf16[96,576]{1,0:T(8,128)(2,1)S(1)}, u32[]{:S(2)}, u32[]{:S(2)}) collective-permute-start(bf16[96,576]{1,0:T(8,128)(2,1)S(1)} %collective-permute-done.3.refs_5_), channel_id=1, source_target_pairs={{0,16},{4,20},{8,24},{12,28},{16,0},{20,4},{24,8},{28,12},{1,17},{... | collective-permute-start | bytes 331784 | tf_op jit(solution)/shard_map/ppermute | solution.py:41
  25.3 3.6 %collective-permute-done.7.refs_9_ = bf16[96,576]{1,0:T(8,128)(2,1)S(1)} collective-permute-done((bf16[96,576]{1,0:T(8,128)(2,1)S(1)}, bf16[96,576]{1,0:T(8,128)(2,1)S(1)}, u32[]{:S(2)}, u32[]{:S(2)}) %collective-permute-start.7) | collective-permute-done | bytes 110624 | tf_op jit(solution)/shard_map/ppermute | solution.py:41
  28.9 1.2 %collective-permute-start.15 = (bf16[96,768]{1,0:T(8,128)(2,1)S(1)}, bf16[96,768]{1,0:T(8,128)(2,1)S(1)}, u32[]{:S(2)}, u32[]{:S(2)}) collective-permute-start(bf16[96,768]{1,0:T(8,128)(2,1)S(1)} %constant_dynamic-slice_fusion), channel_id=1, source_target_pairs={{0,2},{1,3},{2,0},{3,1},{4,6},{5,7},{6,4},{7,5},{8,10},{9,11},{10,... | collective-permute-start | bytes 442376 | tf_op jit(solution)/shard_map/ppermute | solution.py:41
  30.1 0.5 collective-permute-start.17
  30.6 1.5 %collective-permute-start.6 = (bf16[96,576]{1,0:T(8,128)(2,1)S(1)}, bf16[96,576]{1,0:T(8,128)(2,1)S(1)}, u32[]{:S(2)}, u32[]{:S(2)}) collective-permute-start(bf16[96,576]{1,0:T(8,128)(2,1)S(1)} %collective-permute-done.5.refs_7_), channel_id=1, source_target_pairs={{0,16},{4,20},{8,24},{12,28},{16,0},{20,4},{24,8},{28,12},{1,17},{... | collective-permute-start | bytes 331784 | tf_op jit(solution)/shard_map/ppermute | solution.py:41
  32.1 0.5 collective-permute-start.8
  32.7 0.6 reshape.6.refs_4_
  33.3 0.6 reshape.7.refs_5_
  33.9 3.7 %shard_map.64 = (bf16[256,768]{1,0:T(8,128)(2,1)}, bf16[256,768]{1,0:T(8,128)(2,1)}, bf16[256,768]{1,0:T(8,128)(2,1)}, bf16[256,768]{1,0:T(8,128)(2,1)}) custom-call(bf16[256,768]{1,0:T(8,128)(2,1)} %bitcast.4, bf16[256,768]{1,0:T(8,128)(2,1)} %copy-done.3, bf16[256,768]{1,0:T(8,128)(2,1)} %copy-done.2, bf16[256,768]{1,0:T(8,128)(2,1)} %copy-done.4, ...), custom_call_target="tpu_custom_call" | custom-call | tf_op jit(solution)/shard_map/pallas_call | solution.py:322
  37.7 0.6 copy-done.18
  38.3 3.9 %shard_map.65 = (bf16[4,4,16,576]{3,2,1,0:T(8,128)(2,1)}, bf16[4,4,16,576]{3,2,1,0:T(8,128)(2,1)}, bf16[4,4,16,576]{3,2,1,0:T(8,128)(2,1)}, bf16[4,4,16,576]{3,2,1,0:T(8,128)(2,1)}, bf16[3,64,128]{2,1,0:T(8,128)(2,1)}) custom-call(bf16[256,768]{1,0:T(8,128)(2,1)} %get-tuple-element.25.refs_0_, bf16[256,768]{1,0:T(8,128)(2,1)} %get-tuple-element.26.refs_1_, ...), custom_call_target="tpu_custom_call" | custom-call | tf_op jit(solution)/shard_map/pallas_call | solution.py:326
  42.2 1.5 %collective-permute-start.9 = (bf16[3,64,128]{2,1,0:T(8,128)(2,1)}, bf16[3,64,128]{2,1,0:T(8,128)(2,1)S(1)}, u32[]{:S(2)}, u32[]{:S(2)}) collective-permute-start(bf16[3,64,128]{2,1,0:T(8,128)(2,1)} %get-tuple-element.33.refs_5_), channel_id=1, source_target_pairs={{0,16},{4,20},{8,24},{12,28},{16,0},{20,4},{24,8},{28,12},{1,17},{... | collective-permute-start | bytes 147464 | tf_op jit(solution)/shard_map/ppermute | solution.py:41
  43.9 0.3 collective-permute-start.18
  44.9 7.6 %shard_map.66 = (bf16[4,4,16,192]{3,2,1,0:T(8,128)(2,1)}, bf16[4,4,16,192]{3,2,1,0:T(8,128)(2,1)}, bf16[4,4,16,192]{3,2,1,0:T(8,128)(2,1)}, bf16[4,4,16,192]{3,2...) custom-call(s32[1]{0:T(128)S(6)} %copy.15.valid_ref.refs_0_, ...), custom_call_target="tpu_custom_call" | custom-call | tf_op jit(solution)/shard_map/pallas_call | solution.py:341
  52.5 0.6 copy-done.20
  53.1 3.2 %shard_map.67 = (bf16[4,4,16,192]{3,2,1,0:T(8,128)(2,1)}, bf16[4,4,16,192]{3,2,1,0:T(8,128)(2,1)}, bf16[4,4,16,192]{3,2,1,0:T(8,128)(2,1)}, bf16[4,4,16,192]{3,2,1,0:T(8,128)(2,1)}) custom-call(s32[1]{0:T(128)S(6)} %copy.15.valid_ref.refs_0_, ...), custom_call_target="tpu_custom_call", output_to_operand_aliasing={{0}: (10, {}), {1}: (11, {}), {2}: (12, {}), {3}: (13, {})} | custom-call | tf_op jit(solution)/shard_map/pallas_call | solution.py:352
  56.6 1.5 %collective-permute-start.11 = (bf16[4,4,16,192]{3,2,1,0:T(8,128)(2,1)}, bf16[4,4,16,192]{3,2,1,0:T(8,128)(2,1)S(1)}, u32[]{:S(2)}, u32[]{:S(2)}) collective-permute-start(bf16[4,4,16,192]{3,2,1,0:T(8,128)(2,1)} %get-tuple-element.43), channel_id=1, source_target_pairs={{0,8},{4,12},{8,0},{12,4},{16,24},{20,28},{24,16},{28,20},{1,9},{5... | collective-permute-start | bytes 294920 | tf_op jit(solution)/shard_map/ppermute | solution.py:41
  58.3 0.5 copy-done.8
  59.0 0.7 copy-done.10
  59.6 2.4 %shard_map.68.refs_4_ = bf16[768,768]{1,0:T(8,128)(2,1)} custom-call(bf16[192,768]{1,0:T(8,128)(2,1)} %refs_0_.2, bf16[96,768]{1,0:T(8,128)(2,1)} %copy-done.5, bf16[96,768]{1,0:T(8,128)(2,1)} %copy-done.8, bf16[96,768]{1,0:T(8,128)(2,1)} %copy-done.6, bf16[96,768]{1,0:T(8,128)(2,1)} %copy-done.9, bf16[96,768]{1,0:T(8,128)(2,1)} %copy-done.7, ...), custom_call_target="tpu_custom_call" | custom-call | tf_op jit(solution)/shard_map/pallas_call | solution.py:360
  62.0 1.1 %collective-permute-done.11.refs_2_ = bf16[4,4,16,192]{3,2,1,0:T(8,128)(2,1)S(1)} collective-permute-done((bf16[4,4,16,192]{3,2,1,0:T(8,128)(2,1)}, bf16[4,4,16,192]{3,2,1,0:T(8,128)(2,1)S(1)}, u32[]{:S(2)}, u32[]{:S(2)}) %collective-permute-start.11) | collective-permute-done | bytes 98336 | tf_op jit(solution)/shard_map/ppermute | solution.py:41
  63.1 1.6 %collective-permute-done.12.refs_3_ = bf16[4,4,16,192]{3,2,1,0:T(8,128)(2,1)S(1)} collective-permute-done((bf16[4,4,16,192]{3,2,1,0:T(8,128)(2,1)}, bf16[4,4,16,192]{3,2,1,0:T(8,128)(2,1)S(1)}, u32[]{:S(2)}, u32[]{:S(2)}) %collective-permute-start.12) | collective-permute-done | bytes 98336 | tf_op jit(solution)/shard_map/ppermute | solution.py:41
  64.8 0.7 copy-done.13
  65.4 3.3 %shard_map.69 = bf16[256,768]{1,0:T(8,128)(2,1)} custom-call(bf16[256,768]{1,0:T(8,128)(2,1)} %bitcast.5, bf16[4,4,16,192]{3,2,1,0:T(8,128)(2,1)} %get-tuple-element.41.refs_0_, bf16[4,4,16,192]{3,2,1,0:T(8,128)(2,1)} %copy-done.11, bf16[4,4,16,192]{3,2,1,0:T(8,128)(2,1)} %copy-done.12, bf16[4,4,16,192]{3,2,1,0:T(8,128)(2,1)} %copy-done.13, ...), custom_call_target="tpu_custom_call" | custom-call | tf_op jit(solution)/shard_map/pallas_call | solution.py:363
  (64 shorter events, 1.1 us)
Async XLA Ops:
  0.0 16.8 %copy-start.1 = (bf16[192,768]{1,0:T(8,128)(2,1)S(1)}, bf16[192,768]{1,0:T(8,128)(2,1)}, u32[]{:S(2)}) copy-start(bf16[192,768]{1,0:T(8,128)(2,1)} %refs_0_.2) | copy-start | bytes 884740
  0.0 32.7 %copy-start.21 = (f32[768]{0:T(1024)S(1)}, f32[768]{0:T(1024)}, u32[]{:S(2)}) copy-start(f32[768]{0:T(1024)} %param.7) | copy-start | bytes 9220
  0.0 33.3 %copy-start.22 = (f32[768]{0:T(1024)S(1)}, f32[768]{0:T(1024)}, u32[]{:S(2)}) copy-start(f32[768]{0:T(1024)} %param.8) | copy-start | bytes 9220
  0.0 12.3 %collective-permute-start.1 = (bf16[256,768]{1,0:T(8,128)(2,1)}, bf16[256,768]{1,0:T(8,128)(2,1)S(1)}, u32[]{:S(2)}, u32[]{:S(2)}) collective-permute-start(bf16[256,768]{1,0:T(8,128)(2,1)} %bitcast.2), channel_id=1, source_target_pairs={{0,8},{4,12},{8,0},{12,4},{16,24},{20,28},{24,16},{28,20},{1,9},{5... | collective-permute-start | bytes 1179656 | tf_op jit(solution)/shard_map/ppermute | solution.py:41
  3.0 29.1 %collective-permute-start = (bf16[256,768]{1,0:T(8,128)(2,1)}, bf16[256,768]{1,0:T(8,128)(2,1)S(1)}, u32[]{:S(2)}, u32[]{:S(2)}) collective-permute-start(bf16[256,768]{1,0:T(8,128)(2,1)} %bitcast.3), channel_id=1, source_target_pairs={{0,4},{4,0},{8,12},{12,8},{16,20},{20,16},{24,28},{28,24},{1,5},{5... | collective-permute-start | bytes 1179656 | tf_op jit(solution)/shard_map/ppermute | solution.py:41
  4.3 33.3 %copy-start = (bf16[192,576]{1,0:T(8,128)(2,1)}, bf16[192,576]{1,0:T(8,128)(2,1)S(1)}, u32[]{:S(2)}) copy-start(bf16[192,576]{1,0:T(8,128)(2,1)S(1)} %pad_maximum_fusion.refs_4_) | copy-start | bytes 663556
  12.3 21.5 %copy-start.2 = (bf16[256,768]{1,0:T(8,128)(2,1)}, bf16[256,768]{1,0:T(8,128)(2,1)S(1)}, u32[]{:S(2)}) copy-start(bf16[256,768]{1,0:T(8,128)(2,1)S(1)} %collective-permute-done.1.refs_2_) | copy-start | bytes 1179652
  12.3 20.3 %collective-permute-start.2 = (bf16[256,768]{1,0:T(8,128)(2,1)S(1)}, bf16[256,768]{1,0:T(8,128)(2,1)S(1)}, u32[]{:S(2)}, u32[]{:S(2)}) collective-permute-start(bf16[256,768]{1,0:T(8,128)(2,1)S(1)} %collective-permute-done.1.refs_2_), channel_id=1, source_target_pairs={{0,4},{4,0},{8,12},{12,8},{16,20},{20,16},{24,28},{28,24},{1,5},{5... | collective-permute-start | bytes 1179656 | tf_op jit(solution)/shard_map/ppermute | solution.py:41
  12.4 8.3 %collective-permute-start.3 = (bf16[96,576]{1,0:T(8,128)(2,1)S(1)}, bf16[96,576]{1,0:T(8,128)(2,1)S(1)}, u32[]{:S(2)}, u32[]{:S(2)}) collective-permute-start(bf16[96,576]{1,0:T(8,128)(2,1)S(1)} %constant_dynamic-slice_fusion.1), channel_id=1, source_target_pairs={{0,1},{1,0},{2,3},{3,2},{4,5},{5,4},{6,7},{7,6},{8,9},{9,8},{10,11... | collective-permute-start | bytes 331784 | tf_op jit(solution)/shard_map/ppermute | solution.py:41
  14.3 9.5 %collective-permute-start.5 = (bf16[96,576]{1,0:T(8,128)(2,1)S(1)}, bf16[96,576]{1,0:T(8,128)(2,1)S(1)}, u32[]{:S(2)}, u32[]{:S(2)}) collective-permute-start(bf16[96,576]{1,0:T(8,128)(2,1)S(1)} %constant_dynamic-slice_fusion.1), channel_id=1, source_target_pairs={{0,2},{1,3},{2,0},{3,1},{4,6},{5,7},{6,4},{7,5},{8,10},{9,11},{10,... | collective-permute-start | bytes 331784 | tf_op jit(solution)/shard_map/ppermute | solution.py:41
  16.9 13.3 %collective-permute-start.13 = (bf16[96,768]{1,0:T(8,128)(2,1)S(1)}, bf16[96,768]{1,0:T(8,128)(2,1)S(1)}, u32[]{:S(2)}, u32[]{:S(2)}) collective-permute-start(bf16[96,768]{1,0:T(8,128)(2,1)S(1)} %constant_dynamic-slice_fusion), channel_id=1, source_target_pairs={{0,1},{1,0},{2,3},{3,2},{4,5},{5,4},{6,7},{7,6},{8,9},{9,8},{10,11... | collective-permute-start | bytes 442376 | tf_op jit(solution)/shard_map/ppermute | solution.py:41
  20.7 17.0 %copy-start.14 = (bf16[96,576]{1,0:T(8,128)(2,1)}, bf16[96,576]{1,0:T(8,128)(2,1)S(1)}, u32[]{:S(2)}) copy-start(bf16[96,576]{1,0:T(8,128)(2,1)S(1)} %collective-permute-done.3.refs_5_) | copy-start | bytes 331780
  20.7 8.2 %collective-permute-start.7 = (bf16[96,576]{1,0:T(8,128)(2,1)S(1)}, bf16[96,576]{1,0:T(8,128)(2,1)S(1)}, u32[]{:S(2)}, u32[]{:S(2)}) collective-permute-start(bf16[96,576]{1,0:T(8,128)(2,1)S(1)} %constant_dynamic-slice_fusion.1), channel_id=1, source_target_pairs={{0,3},{1,2},{2,1},{3,0},{4,7},{5,6},{6,5},{7,4},{8,11},{9,10},{10,... | collective-permute-start | bytes 331784 | tf_op jit(solution)/shard_map/ppermute | solution.py:41
  23.8 13.9 %copy-start.15 = (bf16[96,576]{1,0:T(8,128)(2,1)}, bf16[96,576]{1,0:T(8,128)(2,1)S(1)}, u32[]{:S(2)}) copy-start(bf16[96,576]{1,0:T(8,128)(2,1)S(1)} %collective-permute-done.5.refs_7_) | copy-start | bytes 331780
  23.8 6.8 %collective-permute-start.4 = (bf16[96,576]{1,0:T(8,128)(2,1)S(1)}, bf16[96,576]{1,0:T(8,128)(2,1)S(1)}, u32[]{:S(2)}, u32[]{:S(2)}) collective-permute-start(bf16[96,576]{1,0:T(8,128)(2,1)S(1)} %collective-permute-done.3.refs_5_), channel_id=1, source_target_pairs={{0,16},{4,20},{8,24},{12,28},{16,0},{20,4},{24,8},{28,12},{1,17},{... | collective-permute-start | bytes 331784 | tf_op jit(solution)/shard_map/ppermute | solution.py:41
  28.9 8.8 %copy-start.16 = (bf16[96,576]{1,0:T(8,128)(2,1)}, bf16[96,576]{1,0:T(8,128)(2,1)S(1)}, u32[]{:S(2)}) copy-start(bf16[96,576]{1,0:T(8,128)(2,1)S(1)} %collective-permute-done.7.refs_9_) | copy-start | bytes 331780
  28.9 14.8 %collective-permute-start.15 = (bf16[96,768]{1,0:T(8,128)(2,1)S(1)}, bf16[96,768]{1,0:T(8,128)(2,1)S(1)}, u32[]{:S(2)}, u32[]{:S(2)}) collective-permute-start(bf16[96,768]{1,0:T(8,128)(2,1)S(1)} %constant_dynamic-slice_fusion), channel_id=1, source_target_pairs={{0,2},{1,3},{2,0},{3,1},{4,6},{5,7},{6,4},{7,5},{8,10},{9,11},{10,... | collective-permute-start | bytes 442376 | tf_op jit(solution)/shard_map/ppermute | solution.py:41
  30.1 26.2 %copy-start.5 = (bf16[96,768]{1,0:T(8,128)(2,1)}, bf16[96,768]{1,0:T(8,128)(2,1)S(1)}, u32[]{:S(2)}) copy-start(bf16[96,768]{1,0:T(8,128)(2,1)S(1)} %collective-permute-done.13.refs_1_) | copy-start | bytes 442372
  30.1 13.8 %collective-permute-start.17 = (bf16[96,768]{1,0:T(8,128)(2,1)S(1)}, bf16[96,768]{1,0:T(8,128)(2,1)S(1)}, u32[]{:S(2)}, u32[]{:S(2)}) collective-permute-start(bf16[96,768]{1,0:T(8,128)(2,1)S(1)} %constant_dynamic-slice_fusion), channel_id=1, source_target_pairs={{0,3},{1,2},{2,1},{3,0},{4,7},{5,6},{6,5},{7,4},{8,11},{9,10},{10,... | collective-permute-start | bytes 442376 | tf_op jit(solution)/shard_map/ppermute | solution.py:41
  30.6 7.1 %copy-start.17 = (bf16[96,576]{1,0:T(8,128)(2,1)}, bf16[96,576]{1,0:T(8,128)(2,1)S(1)}, u32[]{:S(2)}) copy-start(bf16[96,576]{1,0:T(8,128)(2,1)S(1)} %collective-permute-done.4.refs_6_) | copy-start | bytes 331780
  30.6 7.0 %collective-permute-start.6 = (bf16[96,576]{1,0:T(8,128)(2,1)S(1)}, bf16[96,576]{1,0:T(8,128)(2,1)S(1)}, u32[]{:S(2)}, u32[]{:S(2)}) collective-permute-start(bf16[96,576]{1,0:T(8,128)(2,1)S(1)} %collective-permute-done.5.refs_7_), channel_id=1, source_target_pairs={{0,16},{4,20},{8,24},{12,28},{16,0},{20,4},{24,8},{28,12},{1,17},{... | collective-permute-start | bytes 331784 | tf_op jit(solution)/shard_map/ppermute | solution.py:41
  32.1 5.5 %collective-permute-start.8 = (bf16[96,576]{1,0:T(8,128)(2,1)S(1)}, bf16[96,576]{1,0:T(8,128)(2,1)S(1)}, u32[]{:S(2)}, u32[]{:S(2)}) collective-permute-start(bf16[96,576]{1,0:T(8,128)(2,1)S(1)} %collective-permute-done.7.refs_9_), channel_id=1, source_target_pairs={{0,16},{4,20},{8,24},{12,28},{16,0},{20,4},{24,8},{28,12},{1,17},{... | collective-permute-start | bytes 331784 | tf_op jit(solution)/shard_map/ppermute | solution.py:41
  32.7 25.4 %collective-permute-start.14 = (bf16[96,768]{1,0:T(8,128)(2,1)S(1)}, bf16[96,768]{1,0:T(8,128)(2,1)S(1)}, u32[]{:S(2)}, u32[]{:S(2)}) collective-permute-start(bf16[96,768]{1,0:T(8,128)(2,1)S(1)} %collective-permute-done.13.refs_1_), channel_id=1, source_target_pairs={{0,4},{4,0},{8,12},{12,8},{16,20},{20,16},{24,28},{28,24},{1,5},{5... | collective-permute-start | bytes 442376 | tf_op jit(solution)/shard_map/ppermute | solution.py:41
  42.2 10.3 %collective-permute-start.9 = (bf16[3,64,128]{2,1,0:T(8,128)(2,1)}, bf16[3,64,128]{2,1,0:T(8,128)(2,1)S(1)}, u32[]{:S(2)}, u32[]{:S(2)}) collective-permute-start(bf16[3,64,128]{2,1,0:T(8,128)(2,1)} %get-tuple-element.33.refs_5_), channel_id=1, source_target_pairs={{0,16},{4,20},{8,24},{12,28},{16,0},{20,4},{24,8},{28,12},{1,17},{... | collective-permute-start | bytes 147464 | tf_op jit(solution)/shard_map/ppermute | solution.py:41
  43.7 12.6 %copy-start.6 = (bf16[96,768]{1,0:T(8,128)(2,1)}, bf16[96,768]{1,0:T(8,128)(2,1)S(1)}, u32[]{:S(2)}) copy-start(bf16[96,768]{1,0:T(8,128)(2,1)S(1)} %collective-permute-done.15.refs_3_) | copy-start | bytes 442372
  43.7 14.6 %collective-permute-start.16 = (bf16[96,768]{1,0:T(8,128)(2,1)S(1)}, bf16[96,768]{1,0:T(8,128)(2,1)S(1)}, u32[]{:S(2)}, u32[]{:S(2)}) collective-permute-start(bf16[96,768]{1,0:T(8,128)(2,1)S(1)} %collective-permute-done.15.refs_3_), channel_id=1, source_target_pairs={{0,4},{4,0},{8,12},{12,8},{16,20},{20,16},{24,28},{28,24},{1,5},{5... | collective-permute-start | bytes 442376 | tf_op jit(solution)/shard_map/ppermute | solution.py:41
  43.9 12.4 %copy-start.7 = (bf16[96,768]{1,0:T(8,128)(2,1)}, bf16[96,768]{1,0:T(8,128)(2,1)S(1)}, u32[]{:S(2)}) copy-start(bf16[96,768]{1,0:T(8,128)(2,1)S(1)} %collective-permute-done.17.refs_5_) | copy-start | bytes 442372
  43.9 14.4 %collective-permute-start.18 = (bf16[96,768]{1,0:T(8,128)(2,1)S(1)}, bf16[96,768]{1,0:T(8,128)(2,1)S(1)}, u32[]{:S(2)}, u32[]{:S(2)}) collective-permute-start(bf16[96,768]{1,0:T(8,128)(2,1)S(1)} %collective-permute-done.17.refs_5_), channel_id=1, source_target_pairs={{0,4},{4,0},{8,12},{12,8},{16,20},{20,16},{24,28},{28,24},{1,5},{5... | collective-permute-start | bytes 442376 | tf_op jit(solution)/shard_map/ppermute | solution.py:41
  56.3 5.7 %collective-permute-start.10 = (bf16[4,4,16,192]{3,2,1,0:T(8,128)(2,1)}, bf16[4,4,16,192]{3,2,1,0:T(8,128)(2,1)S(1)}, u32[]{:S(2)}, u32[]{:S(2)}) collective-permute-start(bf16[4,4,16,192]{3,2,1,0:T(8,128)(2,1)} %get-tuple-element.42), channel_id=1, source_target_pairs={{0,4},{4,0},{8,12},{12,8},{16,20},{20,16},{24,28},{28,24},{1,5},{5... | collective-permute-start | bytes 294920 | tf_op jit(solution)/shard_map/ppermute | solution.py:41
  56.6 6.5 %collective-permute-start.11 = (bf16[4,4,16,192]{3,2,1,0:T(8,128)(2,1)}, bf16[4,4,16,192]{3,2,1,0:T(8,128)(2,1)S(1)}, u32[]{:S(2)}, u32[]{:S(2)}) collective-permute-start(bf16[4,4,16,192]{3,2,1,0:T(8,128)(2,1)} %get-tuple-element.43), channel_id=1, source_target_pairs={{0,8},{4,12},{8,0},{12,4},{16,24},{20,28},{24,16},{28,20},{1,9},{5... | collective-permute-start | bytes 294920 | tf_op jit(solution)/shard_map/ppermute | solution.py:41
  58.1 6.6 %collective-permute-start.12 = (bf16[4,4,16,192]{3,2,1,0:T(8,128)(2,1)}, bf16[4,4,16,192]{3,2,1,0:T(8,128)(2,1)S(1)}, u32[]{:S(2)}, u32[]{:S(2)}) collective-permute-start(bf16[4,4,16,192]{3,2,1,0:T(8,128)(2,1)} %get-tuple-element.44), channel_id=1, source_target_pairs={{0,12},{4,8},{8,4},{12,0},{16,28},{20,24},{24,20},{28,16},{1,13},{... | collective-permute-start | bytes 294920 | tf_op jit(solution)/shard_map/ppermute | solution.py:41
  62.0 2.7 %copy-start.11 = (bf16[4,4,16,192]{3,2,1,0:T(8,128)(2,1)}, bf16[4,4,16,192]{3,2,1,0:T(8,128)(2,1)S(1)}, u32[]{:S(2)}) copy-start(bf16[4,4,16,192]{3,2,1,0:T(8,128)(2,1)S(1)} %collective-permute-done.10.refs_1_) | copy-start | bytes 294916
  (10 other events, 9.2 us)

commit v2 on v1

v2 whole, which is shorter than its diff:
```python
import math

import jax
import jax.numpy as jnp
from jax import lax
from jax.experimental import pallas as pl
from jax.experimental.pallas import tpu as pltpu
from jax.sharding import PartitionSpec as P

HEADS = 12
HEAD_DIM = 64
MID = 4
WIDE = 16
SHARDS = 4
STEPS = WIDE // MID
GROUP_HEADS = HEADS // SHARDS
GROUP_WIDTH = GROUP_HEADS * HEAD_DIM
NEG_FILL = -1e30
SCALE = math.log2(math.e) / math.sqrt(HEAD_DIM)
VMEM_LIMIT = 24 * 1024 * 1024
LANES = 128


def call(body, out_shape, scratch=(), n_scalar=0, n_in=0, micros=1):
    specs = [pl.BlockSpec(memory_space=pltpu.SMEM)] * n_scalar + [
        pl.BlockSpec(memory_space=pltpu.VMEM)
    ] * n_in
    outs = [pl.BlockSpec(memory_space=pltpu.VMEM) for _ in out_shape]
    return pl.pallas_call(
        body,
        out_shape=out_shape,
        in_specs=specs,
        out_specs=outs,
        scratch_shapes=list(scratch),
        cost_estimate=pl.CostEstimate(
            flops=micros * 1_000_000_000, transcendentals=0, bytes_accessed=micros * 3_000_000
        ),
        compiler_params=pltpu.CompilerParams(vmem_limit_bytes=VMEM_LIMIT),
    )


def near(value):
    return pltpu.with_memory_space_constraint(value, pltpu.VMEM)


def flip(value, axis, mask):
    pairs = [(source, source ^ mask) for source in range(lax.axis_size(axis))]
    return near(lax.ppermute(value, axis, pairs))


def after(value, *earlier):
    return lax.optimization_barrier((value, *earlier))[0]


def place_of(order, rows):
    depth = rows // WIDE
    return order % depth * WIDE + order // depth % STEPS * MID + order // (STEPS * depth)


def to_order(rows):
    new = lax.broadcasted_iota(jnp.int32, (rows, rows), 0)
    old = lax.broadcasted_iota(jnp.int32, (rows, rows), 1)
    return (old == place_of(new, rows)).astype(jnp.bfloat16)


def to_position(rows):
    new = lax.broadcasted_iota(jnp.int32, (rows, rows), 0)
    old = lax.broadcasted_iota(jnp.int32, (rows, rows), 1)
    return (new == place_of(old, rows)).astype(jnp.bfloat16)


def product(left, right, left_axis=1, right_axis=0):
    return lax.dot_general(
        left,
        right,
        (((left_axis,), (right_axis,)), ((), ())),
        preferred_element_type=jnp.float32,
    )


def norm_body(*refs):
    count = len(refs) // 2 - 1
    x_refs, gain_ref, bias_ref, out_refs = refs[:count], refs[count], refs[count + 1], refs[count + 2 :]
    order = to_order(x_refs[0].shape[0])
    gain = gain_ref[...][None, :]
    bias = bias_ref[...][None, :]
    for x_ref, out_ref in zip(x_refs, out_refs):
        floats = x_ref[...].astype(jnp.float32)
        centred = floats - jnp.mean(floats, axis=-1, keepdims=True)
        spread = jnp.mean(centred * centred, axis=-1, keepdims=True)
        normed = (centred * lax.rsqrt(spread + 1e-05) * gain + bias).astype(jnp.bfloat16)
        out_ref[...] = product(order, normed).astype(jnp.bfloat16)


def group_indices():
    shard = lax.axis_index("ctx")
    return shard % SHARDS, shard // SHARDS


def head_slices(index):
    return [
        slice(part * GROUP_WIDTH + index * HEAD_DIM, part * GROUP_WIDTH + (index + 1) * HEAD_DIM)
        for part in range(3)
    ]


def wide_rows(head, rows):
    depth = rows // WIDE
    start = head % MID * (STEPS * depth) + head % WIDE // MID * depth
    return pl.ds(pl.multiple_of(start, depth), depth)


def middle_rows(head, rows):
    count = rows // MID
    return pl.ds(pl.multiple_of(head % MID * count, count), count)


def qkv_body(n_mp, shared, *refs):
    normed_refs, refs = refs[:SHARDS], refs[SHARDS:]
    n_weights = 1 + (2 if shared else 1) * (n_mp - 1)
    weight_refs, refs = refs[:n_weights], refs[n_weights:]
    out_refs, sent_ref, whole_ref = refs[:SHARDS], refs[SHARDS], refs[SHARDS + 1]
    member, group = group_indices()
    mp_index = lax.axis_index("mp")
    rows = weight_refs[0].shape[0]

    def put(ref, source, offset):
        start = pl.multiple_of(source * rows + offset, 16)
        whole_ref[pl.ds(start, ref.shape[0]), :] = ref[...]

    put(weight_refs[0], mp_index, 0)
    for apart in range(1, n_mp):
        if shared:
            half = group % 2
            put(weight_refs[2 * apart - 1], mp_index ^ apart, half * (rows // 2))
            put(weight_refs[2 * apart], mp_index ^ apart, (1 - half) * (rows // 2))
        else:
            put(weight_refs[apart], mp_index ^ apart, 0)
    shard_rows = out_refs[0].shape[0]
    depth = shard_rows // WIDE
    for normed_ref, out_ref in zip(normed_refs, out_refs):
        out_ref[...] = product(normed_ref[...], whole_ref[...]).astype(jnp.bfloat16)
    for index in range(GROUP_HEADS):
        _, key_at, value_at = head_slices(index)
        taken = wide_rows(member * GROUP_HEADS + index, shard_rows)
        for shard, out_ref in enumerate(out_refs):
            sent_ref[index, shard * depth : (shard + 1) * depth, :] = jnp.concatenate(
                [out_ref[taken, key_at], out_ref[taken, value_at]], axis=1
            )


def branch(query, key, value, bias):
    score = product(key, query, 1, 1) * SCALE + bias
    largest = jnp.max(score, axis=0, keepdims=True)
    weight = jnp.exp2(score - largest)
    total = jnp.sum(weight, axis=0, keepdims=True)
    return largest, total, product(value, weight.astype(jnp.bfloat16), 0, 0)


def key_bias(position, valid):
    return jnp.where(position < valid, 0.0, NEG_FILL).astype(jnp.float32)


def merge(one, two):
    top = jnp.maximum(one[0], two[0])
    left = jnp.exp2(one[0] - top)
    right = jnp.exp2(two[0] - top)
    return top, left * one[1] + right * two[1], left * one[2] + right * two[2]


def near_body(valid_ref, *refs):
    qkv_refs, (max_ref, sum_ref, num_ref) = refs[:SHARDS], refs[SHARDS:]
    member, group = group_indices()
    valid = valid_ref[0]
    rows = qkv_refs[0].shape[0]
    count = rows // MID
    bases = [(group * SHARDS + (member ^ apart)) * rows for apart in range(SHARDS)]
    place = place_of(lax.broadcasted_iota(jnp.int32, (rows, LANES), 0), rows)
    lane = lax.broadcasted_iota(jnp.int32, (1, rows), 1)

    def widen(bias):
        return jnp.concatenate([bias] * (rows // LANES), axis=1)

    for shard, ref in enumerate(qkv_refs):
        bias = widen(key_bias(place + bases[shard], valid))
        for index in range(GROUP_HEADS):
            query_at, key_at, value_at = head_slices(index)
            stats = branch(ref[:, query_at], ref[:, key_at], ref[:, value_at], bias)
            max_ref[index, shard], sum_ref[index, shard], num_ref[index, shard] = stats
    entry = lax.broadcasted_iota(jnp.int32, (count, LANES), 0)
    depth = rows // WIDE
    for index in range(GROUP_HEADS):
        head = member * GROUP_HEADS + index
        taken = middle_rows(head, rows)
        query, key, value = (
            jnp.concatenate([ref[taken, at] for ref in qkv_refs], axis=0)
            for at in head_slices(index)
        )
        position = entry % depth * WIDE + entry // depth * MID + head % MID
        bias = widen(
            jnp.concatenate([key_bias(position + base, valid) for base in bases], axis=0)
        )
        middle = branch(query, key, value, bias)
        inside = lane // count == head % MID
        for shard in range(SHARDS):
            largest, total, number = (
                jnp.concatenate([entry[:, shard * count : (shard + 1) * count]] * MID, axis=1)
                for entry in middle
            )
            merged = merge(
                (max_ref[index, shard], sum_ref[index, shard], num_ref[index, shard]),
                (jnp.where(inside, largest, NEG_FILL), total, number),
            )
            max_ref[index, shard], sum_ref[index, shard], num_ref[index, shard] = merged


def far_body(n_groups, valid_ref, *refs):
    qkv_refs, refs = refs[:SHARDS], refs[SHARDS:]
    sent_refs, refs = refs[:n_groups], refs[n_groups:]
    (max_ref, sum_ref, num_ref), out_refs = refs[:3], refs[3:]
    member, group = group_indices()
    valid = valid_ref[0]
    rows = qkv_refs[0].shape[0]
    depth = rows // WIDE
    count = SHARDS * depth
    entry = lax.broadcasted_iota(jnp.int32, (count, count), 0)
    lane = lax.broadcasted_iota(jnp.int32, (1, rows), 1)
    for index in range(GROUP_HEADS):
        head = member * GROUP_HEADS + index
        taken = wide_rows(head, rows)
        query_at = head_slices(index)[0]
        query = jnp.concatenate([ref[taken, query_at] for ref in qkv_refs], axis=0)
        bias = jnp.concatenate(
            [
                key_bias(
                    ((group ^ apart) * SHARDS + (member ^ (entry // depth))) * rows
                    + entry % depth * WIDE
                    + head,
                    valid,
                )
                for apart in range(n_groups)
            ],
            axis=0,
        )
        both = jnp.concatenate([ref[index] for ref in sent_refs], axis=0)
        stats = branch(query, both[:, :HEAD_DIM], both[:, HEAD_DIM:], bias)
        stacked = jnp.concatenate(
            [stats[2], jnp.broadcast_to(stats[0], (8, count)), jnp.broadcast_to(stats[1], (8, count))],
            axis=0,
        )
        stacked = jnp.concatenate(
            [stacked, jnp.zeros((stacked.shape[0], LANES - count), jnp.float32)], axis=1
        )
        block = head % MID * STEPS + head % WIDE // MID
        inside = lane // depth == block
        for shard, out_ref in enumerate(out_refs):
            shift = (block * depth - shard * depth + LANES) % LANES
            moved = jnp.concatenate(
                [pltpu.roll(stacked, shift, 1)] * (rows // LANES), axis=1
            )
            _, total, number = merge(
                (max_ref[index, shard], sum_ref[index, shard], num_ref[index, shard]),
                (
                    jnp.where(inside, moved[HEAD_DIM : HEAD_DIM + 1], NEG_FILL),
                    moved[HEAD_DIM + 8 : HEAD_DIM + 9],
                    moved[:HEAD_DIM],
                ),
            )
            base = (group * SHARDS + (member ^ shard)) * rows
            attention = jnp.where(
                base + place_of(lane, rows) < valid, number * (1.0 / total), 0.0
            )
            out_ref[index * HEAD_DIM : (index + 1) * HEAD_DIM, :] = attention.astype(jnp.bfloat16)


def gather_body(n_mp, *refs):
    own_ref, pair_refs, out_ref = refs[0], refs[1:-1], refs[-1]
    mp_index = lax.axis_index("mp")
    rows = own_ref.shape[0]
    out_ref[pl.ds(pl.multiple_of(mp_index * rows, 16), rows), :] = own_ref[...]
    for apart in range(1, n_mp):
        if len(pair_refs) == n_mp - 1:
            start = pl.multiple_of((mp_index ^ apart) * rows, 16)
            out_ref[pl.ds(start, rows), :] = pair_refs[apart - 1][...]
        else:
            core = lax.axis_index("ctx") % 2
            half = rows // 2
            for turn in range(2):
                start = (mp_index ^ apart) * rows + (core ^ turn) * half
                out_ref[pl.ds(pl.multiple_of(start, 16), half), :] = pair_refs[
                    2 * (apart - 1) + turn
                ][...]


def out_body(x_ref, *refs):
    part_refs, weight_ref, out_ref = refs[:SHARDS], refs[SHARDS], refs[SHARDS + 1]
    rows = x_ref.shape[0]
    member, _ = group_indices()
    order = to_position(rows)
    update = jnp.zeros(x_ref.shape, jnp.float32)
    for apart, ref in enumerate(part_refs):
        part = product(order, ref[...], 1, 1).astype(jnp.bfloat16)
        start = pl.multiple_of((member ^ apart) * GROUP_WIDTH, GROUP_WIDTH)
        update = update + product(part, weight_ref[pl.ds(start, GROUP_WIDTH), :])
    out_ref[...] = (x_ref[...].astype(jnp.float32) + update).astype(jnp.bfloat16)


def local(tile_embeds, norm_gain, norm_bias, w_qkv, w_out, valid_count):
    x = tile_embeds[0]
    rows, width = x.shape
    n_mp = lax.axis_size("mp")
    n_groups = lax.axis_size("ctx") // SHARDS
    depth = rows // WIDE
    weight_rows = w_qkv.shape[0]
    member, group = group_indices()
    bf16, f32 = jnp.bfloat16, jnp.float32
    shape = pltpu.VMEM

    def columns(first, count):
        return jnp.concatenate(
            [
                lax.dynamic_slice(
                    w_qkv, (first, part * width + member * GROUP_WIDTH), (count, GROUP_WIDTH)
                )
                for part in range(3)
            ],
            axis=1,
        )

    mine = columns(0, weight_rows)
    shared = n_groups % 2 == 0 and weight_rows % 32 == 0
    weights = [near(mine)]
    if shared:
        half = weight_rows // 2
        piece = columns(group % 2 * half, half)
        direct = [flip(piece, "mp", apart) for apart in range(1, n_mp)]
        for value in direct:
            weights += [value, flip(value, "ctx", SHARDS)]
    else:
        direct = [flip(mine, "mp", apart) for apart in range(1, n_mp)]
        weights += direct

    x_pair = flip(x, "ctx", 1)
    x_far = flip(x, "ctx", 2)
    chunks = [near(x), x_pair, x_far, flip(after(x_far, direct[0]), "ctx", 1)]

    out_parts = [near(w_out)]
    if weight_rows % 32 == 0:
        half = weight_rows // 2
        piece = lax.dynamic_slice(w_out, (member % 2 * half, 0), (half, width))
        for apart in range(1, n_mp):
            received = flip(after(piece, *direct), "mp", apart)
            out_parts += [received, flip(received, "ctx", 1)]
    else:
        out_parts += [flip(after(w_out, *direct), "mp", apart) for apart in range(1, n_mp)]

    normed = []
    for pair in (chunks[:2], chunks[2:]):
        normed += call(norm_body, [shape((rows, width), bf16)] * 2, n_in=4, micros=2)(
            *pair, near(norm_gain), near(norm_bias)
        )
    *qkv, sent = call(
        lambda *refs: qkv_body(n_mp, shared, *refs),
        [shape((rows, 3 * GROUP_WIDTH), bf16)] * SHARDS
        + [shape((GROUP_HEADS, SHARDS * depth, 2 * HEAD_DIM), bf16)],
        scratch=[pltpu.VMEM((n_mp * weight_rows, 3 * GROUP_WIDTH), bf16)],
        n_in=SHARDS + len(weights),
        micros=3,
    )(*normed, *weights)
    others = [sent] + [flip(sent, "ctx", SHARDS * apart) for apart in range(1, n_groups)]
    stats = call(
        near_body,
        [
            shape((GROUP_HEADS, SHARDS, 1, rows), f32),
            shape((GROUP_HEADS, SHARDS, 1, rows), f32),
            shape((GROUP_HEADS, SHARDS, HEAD_DIM, rows), f32),
        ],
        n_scalar=1,
        n_in=SHARDS,
        micros=5,
    )(valid_count, *qkv)
    attention = call(
        lambda *refs: far_body(n_groups, *refs),
        [shape((GROUP_WIDTH, rows), bf16)] * SHARDS,
        n_scalar=1,
        n_in=SHARDS + n_groups + 3,
        micros=2,
    )(valid_count, *qkv, *others, *stats)
    received = [attention[0]] + [flip(attention[apart], "ctx", apart) for apart in range(1, SHARDS)]
    (whole_out,) = call(
        lambda *refs: gather_body(n_mp, *refs), [shape((width, width), bf16)], n_in=len(out_parts)
    )(*out_parts)
    (out,) = call(
        out_body, [jax.ShapeDtypeStruct((rows, width), bf16)], n_in=SHARDS + 2, micros=2
    )(near(x), *received, whole_out)
    return out[None]


def solution(mesh):
    placed = (P("mp", "ctx", None), P(), P(), P("mp", None), P("mp", None), P("mp"))
    return jax.shard_map(
        local, mesh=mesh, in_specs=placed, out_specs=P("mp", "ctx", None), check_vma=False
    )
```

time: 69.1 us -> 52.1 us (0.75)
  Pallas kernels: 24.2 us -> 10.3 us
  local copies, waits for them, and re-layouts: 5.72 us -> 2.34 us
  waiting for transfers between devices: 17.6 us -> 18.3 us
    pallas_call x6 -> x7, Pallas kernels: 24.2 us -> 10.3 us  [the longest x1 4.57 us: local(): call(near_body, [shape((GROUP_HEADS, SHARDS, 1, rows), f32), shape((GROUP...]
    unnamed x46 -> x8, local copies, waits for them, and re-layouts: 3.28 us -> 0.01 us
    reshape x2 -> x0, local copies, waits for them, and re-layouts: 1.21 us -> none  [the longest x1 0.63 us: local(): norm_gain.reshape(1, width)]
    dynamic_slice x2, local copies, waits for them, and re-layouts: 1.22 us -> 2.31 us  [columns(): lax.dynamic_slice(w_qkv, (first, part * width + member * GROUP_WIDTH), (c...]
  transfers between devices with their start and end apart: 19 -> 19, of which waited for: 5 -> 7; matrix products, arithmetic and copies ran while one was open for 4% -> 5% of each run, Pallas kernels for 30% -> 17%
where the time goes in v2:
time: 52.1 us; the launch traced here: 51.9 us
  starting transfers between devices  20 us (38%)
  waiting for transfers between devices  18.3 us (35%)
  Pallas kernels  10.3 us (20%)
  local copies, waits for them, and re-layouts  2.34 us (4%)
  between operations  0.78 us (1%)
    ppermute x19, starting transfers between devices, flip(): return near(lax.ppermute(value, axis, pairs))  20 us
    ppermute x19, waiting for transfers between devices, flip(): return near(lax.ppermute(value, axis, pairs))  18.3 us
    pallas_call x1, Pallas kernels, local(): call(near_body, [shape((GROUP_HEADS, SHARDS, 1, rows), f32), shape((GROUP...  4.57 us
    dynamic_slice x2, local copies, waits for them, and re-layouts, columns(): lax.dynamic_slice(w_qkv, (first, part * width + member * GROUP_WIDTH), (c...  2.31 us
    pallas_call x2, Pallas kernels, local(): call(norm_body, [shape((rows, width), bf16)] * 2, n_in=4, micros=2)  1.74 us
    pallas_call x1, Pallas kernels, local(): call(out_body, [jax.ShapeDtypeStruct((rows, width), bf16)], n_in=SHARDS +...  1.73 us
    pallas_call x1, Pallas kernels, local(): call(lambda *refs: qkv_body(n_mp, shared, *refs), [shape((rows, 3 * GROUP...  1.59 us
  transfers between devices with their start and end apart: 19, of which 7 were waited for; matrix products, arithmetic and copies ran while one was open for 5% of the time, Pallas kernels for 17%

profile of v2, /device:TPU:0, one launch (start us, length us, event | category | flops | bytes accessed | tf_op | source)
XLA Modules:
  0.0 51.9 jit_solution(14349211505622965364)
XLA Ops:
  0.0 3.0 %collective-permute-start.1 = (bf16[256,768]{1,0:T(8,128)(2,1)}, bf16[256,768]{1,0:T(8,128)(2,1)S(1)}, u32[]{:S(2)}, u32[]{:S(2)}) collective-permute-start(bf16[256,768]{1,0:T(8,128)(2,1)} %bitcast.2), channel_id=1, source_target_pairs={{0,8},{4,12},{8,0},{12,4},{16,24},{20,28},{24,16},{28,20},{1,9},{5... | collective-permute-start | bytes 1179656 | tf_op jit(solution)/shard_map/ppermute | solution.py:48
  3.0 1.1 %fusion = (bf16[96,192]{1,0:T(8,128)(2,1)S(1)}, bf16[96,192]{1,0:T(8,128)(2,1)S(1)}, bf16[96,192]{1,0:T(8,128)(2,1)S(1)}) fusion(bf16[192,2304]{1,0:T(8,128)(2,1)} %param.9, s32[]{:T(128)S(6)} %select_n.41, s32[]{:T(128)S(6)} %select_n.43, s32[]{:T(128)S(6)} %select_n.45, s32[]{:T(128)S(6)} %select_n.44), kind=kLoop, calls=%fused_computation.6 | loop fusion | bytes 221200 | tf_op jit(solution)/shard_map/dynamic_slice | solution.py:322
  4.1 0.1 pad_maximum_fusion.1
  4.2 1.6 %collective-permute-start.2 = (bf16[96,576]{1,0:T(8,128)(2,1)S(1)}, bf16[96,576]{1,0:T(8,128)(2,1)S(1)}, u32[]{:S(2)}, u32[]{:S(2)}) collective-permute-start(bf16[96,576]{1,0:T(8,128)(2,1)S(1)} %pad_maximum_fusion.1), channel_id=1, source_target_pairs={{0,1},{1,0},{2,3},{3,2},{4,5},{5,4},{6,7},{7,6},{8,9},{9,8},{10,11... | collective-permute-start | bytes 331784 | tf_op jit(solution)/shard_map/ppermute | solution.py:48
  5.9 2.6 %collective-permute-start.5 = (bf16[96,576]{1,0:T(8,128)(2,1)S(1)}, bf16[96,576]{1,0:T(8,128)(2,1)S(1)}, u32[]{:S(2)}, u32[]{:S(2)}) collective-permute-start(bf16[96,576]{1,0:T(8,128)(2,1)S(1)} %pad_maximum_fusion.1), channel_id=1, source_target_pairs={{0,2},{1,3},{2,0},{3,1},{4,6},{5,7},{6,4},{7,5},{8,10},{9,11},{10,... | collective-permute-start | bytes 331784 | tf_op jit(solution)/shard_map/ppermute | solution.py:48
  8.4 0.2 collective-permute-start.7
  9.3 1.2 %constant_dynamic-slice_fusion.3 = (bf16[192,192]{1,0:T(8,128)(2,1)S(1)}, bf16[192,192]{1,0:T(8,128)(2,1)S(1)}, bf16[192,192]{1,0:T(8,128)(2,1)S(1)}) fusion(bf16[192,2304]{1,0:T(8,128)(2,1)} %param.9, s32[]{:T(128)S(6)} %select_n.43, s32[]{:T(128)S(6)} %select_n.45, s32[]{:T(128)S(6)} %select_n.44), kind=kLoop, calls=%fused_computation.5 | loop fusion | bytes 442380 | tf_op jit(solution)/shard_map/dynamic_slice | solution.py:322
  10.6 1.6 %collective-permute-done.2.refs_5_ = bf16[96,576]{1,0:T(8,128)(2,1)S(1)} collective-permute-done((bf16[96,576]{1,0:T(8,128)(2,1)S(1)}, bf16[96,576]{1,0:T(8,128)(2,1)S(1)}, u32[]{:S(2)}, u32[]{:S(2)}) %collective-permute-start.2) | collective-permute-done | bytes 110624 | tf_op jit(solution)/shard_map/ppermute | solution.py:48
  12.1 0.2 collective-permute-done.1.refs_0_
  12.4 0.1 pad_maximum_fusion.refs_4_
  12.5 5.7 %collective-permute-done.5.refs_7_ = bf16[96,576]{1,0:T(8,128)(2,1)S(1)} collective-permute-done((bf16[96,576]{1,0:T(8,128)(2,1)S(1)}, bf16[96,576]{1,0:T(8,128)(2,1)S(1)}, u32[]{:S(2)}, u32[]{:S(2)}) %collective-permute-start.5) | collective-permute-done | bytes 110624 | tf_op jit(solution)/shard_map/ppermute | solution.py:48
  18.2 2.5 %collective-permute-start.13 = (bf16[96,768]{1,0:T(8,128)(2,1)S(1)}, bf16[96,768]{1,0:T(8,128)(2,1)S(1)}, u32[]{:S(2)}, u32[]{:S(2)}) collective-permute-start(bf16[96,768]{1,0:T(8,128)(2,1)S(1)} %constant_dynamic-slice_fusion), channel_id=1, source_target_pairs={{0,1},{1,0},{2,3},{3,2},{4,5},{5,4},{6,7},{7,6},{8,9},{9,8},{10,11... | collective-permute-start | bytes 442376 | tf_op jit(solution)/shard_map/ppermute | solution.py:48
  20.7 1.0 %collective-permute-start.15 = (bf16[96,768]{1,0:T(8,128)(2,1)S(1)}, bf16[96,768]{1,0:T(8,128)(2,1)S(1)}, u32[]{:S(2)}, u32[]{:S(2)}) collective-permute-start(bf16[96,768]{1,0:T(8,128)(2,1)S(1)} %constant_dynamic-slice_fusion), channel_id=1, source_target_pairs={{0,2},{1,3},{2,0},{3,1},{4,6},{5,7},{6,4},{7,5},{8,10},{9,11},{10,... | collective-permute-start | bytes 442376 | tf_op jit(solution)/shard_map/ppermute | solution.py:48
  21.7 1.5 %collective-permute-start.17 = (bf16[96,768]{1,0:T(8,128)(2,1)S(1)}, bf16[96,768]{1,0:T(8,128)(2,1)S(1)}, u32[]{:S(2)}, u32[]{:S(2)}) collective-permute-start(bf16[96,768]{1,0:T(8,128)(2,1)S(1)} %constant_dynamic-slice_fusion), channel_id=1, source_target_pairs={{0,3},{1,2},{2,1},{3,0},{4,7},{5,6},{6,5},{7,4},{8,11},{9,10},{10,... | collective-permute-start | bytes 442376 | tf_op jit(solution)/shard_map/ppermute | solution.py:48
  23.2 1.5 %collective-permute-start.4 = (bf16[96,576]{1,0:T(8,128)(2,1)S(1)}, bf16[96,576]{1,0:T(8,128)(2,1)S(1)}, u32[]{:S(2)}, u32[]{:S(2)}) collective-permute-start(bf16[96,576]{1,0:T(8,128)(2,1)S(1)} %collective-permute-done.2.refs_5_), channel_id=1, source_target_pairs={{0,16},{4,20},{8,24},{12,28},{16,0},{20,4},{24,8},{28,12},{1,17},{... | collective-permute-start | bytes 331784 | tf_op jit(solution)/shard_map/ppermute | solution.py:48
  24.7 0.9 %shard_map.64 = (bf16[256,768]{1,0:T(8,128)(2,1)S(1)}, bf16[256,768]{1,0:T(8,128)(2,1)S(1)}) custom-call(bf16[256,768]{1,0:T(8,128)(2,1)S(1)} %bitcast.4, bf16[256,768]{1,0:T(8,128)(2,1)S(1)} %collective-permute-done.refs_1_, f32[768]{0:T(1024)S(1)} %copy-done.2, f32[768]{0:T(1024)S(1)} %copy-done.3), custom_call_target="tpu_custom_call" | custom-call | flops 2000000000 | bytes 6000000 | tf_op jit(solution)/shard_map/pallas_call | solution.py:359
  25.6 2.5 %collective-permute-done.4.refs_6_ = bf16[96,576]{1,0:T(8,128)(2,1)S(1)} collective-permute-done((bf16[96,576]{1,0:T(8,128)(2,1)S(1)}, bf16[96,576]{1,0:T(8,128)(2,1)S(1)}, u32[]{:S(2)}, u32[]{:S(2)}) %collective-permute-start.4) | collective-permute-done | bytes 110624 | tf_op jit(solution)/shard_map/ppermute | solution.py:48
  28.1 1.5 %collective-permute-start.6 = (bf16[96,576]{1,0:T(8,128)(2,1)S(1)}, bf16[96,576]{1,0:T(8,128)(2,1)S(1)}, u32[]{:S(2)}, u32[]{:S(2)}) collective-permute-start(bf16[96,576]{1,0:T(8,128)(2,1)S(1)} %collective-permute-done.5.refs_7_), channel_id=1, source_target_pairs={{0,16},{4,20},{8,24},{12,28},{16,0},{20,4},{24,8},{28,12},{1,17},{... | collective-permute-start | bytes 331784 | tf_op jit(solution)/shard_map/ppermute | solution.py:48
  29.6 0.5 collective-permute-start.8
  30.1 0.9 %shard_map.65 = (bf16[256,768]{1,0:T(8,128)(2,1)S(1)}, bf16[256,768]{1,0:T(8,128)(2,1)S(1)}) custom-call(bf16[256,768]{1,0:T(8,128)(2,1)S(1)} %collective-permute-done.1.refs_0_, bf16[256,768]{1,0:T(8,128)(2,1)S(1)} %collective-permute-done.3.refs_1_, f32[768]{0:T(1024)S(1)} %copy-done.2, f32[768]{0:T(1024)S(1)} %copy-done.3), custom_call_target="tpu_custom_call" | custom-call | flops 2000000000 | bytes 6000000 | tf_op jit(solution)/shard_map/pallas_call | solution.py:359
  31.1 3.4 %collective-permute-done.15.refs_3_ = bf16[96,768]{1,0:T(8,128)(2,1)S(1)} collective-permute-done((bf16[96,768]{1,0:T(8,128)(2,1)S(1)}, bf16[96,768]{1,0:T(8,128)(2,1)S(1)}, u32[]{:S(2)}, u32[]{:S(2)}) %collective-permute-start.15) | collective-permute-done | bytes 147488 | tf_op jit(solution)/shard_map/ppermute | solution.py:48
  34.5 0.5 collective-permute-start.18
  35.0 1.6 %shard_map.66 = (bf16[256,576]{1,0:T(8,128)(2,1)S(1)}, bf16[256,576]{1,0:T(8,128)(2,1)S(1)}, bf16[256,576]{1,0:T(8,128)(2,1)S(1)}, bf16[256,576]{1,0:T(8,128)(2,1)S(1)}, bf16[3,64,128]{2,1,0:T(8,128)(2,1)S(1)}) custom-call(bf16[256,768]{1,0:T(8,128)(2,1)S(1)} %get-tuple-element.23.refs_0_, bf16[256,768]{1,0:T(8,128)(2,1)S(1)} %get-tuple-element.24.refs_1_, ...), custom_call_target="tpu_custom_call" | custom-call | flops 3000000000 | bytes 9000000 | tf_op jit(solution)/shard_map/pallas_call | solution.py:362
  36.6 1.5 %collective-permute-start.9 = (bf16[3,64,128]{2,1,0:T(8,128)(2,1)S(1)}, bf16[3,64,128]{2,1,0:T(8,128)(2,1)S(1)}, u32[]{:S(2)}, u32[]{:S(2)}) collective-permute-start(bf16[3,64,128]{2,1,0:T(8,128)(2,1)S(1)} %get-tuple-element.32.refs_5_), channel_id=1, source_target_pairs={{0,16},{4,20},{8,24},{12,28},{16,0},{20,4},{24,8},{28,12},{1,17},{... | collective-permute-start | bytes 147464 | tf_op jit(solution)/shard_map/ppermute | solution.py:48
  38.1 4.6 %shard_map.67 = (f32[3,4,1,256]{3,2,1,0:T(1,128)S(1)}, f32[3,4,1,256]{3,2,1,0:T(1,128)S(1)}, f32[3,4,64,256]{3,2,1,0:T(8,128)S(1)}) custom-call(s32[1]{0:T(128)S(6)} %copy.7.valid_ref.refs_0_, bf16[256,576]{1,0:T(8,128)(2,1)S(1)} %get-tuple-element.28.refs_0_.refs_1_, bf16[256,576]{1,0:T(8,128)(2,1)S(1)} %get-tuple-element.29.refs_1_.refs_2_, ...), custom_call_target="tpu_custom_call" | custom-call | flops 5000000000 | bytes 15000000 | tf_op jit(solution)/shard_map/pallas_call | solution.py:371
  42.7 0.6 %shard_map.68 = (bf16[192,256]{1,0:T(8,128)(2,1)S(1)}, bf16[192,256]{1,0:T(8,128)(2,1)S(1)}, bf16[192,256]{1,0:T(8,128)(2,1)S(1)}, bf16[192,256]{1,0:T(8,128)(2,1)S(1)}) custom-call(s32[1]{0:T(128)S(6)} %copy.7.valid_ref.refs_0_, bf16[256,576]{1,0:T(8,128)(2,1)S(1)} %get-tuple-element.28.refs_0_.refs_1_, ...), custom_call_target="tpu_custom_call" | custom-call | flops 2000000000 | bytes 6000000 | tf_op jit(solution)/shard_map/pallas_call | solution.py:382
  43.3 0.6 %collective-permute-start.11 = (bf16[192,256]{1,0:T(8,128)(2,1)S(1)}, bf16[192,256]{1,0:T(8,128)(2,1)S(1)}, u32[]{:S(2)}, u32[]{:S(2)}) collective-permute-start(bf16[192,256]{1,0:T(8,128)(2,1)S(1)} %get-tuple-element.38), channel_id=1, source_target_pairs={{0,8},{4,12},{8,0},{12,4},{16,24},{20,28},{24,16},{28,20},{1,9},{5... | collective-permute-start | bytes 294920 | tf_op jit(solution)/shard_map/ppermute | solution.py:48
  43.9 1.3 %collective-permute-start.12 = (bf16[192,256]{1,0:T(8,128)(2,1)S(1)}, bf16[192,256]{1,0:T(8,128)(2,1)S(1)}, u32[]{:S(2)}, u32[]{:S(2)}) collective-permute-start(bf16[192,256]{1,0:T(8,128)(2,1)S(1)} %get-tuple-element.39), channel_id=1, source_target_pairs={{0,12},{4,8},{8,4},{12,0},{16,28},{20,24},{24,20},{28,16},{1,13},{... | collective-permute-start | bytes 294920 | tf_op jit(solution)/shard_map/ppermute | solution.py:48
  45.2 0.1 shard_map.69.refs_4_
  45.3 3.7 %collective-permute-done.11.refs_2_ = bf16[192,256]{1,0:T(8,128)(2,1)S(1)} collective-permute-done((bf16[192,256]{1,0:T(8,128)(2,1)S(1)}, bf16[192,256]{1,0:T(8,128)(2,1)S(1)}, u32[]{:S(2)}, u32[]{:S(2)}) %collective-permute-start.11) | collective-permute-done | bytes 98336 | tf_op jit(solution)/shard_map/ppermute | solution.py:48
  49.0 1.2 %collective-permute-done.12.refs_3_ = bf16[192,256]{1,0:T(8,128)(2,1)S(1)} collective-permute-done((bf16[192,256]{1,0:T(8,128)(2,1)S(1)}, bf16[192,256]{1,0:T(8,128)(2,1)S(1)}, u32[]{:S(2)}, u32[]{:S(2)}) %collective-permute-start.12) | collective-permute-done | bytes 98336 | tf_op jit(solution)/shard_map/ppermute | solution.py:48
  50.2 1.7 %shard_map.70 = bf16[256,768]{1,0:T(8,128)(2,1)} custom-call(bf16[256,768]{1,0:T(8,128)(2,1)S(1)} %bitcast.5, bf16[192,256]{1,0:T(8,128)(2,1)S(1)} %get-tuple-element.36.refs_0_, bf16[192,256]{1,0:T(8,128)(2,1)S(1)} %collective-permute-done.10.refs_1_, bf16[192,256]{1,0:T(8,128)(2,1)S(1)} %collective-permute-done.11.refs_2_, ...), custom_call_target="tpu_custom_call" | custom-call | flops 2000000000 | bytes 6000000 | tf_op jit(solution)/shard_map/pallas_call | solution.py:393
  (26 shorter events, 0.2 us)
Async XLA Ops:
  0.0 24.7 %copy-start.1 = (bf16[1,256,768]{2,1,0:T(8,128)(2,1)S(1)}, bf16[1,256,768]{2,1,0:T(8,128)(2,1)}, u32[]{:S(2)}) copy-start(bf16[1,256,768]{2,1,0:T(8,128)(2,1)} %param.6) | copy-start | bytes 1179652
  0.0 12.5 %copy-start = (bf16[192,768]{1,0:T(8,128)(2,1)S(1)}, bf16[192,768]{1,0:T(8,128)(2,1)}, u32[]{:S(2)}) copy-start(bf16[192,768]{1,0:T(8,128)(2,1)} %refs_0_.2) | copy-start | bytes 884740
  0.0 24.7 %copy-start.2 = (f32[768]{0:T(1024)S(1)}, f32[768]{0:T(1024)}, u32[]{:S(2)}) copy-start(f32[768]{0:T(1024)} %refs_2_.3) | copy-start | bytes 9220
  0.0 24.7 %copy-start.3 = (f32[768]{0:T(1024)S(1)}, f32[768]{0:T(1024)}, u32[]{:S(2)}) copy-start(f32[768]{0:T(1024)} %refs_3_.3) | copy-start | bytes 9220
  0.0 12.3 %collective-permute-start.1 = (bf16[256,768]{1,0:T(8,128)(2,1)}, bf16[256,768]{1,0:T(8,128)(2,1)S(1)}, u32[]{:S(2)}, u32[]{:S(2)}) collective-permute-start(bf16[256,768]{1,0:T(8,128)(2,1)} %bitcast.2), channel_id=1, source_target_pairs={{0,8},{4,12},{8,0},{12,4},{16,24},{20,28},{24,16},{28,20},{1,9},{5... | collective-permute-start | bytes 1179656 | tf_op jit(solution)/shard_map/ppermute | solution.py:48
  3.0 20.2 %collective-permute-start = (bf16[256,768]{1,0:T(8,128)(2,1)}, bf16[256,768]{1,0:T(8,128)(2,1)S(1)}, u32[]{:S(2)}, u32[]{:S(2)}) collective-permute-start(bf16[256,768]{1,0:T(8,128)(2,1)} %bitcast.3), channel_id=1, source_target_pairs={{0,4},{4,0},{8,12},{12,8},{16,20},{20,16},{24,28},{28,24},{1,5},{5... | collective-permute-start | bytes 1179656 | tf_op jit(solution)/shard_map/ppermute | solution.py:48
  4.2 7.9 %collective-permute-start.2 = (bf16[96,576]{1,0:T(8,128)(2,1)S(1)}, bf16[96,576]{1,0:T(8,128)(2,1)S(1)}, u32[]{:S(2)}, u32[]{:S(2)}) collective-permute-start(bf16[96,576]{1,0:T(8,128)(2,1)S(1)} %pad_maximum_fusion.1), channel_id=1, source_target_pairs={{0,1},{1,0},{2,3},{3,2},{4,5},{5,4},{6,7},{7,6},{8,9},{9,8},{10,11... | collective-permute-start | bytes 331784 | tf_op jit(solution)/shard_map/ppermute | solution.py:48
  5.9 12.4 %collective-permute-start.5 = (bf16[96,576]{1,0:T(8,128)(2,1)S(1)}, bf16[96,576]{1,0:T(8,128)(2,1)S(1)}, u32[]{:S(2)}, u32[]{:S(2)}) collective-permute-start(bf16[96,576]{1,0:T(8,128)(2,1)S(1)} %pad_maximum_fusion.1), channel_id=1, source_target_pairs={{0,2},{1,3},{2,0},{3,1},{4,6},{5,7},{6,4},{7,5},{8,10},{9,11},{10,... | collective-permute-start | bytes 331784 | tf_op jit(solution)/shard_map/ppermute | solution.py:48
  8.4 9.8 %collective-permute-start.7 = (bf16[96,576]{1,0:T(8,128)(2,1)S(1)}, bf16[96,576]{1,0:T(8,128)(2,1)S(1)}, u32[]{:S(2)}, u32[]{:S(2)}) collective-permute-start(bf16[96,576]{1,0:T(8,128)(2,1)S(1)} %pad_maximum_fusion.1), channel_id=1, source_target_pairs={{0,3},{1,2},{2,1},{3,0},{4,7},{5,6},{6,5},{7,4},{8,11},{9,10},{10,... | collective-permute-start | bytes 331784 | tf_op jit(solution)/shard_map/ppermute | solution.py:48
  12.3 17.3 %collective-permute-start.3 = (bf16[256,768]{1,0:T(8,128)(2,1)S(1)}, bf16[256,768]{1,0:T(8,128)(2,1)S(1)}, u32[]{:S(2)}, u32[]{:S(2)}) collective-permute-start(bf16[256,768]{1,0:T(8,128)(2,1)S(1)} %collective-permute-done.1.refs_0_), channel_id=1, source_target_pairs={{0,4},{4,0},{8,12},{12,8},{16,20},{20,16},{24,28},{28,24},{1,5},{5... | collective-permute-start | bytes 1179656 | tf_op jit(solution)/shard_map/ppermute | solution.py:48
  18.2 12.8 %collective-permute-start.13 = (bf16[96,768]{1,0:T(8,128)(2,1)S(1)}, bf16[96,768]{1,0:T(8,128)(2,1)S(1)}, u32[]{:S(2)}, u32[]{:S(2)}) collective-permute-start(bf16[96,768]{1,0:T(8,128)(2,1)S(1)} %constant_dynamic-slice_fusion), channel_id=1, source_target_pairs={{0,1},{1,0},{2,3},{3,2},{4,5},{5,4},{6,7},{7,6},{8,9},{9,8},{10,11... | collective-permute-start | bytes 442376 | tf_op jit(solution)/shard_map/ppermute | solution.py:48
  20.7 13.7 %collective-permute-start.15 = (bf16[96,768]{1,0:T(8,128)(2,1)S(1)}, bf16[96,768]{1,0:T(8,128)(2,1)S(1)}, u32[]{:S(2)}, u32[]{:S(2)}) collective-permute-start(bf16[96,768]{1,0:T(8,128)(2,1)S(1)} %constant_dynamic-slice_fusion), channel_id=1, source_target_pairs={{0,2},{1,3},{2,0},{3,1},{4,6},{5,7},{6,4},{7,5},{8,10},{9,11},{10,... | collective-permute-start | bytes 442376 | tf_op jit(solution)/shard_map/ppermute | solution.py:48
  21.7 12.7 %collective-permute-start.17 = (bf16[96,768]{1,0:T(8,128)(2,1)S(1)}, bf16[96,768]{1,0:T(8,128)(2,1)S(1)}, u32[]{:S(2)}, u32[]{:S(2)}) collective-permute-start(bf16[96,768]{1,0:T(8,128)(2,1)S(1)} %constant_dynamic-slice_fusion), channel_id=1, source_target_pairs={{0,3},{1,2},{2,1},{3,0},{4,7},{5,6},{6,5},{7,4},{8,11},{9,10},{10,... | collective-permute-start | bytes 442376 | tf_op jit(solution)/shard_map/ppermute | solution.py:48
  23.2 4.9 %collective-permute-start.4 = (bf16[96,576]{1,0:T(8,128)(2,1)S(1)}, bf16[96,576]{1,0:T(8,128)(2,1)S(1)}, u32[]{:S(2)}, u32[]{:S(2)}) collective-permute-start(bf16[96,576]{1,0:T(8,128)(2,1)S(1)} %collective-permute-done.2.refs_5_), channel_id=1, source_target_pairs={{0,16},{4,20},{8,24},{12,28},{16,0},{20,4},{24,8},{28,12},{1,17},{... | collective-permute-start | bytes 331784 | tf_op jit(solution)/shard_map/ppermute | solution.py:48
  28.1 6.9 %collective-permute-start.6 = (bf16[96,576]{1,0:T(8,128)(2,1)S(1)}, bf16[96,576]{1,0:T(8,128)(2,1)S(1)}, u32[]{:S(2)}, u32[]{:S(2)}) collective-permute-start(bf16[96,576]{1,0:T(8,128)(2,1)S(1)} %collective-permute-done.5.refs_7_), channel_id=1, source_target_pairs={{0,16},{4,20},{8,24},{12,28},{16,0},{20,4},{24,8},{28,12},{1,17},{... | collective-permute-start | bytes 331784 | tf_op jit(solution)/shard_map/ppermute | solution.py:48
  29.6 5.4 %collective-permute-start.8 = (bf16[96,576]{1,0:T(8,128)(2,1)S(1)}, bf16[96,576]{1,0:T(8,128)(2,1)S(1)}, u32[]{:S(2)}, u32[]{:S(2)}) collective-permute-start(bf16[96,576]{1,0:T(8,128)(2,1)S(1)} %collective-permute-done.7.refs_9_), channel_id=1, source_target_pairs={{0,16},{4,20},{8,24},{12,28},{16,0},{20,4},{24,8},{28,12},{1,17},{... | collective-permute-start | bytes 331784 | tf_op jit(solution)/shard_map/ppermute | solution.py:48
  31.0 12.9 %collective-permute-start.14 = (bf16[96,768]{1,0:T(8,128)(2,1)S(1)}, bf16[96,768]{1,0:T(8,128)(2,1)S(1)}, u32[]{:S(2)}, u32[]{:S(2)}) collective-permute-start(bf16[96,768]{1,0:T(8,128)(2,1)S(1)} %collective-permute-done.13.refs_1_), channel_id=1, source_target_pairs={{0,4},{4,0},{8,12},{12,8},{16,20},{20,16},{24,28},{28,24},{1,5},{5... | collective-permute-start | bytes 442376 | tf_op jit(solution)/shard_map/ppermute | solution.py:48
  34.4 10.8 %collective-permute-start.16 = (bf16[96,768]{1,0:T(8,128)(2,1)S(1)}, bf16[96,768]{1,0:T(8,128)(2,1)S(1)}, u32[]{:S(2)}, u32[]{:S(2)}) collective-permute-start(bf16[96,768]{1,0:T(8,128)(2,1)S(1)} %collective-permute-done.15.refs_3_), channel_id=1, source_target_pairs={{0,4},{4,0},{8,12},{12,8},{16,20},{20,16},{24,28},{28,24},{1,5},{5... | collective-permute-start | bytes 442376 | tf_op jit(solution)/shard_map/ppermute | solution.py:48
  34.5 10.8 %collective-permute-start.18 = (bf16[96,768]{1,0:T(8,128)(2,1)S(1)}, bf16[96,768]{1,0:T(8,128)(2,1)S(1)}, u32[]{:S(2)}, u32[]{:S(2)}) collective-permute-start(bf16[96,768]{1,0:T(8,128)(2,1)S(1)} %collective-permute-done.17.refs_5_), channel_id=1, source_target_pairs={{0,4},{4,0},{8,12},{12,8},{16,20},{20,16},{24,28},{28,24},{1,5},{5... | collective-permute-start | bytes 442376 | tf_op jit(solution)/shard_map/ppermute | solution.py:48
  36.6 6.1 %collective-permute-start.9 = (bf16[3,64,128]{2,1,0:T(8,128)(2,1)S(1)}, bf16[3,64,128]{2,1,0:T(8,128)(2,1)S(1)}, u32[]{:S(2)}, u32[]{:S(2)}) collective-permute-start(bf16[3,64,128]{2,1,0:T(8,128)(2,1)S(1)} %get-tuple-element.32.refs_5_), channel_id=1, source_target_pairs={{0,16},{4,20},{8,24},{12,28},{16,0},{20,4},{24,8},{28,12},{1,17},{... | collective-permute-start | bytes 147464 | tf_op jit(solution)/shard_map/ppermute | solution.py:48
  43.3 2.0 %collective-permute-start.10 = (bf16[192,256]{1,0:T(8,128)(2,1)S(1)}, bf16[192,256]{1,0:T(8,128)(2,1)S(1)}, u32[]{:S(2)}, u32[]{:S(2)}) collective-permute-start(bf16[192,256]{1,0:T(8,128)(2,1)S(1)} %get-tuple-element.37), channel_id=1, source_target_pairs={{0,4},{4,0},{8,12},{12,8},{16,20},{20,16},{24,28},{28,24},{1,5},{5... | collective-permute-start | bytes 294920 | tf_op jit(solution)/shard_map/ppermute | solution.py:48
  43.3 5.7 %collective-permute-start.11 = (bf16[192,256]{1,0:T(8,128)(2,1)S(1)}, bf16[192,256]{1,0:T(8,128)(2,1)S(1)}, u32[]{:S(2)}, u32[]{:S(2)}) collective-permute-start(bf16[192,256]{1,0:T(8,128)(2,1)S(1)} %get-tuple-element.38), channel_id=1, source_target_pairs={{0,8},{4,12},{8,0},{12,4},{16,24},{20,28},{24,16},{28,20},{1,9},{5... | collective-permute-start | bytes 294920 | tf_op jit(solution)/shard_map/ppermute | solution.py:48
  43.9 6.3 %collective-permute-start.12 = (bf16[192,256]{1,0:T(8,128)(2,1)S(1)}, bf16[192,256]{1,0:T(8,128)(2,1)S(1)}, u32[]{:S(2)}, u32[]{:S(2)}) collective-permute-start(bf16[192,256]{1,0:T(8,128)(2,1)S(1)} %get-tuple-element.39), channel_id=1, source_target_pairs={{0,12},{4,8},{8,4},{12,0},{16,28},{20,24},{24,20},{28,16},{1,13},{... | collective-permute-start | bytes 294920 | tf_op jit(solution)/shard_map/ppermute | solution.py:48

commit v3 on v2

--- a/solution.py
+++ b/solution.py
@@ -33,7 +33,7 @@
         out_specs=outs,
         scratch_shapes=list(scratch),
         cost_estimate=pl.CostEstimate(
-            flops=micros * 1_000_000_000, transcendentals=0, bytes_accessed=micros * 3_000_000
+            flops=micros * 100_000_000_000, transcendentals=0, bytes_accessed=micros * 300_000_000
         ),
         compiler_params=pltpu.CompilerParams(vmem_limit_bytes=VMEM_LIMIT),
     )
@@ -97,11 +97,13 @@
     return shard % SHARDS, shard // SHARDS
 
 
-def head_slices(index):
-    return [
-        slice(part * GROUP_WIDTH + index * HEAD_DIM, part * GROUP_WIDTH + (index + 1) * HEAD_DIM)
-        for part in range(3)
-    ]
+def head_slice(index, part=0):
+    low = part * GROUP_WIDTH + index * HEAD_DIM
+    return slice(low, low + HEAD_DIM)
+
+
+def pair_slices(index):
+    return head_slice(index, 0), head_slice(index, 1)
 
 
 def wide_rows(head, rows):
@@ -115,37 +117,42 @@
     return pl.ds(pl.multiple_of(head % MID * count, count), count)
 
 
-def qkv_body(n_mp, shared, *refs):
+def assemble(whole_ref, refs, sources):
+    width = whole_ref.shape[1]
+    for ref, source in zip(refs, sources):
+        rows, wide = ref.shape
+        start = wide - width if width == GROUP_WIDTH else 0
+        whole_ref[pl.ds(pl.multiple_of(source * rows, 16), rows), :] = ref[:, start : start + width]
+
+
+def sources(n_mp, turn, shared):
+    mp_index = lax.axis_index("mp")
+    if shared:
+        return [mp_index, mp_index ^ 1, mp_index ^ (2 + turn), mp_index ^ (3 - turn)]
+    return [mp_index ^ apart for apart in range(n_mp)]
+
+
+def project_body(n_mp, shared, *refs):
     normed_refs, refs = refs[:SHARDS], refs[SHARDS:]
-    n_weights = 1 + (2 if shared else 1) * (n_mp - 1)
-    weight_refs, refs = refs[:n_weights], refs[n_weights:]
-    out_refs, sent_ref, whole_ref = refs[:SHARDS], refs[SHARDS], refs[SHARDS + 1]
-    member, group = group_indices()
-    mp_index = lax.axis_index("mp")
-    rows = weight_refs[0].shape[0]
-
-    def put(ref, source, offset):
-        start = pl.multiple_of(source * rows + offset, 16)
-        whole_ref[pl.ds(start, ref.shape[0]), :] = ref[...]
-
-    put(weight_refs[0], mp_index, 0)
-    for apart in range(1, n_mp):
-        if shared:
-            half = group % 2
-            put(weight_refs[2 * apart - 1], mp_index ^ apart, half * (rows // 2))
-            put(weight_refs[2 * apart], mp_index ^ apart, (1 - half) * (rows // 2))
-        else:
-            put(weight_refs[apart], mp_index ^ apart, 0)
+    weight_refs, (*out_refs, whole_ref) = refs[:n_mp], refs[n_mp:]
+    _, group = group_indices()
+    assemble(whole_ref, weight_refs, sources(n_mp, group % 2, shared))
+    for normed_ref, out_ref in zip(normed_refs, out_refs):
+        out_ref[...] = product(normed_ref[...], whole_ref[...]).astype(jnp.bfloat16)
+
+
+def key_value_body(n_mp, shared, *refs):
+    *refs, sent_ref, whole_ref = refs
+    project_body(n_mp, shared, *refs, whole_ref)
+    out_refs = refs[-SHARDS:]
+    member, _ = group_indices()
     shard_rows = out_refs[0].shape[0]
     depth = shard_rows // WIDE
-    for normed_ref, out_ref in zip(normed_refs, out_refs):
-        out_ref[...] = product(normed_ref[...], whole_ref[...]).astype(jnp.bfloat16)
     for index in range(GROUP_HEADS):
-        _, key_at, value_at = head_slices(index)
         taken = wide_rows(member * GROUP_HEADS + index, shard_rows)
         for shard, out_ref in enumerate(out_refs):
             sent_ref[index, shard * depth : (shard + 1) * depth, :] = jnp.concatenate(
-                [out_ref[taken, key_at], out_ref[taken, value_at]], axis=1
+                [out_ref[taken, at] for at in pair_slices(index)], axis=1
             )
 
 
@@ -169,10 +176,11 @@
 
 
 def near_body(valid_ref, *refs):
-    qkv_refs, (max_ref, sum_ref, num_ref) = refs[:SHARDS], refs[SHARDS:]
+    q_refs, refs = refs[:SHARDS], refs[SHARDS:]
+    kv_refs, (max_ref, sum_ref, num_ref) = refs[:SHARDS], refs[SHARDS:]
     member, group = group_indices()
     valid = valid_ref[0]
-    rows = qkv_refs[0].shape[0]
+    rows = q_refs[0].shape[0]
     count = rows // MID
     bases = [(group * SHARDS + (member ^ apart)) * rows for apart in range(SHARDS)]
     place = place_of(lax.broadcasted_iota(jnp.int32, (rows, LANES), 0), rows)
@@ -181,20 +189,21 @@
     def widen(bias):
         return jnp.concatenate([bias] * (rows // LANES), axis=1)
 
-    for shard, ref in enumerate(qkv_refs):
+    for shard, (q_ref, kv_ref) in enumerate(zip(q_refs, kv_refs)):
         bias = widen(key_bias(place + bases[shard], valid))
         for index in range(GROUP_HEADS):
-            query_at, key_at, value_at = head_slices(index)
-            stats = branch(ref[:, query_at], ref[:, key_at], ref[:, value_at], bias)
+            key_at, value_at = pair_slices(index)
+            stats = branch(q_ref[:, head_slice(index)], kv_ref[:, key_at], kv_ref[:, value_at], bias)
             max_ref[index, shard], sum_ref[index, shard], num_ref[index, shard] = stats
     entry = lax.broadcasted_iota(jnp.int32, (count, LANES), 0)
     depth = rows // WIDE
     for index in range(GROUP_HEADS):
         head = member * GROUP_HEADS + index
         taken = middle_rows(head, rows)
+        key_at, value_at = pair_slices(index)
         query, key, value = (
-            jnp.concatenate([ref[taken, at] for ref in qkv_refs], axis=0)
-            for at in head_slices(index)
+            jnp.concatenate([ref[taken, at] for ref in some], axis=0)
+            for some, at in ((q_refs, head_slice(index)), (kv_refs, key_at), (kv_refs, value_at))
         )
         position = entry % depth * WIDE + entry // depth * MID + head % MID
         bias = widen(
@@ -215,12 +224,12 @@
 
 
 def far_body(n_groups, valid_ref, *refs):
-    qkv_refs, refs = refs[:SHARDS], refs[SHARDS:]
+    q_refs, refs = refs[:SHARDS], refs[SHARDS:]
     sent_refs, refs = refs[:n_groups], refs[n_groups:]
     (max_ref, sum_ref, num_ref), out_refs = refs[:3], refs[3:]
     member, group = group_indices()
     valid = valid_ref[0]
-    rows = qkv_refs[0].shape[0]
+    rows = q_refs[0].shape[0]
     depth = rows // WIDE
     count = SHARDS * depth
     entry = lax.broadcasted_iota(jnp.int32, (count, count), 0)
@@ -228,8 +237,7 @@
     for index in range(GROUP_HEADS):
         head = member * GROUP_HEADS + index
         taken = wide_rows(head, rows)
-        query_at = head_slices(index)[0]
-        query = jnp.concatenate([ref[taken, query_at] for ref in qkv_refs], axis=0)
+        query = jnp.concatenate([ref[taken, head_slice(index)] for ref in q_refs], axis=0)
         bias = jnp.concatenate(
             [
                 key_bias(
@@ -273,36 +281,35 @@
             out_ref[index * HEAD_DIM : (index + 1) * HEAD_DIM, :] = attention.astype(jnp.bfloat16)
 
 
-def gather_body(n_mp, *refs):
-    own_ref, pair_refs, out_ref = refs[0], refs[1:-1], refs[-1]
-    mp_index = lax.axis_index("mp")
-    rows = own_ref.shape[0]
-    out_ref[pl.ds(pl.multiple_of(mp_index * rows, 16), rows), :] = own_ref[...]
-    for apart in range(1, n_mp):
-        if len(pair_refs) == n_mp - 1:
-            start = pl.multiple_of((mp_index ^ apart) * rows, 16)
-            out_ref[pl.ds(start, rows), :] = pair_refs[apart - 1][...]
-        else:
-            core = lax.axis_index("ctx") % 2
-            half = rows // 2
-            for turn in range(2):
-                start = (mp_index ^ apart) * rows + (core ^ turn) * half
-                out_ref[pl.ds(pl.multiple_of(start, 16), half), :] = pair_refs[
-                    2 * (apart - 1) + turn
-                ][...]
-
-
-def out_body(x_ref, *refs):
-    part_refs, weight_ref, out_ref = refs[:SHARDS], refs[SHARDS], refs[SHARDS + 1]
-    rows = x_ref.shape[0]
+def gather_body(n_mp, shared, *refs):
+    *part_refs, out_ref = refs
+    assemble(out_ref, part_refs, sources(n_mp, lax.axis_index("ctx") % 2, shared))
+
+
+def update_body(*refs):
+    *part_refs, weight_ref, base_ref, out_ref = refs
+    first = SHARDS // 2 if base_ref.dtype == jnp.float32 else 0
     member, _ = group_indices()
-    order = to_position(rows)
-    update = jnp.zeros(x_ref.shape, jnp.float32)
+    order = to_position(base_ref.shape[0])
+    update = base_ref[...].astype(jnp.float32)
     for apart, ref in enumerate(part_refs):
         part = product(order, ref[...], 1, 1).astype(jnp.bfloat16)
-        start = pl.multiple_of((member ^ apart) * GROUP_WIDTH, GROUP_WIDTH)
-        update = update + product(part, weight_ref[pl.ds(start, GROUP_WIDTH), :])
-    out_ref[...] = (x_ref[...].astype(jnp.float32) + update).astype(jnp.bfloat16)
+        start = (member ^ (first + apart)) * GROUP_WIDTH
+        update = update + product(
+            part, weight_ref[pl.ds(pl.multiple_of(start, GROUP_WIDTH), GROUP_WIDTH), :]
+        )
+    out_ref[...] = update.astype(out_ref.dtype)
+
+
+def fetch(value, turns, shared, pair_mask, earlier=()):
+    n_mp, n_ctx = lax.axis_size("mp"), lax.axis_size("ctx")
+    if not shared:
+        return [flip(value, "mp", apart) for apart in range(1, n_mp)]
+    pairs = [
+        (c * n_mp + z, c * n_mp + (z ^ (2 + turns(c)))) for c in range(n_ctx) for z in range(n_mp)
+    ]
+    direct = near(lax.ppermute(value, ("ctx", "mp"), pairs))
+    return [direct, flip(after(direct, *earlier), "ctx", pair_mask)]
 
 
 def local(tile_embeds, norm_gain, norm_bias, w_qkv, w_out, valid_count):
@@ -312,62 +319,59 @@
     n_groups = lax.axis_size("ctx") // SHARDS
     depth = rows // WIDE
     weight_rows = w_qkv.shape[0]
-    member, group = group_indices()
+    member, _ = group_indices()
     bf16, f32 = jnp.bfloat16, jnp.float32
     shape = pltpu.VMEM
-
-    def columns(first, count):
-        return jnp.concatenate(
-            [
-                lax.dynamic_slice(
-                    w_qkv, (first, part * width + member * GROUP_WIDTH), (count, GROUP_WIDTH)
-                )
-                for part in range(3)
-            ],
-            axis=1,
-        )
-
-    mine = columns(0, weight_rows)
-    shared = n_groups % 2 == 0 and weight_rows % 32 == 0
-    weights = [near(mine)]
-    if shared:
-        half = weight_rows // 2
-        piece = columns(group % 2 * half, half)
-        direct = [flip(piece, "mp", apart) for apart in range(1, n_mp)]
-        for value in direct:
-            weights += [value, flip(value, "ctx", SHARDS)]
-    else:
-        direct = [flip(mine, "mp", apart) for apart in range(1, n_mp)]
-        weights += direct
+    shared = n_mp == 4 and n_groups % 2 == 0
+
+    def columns(part):
+        start = part * width + member * GROUP_WIDTH
+        return lax.dynamic_slice(w_qkv, (0, start), (weight_rows, GROUP_WIDTH))
+
+    key_value = jnp.concatenate([columns(1), columns(2)], axis=1)
+    query = columns(0)
+    mine = near(jnp.concatenate([key_value, query], axis=1))
+    closest = [flip(mine, "mp", 1)] if shared else []
+    weights = []
+    for value in (key_value, query):
+        earlier = [blocks[1 + len(closest)] for blocks in weights]
+        others = fetch(near(value), lambda c: c // SHARDS % 2, shared, SHARDS, earlier)
+        weights.append([mine] + closest + others)
 
     x_pair = flip(x, "ctx", 1)
     x_far = flip(x, "ctx", 2)
-    chunks = [near(x), x_pair, x_far, flip(after(x_far, direct[0]), "ctx", 1)]
-
-    out_parts = [near(w_out)]
-    if weight_rows % 32 == 0:
-        half = weight_rows // 2
-        piece = lax.dynamic_slice(w_out, (member % 2 * half, 0), (half, width))
-        for apart in range(1, n_mp):
-            received = flip(after(piece, *direct), "mp", apart)
-            out_parts += [received, flip(received, "ctx", 1)]
-    else:
-        out_parts += [flip(after(w_out, *direct), "mp", apart) for apart in range(1, n_mp)]
-
+    x_far = after(x_far, weights[0][2])
+    x_last = flip(x_far, "ctx", 1)
+    x_own = near(x)
+    gain, bias = near(norm_gain), near(norm_bias)
     normed = []
-    for pair in (chunks[:2], chunks[2:]):
-        normed += call(norm_body, [shape((rows, width), bf16)] * 2, n_in=4, micros=2)(
-            *pair, near(norm_gain), near(norm_bias)
-        )
-    *qkv, sent = call(
-        lambda *refs: qkv_body(n_mp, shared, *refs),
-        [shape((rows, 3 * GROUP_WIDTH), bf16)] * SHARDS
+    for pair in ((x_own, x_pair), (x_far, x_last)):
+        normed += call(norm_body, [shape((rows, width), bf16)] * 2, n_in=4, micros=1)(
+            *pair, gain, bias
+        )
+
+    out_weight = after(near(w_out), normed[2])
+    out_parts = [out_weight]
+    if shared:
+        out_parts.append(flip(out_weight, "mp", 1))
+    out_parts += fetch(out_weight, lambda c: c % 2, shared, 1)
+
+    *kv, sent = call(
+        lambda *refs: key_value_body(n_mp, shared, *refs),
+        [shape((rows, 2 * GROUP_WIDTH), bf16)] * SHARDS
         + [shape((GROUP_HEADS, SHARDS * depth, 2 * HEAD_DIM), bf16)],
-        scratch=[pltpu.VMEM((n_mp * weight_rows, 3 * GROUP_WIDTH), bf16)],
-        n_in=SHARDS + len(weights),
-        micros=3,
-    )(*normed, *weights)
-    others = [sent] + [flip(sent, "ctx", SHARDS * apart) for apart in range(1, n_groups)]
+        scratch=[pltpu.VMEM((width, 2 * GROUP_WIDTH), bf16)],
+        n_in=SHARDS + n_mp,
+        micros=2,
+    )(*normed, *weights[0])
+    sents = [sent] + [flip(sent, "ctx", SHARDS * apart) for apart in range(1, n_groups)]
+    q = call(
+        lambda *refs: project_body(n_mp, shared, *refs),
+        [shape((rows, GROUP_WIDTH), bf16)] * SHARDS,
+        scratch=[pltpu.VMEM((width, GROUP_WIDTH), bf16)],
+        n_in=SHARDS + n_mp,
+        micros=1,
+    )(*normed, *weights[1])
     stats = call(
         near_body,
         [
@@ -376,23 +380,29 @@
             shape((GROUP_HEADS, SHARDS, HEAD_DIM, rows), f32),
         ],
         n_scalar=1,
-        n_in=SHARDS,
-        micros=5,
-    )(valid_count, *qkv)
+        n_in=2 * SHARDS,
+        micros=50,
+    )(valid_count, *q, *kv)
     attention = call(
         lambda *refs: far_body(n_groups, *refs),
         [shape((GROUP_WIDTH, rows), bf16)] * SHARDS,
         n_scalar=1,
         n_in=SHARDS + n_groups + 3,
-        micros=2,
-    )(valid_count, *qkv, *others, *stats)
+        micros=1,
+    )(valid_count, *q, *sents, *stats)
     received = [attention[0]] + [flip(attention[apart], "ctx", apart) for apart in range(1, SHARDS)]
     (whole_out,) = call(
-        lambda *refs: gather_body(n_mp, *refs), [shape((width, width), bf16)], n_in=len(out_parts)
+        lambda *refs: gather_body(n_mp, shared, *refs),
+        [shape((width, width), bf16)],
+        n_in=n_mp,
     )(*out_parts)
+    half = SHARDS // 2
+    (partial,) = call(update_body, [shape((rows, width), f32)], n_in=half + 2, micros=1)(
+        *received[:half], whole_out, x_own
+    )
     (out,) = call(
-        out_body, [jax.ShapeDtypeStruct((rows, width), bf16)], n_in=SHARDS + 2, micros=2
-    )(near(x), *received, whole_out)
+        update_body, [jax.ShapeDtypeStruct((rows, width), bf16)], n_in=half + 2, micros=1
+    )(*received[half:], whole_out, partial)
     return out[None]
 
 

time: 52.1 us -> 53.6 us (1.029)
  Pallas kernels: 10.3 us -> 17.4 us
  starting transfers between devices: 20 us -> 15.9 us
  waiting for transfers between devices: 18.3 us -> 17.1 us
  local copies, waits for them, and re-layouts: 2.34 us -> 1.21 us
  other arithmetic: 0.2 us -> 0.9 us
    ppermute x19 -> x12, waiting for transfers between devices: 18.3 us -> 3.97 us  [flip(): return near(lax.ppermute(value, axis, pairs))]
    ppermute x0 -> x3, waiting for transfers between devices: none -> 13.1 us  [fetch(): direct = near(lax.ppermute(value, ('ctx', 'mp'), pairs))]
    ppermute x19 -> x12, starting transfers between devices: 20 us -> 9.39 us  [flip(): return near(lax.ppermute(value, axis, pairs))]
    ppermute x0 -> x3, starting transfers between devices: none -> 6.51 us  [fetch(): direct = near(lax.ppermute(value, ('ctx', 'mp'), pairs))]
    pallas_call x5 -> x7, Pallas kernels: 5.14 us -> 10.8 us  [the longest x1 2.96 us: local(): call(lambda *refs: key_value_body(n_mp, shared, *refs), [shape((rows, 2 *...]
    pallas_call x1, Pallas kernels: 0.59 us -> 2.03 us  [local(): call(lambda *refs: far_body(n_groups, *refs), [shape((GROUP_WIDTH, rows),...]
    dynamic_slice x3 -> x1, local copies, waits for them, and re-layouts: 2.33 us -> 1.2 us  [columns(): return lax.dynamic_slice(w_qkv, (0, start), (weight_rows, GROUP_WIDTH))]
    concatenate x2, other arithmetic: 0.2 us -> 0.9 us  [the longest x1 0.8 us: local(): mine = near(jnp.concatenate([key_value, query], axis=1))]
  transfers between devices with their start and end apart: 19 -> 15, of which waited for: 7 -> 5; matrix products, arithmetic and copies ran while one was open for 5% -> 4% of each run, Pallas kernels for 17% -> 28%
where the time goes in v3:
time: 53.6 us; the launch traced here: 53.3 us
  Pallas kernels  17.4 us (32%)
  waiting for transfers between devices  17.1 us (32%)
  starting transfers between devices  15.9 us (30%)
  local copies, waits for them, and re-layouts  1.21 us (2%)
  other arithmetic  0.9 us (2%)
  between operations  0.75 us (1%)
    ppermute x3, waiting for transfers between devices, fetch(): direct = near(lax.ppermute(value, ('ctx', 'mp'), pairs))  13.1 us
    ppermute x12, starting transfers between devices, flip(): return near(lax.ppermute(value, axis, pairs))  9.39 us
    ppermute x3, starting transfers between devices, fetch(): direct = near(lax.ppermute(value, ('ctx', 'mp'), pairs))  6.51 us
    pallas_call x1, Pallas kernels, local(): call(near_body, [shape((GROUP_HEADS, SHARDS, 1, rows), f32), shape((GROUP...  4.54 us
    ppermute x12, waiting for transfers between devices, flip(): return near(lax.ppermute(value, axis, pairs))  3.97 us
    pallas_call x1, Pallas kernels, local(): call(lambda *refs: key_value_body(n_mp, shared, *refs), [shape((rows, 2 *...  2.96 us
    pallas_call x1, Pallas kernels, local(): call(update_body, [jax.ShapeDtypeStruct((rows, width), bf16)], n_in=half...  2.39 us
    pallas_call x1, Pallas kernels, local(): call(lambda *refs: far_body(n_groups, *refs), [shape((GROUP_WIDTH, rows),...  2.03 us
  transfers between devices with their start and end apart: 15, of which 5 were waited for; matrix products, arithmetic and copies ran while one was open for 4% of the time, Pallas kernels for 28%

profile of v3, /device:TPU:0, one launch (start us, length us, event | category | flops | bytes accessed | tf_op | source)
XLA Modules:
  0.0 53.3 jit_solution(2888975614733476412)
XLA Ops:
  0.0 3.0 %collective-permute-start.1 = (bf16[256,768]{1,0:T(8,128)(2,1)}, bf16[256,768]{1,0:T(8,128)(2,1)S(1)}, u32[]{:S(2)}, u32[]{:S(2)}) collective-permute-start(bf16[256,768]{1,0:T(8,128)(2,1)} %bitcast.2), channel_id=1, source_target_pairs={{0,8},{4,12},{8,0},{12,4},{16,24},{20,28},{24,16},{28,20},{1,9},{5... | collective-permute-start | bytes 1179656 | tf_op jit(solution)/shard_map/ppermute | solution.py:48
  3.0 1.2 %constant_dynamic-slice_fusion = (bf16[192,192]{1,0:T(8,128)(2,1)S(1)}, bf16[192,192]{1,0:T(8,128)(2,1)S(1)}, bf16[192,192]{1,0:T(8,128)(2,1)S(1)}) fusion(bf16[192,2304]{1,0:T(8,128)(2,1)} %param.9, s32[]{:T(128)S(6)} %select_n.19, s32[]{:T(128)S(6)} %select_n.17, s32[]{:T(128)S(6)} %select_n.18), kind=kLoop, calls=%fused_computation.2 | loop fusion | bytes 442380 | tf_op jit(solution)/shard_map/dynamic_slice | solution.py:329
  4.2 0.1 pad_maximum_fusion.1
  4.3 2.7 %collective-permute-start.2 = (bf16[192,384]{1,0:T(8,128)(2,1)S(1)}, bf16[192,384]{1,0:T(8,128)(2,1)}, u32[]{:S(2)}, u32[]{:S(2)}) collective-permute-start(bf16[192,384]{1,0:T(8,128)(2,1)S(1)} %pad_maximum_fusion.1), channel_id=1, source_target_pairs={{0,2},{1,3},{2,0},{3,1},{4,6},{5,7},{6,4},{7,5},{8,10},{9,11},{10,... | collective-permute-start | bytes 442376 | tf_op jit(solution)/shard_map/ppermute | solution.py:311
  7.0 0.3 collective-permute-start.5
  7.3 0.8 %pad_maximum_fusion.refs_4_ = bf16[192,576]{1,0:T(8,128)(2,1)} fusion(bf16[192,192]{1,0:T(8,128)(2,1)S(1)} %get-tuple-element.51, bf16[192,192]{1,0:T(8,128)(2,1)S(1)} %get-tuple-element.53, bf16[192,192]{1,0:T(8,128)(2,1)S(1)} %get-tuple-element.52), kind=kLoop, calls=%fused_computation | loop fusion | flops 663552 | bytes 442368 | tf_op jit(solution)/shard_map/concatenate | solution.py:333
  8.1 1.6 %collective-permute-start.4 = (bf16[192,576]{1,0:T(8,128)(2,1)}, bf16[192,576]{1,0:T(8,128)(2,1)}, u32[]{:S(2)}, u32[]{:S(2)}) collective-permute-start(bf16[192,576]{1,0:T(8,128)(2,1)} %pad_maximum_fusion.refs_4_), channel_id=1, source_target_pairs={{0,1},{1,0},{2,3},{3,2},{4,5},{5,4},{6,7},{7,6},{8,9},{9,8},{10,11... | collective-permute-start | bytes 663560 | tf_op jit(solution)/shard_map/ppermute | solution.py:48
  10.4 8.8 %collective-permute-done.5.refs_6_ = bf16[192,192]{1,0:T(8,128)(2,1)} collective-permute-done((bf16[192,192]{1,0:T(8,128)(2,1)S(1)}, bf16[192,192]{1,0:T(8,128)(2,1)}, u32[]{:S(2)}, u32[]{:S(2)}) %collective-permute-start.5) | collective-permute-done | bytes 73760 | tf_op jit(solution)/shard_map/ppermute | solution.py:311
  19.1 0.0 collective-permute-done.2.refs_6_
  19.1 0.0 collective-permute-start.6
  19.1 2.0 %collective-permute-start.7 = (bf16[192,384]{1,0:T(8,128)(2,1)}, bf16[192,384]{1,0:T(8,128)(2,1)}, u32[]{:S(2)}, u32[]{:S(2)}) collective-permute-start(bf16[192,384]{1,0:T(8,128)(2,1)} %collective-permute-done.2.refs_6_), channel_id=1, source_target_pairs={{0,16},{4,20},{8,24},{12,28},{16,0},{20,4},{24,8},{28,12},{1,17},{... | collective-permute-start | bytes 442376 | tf_op jit(solution)/shard_map/ppermute | solution.py:48
  21.2 0.9 %shard_map.64 = (bf16[256,768]{1,0:T(8,128)(2,1)S(1)}, bf16[256,768]{1,0:T(8,128)(2,1)S(1)}) custom-call(bf16[256,768]{1,0:T(8,128)(2,1)S(1)} %bitcast.4, bf16[256,768]{1,0:T(8,128)(2,1)S(1)} %collective-permute-done.refs_1_, f32[768]{0:T(1024)S(1)} %copy-done.1, f32[768]{0:T(1024)S(1)} %copy-done.2), custom_call_target="tpu_custom_call" | custom-call | flops 99999997952 | bytes 300000000 | tf_op jit(solution)/shard_map/pallas_call | solution.py:349
  22.1 0.8 %collective-permute-done.3.refs_1_ = bf16[256,768]{1,0:T(8,128)(2,1)S(1)} collective-permute-done((bf16[256,768]{1,0:T(8,128)(2,1)S(1)}, bf16[256,768]{1,0:T(8,128)(2,1)S(1)}, u32[]{:S(2)}, u32[]{:S(2)}) %collective-permute-start.3) | collective-permute-done | bytes 393248 | tf_op jit(solution)/shard_map/ppermute | solution.py:48
  22.9 0.9 %shard_map.65 = (bf16[256,768]{1,0:T(8,128)(2,1)S(1)}, bf16[256,768]{1,0:T(8,128)(2,1)S(1)}) custom-call(bf16[256,768]{1,0:T(8,128)(2,1)S(1)} %collective-permute-done.1.refs_0_, bf16[256,768]{1,0:T(8,128)(2,1)S(1)} %collective-permute-done.3.refs_1_, f32[768]{0:T(1024)S(1)} %copy-done.1, f32[768]{0:T(1024)S(1)} %copy-done.2), custom_call_target="tpu_custom_call" | custom-call | flops 99999997952 | bytes 300000000 | tf_op jit(solution)/shard_map/pallas_call | solution.py:349
  23.8 0.6 %collective-permute-start.11 = (bf16[192,768]{1,0:T(8,128)(2,1)}, bf16[192,768]{1,0:T(8,128)(2,1)}, u32[]{:S(2)}, u32[]{:S(2)}) collective-permute-start(bf16[192,768]{1,0:T(8,128)(2,1)} %refs_0_.1), channel_id=1, source_target_pairs={{0,1},{1,0},{2,3},{3,2},{4,5},{5,4},{6,7},{7,6},{8,9},{9,8},{10,11... | collective-permute-start | bytes 884744 | tf_op jit(solution)/shard_map/ppermute | solution.py:48
  24.4 3.5 %collective-permute-start.12 = (bf16[192,768]{1,0:T(8,128)(2,1)}, bf16[192,768]{1,0:T(8,128)(2,1)}, u32[]{:S(2)}, u32[]{:S(2)}) collective-permute-start(bf16[192,768]{1,0:T(8,128)(2,1)} %refs_0_.1), channel_id=1, source_target_pairs={{0,2},{1,3},{2,0},{3,1},{4,7},{5,6},{6,5},{7,4},{8,10},{9,11},{10,... | collective-permute-start | bytes 884744 | tf_op jit(solution)/shard_map/ppermute | solution.py:311
  27.9 3.0 %shard_map.67 = (bf16[256,384]{1,0:T(8,128)(2,1)S(1)}, bf16[256,384]{1,0:T(8,128)(2,1)S(1)}, bf16[256,384]{1,0:T(8,128)(2,1)S(1)}, bf16[256,384]{1,0:T(8,128)(2,1)S(1)}, bf16[3,64,128]{2,1,0:T(8,128)(2,1)}) custom-call(bf16[256,768]{1,0:T(8,128)(2,1)S(1)} %get-tuple-element.28.refs_0_, bf16[256,768]{1,0:T(8,128)(2,1)S(1)} %get-tuple-element.29.refs_1_, ...), custom_call_target="tpu_custom_call" | custom-call | flops 199999995904 | bytes 600000000 | tf_op jit(solution)/shard_map/pallas_call | solution.py:359
  30.9 0.0 collective-permute-start.8
  30.9 1.8 %shard_map.66 = (bf16[256,192]{1,0:T(8,128)(2,1)S(1)}, bf16[256,192]{1,0:T(8,128)(2,1)S(1)}, bf16[256,192]{1,0:T(8,128)(2,1)S(1)}, bf16[256,192]{1,0:T(8,128)(2,1)S(1)}) custom-call(bf16[256,768]{1,0:T(8,128)(2,1)S(1)} %get-tuple-element.28.refs_0_, bf16[256,768]{1,0:T(8,128)(2,1)S(1)} %get-tuple-element.29.refs_1_, ...), custom_call_target="tpu_custom_call" | custom-call | flops 99999997952 | bytes 300000000 | tf_op jit(solution)/shard_map/pallas_call | solution.py:368
  32.7 4.5 %shard_map.68 = (f32[3,4,1,256]{3,2,1,0:T(1,128)S(1)}, f32[3,4,1,256]{3,2,1,0:T(1,128)S(1)}, f32[3,4,64,256]{3,2,1,0:T(8,128)S(1)}) custom-call(s32[1]{0:T(128)S(6)} %copy.7.valid_ref.refs_0_, bf16[256,192]{1,0:T(8,128)(2,1)S(1)} %get-tuple-element.34.refs_0_.refs_1_, bf16[256,192]{1,0:T(8,128)(2,1)S(1)} %get-tuple-element.35.refs_1_.refs_2_, ...), custom_call_target="tpu_custom_call" | custom-call | flops 4999999913984 | bytes 15000000512 | tf_op jit(solution)/shard_map/pallas_call | solution.py:375
  37.2 4.3 %collective-permute-done.12.refs_2_ = bf16[192,768]{1,0:T(8,128)(2,1)} collective-permute-done((bf16[192,768]{1,0:T(8,128)(2,1)}, bf16[192,768]{1,0:T(8,128)(2,1)}, u32[]{:S(2)}, u32[]{:S(2)}) %collective-permute-start.12) | collective-permute-done | bytes 294944 | tf_op jit(solution)/shard_map/ppermute | solution.py:311
  41.6 0.0 collective-permute-start.13
  41.6 0.0 collective-permute-done.8.refs_6_
  41.6 2.0 %shard_map.69 = (bf16[192,256]{1,0:T(8,128)(2,1)S(1)}, bf16[192,256]{1,0:T(8,128)(2,1)S(1)}, bf16[192,256]{1,0:T(8,128)(2,1)}, bf16[192,256]{1,0:T(8,128)(2,1)}) custom-call(s32[1]{0:T(128)S(6)} %copy.7.valid_ref.refs_0_, bf16[256,192]{1,0:T(8,128)(2,1)S(1)} %get-tuple-element.34.refs_0_.refs_1_, bf16[256,192]{1,0:T(8,128)(2,1)S(1)} %get-tuple-element.35.refs_1_.refs_2_, ...), custom_call_target="tpu_custom_call" | custom-call | flops 99999997952 | bytes 300000000 | tf_op jit(solution)/shard_map/pallas_call | solution.py:386
  43.6 0.5 %collective-permute-start.9 = (bf16[192,256]{1,0:T(8,128)(2,1)}, bf16[192,256]{1,0:T(8,128)(2,1)}, u32[]{:S(2)}, u32[]{:S(2)}) collective-permute-start(bf16[192,256]{1,0:T(8,128)(2,1)} %get-tuple-element.46), channel_id=1, source_target_pairs={{0,8},{4,12},{8,0},{12,4},{16,24},{20,28},{24,16},{28,20},{1,9},{5... | collective-permute-start | bytes 294920 | tf_op jit(solution)/shard_map/ppermute | solution.py:48
  44.2 1.3 %collective-permute-start.10 = (bf16[192,256]{1,0:T(8,128)(2,1)}, bf16[192,256]{1,0:T(8,128)(2,1)}, u32[]{:S(2)}, u32[]{:S(2)}) collective-permute-start(bf16[192,256]{1,0:T(8,128)(2,1)} %get-tuple-element.47), channel_id=1, source_target_pairs={{0,12},{4,8},{8,4},{12,0},{16,28},{20,24},{24,20},{28,16},{1,13},{... | collective-permute-start | bytes 294920 | tf_op jit(solution)/shard_map/ppermute | solution.py:48
  45.5 0.3 collective-permute-start.14
  45.8 1.2 %shard_map.70.refs_2_ = bf16[768,768]{1,0:T(8,128)(2,1)S(1)} custom-call(bf16[192,768]{1,0:T(8,128)(2,1)} %refs_0_.1, bf16[192,768]{1,0:T(8,128)(2,1)} %collective-permute-done.11.refs_1_, bf16[192,768]{1,0:T(8,128)(2,1)} %collective-permute-done.12.refs_2_, bf16[192,768]{1,0:T(8,128)(2,1)S(1)} %collective-permute-done.13.refs_3_), custom_call_target="tpu_custom_call" | custom-call | flops 99999997952 | bytes 300000000 | tf_op jit(solution)/shard_map/pallas_call | solution.py:394
  47.0 0.7 %shard_map.71.refs_3_ = f32[256,768]{1,0:T(8,128)S(1)} custom-call(bf16[192,256]{1,0:T(8,128)(2,1)S(1)} %get-tuple-element.49.refs_0_, bf16[192,256]{1,0:T(8,128)(2,1)S(1)} %collective-permute-done.14.refs_1_, bf16[768,768]{1,0:T(8,128)(2,1)S(1)} %shard_map.70.refs_2_, bf16[256,768]{1,0:T(8,128)(2,1)S(1)} %bitcast.5), custom_call_target="tpu_custom_call" | custom-call | flops 99999997952 | bytes 300000000 | tf_op jit(solution)/shard_map/pallas_call | solution.py:400
  47.7 1.8 %collective-permute-done.9.refs_0_ = bf16[192,256]{1,0:T(8,128)(2,1)} collective-permute-done((bf16[192,256]{1,0:T(8,128)(2,1)}, bf16[192,256]{1,0:T(8,128)(2,1)}, u32[]{:S(2)}, u32[]{:S(2)}) %collective-permute-start.9) | collective-permute-done | bytes 98336 | tf_op jit(solution)/shard_map/ppermute | solution.py:48
  49.5 1.3 %collective-permute-done.10.refs_1_ = bf16[192,256]{1,0:T(8,128)(2,1)} collective-permute-done((bf16[192,256]{1,0:T(8,128)(2,1)}, bf16[192,256]{1,0:T(8,128)(2,1)}, u32[]{:S(2)}, u32[]{:S(2)}) %collective-permute-start.10) | collective-permute-done | bytes 98336 | tf_op jit(solution)/shard_map/ppermute | solution.py:48
  50.9 2.4 %shard_map.72 = bf16[256,768]{1,0:T(8,128)(2,1)} custom-call(bf16[192,256]{1,0:T(8,128)(2,1)} %collective-permute-done.9.refs_0_, bf16[192,256]{1,0:T(8,128)(2,1)} %collective-permute-done.10.refs_1_, bf16[768,768]{1,0:T(8,128)(2,1)S(1)} %shard_map.70.refs_2_, f32[256,768]{1,0:T(8,128)S(1)} %shard_map.71.refs_3_), custom_call_target="tpu_custom_call" | custom-call | flops 99999997952 | bytes 300000000 | tf_op jit(solution)/shard_map/pallas_call | solution.py:403
  (16 shorter events, 0.0 us)
Async XLA Ops:
  0.0 21.2 %copy-start = (bf16[1,256,768]{2,1,0:T(8,128)(2,1)S(1)}, bf16[1,256,768]{2,1,0:T(8,128)(2,1)}, u32[]{:S(2)}) copy-start(bf16[1,256,768]{2,1,0:T(8,128)(2,1)} %param.6) | copy-start | bytes 1179652
  0.0 21.2 %copy-start.1 = (f32[768]{0:T(1024)S(1)}, f32[768]{0:T(1024)}, u32[]{:S(2)}) copy-start(f32[768]{0:T(1024)} %refs_2_.3) | copy-start | bytes 9220
  0.0 21.2 %copy-start.2 = (f32[768]{0:T(1024)S(1)}, f32[768]{0:T(1024)}, u32[]{:S(2)}) copy-start(f32[768]{0:T(1024)} %refs_3_.3) | copy-start | bytes 9220
  0.0 21.2 %collective-permute-start.1 = (bf16[256,768]{1,0:T(8,128)(2,1)}, bf16[256,768]{1,0:T(8,128)(2,1)S(1)}, u32[]{:S(2)}, u32[]{:S(2)}) collective-permute-start(bf16[256,768]{1,0:T(8,128)(2,1)} %bitcast.2), channel_id=1, source_target_pairs={{0,8},{4,12},{8,0},{12,4},{16,24},{20,28},{24,16},{28,20},{1,9},{5... | collective-permute-start | bytes 1179656 | tf_op jit(solution)/shard_map/ppermute | solution.py:48
  3.0 18.2 %collective-permute-start = (bf16[256,768]{1,0:T(8,128)(2,1)}, bf16[256,768]{1,0:T(8,128)(2,1)S(1)}, u32[]{:S(2)}, u32[]{:S(2)}) collective-permute-start(bf16[256,768]{1,0:T(8,128)(2,1)} %bitcast.3), channel_id=1, source_target_pairs={{0,4},{4,0},{8,12},{12,8},{16,20},{20,16},{24,28},{28,24},{1,5},{5... | collective-permute-start | bytes 1179656 | tf_op jit(solution)/shard_map/ppermute | solution.py:48
  4.3 14.8 %collective-permute-start.2 = (bf16[192,384]{1,0:T(8,128)(2,1)S(1)}, bf16[192,384]{1,0:T(8,128)(2,1)}, u32[]{:S(2)}, u32[]{:S(2)}) collective-permute-start(bf16[192,384]{1,0:T(8,128)(2,1)S(1)} %pad_maximum_fusion.1), channel_id=1, source_target_pairs={{0,2},{1,3},{2,0},{3,1},{4,6},{5,7},{6,4},{7,5},{8,10},{9,11},{10,... | collective-permute-start | bytes 442376 | tf_op jit(solution)/shard_map/ppermute | solution.py:311
  7.0 12.2 %collective-permute-start.5 = (bf16[192,192]{1,0:T(8,128)(2,1)S(1)}, bf16[192,192]{1,0:T(8,128)(2,1)}, u32[]{:S(2)}, u32[]{:S(2)}) collective-permute-start(bf16[192,192]{1,0:T(8,128)(2,1)S(1)} %get-tuple-element.51), channel_id=1, source_target_pairs={{0,2},{1,3},{2,0},{3,1},{4,6},{5,7},{6,4},{7,5},{8,10},{9,11},{10,... | collective-permute-start | bytes 221192 | tf_op jit(solution)/shard_map/ppermute | solution.py:311
  8.1 19.8 %collective-permute-start.4 = (bf16[192,576]{1,0:T(8,128)(2,1)}, bf16[192,576]{1,0:T(8,128)(2,1)}, u32[]{:S(2)}, u32[]{:S(2)}) collective-permute-start(bf16[192,576]{1,0:T(8,128)(2,1)} %pad_maximum_fusion.refs_4_), channel_id=1, source_target_pairs={{0,1},{1,0},{2,3},{3,2},{4,5},{5,4},{6,7},{7,6},{8,9},{9,8},{10,11... | collective-permute-start | bytes 663560 | tf_op jit(solution)/shard_map/ppermute | solution.py:48
  19.1 11.8 %collective-permute-start.6 = (bf16[192,192]{1,0:T(8,128)(2,1)}, bf16[192,192]{1,0:T(8,128)(2,1)}, u32[]{:S(2)}, u32[]{:S(2)}) collective-permute-start(bf16[192,192]{1,0:T(8,128)(2,1)} %collective-permute-done.5.refs_6_), channel_id=1, source_target_pairs={{0,16},{4,20},{8,24},{12,28},{16,0},{20,4},{24,8},{28,12},{1,17},{... | collective-permute-start | bytes 221192 | tf_op jit(solution)/shard_map/ppermute | solution.py:48
  19.1 8.7 %collective-permute-start.7 = (bf16[192,384]{1,0:T(8,128)(2,1)}, bf16[192,384]{1,0:T(8,128)(2,1)}, u32[]{:S(2)}, u32[]{:S(2)}) collective-permute-start(bf16[192,384]{1,0:T(8,128)(2,1)} %collective-permute-done.2.refs_6_), channel_id=1, source_target_pairs={{0,16},{4,20},{8,24},{12,28},{16,0},{20,4},{24,8},{28,12},{1,17},{... | collective-permute-start | bytes 442376 | tf_op jit(solution)/shard_map/ppermute | solution.py:48
  21.2 1.7 %collective-permute-start.3 = (bf16[256,768]{1,0:T(8,128)(2,1)S(1)}, bf16[256,768]{1,0:T(8,128)(2,1)S(1)}, u32[]{:S(2)}, u32[]{:S(2)}) collective-permute-start(bf16[256,768]{1,0:T(8,128)(2,1)S(1)} %collective-permute-done.1.refs_0_), channel_id=1, source_target_pairs={{0,4},{4,0},{8,12},{12,8},{16,20},{20,16},{24,28},{28,24},{1,5},{5... | collective-permute-start | bytes 1179656 | tf_op jit(solution)/shard_map/ppermute | solution.py:48
  23.8 22.0 %collective-permute-start.11 = (bf16[192,768]{1,0:T(8,128)(2,1)}, bf16[192,768]{1,0:T(8,128)(2,1)}, u32[]{:S(2)}, u32[]{:S(2)}) collective-permute-start(bf16[192,768]{1,0:T(8,128)(2,1)} %refs_0_.1), channel_id=1, source_target_pairs={{0,1},{1,0},{2,3},{3,2},{4,5},{5,4},{6,7},{7,6},{8,9},{9,8},{10,11... | collective-permute-start | bytes 884744 | tf_op jit(solution)/shard_map/ppermute | solution.py:48
  24.4 17.2 %collective-permute-start.12 = (bf16[192,768]{1,0:T(8,128)(2,1)}, bf16[192,768]{1,0:T(8,128)(2,1)}, u32[]{:S(2)}, u32[]{:S(2)}) collective-permute-start(bf16[192,768]{1,0:T(8,128)(2,1)} %refs_0_.1), channel_id=1, source_target_pairs={{0,2},{1,3},{2,0},{3,1},{4,7},{5,6},{6,5},{7,4},{8,10},{9,11},{10,... | collective-permute-start | bytes 884744 | tf_op jit(solution)/shard_map/ppermute | solution.py:311
  30.9 10.7 %collective-permute-start.8 = (bf16[3,64,128]{2,1,0:T(8,128)(2,1)}, bf16[3,64,128]{2,1,0:T(8,128)(2,1)}, u32[]{:S(2)}, u32[]{:S(2)}) collective-permute-start(bf16[3,64,128]{2,1,0:T(8,128)(2,1)} %get-tuple-element.38.refs_5_), channel_id=1, source_target_pairs={{0,16},{4,20},{8,24},{12,28},{16,0},{20,4},{24,8},{28,12},{1,17},{... | collective-permute-start | bytes 147464 | tf_op jit(solution)/shard_map/ppermute | solution.py:48
  41.6 4.2 %collective-permute-start.13 = (bf16[192,768]{1,0:T(8,128)(2,1)}, bf16[192,768]{1,0:T(8,128)(2,1)S(1)}, u32[]{:S(2)}, u32[]{:S(2)}) collective-permute-start(bf16[192,768]{1,0:T(8,128)(2,1)} %collective-permute-done.12.refs_2_), channel_id=1, source_target_pairs={{0,4},{4,0},{8,12},{12,8},{16,20},{20,16},{24,28},{28,24},{1,5},{5... | collective-permute-start | bytes 884744 | tf_op jit(solution)/shard_map/ppermute | solution.py:48
  43.6 5.9 %collective-permute-start.9 = (bf16[192,256]{1,0:T(8,128)(2,1)}, bf16[192,256]{1,0:T(8,128)(2,1)}, u32[]{:S(2)}, u32[]{:S(2)}) collective-permute-start(bf16[192,256]{1,0:T(8,128)(2,1)} %get-tuple-element.46), channel_id=1, source_target_pairs={{0,8},{4,12},{8,0},{12,4},{16,24},{20,28},{24,16},{28,20},{1,9},{5... | collective-permute-start | bytes 294920 | tf_op jit(solution)/shard_map/ppermute | solution.py:48
  44.2 6.7 %collective-permute-start.10 = (bf16[192,256]{1,0:T(8,128)(2,1)}, bf16[192,256]{1,0:T(8,128)(2,1)}, u32[]{:S(2)}, u32[]{:S(2)}) collective-permute-start(bf16[192,256]{1,0:T(8,128)(2,1)} %get-tuple-element.47), channel_id=1, source_target_pairs={{0,12},{4,8},{8,4},{12,0},{16,28},{20,24},{24,20},{28,16},{1,13},{... | collective-permute-start | bytes 294920 | tf_op jit(solution)/shard_map/ppermute | solution.py:48
  45.5 1.5 %collective-permute-start.14 = (bf16[192,256]{1,0:T(8,128)(2,1)S(1)}, bf16[192,256]{1,0:T(8,128)(2,1)S(1)}, u32[]{:S(2)}, u32[]{:S(2)}) collective-permute-start(bf16[192,256]{1,0:T(8,128)(2,1)S(1)} %get-tuple-element.50), channel_id=1, source_target_pairs={{0,4},{4,0},{8,12},{12,8},{16,20},{20,16},{24,28},{28,24},{1,5},{5... | collective-permute-start | bytes 294920 | tf_op jit(solution)/shard_map/ppermute | solution.py:48

commit v4 on v3

--- a/solution.py
+++ b/solution.py
@@ -33,7 +33,7 @@
         out_specs=outs,
         scratch_shapes=list(scratch),
         cost_estimate=pl.CostEstimate(
-            flops=micros * 100_000_000_000, transcendentals=0, bytes_accessed=micros * 300_000_000
+            flops=int(micros * 3_000_000_000), transcendentals=0, bytes_accessed=int(micros * 9_000_000)
         ),
         compiler_params=pltpu.CompilerParams(vmem_limit_bytes=VMEM_LIMIT),
     )
@@ -97,13 +97,11 @@
     return shard % SHARDS, shard // SHARDS
 
 
-def head_slice(index, part=0):
-    low = part * GROUP_WIDTH + index * HEAD_DIM
-    return slice(low, low + HEAD_DIM)
-
-
-def pair_slices(index):
-    return head_slice(index, 0), head_slice(index, 1)
+def head_slices(index):
+    return [
+        slice(part * GROUP_WIDTH + index * HEAD_DIM, part * GROUP_WIDTH + (index + 1) * HEAD_DIM)
+        for part in range(3)
+    ]
 
 
 def wide_rows(head, rows):
@@ -118,11 +116,9 @@
 
 
 def assemble(whole_ref, refs, sources):
-    width = whole_ref.shape[1]
     for ref, source in zip(refs, sources):
-        rows, wide = ref.shape
-        start = wide - width if width == GROUP_WIDTH else 0
-        whole_ref[pl.ds(pl.multiple_of(source * rows, 16), rows), :] = ref[:, start : start + width]
+        rows = ref.shape[0]
+        whole_ref[pl.ds(pl.multiple_of(source * rows, 16), rows), :] = ref[...]
 
 
 def sources(n_mp, turn, shared):
@@ -134,25 +130,19 @@
 
 def project_body(n_mp, shared, *refs):
     normed_refs, refs = refs[:SHARDS], refs[SHARDS:]
-    weight_refs, (*out_refs, whole_ref) = refs[:n_mp], refs[n_mp:]
-    _, group = group_indices()
+    weight_refs, (*out_refs, sent_ref, whole_ref) = refs[:n_mp], refs[n_mp:]
+    member, group = group_indices()
     assemble(whole_ref, weight_refs, sources(n_mp, group % 2, shared))
     for normed_ref, out_ref in zip(normed_refs, out_refs):
         out_ref[...] = product(normed_ref[...], whole_ref[...]).astype(jnp.bfloat16)
-
-
-def key_value_body(n_mp, shared, *refs):
-    *refs, sent_ref, whole_ref = refs
-    project_body(n_mp, shared, *refs, whole_ref)
-    out_refs = refs[-SHARDS:]
-    member, _ = group_indices()
     shard_rows = out_refs[0].shape[0]
     depth = shard_rows // WIDE
     for index in range(GROUP_HEADS):
+        _, key_at, value_at = head_slices(index)
         taken = wide_rows(member * GROUP_HEADS + index, shard_rows)
         for shard, out_ref in enumerate(out_refs):
             sent_ref[index, shard * depth : (shard + 1) * depth, :] = jnp.concatenate(
-                [out_ref[taken, at] for at in pair_slices(index)], axis=1
+                [out_ref[taken, key_at], out_ref[taken, value_at]], axis=1
             )
 
 
@@ -176,11 +166,10 @@
 
 
 def near_body(valid_ref, *refs):
-    q_refs, refs = refs[:SHARDS], refs[SHARDS:]
-    kv_refs, (max_ref, sum_ref, num_ref) = refs[:SHARDS], refs[SHARDS:]
+    qkv_refs, (max_ref, sum_ref, num_ref) = refs[:SHARDS], refs[SHARDS:]
     member, group = group_indices()
     valid = valid_ref[0]
-    rows = q_refs[0].shape[0]
+    rows = qkv_refs[0].shape[0]
     count = rows // MID
     bases = [(group * SHARDS + (member ^ apart)) * rows for apart in range(SHARDS)]
     place = place_of(lax.broadcasted_iota(jnp.int32, (rows, LANES), 0), rows)
@@ -189,21 +178,19 @@
     def widen(bias):
         return jnp.concatenate([bias] * (rows // LANES), axis=1)
 
-    for shard, (q_ref, kv_ref) in enumerate(zip(q_refs, kv_refs)):
+    for shard, ref in enumerate(qkv_refs):
         bias = widen(key_bias(place + bases[shard], valid))
         for index in range(GROUP_HEADS):
-            key_at, value_at = pair_slices(index)
-            stats = branch(q_ref[:, head_slice(index)], kv_ref[:, key_at], kv_ref[:, value_at], bias)
+            stats = branch(*(ref[:, at] for at in head_slices(index)), bias)
             max_ref[index, shard], sum_ref[index, shard], num_ref[index, shard] = stats
     entry = lax.broadcasted_iota(jnp.int32, (count, LANES), 0)
     depth = rows // WIDE
     for index in range(GROUP_HEADS):
         head = member * GROUP_HEADS + index
         taken = middle_rows(head, rows)
-        key_at, value_at = pair_slices(index)
         query, key, value = (
-            jnp.concatenate([ref[taken, at] for ref in some], axis=0)
-            for some, at in ((q_refs, head_slice(index)), (kv_refs, key_at), (kv_refs, value_at))
+            jnp.concatenate([ref[taken, at] for ref in qkv_refs], axis=0)
+            for at in head_slices(index)
         )
         position = entry % depth * WIDE + entry // depth * MID + head % MID
         bias = widen(
@@ -224,12 +211,12 @@
 
 
 def far_body(n_groups, valid_ref, *refs):
-    q_refs, refs = refs[:SHARDS], refs[SHARDS:]
+    qkv_refs, refs = refs[:SHARDS], refs[SHARDS:]
     sent_refs, refs = refs[:n_groups], refs[n_groups:]
     (max_ref, sum_ref, num_ref), out_refs = refs[:3], refs[3:]
     member, group = group_indices()
     valid = valid_ref[0]
-    rows = q_refs[0].shape[0]
+    rows = qkv_refs[0].shape[0]
     depth = rows // WIDE
     count = SHARDS * depth
     entry = lax.broadcasted_iota(jnp.int32, (count, count), 0)
@@ -237,7 +224,8 @@
     for index in range(GROUP_HEADS):
         head = member * GROUP_HEADS + index
         taken = wide_rows(head, rows)
-        query = jnp.concatenate([ref[taken, head_slice(index)] for ref in q_refs], axis=0)
+        query_at = head_slices(index)[0]
+        query = jnp.concatenate([ref[taken, query_at] for ref in qkv_refs], axis=0)
         bias = jnp.concatenate(
             [
                 key_bias(
@@ -328,25 +316,19 @@
         start = part * width + member * GROUP_WIDTH
         return lax.dynamic_slice(w_qkv, (0, start), (weight_rows, GROUP_WIDTH))
 
-    key_value = jnp.concatenate([columns(1), columns(2)], axis=1)
-    query = columns(0)
-    mine = near(jnp.concatenate([key_value, query], axis=1))
-    closest = [flip(mine, "mp", 1)] if shared else []
-    weights = []
-    for value in (key_value, query):
-        earlier = [blocks[1 + len(closest)] for blocks in weights]
-        others = fetch(near(value), lambda c: c // SHARDS % 2, shared, SHARDS, earlier)
-        weights.append([mine] + closest + others)
+    mine = near(jnp.concatenate([columns(part) for part in range(3)], axis=1))
+    others = fetch(mine, lambda c: c // SHARDS % 2, shared, SHARDS)
 
     x_pair = flip(x, "ctx", 1)
-    x_far = flip(x, "ctx", 2)
-    x_far = after(x_far, weights[0][2])
+    x_far = flip(after(x, mine), "ctx", 2)
+    weights = [mine] + ([flip(after(mine, x_far), "mp", 1)] if shared else []) + others
+    x_far = after(x_far, others[0])
     x_last = flip(x_far, "ctx", 1)
     x_own = near(x)
     gain, bias = near(norm_gain), near(norm_bias)
     normed = []
     for pair in ((x_own, x_pair), (x_far, x_last)):
-        normed += call(norm_body, [shape((rows, width), bf16)] * 2, n_in=4, micros=1)(
+        normed += call(norm_body, [shape((rows, width), bf16)] * 2, n_in=4, micros=0.01)(
             *pair, gain, bias
         )
 
@@ -354,24 +336,15 @@
     out_parts = [out_weight]
     if shared:
         out_parts.append(flip(out_weight, "mp", 1))
-    out_parts += fetch(out_weight, lambda c: c % 2, shared, 1)
-
-    *kv, sent = call(
-        lambda *refs: key_value_body(n_mp, shared, *refs),
-        [shape((rows, 2 * GROUP_WIDTH), bf16)] * SHARDS
+    *qkv, sent = call(
+        lambda *refs: project_body(n_mp, shared, *refs),
+        [shape((rows, 3 * GROUP_WIDTH), bf16)] * SHARDS
         + [shape((GROUP_HEADS, SHARDS * depth, 2 * HEAD_DIM), bf16)],
-        scratch=[pltpu.VMEM((width, 2 * GROUP_WIDTH), bf16)],
+        scratch=[pltpu.VMEM((width, 3 * GROUP_WIDTH), bf16)],
         n_in=SHARDS + n_mp,
         micros=2,
-    )(*normed, *weights[0])
+    )(*normed, *weights)
     sents = [sent] + [flip(sent, "ctx", SHARDS * apart) for apart in range(1, n_groups)]
-    q = call(
-        lambda *refs: project_body(n_mp, shared, *refs),
-        [shape((rows, GROUP_WIDTH), bf16)] * SHARDS,
-        scratch=[pltpu.VMEM((width, GROUP_WIDTH), bf16)],
-        n_in=SHARDS + n_mp,
-        micros=1,
-    )(*normed, *weights[1])
     stats = call(
         near_body,
         [
@@ -380,16 +353,17 @@
             shape((GROUP_HEADS, SHARDS, HEAD_DIM, rows), f32),
         ],
         n_scalar=1,
-        n_in=2 * SHARDS,
-        micros=50,
-    )(valid_count, *q, *kv)
+        n_in=SHARDS,
+        micros=5,
+    )(valid_count, *qkv)
+    out_parts += fetch(out_weight, lambda c: c % 2, shared, 1, stats[:1])
     attention = call(
         lambda *refs: far_body(n_groups, *refs),
         [shape((GROUP_WIDTH, rows), bf16)] * SHARDS,
         n_scalar=1,
         n_in=SHARDS + n_groups + 3,
         micros=1,
-    )(valid_count, *q, *sents, *stats)
+    )(valid_count, *qkv, *sents, after(stats[0], *out_parts[:3]), *stats[1:])
     received = [attention[0]] + [flip(attention[apart], "ctx", apart) for apart in range(1, SHARDS)]
     (whole_out,) = call(
         lambda *refs: gather_body(n_mp, shared, *refs),

time: 53.6 us -> 48.9 us (0.912)
  Pallas kernels: 17.4 us -> 10.7 us
  waiting for transfers between devices: 17.1 us -> 18.6 us
  starting transfers between devices: 15.9 us -> 17.1 us
  other arithmetic: 0.9 us -> 0.11 us
    pallas_call x4 -> x3, Pallas kernels: 6.48 us -> 3.29 us  [the longest x2 1.73 us: local(): call(norm_body, [shape((rows, width), bf16)] * 2, n_in=4, micros=0.01)]
    ppermute x12 -> x11, starting transfers between devices: 9.39 us -> 11.4 us  [flip(): return near(lax.ppermute(value, axis, pairs))]
    pallas_call x1, Pallas kernels: 2.03 us -> 0.59 us  [local(): call(lambda *refs: far_body(n_groups, *refs), [shape((GROUP_WIDTH, rows),...]
    ppermute x3 -> x2, waiting for transfers between devices: 13.1 us -> 14.4 us  [fetch(): direct = near(lax.ppermute(value, ('ctx', 'mp'), pairs))]
    pallas_call x1, Pallas kernels: 1.23 us -> 0.09 us  [local(): call(lambda *refs: gather_body(n_mp, shared, *refs), [shape((width, width...]
    pallas_call x1, Pallas kernels: 2.39 us -> 1.45 us  [local(): call(update_body, [jax.ShapeDtypeStruct((rows, width), bf16)], n_in=half...]
    ppermute x3 -> x2, starting transfers between devices: 6.51 us -> 5.62 us  [fetch(): direct = near(lax.ppermute(value, ('ctx', 'mp'), pairs))]
    concatenate x2 -> x1, other arithmetic: 0.9 us -> 0.11 us  [local(): mine = near(jnp.concatenate([columns(part) for part in range(3)], axis=1))]
  transfers between devices with their start and end apart: 15 -> 13, of which waited for: 5 -> 7; matrix products, arithmetic and copies ran while one was open for 4% -> 0% of each run, Pallas kernels for 28% -> 19%
where the time goes in v4:
time: 48.9 us; the launch traced here: 48.5 us
  waiting for transfers between devices  18.6 us (38%)
  starting transfers between devices  17.1 us (35%)
  Pallas kernels  10.7 us (22%)
  local copies, waits for them, and re-layouts  1.27 us (3%)
  between operations  0.78 us (2%)
    ppermute x2, waiting for transfers between devices, fetch(): direct = near(lax.ppermute(value, ('ctx', 'mp'), pairs))  14.4 us
    ppermute x11, starting transfers between devices, flip(): return near(lax.ppermute(value, axis, pairs))  11.4 us
    ppermute x2, starting transfers between devices, fetch(): direct = near(lax.ppermute(value, ('ctx', 'mp'), pairs))  5.62 us
    pallas_call x1, Pallas kernels, local(): call(near_body, [shape((GROUP_HEADS, SHARDS, 1, rows), f32), shape((GROUP...  4.57 us
    ppermute x11, waiting for transfers between devices, flip(): return near(lax.ppermute(value, axis, pairs))  4.11 us
    pallas_call x2, Pallas kernels, local(): call(norm_body, [shape((rows, width), bf16)] * 2, n_in=4, micros=0.01)  1.73 us
    pallas_call x1, Pallas kernels, local(): call(lambda *refs: project_body(n_mp, shared, *refs), [shape((rows, 3 * G...  1.56 us
    pallas_call x1, Pallas kernels, local(): call(update_body, [jax.ShapeDtypeStruct((rows, width), bf16)], n_in=half...  1.45 us
  transfers between devices with their start and end apart: 13, of which 7 were waited for; matrix products, arithmetic and copies ran while one was open for 0% of the time, Pallas kernels for 19%

profile of v4, /device:TPU:0, one launch (start us, length us, event | category | flops | bytes accessed | tf_op | source)
XLA Modules:
  0.0 48.5 jit_solution(2538529232193295941)
XLA Ops:
  0.0 1.3 %constant_dynamic-slice_fusion.2 = (bf16[192,192]{1,0:T(8,128)(2,1)S(1)}, bf16[192,192]{1,0:T(8,128)(2,1)S(1)}, bf16[192,192]{1,0:T(8,128)(2,1)S(1)}) fusion(bf16[192,2304]{1,0:T(8,128)(2,1)} %param.9, s32[]{:T(128)S(6)} %select_n.17, s32[]{:T(128)S(6)} %select_n.19, s32[]{:T(128)S(6)} %select_n.18), kind=kLoop, calls=%fused_computation.3 | loop fusion | bytes 442380 | tf_op jit(solution)/shard_map/dynamic_slice | solution.py:317
  1.3 0.0 copy-start.3
  1.3 0.1 pad_maximum_fusion.refs_4_
  1.4 3.0 %collective-permute-start.1 = (bf16[256,768]{1,0:T(8,128)(2,1)S(1)}, bf16[256,768]{1,0:T(8,128)(2,1)S(1)}, u32[]{:S(2)}, u32[]{:S(2)}) collective-permute-start(bf16[256,768]{1,0:T(8,128)(2,1)S(1)} %bitcast.2), channel_id=1, source_target_pairs={{0,8},{4,12},{8,0},{12,4},{16,24},{20,28},{24,16},{28,20},{1,9},{5... | collective-permute-start | bytes 1179656 | tf_op jit(solution)/shard_map/ppermute | solution.py:48
  4.4 2.6 %collective-permute-start.2 = (bf16[192,576]{1,0:T(8,128)(2,1)S(1)}, bf16[192,576]{1,0:T(8,128)(2,1)S(1)}, u32[]{:S(2)}, u32[]{:S(2)}) collective-permute-start(bf16[192,576]{1,0:T(8,128)(2,1)S(1)} %pad_maximum_fusion.refs_4_), channel_id=1, source_target_pairs={{0,2},{1,3},{2,0},{3,1},{4,6},{5,7},{6,4},{7,5},{8,10},{9,11},{10,... | collective-permute-start | bytes 663560 | tf_op jit(solution)/shard_map/ppermute | solution.py:299
  7.0 11.0 %collective-permute-done.2.refs_6_ = bf16[192,576]{1,0:T(8,128)(2,1)S(1)} collective-permute-done((bf16[192,576]{1,0:T(8,128)(2,1)S(1)}, bf16[192,576]{1,0:T(8,128)(2,1)S(1)}, u32[]{:S(2)}, u32[]{:S(2)}) %collective-permute-start.2) | collective-permute-done | bytes 221216 | tf_op jit(solution)/shard_map/ppermute | solution.py:299
  18.0 0.0 collective-permute-done.1.refs_0_
  18.0 0.0 collective-permute-start.3
  18.0 0.0 collective-permute-start.5
  18.0 2.2 %collective-permute-start.4 = (bf16[192,576]{1,0:T(8,128)(2,1)S(1)}, bf16[192,576]{1,0:T(8,128)(2,1)S(1)}, u32[]{:S(2)}, u32[]{:S(2)}) collective-permute-start(bf16[192,576]{1,0:T(8,128)(2,1)S(1)} %pad_maximum_fusion.refs_4_), channel_id=1, source_target_pairs={{0,1},{1,0},{2,3},{3,2},{4,5},{5,4},{6,7},{7,6},{8,9},{9,8},{10,11... | collective-permute-start | bytes 663560 | tf_op jit(solution)/shard_map/ppermute | solution.py:48
  20.9 0.9 %shard_map.64 = (bf16[256,768]{1,0:T(8,128)(2,1)S(1)}, bf16[256,768]{1,0:T(8,128)(2,1)S(1)}) custom-call(bf16[256,768]{1,0:T(8,128)(2,1)S(1)} %bitcast.4, bf16[256,768]{1,0:T(8,128)(2,1)S(1)} %collective-permute-done.refs_1_, f32[768]{0:T(1024)S(1)} %copy-done.1, f32[768]{0:T(1024)S(1)} %copy-done.2), custom_call_target="tpu_custom_call" | custom-call | flops 30000000 | bytes 90000 | tf_op jit(solution)/shard_map/pallas_call | solution.py:331
  21.8 0.0 collective-permute-done.3.refs_1_
  21.8 0.9 %shard_map.65 = (bf16[256,768]{1,0:T(8,128)(2,1)S(1)}, bf16[256,768]{1,0:T(8,128)(2,1)S(1)}) custom-call(bf16[256,768]{1,0:T(8,128)(2,1)S(1)} %collective-permute-done.1.refs_0_, bf16[256,768]{1,0:T(8,128)(2,1)S(1)} %collective-permute-done.3.refs_1_, f32[768]{0:T(1024)S(1)} %copy-done.1, f32[768]{0:T(1024)S(1)} %copy-done.2), custom_call_target="tpu_custom_call" | custom-call | flops 30000000 | bytes 90000 | tf_op jit(solution)/shard_map/pallas_call | solution.py:331
  22.6 0.1 collective-permute-start.7
  22.7 3.0 %collective-permute-start.8 = (bf16[192,768]{1,0:T(8,128)(2,1)S(1)}, bf16[192,768]{1,0:T(8,128)(2,1)S(1)}, u32[]{:S(2)}, u32[]{:S(2)}) collective-permute-start(bf16[192,768]{1,0:T(8,128)(2,1)S(1)} %copy-done.3), channel_id=1, source_target_pairs={{0,2},{1,3},{2,0},{3,1},{4,7},{5,6},{6,5},{7,4},{8,10},{9,11},{10,... | collective-permute-start | bytes 884744 | tf_op jit(solution)/shard_map/ppermute | solution.py:299
  25.8 0.6 %collective-permute-done.5.refs_7_ = bf16[192,576]{1,0:T(8,128)(2,1)S(1)} collective-permute-done((bf16[192,576]{1,0:T(8,128)(2,1)S(1)}, bf16[192,576]{1,0:T(8,128)(2,1)S(1)}, u32[]{:S(2)}, u32[]{:S(2)}) %collective-permute-start.5) | collective-permute-done | bytes 221216 | tf_op jit(solution)/shard_map/ppermute | solution.py:48
  26.4 0.6 %collective-permute-done.4.refs_5_ = bf16[192,576]{1,0:T(8,128)(2,1)S(1)} collective-permute-done((bf16[192,576]{1,0:T(8,128)(2,1)S(1)}, bf16[192,576]{1,0:T(8,128)(2,1)S(1)}, u32[]{:S(2)}, u32[]{:S(2)}) %collective-permute-start.4) | collective-permute-done | bytes 221216 | tf_op jit(solution)/shard_map/ppermute | solution.py:48
  26.9 1.6 %shard_map.66 = (bf16[256,576]{1,0:T(8,128)(2,1)S(1)}, bf16[256,576]{1,0:T(8,128)(2,1)S(1)}, bf16[256,576]{1,0:T(8,128)(2,1)S(1)}, bf16[256,576]{1,0:T(8,128)(2,1)S(1)}, bf16[3,64,128]{2,1,0:T(8,128)(2,1)S(1)}) custom-call(bf16[256,768]{1,0:T(8,128)(2,1)S(1)} %get-tuple-element.27.refs_0_, bf16[256,768]{1,0:T(8,128)(2,1)S(1)} %get-tuple-element.28.refs_1_, ...), custom_call_target="tpu_custom_call" | custom-call | flops 6000000000 | bytes 18000000 | tf_op jit(solution)/shard_map/pallas_call | solution.py:339
  28.5 1.9 %collective-permute-start.6 = (bf16[3,64,128]{2,1,0:T(8,128)(2,1)S(1)}, bf16[3,64,128]{2,1,0:T(8,128)(2,1)S(1)}, u32[]{:S(2)}, u32[]{:S(2)}) collective-permute-start(bf16[3,64,128]{2,1,0:T(8,128)(2,1)S(1)} %get-tuple-element.38.refs_5_), channel_id=1, source_target_pairs={{0,16},{4,20},{8,24},{12,28},{16,0},{20,4},{24,8},{28,12},{1,17},{... | collective-permute-start | bytes 147464 | tf_op jit(solution)/shard_map/ppermute | solution.py:48
  30.4 4.6 %shard_map.67 = (f32[3,4,1,256]{3,2,1,0:T(1,128)S(1)}, f32[3,4,1,256]{3,2,1,0:T(1,128)S(1)}, f32[3,4,64,256]{3,2,1,0:T(8,128)S(1)}) custom-call(s32[1]{0:T(128)S(6)} %copy.7.valid_ref.refs_0_, bf16[256,576]{1,0:T(8,128)(2,1)S(1)} %get-tuple-element.34.refs_0_.refs_1_, bf16[256,576]{1,0:T(8,128)(2,1)S(1)} %get-tuple-element.35.refs_1_.refs_2_, ...), custom_call_target="tpu_custom_call" | custom-call | flops 15000000512 | bytes 45000000 | tf_op jit(solution)/shard_map/pallas_call | solution.py:348
  35.0 3.5 %collective-permute-done.8.refs_2_ = bf16[192,768]{1,0:T(8,128)(2,1)S(1)} collective-permute-done((bf16[192,768]{1,0:T(8,128)(2,1)S(1)}, bf16[192,768]{1,0:T(8,128)(2,1)S(1)}, u32[]{:S(2)}, u32[]{:S(2)}) %collective-permute-start.8) | collective-permute-done | bytes 294944 | tf_op jit(solution)/shard_map/ppermute | solution.py:299
  38.4 2.0 %collective-permute-start.11 = (bf16[192,768]{1,0:T(8,128)(2,1)S(1)}, bf16[192,768]{1,0:T(8,128)(2,1)S(1)}, u32[]{:S(2)}, u32[]{:S(2)}) collective-permute-start(bf16[192,768]{1,0:T(8,128)(2,1)S(1)} %collective-permute-done.8.refs_2_), channel_id=1, source_target_pairs={{0,4},{4,0},{8,12},{12,8},{16,20},{20,16},{24,28},{28,24},{1,5},{5... | collective-permute-start | bytes 884744 | tf_op jit(solution)/shard_map/ppermute | solution.py:48
  40.5 0.6 %shard_map.68 = (bf16[192,256]{1,0:T(8,128)(2,1)S(1)}, bf16[192,256]{1,0:T(8,128)(2,1)S(1)}, bf16[192,256]{1,0:T(8,128)(2,1)S(1)}, bf16[192,256]{1,0:T(8,128)(2,1)S(1)}) custom-call(s32[1]{0:T(128)S(6)} %copy.7.valid_ref.refs_0_, bf16[256,576]{1,0:T(8,128)(2,1)S(1)} %get-tuple-element.34.refs_0_.refs_1_, ...), custom_call_target="tpu_custom_call" | custom-call | flops 3000000000 | bytes 9000000 | tf_op jit(solution)/shard_map/pallas_call | solution.py:360
  41.1 0.6 %collective-permute-start.9 = (bf16[192,256]{1,0:T(8,128)(2,1)S(1)}, bf16[192,256]{1,0:T(8,128)(2,1)S(1)}, u32[]{:S(2)}, u32[]{:S(2)}) collective-permute-start(bf16[192,256]{1,0:T(8,128)(2,1)S(1)} %get-tuple-element.44), channel_id=1, source_target_pairs={{0,8},{4,12},{8,0},{12,4},{16,24},{20,28},{24,16},{28,20},{1,9},{5... | collective-permute-start | bytes 294920 | tf_op jit(solution)/shard_map/ppermute | solution.py:48
  41.7 0.8 %collective-permute-start.10 = (bf16[192,256]{1,0:T(8,128)(2,1)S(1)}, bf16[192,256]{1,0:T(8,128)(2,1)S(1)}, u32[]{:S(2)}, u32[]{:S(2)}) collective-permute-start(bf16[192,256]{1,0:T(8,128)(2,1)S(1)} %get-tuple-element.45), channel_id=1, source_target_pairs={{0,12},{4,8},{8,4},{12,0},{16,28},{20,24},{24,20},{28,16},{1,13},{... | collective-permute-start | bytes 294920 | tf_op jit(solution)/shard_map/ppermute | solution.py:48
  42.5 0.8 %collective-permute-start.12 = (bf16[192,256]{1,0:T(8,128)(2,1)S(1)}, bf16[192,256]{1,0:T(8,128)(2,1)S(1)}, u32[]{:S(2)}, u32[]{:S(2)}) collective-permute-start(bf16[192,256]{1,0:T(8,128)(2,1)S(1)} %get-tuple-element.48), channel_id=1, source_target_pairs={{0,4},{4,0},{8,12},{12,8},{16,20},{20,16},{24,28},{28,24},{1,5},{5... | collective-permute-start | bytes 294920 | tf_op jit(solution)/shard_map/ppermute | solution.py:48
  43.3 0.1 shard_map.69.refs_2_
  43.4 0.8 %collective-permute-done.12.refs_1_ = bf16[192,256]{1,0:T(8,128)(2,1)S(1)} collective-permute-done((bf16[192,256]{1,0:T(8,128)(2,1)S(1)}, bf16[192,256]{1,0:T(8,128)(2,1)S(1)}, u32[]{:S(2)}, u32[]{:S(2)}) %collective-permute-start.12) | collective-permute-done | bytes 98336 | tf_op jit(solution)/shard_map/ppermute | solution.py:48
  44.2 0.7 %shard_map.70.refs_3_ = f32[256,768]{1,0:T(8,128)S(1)} custom-call(bf16[192,256]{1,0:T(8,128)(2,1)S(1)} %get-tuple-element.47.refs_0_, bf16[192,256]{1,0:T(8,128)(2,1)S(1)} %collective-permute-done.12.refs_1_, bf16[768,768]{1,0:T(8,128)(2,1)S(1)} %shard_map.69.refs_2_, bf16[256,768]{1,0:T(8,128)(2,1)S(1)} %bitcast.5), custom_call_target="tpu_custom_call" | custom-call | flops 3000000000 | bytes 9000000 | tf_op jit(solution)/shard_map/pallas_call | solution.py:374
  45.0 1.9 %collective-permute-done.9.refs_0_ = bf16[192,256]{1,0:T(8,128)(2,1)S(1)} collective-permute-done((bf16[192,256]{1,0:T(8,128)(2,1)S(1)}, bf16[192,256]{1,0:T(8,128)(2,1)S(1)}, u32[]{:S(2)}, u32[]{:S(2)}) %collective-permute-start.9) | collective-permute-done | bytes 98336 | tf_op jit(solution)/shard_map/ppermute | solution.py:48
  46.8 0.2 collective-permute-done.10.refs_1_
  47.0 1.5 %shard_map.71 = bf16[256,768]{1,0:T(8,128)(2,1)} custom-call(bf16[192,256]{1,0:T(8,128)(2,1)S(1)} %collective-permute-done.9.refs_0_, bf16[192,256]{1,0:T(8,128)(2,1)S(1)} %collective-permute-done.10.refs_1_, bf16[768,768]{1,0:T(8,128)(2,1)S(1)} %shard_map.69.refs_2_, f32[256,768]{1,0:T(8,128)S(1)} %shard_map.70.refs_3_), custom_call_target="tpu_custom_call" | custom-call | flops 3000000000 | bytes 9000000 | tf_op jit(solution)/shard_map/pallas_call | solution.py:377
  (12 shorter events, 0.0 us)
Async XLA Ops:
  0.0 1.4 %copy-start = (bf16[1,256,768]{2,1,0:T(8,128)(2,1)S(1)}, bf16[1,256,768]{2,1,0:T(8,128)(2,1)}, u32[]{:S(2)}) copy-start(bf16[1,256,768]{2,1,0:T(8,128)(2,1)} %param.6) | copy-start | bytes 1179652
  0.0 20.9 %copy-start.1 = (f32[768]{0:T(1024)S(1)}, f32[768]{0:T(1024)}, u32[]{:S(2)}) copy-start(f32[768]{0:T(1024)} %refs_2_.3) | copy-start | bytes 9220
  0.0 20.9 %copy-start.2 = (f32[768]{0:T(1024)S(1)}, f32[768]{0:T(1024)}, u32[]{:S(2)}) copy-start(f32[768]{0:T(1024)} %refs_3_.3) | copy-start | bytes 9220
  1.3 21.4 %copy-start.3 = (bf16[192,768]{1,0:T(8,128)(2,1)S(1)}, bf16[192,768]{1,0:T(8,128)(2,1)}, u32[]{:S(2)}) copy-start(bf16[192,768]{1,0:T(8,128)(2,1)} %refs_0_.1) | copy-start | bytes 884740
  1.4 16.6 %collective-permute-start.1 = (bf16[256,768]{1,0:T(8,128)(2,1)S(1)}, bf16[256,768]{1,0:T(8,128)(2,1)S(1)}, u32[]{:S(2)}, u32[]{:S(2)}) collective-permute-start(bf16[256,768]{1,0:T(8,128)(2,1)S(1)} %bitcast.2), channel_id=1, source_target_pairs={{0,8},{4,12},{8,0},{12,4},{16,24},{20,28},{24,16},{28,20},{1,9},{5... | collective-permute-start | bytes 1179656 | tf_op jit(solution)/shard_map/ppermute | solution.py:48
  4.4 13.6 %collective-permute-start.2 = (bf16[192,576]{1,0:T(8,128)(2,1)S(1)}, bf16[192,576]{1,0:T(8,128)(2,1)S(1)}, u32[]{:S(2)}, u32[]{:S(2)}) collective-permute-start(bf16[192,576]{1,0:T(8,128)(2,1)S(1)} %pad_maximum_fusion.refs_4_), channel_id=1, source_target_pairs={{0,2},{1,3},{2,0},{3,1},{4,6},{5,7},{6,4},{7,5},{8,10},{9,11},{10,... | collective-permute-start | bytes 663560 | tf_op jit(solution)/shard_map/ppermute | solution.py:299
  7.0 13.8 %collective-permute-start = (bf16[256,768]{1,0:T(8,128)(2,1)S(1)}, bf16[256,768]{1,0:T(8,128)(2,1)S(1)}, u32[]{:S(2)}, u32[]{:S(2)}) collective-permute-start(bf16[256,768]{1,0:T(8,128)(2,1)S(1)} %bitcast.3), channel_id=1, source_target_pairs={{0,4},{4,0},{8,12},{12,8},{16,20},{20,16},{24,28},{28,24},{1,5},{5... | collective-permute-start | bytes 1179656 | tf_op jit(solution)/shard_map/ppermute | solution.py:48
  18.0 3.8 %collective-permute-start.3 = (bf16[256,768]{1,0:T(8,128)(2,1)S(1)}, bf16[256,768]{1,0:T(8,128)(2,1)S(1)}, u32[]{:S(2)}, u32[]{:S(2)}) collective-permute-start(bf16[256,768]{1,0:T(8,128)(2,1)S(1)} %collective-permute-done.1.refs_0_), channel_id=1, source_target_pairs={{0,4},{4,0},{8,12},{12,8},{16,20},{20,16},{24,28},{28,24},{1,5},{5... | collective-permute-start | bytes 1179656 | tf_op jit(solution)/shard_map/ppermute | solution.py:48
  18.0 8.4 %collective-permute-start.5 = (bf16[192,576]{1,0:T(8,128)(2,1)S(1)}, bf16[192,576]{1,0:T(8,128)(2,1)S(1)}, u32[]{:S(2)}, u32[]{:S(2)}) collective-permute-start(bf16[192,576]{1,0:T(8,128)(2,1)S(1)} %collective-permute-done.2.refs_6_), channel_id=1, source_target_pairs={{0,16},{4,20},{8,24},{12,28},{16,0},{20,4},{24,8},{28,12},{1,17},{... | collective-permute-start | bytes 663560 | tf_op jit(solution)/shard_map/ppermute | solution.py:48
  18.0 8.9 %collective-permute-start.4 = (bf16[192,576]{1,0:T(8,128)(2,1)S(1)}, bf16[192,576]{1,0:T(8,128)(2,1)S(1)}, u32[]{:S(2)}, u32[]{:S(2)}) collective-permute-start(bf16[192,576]{1,0:T(8,128)(2,1)S(1)} %pad_maximum_fusion.refs_4_), channel_id=1, source_target_pairs={{0,1},{1,0},{2,3},{3,2},{4,5},{5,4},{6,7},{7,6},{8,9},{9,8},{10,11... | collective-permute-start | bytes 663560 | tf_op jit(solution)/shard_map/ppermute | solution.py:48
  22.6 17.8 %collective-permute-start.7 = (bf16[192,768]{1,0:T(8,128)(2,1)S(1)}, bf16[192,768]{1,0:T(8,128)(2,1)S(1)}, u32[]{:S(2)}, u32[]{:S(2)}) collective-permute-start(bf16[192,768]{1,0:T(8,128)(2,1)S(1)} %copy-done.3), channel_id=1, source_target_pairs={{0,1},{1,0},{2,3},{3,2},{4,5},{5,4},{6,7},{7,6},{8,9},{9,8},{10,11... | collective-permute-start | bytes 884744 | tf_op jit(solution)/shard_map/ppermute | solution.py:48
  22.7 15.7 %collective-permute-start.8 = (bf16[192,768]{1,0:T(8,128)(2,1)S(1)}, bf16[192,768]{1,0:T(8,128)(2,1)S(1)}, u32[]{:S(2)}, u32[]{:S(2)}) collective-permute-start(bf16[192,768]{1,0:T(8,128)(2,1)S(1)} %copy-done.3), channel_id=1, source_target_pairs={{0,2},{1,3},{2,0},{3,1},{4,7},{5,6},{6,5},{7,4},{8,10},{9,11},{10,... | collective-permute-start | bytes 884744 | tf_op jit(solution)/shard_map/ppermute | solution.py:299
  28.5 12.0 %collective-permute-start.6 = (bf16[3,64,128]{2,1,0:T(8,128)(2,1)S(1)}, bf16[3,64,128]{2,1,0:T(8,128)(2,1)S(1)}, u32[]{:S(2)}, u32[]{:S(2)}) collective-permute-start(bf16[3,64,128]{2,1,0:T(8,128)(2,1)S(1)} %get-tuple-element.38.refs_5_), channel_id=1, source_target_pairs={{0,16},{4,20},{8,24},{12,28},{16,0},{20,4},{24,8},{28,12},{1,17},{... | collective-permute-start | bytes 147464 | tf_op jit(solution)/shard_map/ppermute | solution.py:48
  38.4 4.9 %collective-permute-start.11 = (bf16[192,768]{1,0:T(8,128)(2,1)S(1)}, bf16[192,768]{1,0:T(8,128)(2,1)S(1)}, u32[]{:S(2)}, u32[]{:S(2)}) collective-permute-start(bf16[192,768]{1,0:T(8,128)(2,1)S(1)} %collective-permute-done.8.refs_2_), channel_id=1, source_target_pairs={{0,4},{4,0},{8,12},{12,8},{16,20},{20,16},{24,28},{28,24},{1,5},{5... | collective-permute-start | bytes 884744 | tf_op jit(solution)/shard_map/ppermute | solution.py:48
  41.1 5.7 %collective-permute-start.9 = (bf16[192,256]{1,0:T(8,128)(2,1)S(1)}, bf16[192,256]{1,0:T(8,128)(2,1)S(1)}, u32[]{:S(2)}, u32[]{:S(2)}) collective-permute-start(bf16[192,256]{1,0:T(8,128)(2,1)S(1)} %get-tuple-element.44), channel_id=1, source_target_pairs={{0,8},{4,12},{8,0},{12,4},{16,24},{20,28},{24,16},{28,20},{1,9},{5... | collective-permute-start | bytes 294920 | tf_op jit(solution)/shard_map/ppermute | solution.py:48
  41.7 5.3 %collective-permute-start.10 = (bf16[192,256]{1,0:T(8,128)(2,1)S(1)}, bf16[192,256]{1,0:T(8,128)(2,1)S(1)}, u32[]{:S(2)}, u32[]{:S(2)}) collective-permute-start(bf16[192,256]{1,0:T(8,128)(2,1)S(1)} %get-tuple-element.45), channel_id=1, source_target_pairs={{0,12},{4,8},{8,4},{12,0},{16,28},{20,24},{24,20},{28,16},{1,13},{... | collective-permute-start | bytes 294920 | tf_op jit(solution)/shard_map/ppermute | solution.py:48
  42.5 1.7 %collective-permute-start.12 = (bf16[192,256]{1,0:T(8,128)(2,1)S(1)}, bf16[192,256]{1,0:T(8,128)(2,1)S(1)}, u32[]{:S(2)}, u32[]{:S(2)}) collective-permute-start(bf16[192,256]{1,0:T(8,128)(2,1)S(1)} %get-tuple-element.48), channel_id=1, source_target_pairs={{0,4},{4,0},{8,12},{12,8},{16,20},{20,16},{24,28},{28,24},{1,5},{5... | collective-permute-start | bytes 294920 | tf_op jit(solution)/shard_map/ppermute | solution.py:48

commit v5 on v4

--- a/solution.py
+++ b/solution.py
@@ -321,9 +321,8 @@
 
     x_pair = flip(x, "ctx", 1)
     x_far = flip(after(x, mine), "ctx", 2)
-    weights = [mine] + ([flip(after(mine, x_far), "mp", 1)] if shared else []) + others
-    x_far = after(x_far, others[0])
-    x_last = flip(x_far, "ctx", 1)
+    x_last = flip(after(x, mine), "ctx", 3)
+    weights = [mine] + ([flip(mine, "mp", 1)] if shared else []) + others
     x_own = near(x)
     gain, bias = near(norm_gain), near(norm_bias)
     normed = []
@@ -332,7 +331,7 @@
             *pair, gain, bias
         )
 
-    out_weight = after(near(w_out), normed[2])
+    out_weight = after(near(w_out), others[0])
     out_parts = [out_weight]
     if shared:
         out_parts.append(flip(out_weight, "mp", 1))
@@ -356,14 +355,14 @@
         n_in=SHARDS,
         micros=5,
     )(valid_count, *qkv)
-    out_parts += fetch(out_weight, lambda c: c % 2, shared, 1, stats[:1])
     attention = call(
         lambda *refs: far_body(n_groups, *refs),
         [shape((GROUP_WIDTH, rows), bf16)] * SHARDS,
         n_scalar=1,
         n_in=SHARDS + n_groups + 3,
         micros=1,
-    )(valid_count, *qkv, *sents, after(stats[0], *out_parts[:3]), *stats[1:])
+    )(valid_count, *qkv, *sents, *stats)
+    out_parts += fetch(out_weight, lambda c: c % 2, shared, 1, attention[1:2])
     received = [attention[0]] + [flip(attention[apart], "ctx", apart) for apart in range(1, SHARDS)]
     (whole_out,) = call(
         lambda *refs: gather_body(n_mp, shared, *refs),

time: 48.9 us -> 44.1 us (0.902)
  waiting for transfers between devices: 18.6 us -> 14.5 us
  starting transfers between devices: 17.1 us -> 16.5 us
    ppermute x2, waiting for transfers between devices: 14.4 us -> 7.89 us  [fetch(): direct = near(lax.ppermute(value, ('ctx', 'mp'), pairs))]
    ppermute x11, waiting for transfers between devices: 4.11 us -> 6.65 us  [flip(): return near(lax.ppermute(value, axis, pairs))]
    ppermute x11, starting transfers between devices: 11.4 us -> 9.15 us  [flip(): return near(lax.ppermute(value, axis, pairs))]
    ppermute x2, starting transfers between devices: 5.62 us -> 7.35 us  [fetch(): direct = near(lax.ppermute(value, ('ctx', 'mp'), pairs))]
  transfers between devices with their start and end apart: 13 -> 13, of which waited for: 7 -> 4; matrix products, arithmetic and copies ran while one was open for 0% -> 0% of each run, Pallas kernels for 19% -> 21%
where the time goes in v5:
time: 44.1 us; the launch traced here: 43.9 us
  starting transfers between devices  16.5 us (37%)
  waiting for transfers between devices  14.5 us (33%)
  Pallas kernels  10.7 us (24%)
  local copies, waits for them, and re-layouts  1.29 us (3%)
  between operations  0.78 us (2%)
    ppermute x11, starting transfers between devices, flip(): return near(lax.ppermute(value, axis, pairs))  9.15 us
    ppermute x2, waiting for transfers between devices, fetch(): direct = near(lax.ppermute(value, ('ctx', 'mp'), pairs))  7.89 us
    ppermute x2, starting transfers between devices, fetch(): direct = near(lax.ppermute(value, ('ctx', 'mp'), pairs))  7.35 us
    ppermute x11, waiting for transfers between devices, flip(): return near(lax.ppermute(value, axis, pairs))  6.65 us
    pallas_call x1, Pallas kernels, local(): call(near_body, [shape((GROUP_HEADS, SHARDS, 1, rows), f32), shape((GROUP...  4.56 us
    pallas_call x2, Pallas kernels, local(): call(norm_body, [shape((rows, width), bf16)] * 2, n_in=4, micros=0.01)  1.73 us
    pallas_call x1, Pallas kernels, local(): call(lambda *refs: project_body(n_mp, shared, *refs), [shape((rows, 3 * G...  1.57 us
    pallas_call x1, Pallas kernels, local(): call(update_body, [jax.ShapeDtypeStruct((rows, width), bf16)], n_in=half...  1.46 us
  transfers between devices with their start and end apart: 13, of which 4 were waited for; matrix products, arithmetic and copies ran while one was open for 0% of the time, Pallas kernels for 21%

profile of v5, /device:TPU:0, one launch (start us, length us, event | category | flops | bytes accessed | tf_op | source)
XLA Modules:
  0.0 43.9 jit_solution(10215894156835642813)
XLA Ops:
  0.0 1.3 %constant_dynamic-slice_fusion.2 = (bf16[192,192]{1,0:T(8,128)(2,1)S(1)}, bf16[192,192]{1,0:T(8,128)(2,1)S(1)}, bf16[192,192]{1,0:T(8,128)(2,1)S(1)}) fusion(bf16[192,2304]{1,0:T(8,128)(2,1)} %param.9, s32[]{:T(128)S(6)} %select_n.17, s32[]{:T(128)S(6)} %select_n.19, s32[]{:T(128)S(6)} %select_n.18), kind=kLoop, calls=%fused_computation.3 | loop fusion | bytes 442380 | tf_op jit(solution)/shard_map/dynamic_slice | solution.py:317
  1.3 0.1 pad_maximum_fusion.refs_4_
  1.4 4.1 %collective-permute-start.4 = (bf16[192,576]{1,0:T(8,128)(2,1)S(1)}, bf16[192,576]{1,0:T(8,128)(2,1)S(1)}, u32[]{:S(2)}, u32[]{:S(2)}) collective-permute-start(bf16[192,576]{1,0:T(8,128)(2,1)S(1)} %pad_maximum_fusion.refs_4_), channel_id=1, source_target_pairs={{0,2},{1,3},{2,0},{3,1},{4,6},{5,7},{6,4},{7,5},{8,10},{9,11},{10,... | collective-permute-start | bytes 663560 | tf_op jit(solution)/shard_map/ppermute | solution.py:299
  5.5 0.0 collective-permute-start
  5.5 1.5 %collective-permute-start.1 = (bf16[256,768]{1,0:T(8,128)(2,1)S(1)}, bf16[256,768]{1,0:T(8,128)(2,1)S(1)}, u32[]{:S(2)}, u32[]{:S(2)}) collective-permute-start(bf16[256,768]{1,0:T(8,128)(2,1)S(1)} %bitcast.3), channel_id=1, source_target_pairs={{0,8},{4,12},{8,0},{12,4},{16,24},{20,28},{24,16},{28,20},{1,9},{5... | collective-permute-start | bytes 1179656 | tf_op jit(solution)/shard_map/ppermute | solution.py:48
  7.0 0.4 collective-permute-start.2
  7.4 1.6 %collective-permute-start.3 = (bf16[192,576]{1,0:T(8,128)(2,1)S(1)}, bf16[192,576]{1,0:T(8,128)(2,1)S(1)}, u32[]{:S(2)}, u32[]{:S(2)}) collective-permute-start(bf16[192,576]{1,0:T(8,128)(2,1)S(1)} %pad_maximum_fusion.refs_4_), channel_id=1, source_target_pairs={{0,1},{1,0},{2,3},{3,2},{4,5},{5,4},{6,7},{7,6},{8,9},{9,8},{10,11... | collective-permute-start | bytes 663560 | tf_op jit(solution)/shard_map/ppermute | solution.py:48
  9.0 7.9 %collective-permute-done.4.refs_6_ = bf16[192,576]{1,0:T(8,128)(2,1)S(1)} collective-permute-done((bf16[192,576]{1,0:T(8,128)(2,1)S(1)}, bf16[192,576]{1,0:T(8,128)(2,1)S(1)}, u32[]{:S(2)}, u32[]{:S(2)}) %collective-permute-start.4) | collective-permute-done | bytes 221216 | tf_op jit(solution)/shard_map/ppermute | solution.py:299
  16.9 0.0 collective-permute-start.5
  17.5 0.0 collective-permute-done.refs_1_
  17.5 3.2 %collective-permute-start.10 = (bf16[192,768]{1,0:T(8,128)(2,1)S(1)}, bf16[192,768]{1,0:T(8,128)(2,1)S(1)}, u32[]{:S(2)}, u32[]{:S(2)}) collective-permute-start(bf16[192,768]{1,0:T(8,128)(2,1)S(1)} %copy-done.3), channel_id=1, source_target_pairs={{0,2},{1,3},{2,0},{3,1},{4,7},{5,6},{6,5},{7,4},{8,10},{9,11},{10,... | collective-permute-start | bytes 884744 | tf_op jit(solution)/shard_map/ppermute | solution.py:299
  20.8 0.9 %shard_map.64 = (bf16[256,768]{1,0:T(8,128)(2,1)S(1)}, bf16[256,768]{1,0:T(8,128)(2,1)S(1)}) custom-call(bf16[256,768]{1,0:T(8,128)(2,1)S(1)} %bitcast.5, bf16[256,768]{1,0:T(8,128)(2,1)S(1)} %collective-permute-done.refs_1_, f32[768]{0:T(1024)S(1)} %copy-done.1, f32[768]{0:T(1024)S(1)} %copy-done.2), custom_call_target="tpu_custom_call" | custom-call | flops 30000000 | bytes 90000 | tf_op jit(solution)/shard_map/pallas_call | solution.py:330
  21.6 0.0 collective-permute-done.1.refs_0_
  21.6 1.0 %collective-permute-start.9 = (bf16[192,768]{1,0:T(8,128)(2,1)S(1)}, bf16[192,768]{1,0:T(8,128)(2,1)S(1)}, u32[]{:S(2)}, u32[]{:S(2)}) collective-permute-start(bf16[192,768]{1,0:T(8,128)(2,1)S(1)} %copy-done.3), channel_id=1, source_target_pairs={{0,1},{1,0},{2,3},{3,2},{4,5},{5,4},{6,7},{7,6},{8,9},{9,8},{10,11... | collective-permute-start | bytes 884744 | tf_op jit(solution)/shard_map/ppermute | solution.py:48
  22.7 2.4 %collective-permute-done.2.refs_1_ = bf16[256,768]{1,0:T(8,128)(2,1)S(1)} collective-permute-done((bf16[256,768]{1,0:T(8,128)(2,1)S(1)}, bf16[256,768]{1,0:T(8,128)(2,1)S(1)}, u32[]{:S(2)}, u32[]{:S(2)}) %collective-permute-start.2) | collective-permute-done | bytes 393248 | tf_op jit(solution)/shard_map/ppermute | solution.py:48
  25.1 0.9 %shard_map.65 = (bf16[256,768]{1,0:T(8,128)(2,1)S(1)}, bf16[256,768]{1,0:T(8,128)(2,1)S(1)}) custom-call(bf16[256,768]{1,0:T(8,128)(2,1)S(1)} %collective-permute-done.1.refs_0_, bf16[256,768]{1,0:T(8,128)(2,1)S(1)} %collective-permute-done.2.refs_1_, f32[768]{0:T(1024)S(1)} %copy-done.1, f32[768]{0:T(1024)S(1)} %copy-done.2), custom_call_target="tpu_custom_call" | custom-call | flops 30000000 | bytes 90000 | tf_op jit(solution)/shard_map/pallas_call | solution.py:330
  26.0 0.0 collective-permute-done.3.refs_5_
  26.0 1.6 %shard_map.66 = (bf16[256,576]{1,0:T(8,128)(2,1)S(1)}, bf16[256,576]{1,0:T(8,128)(2,1)S(1)}, bf16[256,576]{1,0:T(8,128)(2,1)S(1)}, bf16[256,576]{1,0:T(8,128)(2,1)S(1)}, bf16[3,64,128]{2,1,0:T(8,128)(2,1)S(1)}) custom-call(bf16[256,768]{1,0:T(8,128)(2,1)S(1)} %get-tuple-element.24.refs_0_, bf16[256,768]{1,0:T(8,128)(2,1)S(1)} %get-tuple-element.25.refs_1_, ...), custom_call_target="tpu_custom_call" | custom-call | flops 6000000000 | bytes 18000000 | tf_op jit(solution)/shard_map/pallas_call | solution.py:338
  27.6 2.5 %collective-permute-start.6 = (bf16[3,64,128]{2,1,0:T(8,128)(2,1)S(1)}, bf16[3,64,128]{2,1,0:T(8,128)(2,1)S(1)}, u32[]{:S(2)}, u32[]{:S(2)}) collective-permute-start(bf16[3,64,128]{2,1,0:T(8,128)(2,1)S(1)} %get-tuple-element.33.refs_5_), channel_id=1, source_target_pairs={{0,16},{4,20},{8,24},{12,28},{16,0},{20,4},{24,8},{28,12},{1,17},{... | collective-permute-start | bytes 147464 | tf_op jit(solution)/shard_map/ppermute | solution.py:48
  30.1 4.6 %shard_map.67 = (f32[3,4,1,256]{3,2,1,0:T(1,128)S(1)}, f32[3,4,1,256]{3,2,1,0:T(1,128)S(1)}, f32[3,4,64,256]{3,2,1,0:T(8,128)S(1)}) custom-call(s32[1]{0:T(128)S(6)} %copy.7.valid_ref.refs_0_, bf16[256,576]{1,0:T(8,128)(2,1)S(1)} %get-tuple-element.29.refs_0_.refs_1_, bf16[256,576]{1,0:T(8,128)(2,1)S(1)} %get-tuple-element.30.refs_1_.refs_2_, ...), custom_call_target="tpu_custom_call" | custom-call | flops 15000000512 | bytes 45000000 | tf_op jit(solution)/shard_map/pallas_call | solution.py:347
  34.7 0.0 collective-permute-done.6.refs_6_
  34.7 0.6 %shard_map.68 = (bf16[192,256]{1,0:T(8,128)(2,1)S(1)}, bf16[192,256]{1,0:T(8,128)(2,1)S(1)}, bf16[192,256]{1,0:T(8,128)(2,1)S(1)}, bf16[192,256]{1,0:T(8,128)(2,1)S(1)}) custom-call(s32[1]{0:T(128)S(6)} %copy.7.valid_ref.refs_0_, bf16[256,576]{1,0:T(8,128)(2,1)S(1)} %get-tuple-element.29.refs_0_.refs_1_, ...), custom_call_target="tpu_custom_call" | custom-call | flops 3000000000 | bytes 9000000 | tf_op jit(solution)/shard_map/pallas_call | solution.py:358
  35.3 0.3 collective-permute-start.11
  35.6 0.3 collective-permute-start.12
  35.9 1.5 %collective-permute-start.7 = (bf16[192,256]{1,0:T(8,128)(2,1)S(1)}, bf16[192,256]{1,0:T(8,128)(2,1)S(1)}, u32[]{:S(2)}, u32[]{:S(2)}) collective-permute-start(bf16[192,256]{1,0:T(8,128)(2,1)S(1)} %get-tuple-element.37), channel_id=1, source_target_pairs={{0,8},{4,12},{8,0},{12,4},{16,24},{20,28},{24,16},{28,20},{1,9},{5... | collective-permute-start | bytes 294920 | tf_op jit(solution)/shard_map/ppermute | solution.py:48
  37.4 0.1 collective-permute-start.8
  37.5 0.1 shard_map.69.refs_2_
  37.6 0.0 collective-permute-done.12.refs_1_
  37.6 0.7 %shard_map.70.refs_3_ = f32[256,768]{1,0:T(8,128)S(1)} custom-call(bf16[192,256]{1,0:T(8,128)(2,1)S(1)} %get-tuple-element.42.refs_0_, bf16[192,256]{1,0:T(8,128)(2,1)S(1)} %collective-permute-done.12.refs_1_, bf16[768,768]{1,0:T(8,128)(2,1)S(1)} %shard_map.69.refs_2_, bf16[256,768]{1,0:T(8,128)(2,1)S(1)} %bitcast.6), custom_call_target="tpu_custom_call" | custom-call | flops 3000000000 | bytes 9000000 | tf_op jit(solution)/shard_map/pallas_call | solution.py:373
  38.3 3.0 %collective-permute-done.7.refs_0_ = bf16[192,256]{1,0:T(8,128)(2,1)S(1)} collective-permute-done((bf16[192,256]{1,0:T(8,128)(2,1)S(1)}, bf16[192,256]{1,0:T(8,128)(2,1)S(1)}, u32[]{:S(2)}, u32[]{:S(2)}) %collective-permute-start.7) | collective-permute-done | bytes 98336 | tf_op jit(solution)/shard_map/ppermute | solution.py:48
  41.2 1.2 %collective-permute-done.8.refs_1_ = bf16[192,256]{1,0:T(8,128)(2,1)S(1)} collective-permute-done((bf16[192,256]{1,0:T(8,128)(2,1)S(1)}, bf16[192,256]{1,0:T(8,128)(2,1)S(1)}, u32[]{:S(2)}, u32[]{:S(2)}) %collective-permute-start.8) | collective-permute-done | bytes 98336 | tf_op jit(solution)/shard_map/ppermute | solution.py:48
  42.5 1.5 %shard_map.71 = bf16[256,768]{1,0:T(8,128)(2,1)} custom-call(bf16[192,256]{1,0:T(8,128)(2,1)S(1)} %collective-permute-done.7.refs_0_, bf16[192,256]{1,0:T(8,128)(2,1)S(1)} %collective-permute-done.8.refs_1_, bf16[768,768]{1,0:T(8,128)(2,1)S(1)} %shard_map.69.refs_2_, f32[256,768]{1,0:T(8,128)S(1)} %shard_map.70.refs_3_), custom_call_target="tpu_custom_call" | custom-call | flops 3000000000 | bytes 9000000 | tf_op jit(solution)/shard_map/pallas_call | solution.py:376
  (12 shorter events, 0.0 us)
Async XLA Ops:
  0.0 5.5 %copy-start = (bf16[1,256,768]{2,1,0:T(8,128)(2,1)S(1)}, bf16[1,256,768]{2,1,0:T(8,128)(2,1)}, u32[]{:S(2)}) copy-start(bf16[1,256,768]{2,1,0:T(8,128)(2,1)} %param.6) | copy-start | bytes 1179652
  0.0 17.5 %copy-start.3 = (bf16[192,768]{1,0:T(8,128)(2,1)S(1)}, bf16[192,768]{1,0:T(8,128)(2,1)}, u32[]{:S(2)}) copy-start(bf16[192,768]{1,0:T(8,128)(2,1)} %refs_0_.1) | copy-start | bytes 884740
  0.0 20.8 %copy-start.1 = (f32[768]{0:T(1024)S(1)}, f32[768]{0:T(1024)}, u32[]{:S(2)}) copy-start(f32[768]{0:T(1024)} %refs_2_.3) | copy-start | bytes 9220
  0.0 20.8 %copy-start.2 = (f32[768]{0:T(1024)S(1)}, f32[768]{0:T(1024)}, u32[]{:S(2)}) copy-start(f32[768]{0:T(1024)} %refs_3_.3) | copy-start | bytes 9220
  1.4 15.5 %collective-permute-start.4 = (bf16[192,576]{1,0:T(8,128)(2,1)S(1)}, bf16[192,576]{1,0:T(8,128)(2,1)S(1)}, u32[]{:S(2)}, u32[]{:S(2)}) collective-permute-start(bf16[192,576]{1,0:T(8,128)(2,1)S(1)} %pad_maximum_fusion.refs_4_), channel_id=1, source_target_pairs={{0,2},{1,3},{2,0},{3,1},{4,6},{5,7},{6,4},{7,5},{8,10},{9,11},{10,... | collective-permute-start | bytes 663560 | tf_op jit(solution)/shard_map/ppermute | solution.py:299
  5.5 12.0 %collective-permute-start = (bf16[256,768]{1,0:T(8,128)(2,1)S(1)}, bf16[256,768]{1,0:T(8,128)(2,1)S(1)}, u32[]{:S(2)}, u32[]{:S(2)}) collective-permute-start(bf16[256,768]{1,0:T(8,128)(2,1)S(1)} %bitcast.2), channel_id=1, source_target_pairs={{0,4},{4,0},{8,12},{12,8},{16,20},{20,16},{24,28},{28,24},{1,5},{5... | collective-permute-start | bytes 1179656 | tf_op jit(solution)/shard_map/ppermute | solution.py:48
  5.5 16.1 %collective-permute-start.1 = (bf16[256,768]{1,0:T(8,128)(2,1)S(1)}, bf16[256,768]{1,0:T(8,128)(2,1)S(1)}, u32[]{:S(2)}, u32[]{:S(2)}) collective-permute-start(bf16[256,768]{1,0:T(8,128)(2,1)S(1)} %bitcast.3), channel_id=1, source_target_pairs={{0,8},{4,12},{8,0},{12,4},{16,24},{20,28},{24,16},{28,20},{1,9},{5... | collective-permute-start | bytes 1179656 | tf_op jit(solution)/shard_map/ppermute | solution.py:48
  7.0 18.1 %collective-permute-start.2 = (bf16[256,768]{1,0:T(8,128)(2,1)S(1)}, bf16[256,768]{1,0:T(8,128)(2,1)S(1)}, u32[]{:S(2)}, u32[]{:S(2)}) collective-permute-start(bf16[256,768]{1,0:T(8,128)(2,1)S(1)} %bitcast.4), channel_id=1, source_target_pairs={{0,12},{4,8},{8,4},{12,0},{16,28},{20,24},{24,20},{28,16},{1,13},{... | collective-permute-start | bytes 1179656 | tf_op jit(solution)/shard_map/ppermute | solution.py:48
  7.4 18.6 %collective-permute-start.3 = (bf16[192,576]{1,0:T(8,128)(2,1)S(1)}, bf16[192,576]{1,0:T(8,128)(2,1)S(1)}, u32[]{:S(2)}, u32[]{:S(2)}) collective-permute-start(bf16[192,576]{1,0:T(8,128)(2,1)S(1)} %pad_maximum_fusion.refs_4_), channel_id=1, source_target_pairs={{0,1},{1,0},{2,3},{3,2},{4,5},{5,4},{6,7},{7,6},{8,9},{9,8},{10,11... | collective-permute-start | bytes 663560 | tf_op jit(solution)/shard_map/ppermute | solution.py:48
  16.9 9.1 %collective-permute-start.5 = (bf16[192,576]{1,0:T(8,128)(2,1)S(1)}, bf16[192,576]{1,0:T(8,128)(2,1)S(1)}, u32[]{:S(2)}, u32[]{:S(2)}) collective-permute-start(bf16[192,576]{1,0:T(8,128)(2,1)S(1)} %collective-permute-done.4.refs_6_), channel_id=1, source_target_pairs={{0,16},{4,20},{8,24},{12,28},{16,0},{20,4},{24,8},{28,12},{1,17},{... | collective-permute-start | bytes 663560 | tf_op jit(solution)/shard_map/ppermute | solution.py:48
  17.5 17.7 %collective-permute-start.10 = (bf16[192,768]{1,0:T(8,128)(2,1)S(1)}, bf16[192,768]{1,0:T(8,128)(2,1)S(1)}, u32[]{:S(2)}, u32[]{:S(2)}) collective-permute-start(bf16[192,768]{1,0:T(8,128)(2,1)S(1)} %copy-done.3), channel_id=1, source_target_pairs={{0,2},{1,3},{2,0},{3,1},{4,7},{5,6},{6,5},{7,4},{8,10},{9,11},{10,... | collective-permute-start | bytes 884744 | tf_op jit(solution)/shard_map/ppermute | solution.py:299
  21.6 15.8 %collective-permute-start.9 = (bf16[192,768]{1,0:T(8,128)(2,1)S(1)}, bf16[192,768]{1,0:T(8,128)(2,1)S(1)}, u32[]{:S(2)}, u32[]{:S(2)}) collective-permute-start(bf16[192,768]{1,0:T(8,128)(2,1)S(1)} %copy-done.3), channel_id=1, source_target_pairs={{0,1},{1,0},{2,3},{3,2},{4,5},{5,4},{6,7},{7,6},{8,9},{9,8},{10,11... | collective-permute-start | bytes 884744 | tf_op jit(solution)/shard_map/ppermute | solution.py:48
  27.6 7.1 %collective-permute-start.6 = (bf16[3,64,128]{2,1,0:T(8,128)(2,1)S(1)}, bf16[3,64,128]{2,1,0:T(8,128)(2,1)S(1)}, u32[]{:S(2)}, u32[]{:S(2)}) collective-permute-start(bf16[3,64,128]{2,1,0:T(8,128)(2,1)S(1)} %get-tuple-element.33.refs_5_), channel_id=1, source_target_pairs={{0,16},{4,20},{8,24},{12,28},{16,0},{20,4},{24,8},{28,12},{1,17},{... | collective-permute-start | bytes 147464 | tf_op jit(solution)/shard_map/ppermute | solution.py:48
  35.3 2.2 %collective-permute-start.11 = (bf16[192,768]{1,0:T(8,128)(2,1)S(1)}, bf16[192,768]{1,0:T(8,128)(2,1)S(1)}, u32[]{:S(2)}, u32[]{:S(2)}) collective-permute-start(bf16[192,768]{1,0:T(8,128)(2,1)S(1)} %collective-permute-done.10.refs_2_), channel_id=1, source_target_pairs={{0,4},{4,0},{8,12},{12,8},{16,20},{20,16},{24,28},{28,24},{1,5},{5... | collective-permute-start | bytes 884744 | tf_op jit(solution)/shard_map/ppermute | solution.py:48
  35.6 2.0 %collective-permute-start.12 = (bf16[192,256]{1,0:T(8,128)(2,1)S(1)}, bf16[192,256]{1,0:T(8,128)(2,1)S(1)}, u32[]{:S(2)}, u32[]{:S(2)}) collective-permute-start(bf16[192,256]{1,0:T(8,128)(2,1)S(1)} %get-tuple-element.40), channel_id=1, source_target_pairs={{0,4},{4,0},{8,12},{12,8},{16,20},{20,16},{24,28},{28,24},{1,5},{5... | collective-permute-start | bytes 294920 | tf_op jit(solution)/shard_map/ppermute | solution.py:48
  35.9 5.4 %collective-permute-start.7 = (bf16[192,256]{1,0:T(8,128)(2,1)S(1)}, bf16[192,256]{1,0:T(8,128)(2,1)S(1)}, u32[]{:S(2)}, u32[]{:S(2)}) collective-permute-start(bf16[192,256]{1,0:T(8,128)(2,1)S(1)} %get-tuple-element.37), channel_id=1, source_target_pairs={{0,8},{4,12},{8,0},{12,4},{16,24},{20,28},{24,16},{28,20},{1,9},{5... | collective-permute-start | bytes 294920 | tf_op jit(solution)/shard_map/ppermute | solution.py:48
  37.4 5.1 %collective-permute-start.8 = (bf16[192,256]{1,0:T(8,128)(2,1)S(1)}, bf16[192,256]{1,0:T(8,128)(2,1)S(1)}, u32[]{:S(2)}, u32[]{:S(2)}) collective-permute-start(bf16[192,256]{1,0:T(8,128)(2,1)S(1)} %get-tuple-element.38), channel_id=1, source_target_pairs={{0,12},{4,8},{8,4},{12,0},{16,28},{20,24},{24,20},{28,16},{1,13},{... | collective-permute-start | bytes 294920 | tf_op jit(solution)/shard_map/ppermute | solution.py:48

commit v6 on v5

--- a/solution.py
+++ b/solution.py
@@ -165,76 +165,70 @@
     return top, left * one[1] + right * two[1], left * one[2] + right * two[2]
 
 
-def near_body(valid_ref, *refs):
-    qkv_refs, (max_ref, sum_ref, num_ref) = refs[:SHARDS], refs[SHARDS:]
+def near_branches(shards, valid_ref, qkv_refs, max_ref, sum_ref, num_ref):
     member, group = group_indices()
     valid = valid_ref[0]
     rows = qkv_refs[0].shape[0]
     count = rows // MID
+    depth = rows // WIDE
     bases = [(group * SHARDS + (member ^ apart)) * rows for apart in range(SHARDS)]
     place = place_of(lax.broadcasted_iota(jnp.int32, (rows, LANES), 0), rows)
     lane = lax.broadcasted_iota(jnp.int32, (1, rows), 1)
 
-    def widen(bias):
-        return jnp.concatenate([bias] * (rows // LANES), axis=1)
-
-    for shard, ref in enumerate(qkv_refs):
-        bias = widen(key_bias(place + bases[shard], valid))
+    for slot, shard in enumerate(shards):
+        ref = qkv_refs[shard]
+        bias = jnp.concatenate(
+            [key_bias(place + bases[shard], valid)] * (rows // LANES), axis=1
+        )
         for index in range(GROUP_HEADS):
             stats = branch(*(ref[:, at] for at in head_slices(index)), bias)
-            max_ref[index, shard], sum_ref[index, shard], num_ref[index, shard] = stats
-    entry = lax.broadcasted_iota(jnp.int32, (count, LANES), 0)
-    depth = rows // WIDE
+            max_ref[index, slot], sum_ref[index, slot], num_ref[index, slot] = stats
+    item = lax.broadcasted_iota(jnp.int32, (count, len(shards) * count), 0)
     for index in range(GROUP_HEADS):
         head = member * GROUP_HEADS + index
         taken = middle_rows(head, rows)
         query, key, value = (
-            jnp.concatenate([ref[taken, at] for ref in qkv_refs], axis=0)
-            for at in head_slices(index)
-        )
-        position = entry % depth * WIDE + entry // depth * MID + head % MID
-        bias = widen(
-            jnp.concatenate([key_bias(position + base, valid) for base in bases], axis=0)
-        )
+            jnp.concatenate([qkv_refs[shard][taken, at] for shard in some], axis=0)
+            for some, at in zip((shards, range(SHARDS), range(SHARDS)), head_slices(index))
+        )
+        position = item % depth * WIDE + item // depth * MID + head % MID
+        bias = jnp.concatenate([key_bias(position + base, valid) for base in bases], axis=0)
         middle = branch(query, key, value, bias)
         inside = lane // count == head % MID
-        for shard in range(SHARDS):
+        for slot in range(len(shards)):
             largest, total, number = (
-                jnp.concatenate([entry[:, shard * count : (shard + 1) * count]] * MID, axis=1)
-                for entry in middle
+                jnp.concatenate([part[:, slot * count : (slot + 1) * count]] * MID, axis=1)
+                for part in middle
             )
             merged = merge(
-                (max_ref[index, shard], sum_ref[index, shard], num_ref[index, shard]),
+                (max_ref[index, slot], sum_ref[index, slot], num_ref[index, slot]),
                 (jnp.where(inside, largest, NEG_FILL), total, number),
             )
-            max_ref[index, shard], sum_ref[index, shard], num_ref[index, shard] = merged
-
-
-def far_body(n_groups, valid_ref, *refs):
-    qkv_refs, refs = refs[:SHARDS], refs[SHARDS:]
-    sent_refs, refs = refs[:n_groups], refs[n_groups:]
-    (max_ref, sum_ref, num_ref), out_refs = refs[:3], refs[3:]
+            max_ref[index, slot], sum_ref[index, slot], num_ref[index, slot] = merged
+
+
+def far_branch(shards, valid_ref, qkv_refs, sent_refs, max_ref, sum_ref, num_ref, out_refs):
     member, group = group_indices()
     valid = valid_ref[0]
     rows = qkv_refs[0].shape[0]
     depth = rows // WIDE
-    count = SHARDS * depth
-    entry = lax.broadcasted_iota(jnp.int32, (count, count), 0)
+    count = len(shards) * depth
+    item = lax.broadcasted_iota(jnp.int32, (SHARDS * depth, count), 0)
     lane = lax.broadcasted_iota(jnp.int32, (1, rows), 1)
     for index in range(GROUP_HEADS):
         head = member * GROUP_HEADS + index
         taken = wide_rows(head, rows)
         query_at = head_slices(index)[0]
-        query = jnp.concatenate([ref[taken, query_at] for ref in qkv_refs], axis=0)
+        query = jnp.concatenate([qkv_refs[shard][taken, query_at] for shard in shards], axis=0)
         bias = jnp.concatenate(
             [
                 key_bias(
-                    ((group ^ apart) * SHARDS + (member ^ (entry // depth))) * rows
-                    + entry % depth * WIDE
+                    ((group ^ apart) * SHARDS + (member ^ (item // depth))) * rows
+                    + item % depth * WIDE
                     + head,
                     valid,
                 )
-                for apart in range(n_groups)
+                for apart in range(len(sent_refs))
             ],
             axis=0,
         )
@@ -249,13 +243,11 @@
         )
         block = head % MID * STEPS + head % WIDE // MID
         inside = lane // depth == block
-        for shard, out_ref in enumerate(out_refs):
-            shift = (block * depth - shard * depth + LANES) % LANES
-            moved = jnp.concatenate(
-                [pltpu.roll(stacked, shift, 1)] * (rows // LANES), axis=1
-            )
+        for slot, (shard, out_ref) in enumerate(zip(shards, out_refs)):
+            shift = (block * depth - slot * depth + LANES) % LANES
+            moved = jnp.concatenate([pltpu.roll(stacked, shift, 1)] * (rows // LANES), axis=1)
             _, total, number = merge(
-                (max_ref[index, shard], sum_ref[index, shard], num_ref[index, shard]),
+                (max_ref[index, slot], sum_ref[index, slot], num_ref[index, slot]),
                 (
                     jnp.where(inside, moved[HEAD_DIM : HEAD_DIM + 1], NEG_FILL),
                     moved[HEAD_DIM + 8 : HEAD_DIM + 9],
@@ -269,23 +261,39 @@
             out_ref[index * HEAD_DIM : (index + 1) * HEAD_DIM, :] = attention.astype(jnp.bfloat16)
 
 
+def near_body(shards, valid_ref, *refs):
+    near_branches(shards, valid_ref, refs[:SHARDS], *refs[SHARDS:])
+
+
+def far_body(shards, valid_ref, *refs):
+    *refs, out_ref = refs
+    sent_refs, stat_refs = refs[SHARDS:-3], refs[-3:]
+    out_refs = [out_ref.at[slot] for slot in range(len(shards))]
+    far_branch(shards, valid_ref, refs[:SHARDS], sent_refs, *stat_refs, out_refs)
+
+
+def all_body(shards, valid_ref, *refs):
+    stat_refs, out_refs = refs[-3:], refs[-len(shards) - 3 : -3]
+    sent_refs = refs[SHARDS : -len(shards) - 3]
+    near_branches(shards, valid_ref, refs[:SHARDS], *stat_refs)
+    far_branch(shards, valid_ref, refs[:SHARDS], sent_refs, *stat_refs, out_refs)
+
+
 def gather_body(n_mp, shared, *refs):
     *part_refs, out_ref = refs
     assemble(out_ref, part_refs, sources(n_mp, lax.axis_index("ctx") % 2, shared))
 
 
-def update_body(*refs):
+def update_body(blocks, *refs):
     *part_refs, weight_ref, base_ref, out_ref = refs
-    first = SHARDS // 2 if base_ref.dtype == jnp.float32 else 0
     member, _ = group_indices()
     order = to_position(base_ref.shape[0])
     update = base_ref[...].astype(jnp.float32)
-    for apart, ref in enumerate(part_refs):
-        part = product(order, ref[...], 1, 1).astype(jnp.bfloat16)
-        start = (member ^ (first + apart)) * GROUP_WIDTH
-        update = update + product(
-            part, weight_ref[pl.ds(pl.multiple_of(start, GROUP_WIDTH), GROUP_WIDTH), :]
-        )
+    for (apart, slot), ref in zip(blocks, part_refs):
+        part = ref[...] if slot is None else ref[slot]
+        part = product(order, part, 1, 1).astype(jnp.bfloat16)
+        start = pl.multiple_of((member ^ apart) * GROUP_WIDTH, GROUP_WIDTH)
+        update = update + product(part, weight_ref[pl.ds(start, GROUP_WIDTH), :])
     out_ref[...] = update.astype(out_ref.dtype)
 
 
@@ -319,9 +327,9 @@
     mine = near(jnp.concatenate([columns(part) for part in range(3)], axis=1))
     others = fetch(mine, lambda c: c // SHARDS % 2, shared, SHARDS)
 
-    x_pair = flip(x, "ctx", 1)
-    x_far = flip(after(x, mine), "ctx", 2)
-    x_last = flip(after(x, mine), "ctx", 3)
+    x_pair = flip(after(x, mine), "ctx", 1)
+    x_far = flip(after(x, x_pair), "ctx", 2)
+    x_last = flip(x_far, "ctx", 1)
     weights = [mine] + ([flip(mine, "mp", 1)] if shared else []) + others
     x_own = near(x)
     gain, bias = near(norm_gain), near(norm_bias)
@@ -344,39 +352,55 @@
         micros=2,
     )(*normed, *weights)
     sents = [sent] + [flip(sent, "ctx", SHARDS * apart) for apart in range(1, n_groups)]
+    half = SHARDS // 2
+    here, there = range(half), range(half, SHARDS)
+    stat_shapes = [
+        shape((GROUP_HEADS, half, 1, rows), f32),
+        shape((GROUP_HEADS, half, 1, rows), f32),
+        shape((GROUP_HEADS, half, HEAD_DIM, rows), f32),
+    ]
     stats = call(
-        near_body,
-        [
-            shape((GROUP_HEADS, SHARDS, 1, rows), f32),
-            shape((GROUP_HEADS, SHARDS, 1, rows), f32),
-            shape((GROUP_HEADS, SHARDS, HEAD_DIM, rows), f32),
-        ],
-        n_scalar=1,
-        n_in=SHARDS,
-        micros=5,
+        lambda *refs: near_body(there, *refs), stat_shapes, n_scalar=1, n_in=SHARDS, micros=3
     )(valid_count, *qkv)
-    attention = call(
-        lambda *refs: far_body(n_groups, *refs),
-        [shape((GROUP_WIDTH, rows), bf16)] * SHARDS,
+    (sending,) = call(
+        lambda *refs: far_body(there, *refs),
+        [shape((half, GROUP_WIDTH, rows), bf16)],
         n_scalar=1,
         n_in=SHARDS + n_groups + 3,
         micros=1,
     )(valid_count, *qkv, *sents, *stats)
-    out_parts += fetch(out_weight, lambda c: c % 2, shared, 1, attention[1:2])
-    received = [attention[0]] + [flip(attention[apart], "ctx", apart) for apart in range(1, SHARDS)]
+    staying = call(
+        lambda *refs: all_body(here, *refs),
+        [shape((GROUP_WIDTH, rows), bf16)] * half,
+        scratch=stat_shapes,
+        n_scalar=1,
+        n_in=SHARDS + n_groups,
+        micros=2,
+    )(valid_count, *qkv, after(sents[0], sending), *sents[1:])
+    far_part = flip(sending, "ctx", 2)
+    out_parts += fetch(out_weight, lambda c: c % 2, shared, 1, staying[:1])
     (whole_out,) = call(
         lambda *refs: gather_body(n_mp, shared, *refs),
         [shape((width, width), bf16)],
         n_in=n_mp,
+        micros=0.001,
     )(*out_parts)
-    half = SHARDS // 2
-    (partial,) = call(update_body, [shape((rows, width), f32)], n_in=half + 2, micros=1)(
-        *received[:half], whole_out, x_own
-    )
-    (out,) = call(
-        update_body, [jax.ShapeDtypeStruct((rows, width), bf16)], n_in=half + 2, micros=1
-    )(*received[half:], whole_out, partial)
-    return out[None]
+    total = x_own
+    pair_part = flip(staying[1], "ctx", 1)
+    last_part = flip(after(far_part, pair_part), "ctx", 1)
+    steps = [
+        ([(0, None), (1, None)], [staying[0], pair_part], shape((rows, width), f32)),
+        ([(2, 0)], [far_part], shape((rows, width), f32)),
+        ([(3, 1)], [last_part], jax.ShapeDtypeStruct((rows, width), bf16)),
+    ]
+    for blocks, operands, out_shape in steps:
+        (total,) = call(
+            lambda *refs, blocks=blocks: update_body(blocks, *refs),
+            [out_shape],
+            n_in=len(operands) + 2,
+            micros=0.001,
+        )(*operands, whole_out, total)
+    return total[None]
 
 
 def solution(mesh):

time: 44.1 us -> 41.9 us (0.950)
  waiting for transfers between devices: 14.5 us -> 12.8 us
  starting transfers between devices: 16.5 us -> 15 us
  Pallas kernels: 10.7 us -> 11.7 us
    ppermute x2, waiting for transfers between devices: 7.89 us -> 2.74 us  [fetch(): direct = near(lax.ppermute(value, ('ctx', 'mp'), pairs))]
    ppermute x11, waiting for transfers between devices: 6.65 us -> 10.1 us  [flip(): return near(lax.ppermute(value, axis, pairs))]
    ppermute x2, starting transfers between devices: 7.35 us -> 5.76 us  [fetch(): direct = near(lax.ppermute(value, ('ctx', 'mp'), pairs))]
    pallas_call x4 -> x6, Pallas kernels: 7.32 us -> 8.36 us  [the longest x1 3.02 us: local(): call(lambda *refs: all_body(here, *refs), [shape((GROUP_WIDTH, rows), bf1...]
  transfers between devices with their start and end apart: 13 -> 13, of which waited for: 4 -> 7; matrix products, arithmetic and copies ran while one was open for 0% -> 0% of each run, Pallas kernels for 21% -> 25%
where the time goes in v6:
time: 41.9 us; the launch traced here: 41.7 us
  starting transfers between devices  15 us (36%)
  waiting for transfers between devices  12.8 us (31%)
  Pallas kernels  11.7 us (28%)
  local copies, waits for them, and re-layouts  1.29 us (3%)
  between operations  0.79 us (2%)
    ppermute x11, waiting for transfers between devices, flip(): return near(lax.ppermute(value, axis, pairs))  10.1 us
    ppermute x11, starting transfers between devices, flip(): return near(lax.ppermute(value, axis, pairs))  9.22 us
    ppermute x2, starting transfers between devices, fetch(): direct = near(lax.ppermute(value, ('ctx', 'mp'), pairs))  5.76 us
    pallas_call x1, Pallas kernels, local(): call(lambda *refs: all_body(here, *refs), [shape((GROUP_WIDTH, rows), bf1...  3.02 us
    ppermute x2, waiting for transfers between devices, fetch(): direct = near(lax.ppermute(value, ('ctx', 'mp'), pairs))  2.74 us
    pallas_call x1, Pallas kernels, local(): call(lambda *refs: near_body(there, *refs), stat_shapes, n_scalar=1, n_in...  2.47 us
    pallas_call x3, Pallas kernels, local(): call(lambda *refs, blocks=blocks: update_body(blocks, *refs), [out_shape]...  2.35 us
    pallas_call x2, Pallas kernels, local(): call(norm_body, [shape((rows, width), bf16)] * 2, n_in=4, micros=0.01)  1.73 us
  transfers between devices with their start and end apart: 13, of which 7 were waited for; matrix products, arithmetic and copies ran while one was open for 0% of the time, Pallas kernels for 25%

profile of v6, /device:TPU:0, one launch (start us, length us, event | category | flops | bytes accessed | tf_op | source)
XLA Modules:
  0.0 41.7 jit_solution(11734703617732770763)
XLA Ops:
  0.0 1.3 %constant_dynamic-slice_fusion.2 = (bf16[192,192]{1,0:T(8,128)(2,1)S(1)}, bf16[192,192]{1,0:T(8,128)(2,1)S(1)}, bf16[192,192]{1,0:T(8,128)(2,1)S(1)}) fusion(bf16[192,2304]{1,0:T(8,128)(2,1)} %param.9, s32[]{:T(128)S(6)} %select_n.17, s32[]{:T(128)S(6)} %select_n.19, s32[]{:T(128)S(6)} %select_n.18), kind=kLoop, calls=%fused_computation.3 | loop fusion | bytes 442380 | tf_op jit(solution)/shard_map/dynamic_slice | solution.py:325
  1.3 0.1 pad_maximum_fusion.refs_4_
  1.4 0.5 %collective-permute-start = (bf16[256,768]{1,0:T(8,128)(2,1)S(1)}, bf16[256,768]{1,0:T(8,128)(2,1)S(1)}, u32[]{:S(2)}, u32[]{:S(2)}) collective-permute-start(bf16[256,768]{1,0:T(8,128)(2,1)S(1)} %bitcast.2), channel_id=1, source_target_pairs={{0,4},{4,0},{8,12},{12,8},{16,20},{20,16},{24,28},{28,24},{1,5},{5... | collective-permute-start | bytes 1179656 | tf_op jit(solution)/shard_map/ppermute | solution.py:48
  2.0 1.3 %collective-permute-done.refs_1_ = bf16[256,768]{1,0:T(8,128)(2,1)S(1)} collective-permute-done((bf16[256,768]{1,0:T(8,128)(2,1)S(1)}, bf16[256,768]{1,0:T(8,128)(2,1)S(1)}, u32[]{:S(2)}, u32[]{:S(2)}) %collective-permute-start) | collective-permute-done | bytes 393248 | tf_op jit(solution)/shard_map/ppermute | solution.py:48
  3.3 2.9 %collective-permute-start.1 = (bf16[256,768]{1,0:T(8,128)(2,1)S(1)}, bf16[256,768]{1,0:T(8,128)(2,1)S(1)}, u32[]{:S(2)}, u32[]{:S(2)}) collective-permute-start(bf16[256,768]{1,0:T(8,128)(2,1)S(1)} %bitcast.3), channel_id=1, source_target_pairs={{0,8},{4,12},{8,0},{12,4},{16,24},{20,28},{24,16},{28,20},{1,9},{5... | collective-permute-start | bytes 1179656 | tf_op jit(solution)/shard_map/ppermute | solution.py:48
  6.2 2.6 %collective-permute-start.4 = (bf16[192,576]{1,0:T(8,128)(2,1)S(1)}, bf16[192,576]{1,0:T(8,128)(2,1)S(1)}, u32[]{:S(2)}, u32[]{:S(2)}) collective-permute-start(bf16[192,576]{1,0:T(8,128)(2,1)S(1)} %pad_maximum_fusion.refs_4_), channel_id=1, source_target_pairs={{0,2},{1,3},{2,0},{3,1},{4,6},{5,7},{6,4},{7,5},{8,10},{9,11},{10,... | collective-permute-start | bytes 663560 | tf_op jit(solution)/shard_map/ppermute | solution.py:307
  8.8 6.8 %collective-permute-done.1.refs_0_ = bf16[256,768]{1,0:T(8,128)(2,1)S(1)} collective-permute-done((bf16[256,768]{1,0:T(8,128)(2,1)S(1)}, bf16[256,768]{1,0:T(8,128)(2,1)S(1)}, u32[]{:S(2)}, u32[]{:S(2)}) %collective-permute-start.1) | collective-permute-done | bytes 393248 | tf_op jit(solution)/shard_map/ppermute | solution.py:48
  15.6 0.0 collective-permute-start.2
  15.6 1.8 %collective-permute-start.3 = (bf16[192,576]{1,0:T(8,128)(2,1)S(1)}, bf16[192,576]{1,0:T(8,128)(2,1)S(1)}, u32[]{:S(2)}, u32[]{:S(2)}) collective-permute-start(bf16[192,576]{1,0:T(8,128)(2,1)S(1)} %pad_maximum_fusion.refs_4_), channel_id=1, source_target_pairs={{0,1},{1,0},{2,3},{3,2},{4,5},{5,4},{6,7},{7,6},{8,9},{9,8},{10,11... | collective-permute-start | bytes 663560 | tf_op jit(solution)/shard_map/ppermute | solution.py:48
  17.4 2.7 %collective-permute-done.4.refs_6_ = bf16[192,576]{1,0:T(8,128)(2,1)S(1)} collective-permute-done((bf16[192,576]{1,0:T(8,128)(2,1)S(1)}, bf16[192,576]{1,0:T(8,128)(2,1)S(1)}, u32[]{:S(2)}, u32[]{:S(2)}) %collective-permute-start.4) | collective-permute-done | bytes 221216 | tf_op jit(solution)/shard_map/ppermute | solution.py:307
  20.8 3.2 %collective-permute-start.11 = (bf16[192,768]{1,0:T(8,128)(2,1)S(1)}, bf16[192,768]{1,0:T(8,128)(2,1)S(1)}, u32[]{:S(2)}, u32[]{:S(2)}) collective-permute-start(bf16[192,768]{1,0:T(8,128)(2,1)S(1)} %copy-done.1), channel_id=1, source_target_pairs={{0,2},{1,3},{2,0},{3,1},{4,7},{5,6},{6,5},{7,4},{8,10},{9,11},{10,... | collective-permute-start | bytes 884744 | tf_op jit(solution)/shard_map/ppermute | solution.py:307
  24.0 0.9 %collective-permute-start.10 = (bf16[192,768]{1,0:T(8,128)(2,1)S(1)}, bf16[192,768]{1,0:T(8,128)(2,1)S(1)}, u32[]{:S(2)}, u32[]{:S(2)}) collective-permute-start(bf16[192,768]{1,0:T(8,128)(2,1)S(1)} %copy-done.1), channel_id=1, source_target_pairs={{0,1},{1,0},{2,3},{3,2},{4,5},{5,4},{6,7},{7,6},{8,9},{9,8},{10,11... | collective-permute-start | bytes 884744 | tf_op jit(solution)/shard_map/ppermute | solution.py:48
  25.0 0.9 %shard_map.64 = (bf16[256,768]{1,0:T(8,128)(2,1)S(1)}, bf16[256,768]{1,0:T(8,128)(2,1)S(1)}) custom-call(bf16[256,768]{1,0:T(8,128)(2,1)S(1)} %bitcast.4, bf16[256,768]{1,0:T(8,128)(2,1)S(1)} %collective-permute-done.refs_1_, f32[768]{0:T(1024)S(1)} %copy-done.2, f32[768]{0:T(1024)S(1)} %copy-done.3), custom_call_target="tpu_custom_call" | custom-call | flops 30000000 | bytes 90000 | tf_op jit(solution)/shard_map/pallas_call | solution.py:338
  25.8 0.0 collective-permute-done.2.refs_1_
  25.8 0.9 %shard_map.65 = (bf16[256,768]{1,0:T(8,128)(2,1)S(1)}, bf16[256,768]{1,0:T(8,128)(2,1)S(1)}) custom-call(bf16[256,768]{1,0:T(8,128)(2,1)S(1)} %collective-permute-done.1.refs_0_, bf16[256,768]{1,0:T(8,128)(2,1)S(1)} %collective-permute-done.2.refs_1_, f32[768]{0:T(1024)S(1)} %copy-done.2, f32[768]{0:T(1024)S(1)} %copy-done.3), custom_call_target="tpu_custom_call" | custom-call | flops 30000000 | bytes 90000 | tf_op jit(solution)/shard_map/pallas_call | solution.py:338
  26.7 0.2 collective-permute-done.5.refs_7_
  26.9 1.6 %shard_map.66 = (bf16[256,576]{1,0:T(8,128)(2,1)S(1)}, bf16[256,576]{1,0:T(8,128)(2,1)S(1)}, bf16[256,576]{1,0:T(8,128)(2,1)S(1)}, bf16[256,576]{1,0:T(8,128)(2,1)S(1)}, bf16[3,64,128]{2,1,0:T(8,128)(2,1)S(1)}) custom-call(bf16[256,768]{1,0:T(8,128)(2,1)S(1)} %get-tuple-element.26.refs_0_, bf16[256,768]{1,0:T(8,128)(2,1)S(1)} %get-tuple-element.27.refs_1_, ...), custom_call_target="tpu_custom_call" | custom-call | flops 6000000000 | bytes 18000000 | tf_op jit(solution)/shard_map/pallas_call | solution.py:346
  28.5 1.8 %collective-permute-start.6 = (bf16[3,64,128]{2,1,0:T(8,128)(2,1)S(1)}, bf16[3,64,128]{2,1,0:T(8,128)(2,1)S(1)}, u32[]{:S(2)}, u32[]{:S(2)}) collective-permute-start(bf16[3,64,128]{2,1,0:T(8,128)(2,1)S(1)} %get-tuple-element.39.refs_5_), channel_id=1, source_target_pairs={{0,16},{4,20},{8,24},{12,28},{16,0},{20,4},{24,8},{28,12},{1,17},{... | collective-permute-start | bytes 147464 | tf_op jit(solution)/shard_map/ppermute | solution.py:48
  30.3 2.5 %shard_map.67 = (f32[3,2,1,256]{3,2,1,0:T(1,128)S(1)}, f32[3,2,1,256]{3,2,1,0:T(1,128)S(1)}, f32[3,2,64,256]{3,2,1,0:T(8,128)S(1)}) custom-call(s32[1]{0:T(128)S(6)} %copy.7.refs_0_, bf16[256,576]{1,0:T(8,128)(2,1)S(1)} %get-tuple-element.31.refs_1_, bf16[256,576]{1,0:T(8,128)(2,1)S(1)} %get-tuple-element.32.refs_2_, ...), custom_call_target="tpu_custom_call" | custom-call | flops 8999999488 | bytes 27000000 | tf_op jit(solution)/shard_map/pallas_call | solution.py:362
  32.8 0.5 %shard_map.68 = bf16[2,192,256]{2,1,0:T(8,128)(2,1)S(1)} custom-call(s32[1]{0:T(128)S(6)} %copy.7.refs_0_, bf16[256,576]{1,0:T(8,128)(2,1)S(1)} %get-tuple-element.31.refs_1_, bf16[256,576]{1,0:T(8,128)(2,1)S(1)} %get-tuple-element.32.refs_2_, bf16[256,576]{1,0:T(8,128)(2,1)S(1)} %get-tuple-element.33.refs_3_, ...), custom_call_target="tpu_custom_call" | custom-call | flops 3000000000 | bytes 9000000 | tf_op jit(solution)/shard_map/pallas_call | solution.py:365
  33.3 0.6 %collective-permute-start.7 = (bf16[2,192,256]{2,1,0:T(8,128)(2,1)S(1)}, bf16[2,192,256]{2,1,0:T(8,128)(2,1)S(1)}, u32[]{:S(2)}, u32[]{:S(2)}) collective-permute-start(bf16[2,192,256]{2,1,0:T(8,128)(2,1)S(1)} %shard_map.68), channel_id=1, source_target_pairs={{0,8},{4,12},{8,0},{12,4},{16,24},{20,28},{24,16},{28,20},{1,9},{5... | collective-permute-start | bytes 589832 | tf_op jit(solution)/shard_map/ppermute | solution.py:48
  34.0 3.0 %shard_map.69 = (bf16[192,256]{1,0:T(8,128)(2,1)S(1)}, bf16[192,256]{1,0:T(8,128)(2,1)S(1)}) custom-call(s32[1]{0:T(128)S(6)} %copy.7.refs_0_, bf16[256,576]{1,0:T(8,128)(2,1)S(1)} %get-tuple-element.31.refs_1_, bf16[256,576]{1,0:T(8,128)(2,1)S(1)} %get-tuple-element.32.refs_2_, bf16[256,576]{1,0:T(8,128)(2,1)S(1)} %get-tuple-element.33.refs_3_, ...), custom_call_target="tpu_custom_call" | custom-call | flops 6000000000 | bytes 18000000 | tf_op jit(solution)/shard_map/pallas_call | solution.py:372
  37.0 0.0 collective-permute-done.11.refs_2_
  37.0 0.1 collective-permute-start.12
  37.1 0.5 %collective-permute-start.8 = (bf16[192,256]{1,0:T(8,128)(2,1)S(1)}, bf16[192,256]{1,0:T(8,128)(2,1)S(1)}, u32[]{:S(2)}, u32[]{:S(2)}) collective-permute-start(bf16[192,256]{1,0:T(8,128)(2,1)S(1)} %get-tuple-element.40), channel_id=1, source_target_pairs={{0,4},{4,0},{8,12},{12,8},{16,20},{20,16},{24,28},{28,24},{1,5},{5... | collective-permute-start | bytes 294920 | tf_op jit(solution)/shard_map/ppermute | solution.py:48
  37.6 1.2 %collective-permute-done.8.refs_1_ = bf16[192,256]{1,0:T(8,128)(2,1)S(1)} collective-permute-done((bf16[192,256]{1,0:T(8,128)(2,1)S(1)}, bf16[192,256]{1,0:T(8,128)(2,1)S(1)}, u32[]{:S(2)}, u32[]{:S(2)}) %collective-permute-start.8) | collective-permute-done | bytes 98336 | tf_op jit(solution)/shard_map/ppermute | solution.py:48
  38.8 0.3 collective-permute-done.7.refs_0_
  39.1 0.1 shard_map.70.refs_2_.refs_1_
  39.2 0.7 %shard_map.71.refs_2_ = f32[256,768]{1,0:T(8,128)S(1)} custom-call(bf16[192,256]{1,0:T(8,128)(2,1)S(1)} %get-tuple-element.43.refs_0_, bf16[192,256]{1,0:T(8,128)(2,1)S(1)} %collective-permute-done.8.refs_1_, bf16[768,768]{1,0:T(8,128)(2,1)S(1)} %shard_map.70.refs_2_.refs_1_, bf16[256,768]{1,0:T(8,128)(2,1)S(1)} %bitcast.5), custom_call_target="tpu_custom_call" | custom-call | flops 3000000 | bytes 9000 | tf_op jit(solution)/shard_map/pallas_call | solution.py:397
  39.9 0.5 %shard_map.72.refs_2_ = f32[256,768]{1,0:T(8,128)S(1)} custom-call(bf16[2,192,256]{2,1,0:T(8,128)(2,1)S(1)} %collective-permute-done.7.refs_0_, bf16[768,768]{1,0:T(8,128)(2,1)S(1)} %shard_map.70.refs_2_.refs_1_, f32[256,768]{1,0:T(8,128)S(1)} %shard_map.71.refs_2_), custom_call_target="tpu_custom_call" | custom-call | flops 3000000 | bytes 9000 | tf_op jit(solution)/shard_map/pallas_call | solution.py:397
  40.3 0.2 collective-permute-done.9.refs_0_
  40.5 1.2 %shard_map.73 = bf16[256,768]{1,0:T(8,128)(2,1)} custom-call(bf16[2,192,256]{2,1,0:T(8,128)(2,1)S(1)} %collective-permute-done.9.refs_0_, bf16[768,768]{1,0:T(8,128)(2,1)S(1)} %shard_map.70.refs_2_.refs_1_, f32[256,768]{1,0:T(8,128)S(1)} %shard_map.72.refs_2_), custom_call_target="tpu_custom_call" | custom-call | flops 3000000 | bytes 9000 | tf_op jit(solution)/shard_map/pallas_call | solution.py:397
  (14 shorter events, 0.0 us)
Async XLA Ops:
  0.0 1.4 %copy-start = (bf16[1,256,768]{2,1,0:T(8,128)(2,1)S(1)}, bf16[1,256,768]{2,1,0:T(8,128)(2,1)}, u32[]{:S(2)}) copy-start(bf16[1,256,768]{2,1,0:T(8,128)(2,1)} %param.6) | copy-start | bytes 1179652
  0.0 20.8 %copy-start.1 = (bf16[192,768]{1,0:T(8,128)(2,1)S(1)}, bf16[192,768]{1,0:T(8,128)(2,1)}, u32[]{:S(2)}) copy-start(bf16[192,768]{1,0:T(8,128)(2,1)} %refs_0_.3) | copy-start | bytes 884740
  0.0 24.9 %copy-start.2 = (f32[768]{0:T(1024)S(1)}, f32[768]{0:T(1024)}, u32[]{:S(2)}) copy-start(f32[768]{0:T(1024)} %refs_2_.3) | copy-start | bytes 9220
  0.0 24.9 %copy-start.3 = (f32[768]{0:T(1024)S(1)}, f32[768]{0:T(1024)}, u32[]{:S(2)}) copy-start(f32[768]{0:T(1024)} %refs_3_.3) | copy-start | bytes 9220
  1.4 1.9 %collective-permute-start = (bf16[256,768]{1,0:T(8,128)(2,1)S(1)}, bf16[256,768]{1,0:T(8,128)(2,1)S(1)}, u32[]{:S(2)}, u32[]{:S(2)}) collective-permute-start(bf16[256,768]{1,0:T(8,128)(2,1)S(1)} %bitcast.2), channel_id=1, source_target_pairs={{0,4},{4,0},{8,12},{12,8},{16,20},{20,16},{24,28},{28,24},{1,5},{5... | collective-permute-start | bytes 1179656 | tf_op jit(solution)/shard_map/ppermute | solution.py:48
  3.3 12.3 %collective-permute-start.1 = (bf16[256,768]{1,0:T(8,128)(2,1)S(1)}, bf16[256,768]{1,0:T(8,128)(2,1)S(1)}, u32[]{:S(2)}, u32[]{:S(2)}) collective-permute-start(bf16[256,768]{1,0:T(8,128)(2,1)S(1)} %bitcast.3), channel_id=1, source_target_pairs={{0,8},{4,12},{8,0},{12,4},{16,24},{20,28},{24,16},{28,20},{1,9},{5... | collective-permute-start | bytes 1179656 | tf_op jit(solution)/shard_map/ppermute | solution.py:48
  6.2 14.0 %collective-permute-start.4 = (bf16[192,576]{1,0:T(8,128)(2,1)S(1)}, bf16[192,576]{1,0:T(8,128)(2,1)S(1)}, u32[]{:S(2)}, u32[]{:S(2)}) collective-permute-start(bf16[192,576]{1,0:T(8,128)(2,1)S(1)} %pad_maximum_fusion.refs_4_), channel_id=1, source_target_pairs={{0,2},{1,3},{2,0},{3,1},{4,6},{5,7},{6,4},{7,5},{8,10},{9,11},{10,... | collective-permute-start | bytes 663560 | tf_op jit(solution)/shard_map/ppermute | solution.py:307
  15.6 10.2 %collective-permute-start.2 = (bf16[256,768]{1,0:T(8,128)(2,1)S(1)}, bf16[256,768]{1,0:T(8,128)(2,1)S(1)}, u32[]{:S(2)}, u32[]{:S(2)}) collective-permute-start(bf16[256,768]{1,0:T(8,128)(2,1)S(1)} %collective-permute-done.1.refs_0_), channel_id=1, source_target_pairs={{0,4},{4,0},{8,12},{12,8},{16,20},{20,16},{24,28},{28,24},{1,5},{5... | collective-permute-start | bytes 1179656 | tf_op jit(solution)/shard_map/ppermute | solution.py:48
  15.6 11.1 %collective-permute-start.3 = (bf16[192,576]{1,0:T(8,128)(2,1)S(1)}, bf16[192,576]{1,0:T(8,128)(2,1)S(1)}, u32[]{:S(2)}, u32[]{:S(2)}) collective-permute-start(bf16[192,576]{1,0:T(8,128)(2,1)S(1)} %pad_maximum_fusion.refs_4_), channel_id=1, source_target_pairs={{0,1},{1,0},{2,3},{3,2},{4,5},{5,4},{6,7},{7,6},{8,9},{9,8},{10,11... | collective-permute-start | bytes 663560 | tf_op jit(solution)/shard_map/ppermute | solution.py:48
  20.2 6.8 %collective-permute-start.5 = (bf16[192,576]{1,0:T(8,128)(2,1)S(1)}, bf16[192,576]{1,0:T(8,128)(2,1)S(1)}, u32[]{:S(2)}, u32[]{:S(2)}) collective-permute-start(bf16[192,576]{1,0:T(8,128)(2,1)S(1)} %collective-permute-done.4.refs_6_), channel_id=1, source_target_pairs={{0,16},{4,20},{8,24},{12,28},{16,0},{20,4},{24,8},{28,12},{1,17},{... | collective-permute-start | bytes 663560 | tf_op jit(solution)/shard_map/ppermute | solution.py:48
  20.8 16.2 %collective-permute-start.11 = (bf16[192,768]{1,0:T(8,128)(2,1)S(1)}, bf16[192,768]{1,0:T(8,128)(2,1)S(1)}, u32[]{:S(2)}, u32[]{:S(2)}) collective-permute-start(bf16[192,768]{1,0:T(8,128)(2,1)S(1)} %copy-done.1), channel_id=1, source_target_pairs={{0,2},{1,3},{2,0},{3,1},{4,7},{5,6},{6,5},{7,4},{8,10},{9,11},{10,... | collective-permute-start | bytes 884744 | tf_op jit(solution)/shard_map/ppermute | solution.py:307
  24.0 15.1 %collective-permute-start.10 = (bf16[192,768]{1,0:T(8,128)(2,1)S(1)}, bf16[192,768]{1,0:T(8,128)(2,1)S(1)}, u32[]{:S(2)}, u32[]{:S(2)}) collective-permute-start(bf16[192,768]{1,0:T(8,128)(2,1)S(1)} %copy-done.1), channel_id=1, source_target_pairs={{0,1},{1,0},{2,3},{3,2},{4,5},{5,4},{6,7},{7,6},{8,9},{9,8},{10,11... | collective-permute-start | bytes 884744 | tf_op jit(solution)/shard_map/ppermute | solution.py:48
  28.5 4.3 %collective-permute-start.6 = (bf16[3,64,128]{2,1,0:T(8,128)(2,1)S(1)}, bf16[3,64,128]{2,1,0:T(8,128)(2,1)S(1)}, u32[]{:S(2)}, u32[]{:S(2)}) collective-permute-start(bf16[3,64,128]{2,1,0:T(8,128)(2,1)S(1)} %get-tuple-element.39.refs_5_), channel_id=1, source_target_pairs={{0,16},{4,20},{8,24},{12,28},{16,0},{20,4},{24,8},{28,12},{1,17},{... | collective-permute-start | bytes 147464 | tf_op jit(solution)/shard_map/ppermute | solution.py:48
  33.3 5.7 %collective-permute-start.7 = (bf16[2,192,256]{2,1,0:T(8,128)(2,1)S(1)}, bf16[2,192,256]{2,1,0:T(8,128)(2,1)S(1)}, u32[]{:S(2)}, u32[]{:S(2)}) collective-permute-start(bf16[2,192,256]{2,1,0:T(8,128)(2,1)S(1)} %shard_map.68), channel_id=1, source_target_pairs={{0,8},{4,12},{8,0},{12,4},{16,24},{20,28},{24,16},{28,20},{1,9},{5... | collective-permute-start | bytes 589832 | tf_op jit(solution)/shard_map/ppermute | solution.py:48
  37.0 2.1 %collective-permute-start.12 = (bf16[192,768]{1,0:T(8,128)(2,1)S(1)}, bf16[192,768]{1,0:T(8,128)(2,1)S(1)}, u32[]{:S(2)}, u32[]{:S(2)}) collective-permute-start(bf16[192,768]{1,0:T(8,128)(2,1)S(1)} %collective-permute-done.11.refs_2_), channel_id=1, source_target_pairs={{0,4},{4,0},{8,12},{12,8},{16,20},{20,16},{24,28},{28,24},{1,5},{5... | collective-permute-start | bytes 884744 | tf_op jit(solution)/shard_map/ppermute | solution.py:48
  37.1 1.7 %collective-permute-start.8 = (bf16[192,256]{1,0:T(8,128)(2,1)S(1)}, bf16[192,256]{1,0:T(8,128)(2,1)S(1)}, u32[]{:S(2)}, u32[]{:S(2)}) collective-permute-start(bf16[192,256]{1,0:T(8,128)(2,1)S(1)} %get-tuple-element.40), channel_id=1, source_target_pairs={{0,4},{4,0},{8,12},{12,8},{16,20},{20,16},{24,28},{28,24},{1,5},{5... | collective-permute-start | bytes 294920 | tf_op jit(solution)/shard_map/ppermute | solution.py:48
  39.1 1.4 %collective-permute-start.9 = (bf16[2,192,256]{2,1,0:T(8,128)(2,1)S(1)}, bf16[2,192,256]{2,1,0:T(8,128)(2,1)S(1)}, u32[]{:S(2)}, u32[]{:S(2)}) collective-permute-start(bf16[2,192,256]{2,1,0:T(8,128)(2,1)S(1)} %collective-permute-done.7.refs_0_), channel_id=1, source_target_pairs={{0,4},{4,0},{8,12},{12,8},{16,20},{20,16},{24,28},{28,24},{1,5},{5... | collective-permute-start | bytes 589832 | tf_op jit(solution)/shard_map/ppermute | solution.py:48

commit v7 on v6

--- a/solution.py
+++ b/solution.py
@@ -280,14 +280,15 @@
 
 
 def gather_body(n_mp, shared, *refs):
-    *part_refs, out_ref = refs
+    *part_refs, out_ref, order_ref = refs
+    order_ref[...] = to_position(order_ref.shape[0])
     assemble(out_ref, part_refs, sources(n_mp, lax.axis_index("ctx") % 2, shared))
 
 
 def update_body(blocks, *refs):
-    *part_refs, weight_ref, base_ref, out_ref = refs
+    *part_refs, weight_ref, order_ref, base_ref, out_ref = refs
     member, _ = group_indices()
-    order = to_position(base_ref.shape[0])
+    order = order_ref[...]
     update = base_ref[...].astype(jnp.float32)
     for (apart, slot), ref in zip(blocks, part_refs):
         part = ref[...] if slot is None else ref[slot]
@@ -297,15 +298,20 @@
     out_ref[...] = update.astype(out_ref.dtype)
 
 
-def fetch(value, turns, shared, pair_mask, earlier=()):
+def fetch(value, turns, shared):
     n_mp, n_ctx = lax.axis_size("mp"), lax.axis_size("ctx")
     if not shared:
         return [flip(value, "mp", apart) for apart in range(1, n_mp)]
     pairs = [
         (c * n_mp + z, c * n_mp + (z ^ (2 + turns(c)))) for c in range(n_ctx) for z in range(n_mp)
     ]
-    direct = near(lax.ppermute(value, ("ctx", "mp"), pairs))
-    return [direct, flip(after(direct, *earlier), "ctx", pair_mask)]
+    return [flip(value, "mp", 1), near(lax.ppermute(value, ("ctx", "mp"), pairs))]
+
+
+def exchange(blocks, shared, mask, *earlier):
+    if not shared:
+        return blocks
+    return blocks + [flip(after(blocks[-1], *earlier), "ctx", mask)]
 
 
 def local(tile_embeds, norm_gain, norm_bias, w_qkv, w_out, valid_count):
@@ -325,24 +331,26 @@
         return lax.dynamic_slice(w_qkv, (0, start), (weight_rows, GROUP_WIDTH))
 
     mine = near(jnp.concatenate([columns(part) for part in range(3)], axis=1))
-    others = fetch(mine, lambda c: c // SHARDS % 2, shared, SHARDS)
-
+    fetched = fetch(mine, lambda c: c // SHARDS % 2, shared)
+
+    x_own = near(x)
     x_pair = flip(after(x, mine), "ctx", 1)
-    x_far = flip(after(x, x_pair), "ctx", 2)
+    x_far = flip(after(x, mine), "ctx", 2)
     x_last = flip(x_far, "ctx", 1)
-    weights = [mine] + ([flip(mine, "mp", 1)] if shared else []) + others
-    x_own = near(x)
     gain, bias = near(norm_gain), near(norm_bias)
-    normed = []
-    for pair in ((x_own, x_pair), (x_far, x_last)):
-        normed += call(norm_body, [shape((rows, width), bf16)] * 2, n_in=4, micros=0.01)(
-            *pair, gain, bias
-        )
-
-    out_weight = after(near(w_out), others[0])
-    out_parts = [out_weight]
-    if shared:
-        out_parts.append(flip(out_weight, "mp", 1))
+
+    def normalized(one, two, micros):
+        return call(norm_body, [shape((rows, width), bf16)] * 2, n_in=4, micros=micros)(
+            one, two, gain, bias
+        )
+
+    normed = normalized(x_own, x_pair, 1)
+    weights = [mine] + exchange(fetched, shared, SHARDS, normed[0])
+    normed += normalized(x_far, x_last, 0.01)
+
+    out_weight = after(near(w_out), x_last)
+    out_fetched = fetch(out_weight, lambda c: c % 2, shared)
+
     *qkv, sent = call(
         lambda *refs: project_body(n_mp, shared, *refs),
         [shape((rows, 3 * GROUP_WIDTH), bf16)] * SHARDS
@@ -378,10 +386,10 @@
         micros=2,
     )(valid_count, *qkv, after(sents[0], sending), *sents[1:])
     far_part = flip(sending, "ctx", 2)
-    out_parts += fetch(out_weight, lambda c: c % 2, shared, 1, staying[:1])
-    (whole_out,) = call(
+    out_parts = [out_weight] + exchange(out_fetched, shared, 1, staying[0])
+    whole_out, order = call(
         lambda *refs: gather_body(n_mp, shared, *refs),
-        [shape((width, width), bf16)],
+        [shape((width, width), bf16), shape((rows, rows), bf16)],
         n_in=n_mp,
         micros=0.001,
     )(*out_parts)
@@ -389,17 +397,17 @@
     pair_part = flip(staying[1], "ctx", 1)
     last_part = flip(after(far_part, pair_part), "ctx", 1)
     steps = [
-        ([(0, None), (1, None)], [staying[0], pair_part], shape((rows, width), f32)),
-        ([(2, 0)], [far_part], shape((rows, width), f32)),
+        ([(0, None)], [staying[0]], shape((rows, width), f32)),
+        ([(1, None), (2, 0)], [pair_part, far_part], shape((rows, width), f32)),
         ([(3, 1)], [last_part], jax.ShapeDtypeStruct((rows, width), bf16)),
     ]
     for blocks, operands, out_shape in steps:
         (total,) = call(
             lambda *refs, blocks=blocks: update_body(blocks, *refs),
             [out_shape],
-            n_in=len(operands) + 2,
+            n_in=len(operands) + 3,
             micros=0.001,
-        )(*operands, whole_out, total)
+        )(*operands, whole_out, order, total)
     return total[None]
 
 

time: 41.9 us -> 41.3 us (0.986)
  starting transfers between devices: 15 us -> 12.8 us
  waiting for transfers between devices: 12.8 us -> 14.4 us
    ppermute x11, starting transfers between devices: 9.22 us -> 7.07 us  [flip(): return near(lax.ppermute(value, axis, pairs))]
    ppermute x2, waiting for transfers between devices: 2.74 us -> 4.66 us  [fetch(): lax.ppermute(value, ('ctx', 'mp'), pairs)]
  transfers between devices with their start and end apart: 13 -> 13, of which waited for: 7 -> 7; matrix products, arithmetic and copies ran while one was open for 0% -> 0% of each run, Pallas kernels for 25% -> 26%
where the time goes in v7:
time: 41.3 us; the launch traced here: 41.2 us
  waiting for transfers between devices  14.4 us (35%)
  starting transfers between devices  12.8 us (31%)
  Pallas kernels  11.7 us (28%)
  local copies, waits for them, and re-layouts  1.27 us (3%)
  between operations  0.8 us (2%)
    ppermute x11, waiting for transfers between devices, flip(): return near(lax.ppermute(value, axis, pairs))  9.74 us
    ppermute x11, starting transfers between devices, flip(): return near(lax.ppermute(value, axis, pairs))  7.07 us
    ppermute x2, starting transfers between devices, fetch(): lax.ppermute(value, ('ctx', 'mp'), pairs)  5.76 us
    ppermute x2, waiting for transfers between devices, fetch(): lax.ppermute(value, ('ctx', 'mp'), pairs)  4.66 us
    pallas_call x1, Pallas kernels, local(): call(lambda *refs: all_body(here, *refs), [shape((GROUP_WIDTH, rows), bf1...  3.01 us
    pallas_call x1, Pallas kernels, local(): call(lambda *refs: near_body(there, *refs), stat_shapes, n_scalar=1, n_in...  2.47 us
    pallas_call x3, Pallas kernels, local(): call(lambda *refs, blocks=blocks: update_body(blocks, *refs), [out_shape]...  2.35 us
    pallas_call x2, Pallas kernels, normalized(): call(norm_body, [shape((rows, width), bf16)] * 2, n_in=4, micros=micros)  1.73 us
  transfers between devices with their start and end apart: 13, of which 7 were waited for; matrix products, arithmetic and copies ran while one was open for 0% of the time, Pallas kernels for 26%

profile of v7, /device:TPU:0, one launch (start us, length us, event | category | flops | bytes accessed | tf_op | source)
XLA Modules:
  0.0 41.2 jit_solution(12343135996688916730)
XLA Ops:
  0.0 1.3 %constant_dynamic-slice_fusion.2 = (bf16[192,192]{1,0:T(8,128)(2,1)S(1)}, bf16[192,192]{1,0:T(8,128)(2,1)S(1)}, bf16[192,192]{1,0:T(8,128)(2,1)S(1)}) fusion(bf16[192,2304]{1,0:T(8,128)(2,1)} %param.9, s32[]{:T(128)S(6)} %select_n.17, s32[]{:T(128)S(6)} %select_n.19, s32[]{:T(128)S(6)} %select_n.18), kind=kLoop, calls=%fused_computation.3 | loop fusion | bytes 442380 | tf_op jit(solution)/shard_map/dynamic_slice | solution.py:331
  1.3 0.1 pad_maximum_fusion.refs_4_
  1.4 0.0 copy-start.1
  1.4 3.0 %collective-permute-start.1 = (bf16[256,768]{1,0:T(8,128)(2,1)S(1)}, bf16[256,768]{1,0:T(8,128)(2,1)S(1)}, u32[]{:S(2)}, u32[]{:S(2)}) collective-permute-start(bf16[256,768]{1,0:T(8,128)(2,1)S(1)} %bitcast.2), channel_id=1, source_target_pairs={{0,8},{4,12},{8,0},{12,4},{16,24},{20,28},{24,16},{28,20},{1,9},{5... | collective-permute-start | bytes 1179656 | tf_op jit(solution)/shard_map/ppermute | solution.py:48
  4.4 2.6 %collective-permute-start.4 = (bf16[192,576]{1,0:T(8,128)(2,1)S(1)}, bf16[192,576]{1,0:T(8,128)(2,1)S(1)}, u32[]{:S(2)}, u32[]{:S(2)}) collective-permute-start(bf16[192,576]{1,0:T(8,128)(2,1)S(1)} %pad_maximum_fusion.refs_4_), channel_id=1, source_target_pairs={{0,2},{1,3},{2,0},{3,1},{4,6},{5,7},{6,4},{7,5},{8,10},{9,11},{10,... | collective-permute-start | bytes 663560 | tf_op jit(solution)/shard_map/ppermute | solution.py:308
  7.0 1.6 %collective-permute-start.3 = (bf16[192,576]{1,0:T(8,128)(2,1)S(1)}, bf16[192,576]{1,0:T(8,128)(2,1)S(1)}, u32[]{:S(2)}, u32[]{:S(2)}) collective-permute-start(bf16[192,576]{1,0:T(8,128)(2,1)S(1)} %pad_maximum_fusion.refs_4_), channel_id=1, source_target_pairs={{0,1},{1,0},{2,3},{3,2},{4,5},{5,4},{6,7},{7,6},{8,9},{9,8},{10,11... | collective-permute-start | bytes 663560 | tf_op jit(solution)/shard_map/ppermute | solution.py:48
  8.6 4.9 %collective-permute-done.1.refs_0_ = bf16[256,768]{1,0:T(8,128)(2,1)S(1)} collective-permute-done((bf16[256,768]{1,0:T(8,128)(2,1)S(1)}, bf16[256,768]{1,0:T(8,128)(2,1)S(1)}, u32[]{:S(2)}, u32[]{:S(2)}) %collective-permute-start.1) | collective-permute-done | bytes 393248 | tf_op jit(solution)/shard_map/ppermute | solution.py:48
  13.5 0.0 collective-permute-start.2
  13.5 0.0 collective-permute-done.refs_1_
  13.6 0.9 %shard_map.64 = (bf16[256,768]{1,0:T(8,128)(2,1)S(1)}, bf16[256,768]{1,0:T(8,128)(2,1)S(1)}) custom-call(bf16[256,768]{1,0:T(8,128)(2,1)S(1)} %bitcast.4, bf16[256,768]{1,0:T(8,128)(2,1)S(1)} %collective-permute-done.refs_1_, f32[768]{0:T(1024)S(1)} %copy-done.2, f32[768]{0:T(1024)S(1)} %copy-done.3), custom_call_target="tpu_custom_call" | custom-call | flops 3000000000 | bytes 9000000 | tf_op jit(solution)/shard_map/pallas_call | solution.py:343
  14.4 4.7 %collective-permute-done.4.refs_6_ = bf16[192,576]{1,0:T(8,128)(2,1)S(1)} collective-permute-done((bf16[192,576]{1,0:T(8,128)(2,1)S(1)}, bf16[192,576]{1,0:T(8,128)(2,1)S(1)}, u32[]{:S(2)}, u32[]{:S(2)}) %collective-permute-start.4) | collective-permute-done | bytes 221216 | tf_op jit(solution)/shard_map/ppermute | solution.py:308
  19.1 0.0 collective-permute-start.5
  19.8 3.2 %collective-permute-start.11 = (bf16[192,768]{1,0:T(8,128)(2,1)S(1)}, bf16[192,768]{1,0:T(8,128)(2,1)S(1)}, u32[]{:S(2)}, u32[]{:S(2)}) collective-permute-start(bf16[192,768]{1,0:T(8,128)(2,1)S(1)} %copy-done.1), channel_id=1, source_target_pairs={{0,2},{1,3},{2,0},{3,1},{4,7},{5,6},{6,5},{7,4},{8,10},{9,11},{10,... | collective-permute-start | bytes 884744 | tf_op jit(solution)/shard_map/ppermute | solution.py:308
  22.9 0.8 %collective-permute-start.10 = (bf16[192,768]{1,0:T(8,128)(2,1)S(1)}, bf16[192,768]{1,0:T(8,128)(2,1)S(1)}, u32[]{:S(2)}, u32[]{:S(2)}) collective-permute-start(bf16[192,768]{1,0:T(8,128)(2,1)S(1)} %copy-done.1), channel_id=1, source_target_pairs={{0,1},{1,0},{2,3},{3,2},{4,5},{5,4},{6,7},{7,6},{8,9},{9,8},{10,11... | collective-permute-start | bytes 884744 | tf_op jit(solution)/shard_map/ppermute | solution.py:48
  23.8 0.9 %shard_map.65 = (bf16[256,768]{1,0:T(8,128)(2,1)S(1)}, bf16[256,768]{1,0:T(8,128)(2,1)S(1)}) custom-call(bf16[256,768]{1,0:T(8,128)(2,1)S(1)} %collective-permute-done.1.refs_0_, bf16[256,768]{1,0:T(8,128)(2,1)S(1)} %collective-permute-done.2.refs_1_, f32[768]{0:T(1024)S(1)} %copy-done.2, f32[768]{0:T(1024)S(1)} %copy-done.3), custom_call_target="tpu_custom_call" | custom-call | flops 30000000 | bytes 90000 | tf_op jit(solution)/shard_map/pallas_call | solution.py:343
  24.6 2.0 %collective-permute-done.5.refs_7_ = bf16[192,576]{1,0:T(8,128)(2,1)S(1)} collective-permute-done((bf16[192,576]{1,0:T(8,128)(2,1)S(1)}, bf16[192,576]{1,0:T(8,128)(2,1)S(1)}, u32[]{:S(2)}, u32[]{:S(2)}) %collective-permute-start.5) | collective-permute-done | bytes 221216 | tf_op jit(solution)/shard_map/ppermute | solution.py:48
  26.6 1.6 %shard_map.66 = (bf16[256,576]{1,0:T(8,128)(2,1)S(1)}, bf16[256,576]{1,0:T(8,128)(2,1)S(1)}, bf16[256,576]{1,0:T(8,128)(2,1)S(1)}, bf16[256,576]{1,0:T(8,128)(2,1)S(1)}, bf16[3,64,128]{2,1,0:T(8,128)(2,1)S(1)}) custom-call(bf16[256,768]{1,0:T(8,128)(2,1)S(1)} %get-tuple-element.28.refs_0_, bf16[256,768]{1,0:T(8,128)(2,1)S(1)} %get-tuple-element.29.refs_1_, ...), custom_call_target="tpu_custom_call" | custom-call | flops 6000000000 | bytes 18000000 | tf_op jit(solution)/shard_map/pallas_call | solution.py:354
  28.2 0.3 collective-permute-start.6
  28.5 2.5 %shard_map.67 = (f32[3,2,1,256]{3,2,1,0:T(1,128)S(1)}, f32[3,2,1,256]{3,2,1,0:T(1,128)S(1)}, f32[3,2,64,256]{3,2,1,0:T(8,128)S(1)}) custom-call(s32[1]{0:T(128)S(6)} %copy.7.refs_0_, bf16[256,576]{1,0:T(8,128)(2,1)S(1)} %get-tuple-element.33.refs_1_, bf16[256,576]{1,0:T(8,128)(2,1)S(1)} %get-tuple-element.34.refs_2_, ...), custom_call_target="tpu_custom_call" | custom-call | flops 8999999488 | bytes 27000000 | tf_op jit(solution)/shard_map/pallas_call | solution.py:370
  30.9 1.3 %collective-permute-done.6.refs_6_ = bf16[3,64,128]{2,1,0:T(8,128)(2,1)S(1)} collective-permute-done((bf16[3,64,128]{2,1,0:T(8,128)(2,1)S(1)}, bf16[3,64,128]{2,1,0:T(8,128)(2,1)S(1)}, u32[]{:S(2)}, u32[]{:S(2)}) %collective-permute-start.6) | collective-permute-done | bytes 49184 | tf_op jit(solution)/shard_map/ppermute | solution.py:48
  32.3 0.5 %shard_map.68 = bf16[2,192,256]{2,1,0:T(8,128)(2,1)S(1)} custom-call(s32[1]{0:T(128)S(6)} %copy.7.refs_0_, bf16[256,576]{1,0:T(8,128)(2,1)S(1)} %get-tuple-element.33.refs_1_, bf16[256,576]{1,0:T(8,128)(2,1)S(1)} %get-tuple-element.34.refs_2_, bf16[256,576]{1,0:T(8,128)(2,1)S(1)} %get-tuple-element.35.refs_3_, ...), custom_call_target="tpu_custom_call" | custom-call | flops 3000000000 | bytes 9000000 | tf_op jit(solution)/shard_map/pallas_call | solution.py:373
  32.8 0.8 %collective-permute-start.7 = (bf16[2,192,256]{2,1,0:T(8,128)(2,1)S(1)}, bf16[2,192,256]{2,1,0:T(8,128)(2,1)S(1)}, u32[]{:S(2)}, u32[]{:S(2)}) collective-permute-start(bf16[2,192,256]{2,1,0:T(8,128)(2,1)S(1)} %shard_map.68), channel_id=1, source_target_pairs={{0,8},{4,12},{8,0},{12,4},{16,24},{20,28},{24,16},{28,20},{1,9},{5... | collective-permute-start | bytes 589832 | tf_op jit(solution)/shard_map/ppermute | solution.py:48
  33.5 3.0 %shard_map.69 = (bf16[192,256]{1,0:T(8,128)(2,1)S(1)}, bf16[192,256]{1,0:T(8,128)(2,1)S(1)}) custom-call(s32[1]{0:T(128)S(6)} %copy.7.refs_0_, bf16[256,576]{1,0:T(8,128)(2,1)S(1)} %get-tuple-element.33.refs_1_, bf16[256,576]{1,0:T(8,128)(2,1)S(1)} %get-tuple-element.34.refs_2_, bf16[256,576]{1,0:T(8,128)(2,1)S(1)} %get-tuple-element.35.refs_3_, ...), custom_call_target="tpu_custom_call" | custom-call | flops 6000000000 | bytes 18000000 | tf_op jit(solution)/shard_map/pallas_call | solution.py:380
  36.6 0.1 collective-permute-start.12
  36.6 0.5 %collective-permute-start.8 = (bf16[192,256]{1,0:T(8,128)(2,1)S(1)}, bf16[192,256]{1,0:T(8,128)(2,1)S(1)}, u32[]{:S(2)}, u32[]{:S(2)}) collective-permute-start(bf16[192,256]{1,0:T(8,128)(2,1)S(1)} %get-tuple-element.42), channel_id=1, source_target_pairs={{0,4},{4,0},{8,12},{12,8},{16,20},{20,16},{24,28},{28,24},{1,5},{5... | collective-permute-start | bytes 294920 | tf_op jit(solution)/shard_map/ppermute | solution.py:48
  37.1 1.2 %collective-permute-done.8.refs_0_ = bf16[192,256]{1,0:T(8,128)(2,1)S(1)} collective-permute-done((bf16[192,256]{1,0:T(8,128)(2,1)S(1)}, bf16[192,256]{1,0:T(8,128)(2,1)S(1)}, u32[]{:S(2)}, u32[]{:S(2)}) %collective-permute-start.8) | collective-permute-done | bytes 98336 | tf_op jit(solution)/shard_map/ppermute | solution.py:48
  38.4 0.2 collective-permute-done.7.refs_1_
  38.5 0.1 shard_map.70
  38.6 0.5 %shard_map.71.refs_4_ = f32[256,768]{1,0:T(8,128)S(1)} custom-call(bf16[192,256]{1,0:T(8,128)(2,1)S(1)} %get-tuple-element.45.refs_0_, bf16[768,768]{1,0:T(8,128)(2,1)S(1)} %get-tuple-element.47.refs_1_.refs_2_, bf16[256,256]{1,0:T(8,128)(2,1)S(1)} %get-tuple-element.48.refs_2_.refs_3_, bf16[256,768]{1,0:T(8,128)(2,1)S(1)} %bitcast.5), custom_call_target="tpu_custom_call" | custom-call | flops 3000000 | bytes 9000 | tf_op jit(solution)/shard_map/pallas_call | solution.py:405
  39.1 0.7 %shard_map.72.refs_3_ = f32[256,768]{1,0:T(8,128)S(1)} custom-call(bf16[192,256]{1,0:T(8,128)(2,1)S(1)} %collective-permute-done.8.refs_0_, bf16[2,192,256]{2,1,0:T(8,128)(2,1)S(1)} %collective-permute-done.7.refs_1_, bf16[768,768]{1,0:T(8,128)(2,1)S(1)} %get-tuple-element.47.refs_1_.refs_2_, bf16[256,256]{1,0:T(8,128)(2,1)S(1)} %get-tuple-element.48.refs_2_.refs_3_, ...), custom_call_target="tpu_custom_call" | custom-call | flops 3000000 | bytes 9000 | tf_op jit(solution)/shard_map/pallas_call | solution.py:405
  39.8 0.2 collective-permute-done.9.refs_0_
  40.0 1.2 %shard_map.73 = bf16[256,768]{1,0:T(8,128)(2,1)} custom-call(bf16[2,192,256]{2,1,0:T(8,128)(2,1)S(1)} %collective-permute-done.9.refs_0_, bf16[768,768]{1,0:T(8,128)(2,1)S(1)} %get-tuple-element.47.refs_1_.refs_2_, bf16[256,256]{1,0:T(8,128)(2,1)S(1)} %get-tuple-element.48.refs_2_.refs_3_, f32[256,768]{1,0:T(8,128)S(1)} %shard_map.72.refs_3_), custom_call_target="tpu_custom_call" | custom-call | flops 3000000 | bytes 9000 | tf_op jit(solution)/shard_map/pallas_call | solution.py:405
  (14 shorter events, 0.0 us)
Async XLA Ops:
  0.0 1.4 %copy-start = (bf16[1,256,768]{2,1,0:T(8,128)(2,1)S(1)}, bf16[1,256,768]{2,1,0:T(8,128)(2,1)}, u32[]{:S(2)}) copy-start(bf16[1,256,768]{2,1,0:T(8,128)(2,1)} %param.6) | copy-start | bytes 1179652
  0.0 13.5 %copy-start.2 = (f32[768]{0:T(1024)S(1)}, f32[768]{0:T(1024)}, u32[]{:S(2)}) copy-start(f32[768]{0:T(1024)} %refs_2_.3) | copy-start | bytes 9220
  0.0 13.5 %copy-start.3 = (f32[768]{0:T(1024)S(1)}, f32[768]{0:T(1024)}, u32[]{:S(2)}) copy-start(f32[768]{0:T(1024)} %refs_3_.3) | copy-start | bytes 9220
  1.4 18.4 %copy-start.1 = (bf16[192,768]{1,0:T(8,128)(2,1)S(1)}, bf16[192,768]{1,0:T(8,128)(2,1)}, u32[]{:S(2)}) copy-start(bf16[192,768]{1,0:T(8,128)(2,1)} %refs_0_.3) | copy-start | bytes 884740
  1.4 12.1 %collective-permute-start.1 = (bf16[256,768]{1,0:T(8,128)(2,1)S(1)}, bf16[256,768]{1,0:T(8,128)(2,1)S(1)}, u32[]{:S(2)}, u32[]{:S(2)}) collective-permute-start(bf16[256,768]{1,0:T(8,128)(2,1)S(1)} %bitcast.2), channel_id=1, source_target_pairs={{0,8},{4,12},{8,0},{12,4},{16,24},{20,28},{24,16},{28,20},{1,9},{5... | collective-permute-start | bytes 1179656 | tf_op jit(solution)/shard_map/ppermute | solution.py:48
  4.4 9.1 %collective-permute-start = (bf16[256,768]{1,0:T(8,128)(2,1)S(1)}, bf16[256,768]{1,0:T(8,128)(2,1)S(1)}, u32[]{:S(2)}, u32[]{:S(2)}) collective-permute-start(bf16[256,768]{1,0:T(8,128)(2,1)S(1)} %bitcast.3), channel_id=1, source_target_pairs={{0,4},{4,0},{8,12},{12,8},{16,20},{20,16},{24,28},{28,24},{1,5},{5... | collective-permute-start | bytes 1179656 | tf_op jit(solution)/shard_map/ppermute | solution.py:48
  4.4 14.6 %collective-permute-start.4 = (bf16[192,576]{1,0:T(8,128)(2,1)S(1)}, bf16[192,576]{1,0:T(8,128)(2,1)S(1)}, u32[]{:S(2)}, u32[]{:S(2)}) collective-permute-start(bf16[192,576]{1,0:T(8,128)(2,1)S(1)} %pad_maximum_fusion.refs_4_), channel_id=1, source_target_pairs={{0,2},{1,3},{2,0},{3,1},{4,6},{5,7},{6,4},{7,5},{8,10},{9,11},{10,... | collective-permute-start | bytes 663560 | tf_op jit(solution)/shard_map/ppermute | solution.py:308
  7.0 17.6 %collective-permute-start.3 = (bf16[192,576]{1,0:T(8,128)(2,1)S(1)}, bf16[192,576]{1,0:T(8,128)(2,1)S(1)}, u32[]{:S(2)}, u32[]{:S(2)}) collective-permute-start(bf16[192,576]{1,0:T(8,128)(2,1)S(1)} %pad_maximum_fusion.refs_4_), channel_id=1, source_target_pairs={{0,1},{1,0},{2,3},{3,2},{4,5},{5,4},{6,7},{7,6},{8,9},{9,8},{10,11... | collective-permute-start | bytes 663560 | tf_op jit(solution)/shard_map/ppermute | solution.py:48
  13.5 6.2 %collective-permute-start.2 = (bf16[256,768]{1,0:T(8,128)(2,1)S(1)}, bf16[256,768]{1,0:T(8,128)(2,1)S(1)}, u32[]{:S(2)}, u32[]{:S(2)}) collective-permute-start(bf16[256,768]{1,0:T(8,128)(2,1)S(1)} %collective-permute-done.1.refs_0_), channel_id=1, source_target_pairs={{0,4},{4,0},{8,12},{12,8},{16,20},{20,16},{24,28},{28,24},{1,5},{5... | collective-permute-start | bytes 1179656 | tf_op jit(solution)/shard_map/ppermute | solution.py:48
  19.1 7.5 %collective-permute-start.5 = (bf16[192,576]{1,0:T(8,128)(2,1)S(1)}, bf16[192,576]{1,0:T(8,128)(2,1)S(1)}, u32[]{:S(2)}, u32[]{:S(2)}) collective-permute-start(bf16[192,576]{1,0:T(8,128)(2,1)S(1)} %collective-permute-done.4.refs_6_), channel_id=1, source_target_pairs={{0,16},{4,20},{8,24},{12,28},{16,0},{20,4},{24,8},{28,12},{1,17},{... | collective-permute-start | bytes 663560 | tf_op jit(solution)/shard_map/ppermute | solution.py:48
  19.8 16.8 %collective-permute-start.11 = (bf16[192,768]{1,0:T(8,128)(2,1)S(1)}, bf16[192,768]{1,0:T(8,128)(2,1)S(1)}, u32[]{:S(2)}, u32[]{:S(2)}) collective-permute-start(bf16[192,768]{1,0:T(8,128)(2,1)S(1)} %copy-done.1), channel_id=1, source_target_pairs={{0,2},{1,3},{2,0},{3,1},{4,7},{5,6},{6,5},{7,4},{8,10},{9,11},{10,... | collective-permute-start | bytes 884744 | tf_op jit(solution)/shard_map/ppermute | solution.py:308
  22.9 15.6 %collective-permute-start.10 = (bf16[192,768]{1,0:T(8,128)(2,1)S(1)}, bf16[192,768]{1,0:T(8,128)(2,1)S(1)}, u32[]{:S(2)}, u32[]{:S(2)}) collective-permute-start(bf16[192,768]{1,0:T(8,128)(2,1)S(1)} %copy-done.1), channel_id=1, source_target_pairs={{0,1},{1,0},{2,3},{3,2},{4,5},{5,4},{6,7},{7,6},{8,9},{9,8},{10,11... | collective-permute-start | bytes 884744 | tf_op jit(solution)/shard_map/ppermute | solution.py:48
  28.2 4.1 %collective-permute-start.6 = (bf16[3,64,128]{2,1,0:T(8,128)(2,1)S(1)}, bf16[3,64,128]{2,1,0:T(8,128)(2,1)S(1)}, u32[]{:S(2)}, u32[]{:S(2)}) collective-permute-start(bf16[3,64,128]{2,1,0:T(8,128)(2,1)S(1)} %get-tuple-element.41.refs_5_), channel_id=1, source_target_pairs={{0,16},{4,20},{8,24},{12,28},{16,0},{20,4},{24,8},{28,12},{1,17},{... | collective-permute-start | bytes 147464 | tf_op jit(solution)/shard_map/ppermute | solution.py:48
  32.8 5.7 %collective-permute-start.7 = (bf16[2,192,256]{2,1,0:T(8,128)(2,1)S(1)}, bf16[2,192,256]{2,1,0:T(8,128)(2,1)S(1)}, u32[]{:S(2)}, u32[]{:S(2)}) collective-permute-start(bf16[2,192,256]{2,1,0:T(8,128)(2,1)S(1)} %shard_map.68), channel_id=1, source_target_pairs={{0,8},{4,12},{8,0},{12,4},{16,24},{20,28},{24,16},{28,20},{1,9},{5... | collective-permute-start | bytes 589832 | tf_op jit(solution)/shard_map/ppermute | solution.py:48
  36.6 2.0 %collective-permute-start.12 = (bf16[192,768]{1,0:T(8,128)(2,1)S(1)}, bf16[192,768]{1,0:T(8,128)(2,1)S(1)}, u32[]{:S(2)}, u32[]{:S(2)}) collective-permute-start(bf16[192,768]{1,0:T(8,128)(2,1)S(1)} %collective-permute-done.11.refs_2_), channel_id=1, source_target_pairs={{0,4},{4,0},{8,12},{12,8},{16,20},{20,16},{24,28},{28,24},{1,5},{5... | collective-permute-start | bytes 884744 | tf_op jit(solution)/shard_map/ppermute | solution.py:48
  36.6 1.7 %collective-permute-start.8 = (bf16[192,256]{1,0:T(8,128)(2,1)S(1)}, bf16[192,256]{1,0:T(8,128)(2,1)S(1)}, u32[]{:S(2)}, u32[]{:S(2)}) collective-permute-start(bf16[192,256]{1,0:T(8,128)(2,1)S(1)} %get-tuple-element.42), channel_id=1, source_target_pairs={{0,4},{4,0},{8,12},{12,8},{16,20},{20,16},{24,28},{28,24},{1,5},{5... | collective-permute-start | bytes 294920 | tf_op jit(solution)/shard_map/ppermute | solution.py:48
  38.5 1.4 %collective-permute-start.9 = (bf16[2,192,256]{2,1,0:T(8,128)(2,1)S(1)}, bf16[2,192,256]{2,1,0:T(8,128)(2,1)S(1)}, u32[]{:S(2)}, u32[]{:S(2)}) collective-permute-start(bf16[2,192,256]{2,1,0:T(8,128)(2,1)S(1)} %collective-permute-done.7.refs_1_), channel_id=1, source_target_pairs={{0,4},{4,0},{8,12},{12,8},{16,20},{20,16},{24,28},{28,24},{1,5},{5... | collective-permute-start | bytes 589832 | tf_op jit(solution)/shard_map/ppermute | solution.py:48

commit v8 on v7

--- a/solution.py
+++ b/solution.py
@@ -89,7 +89,10 @@
         centred = floats - jnp.mean(floats, axis=-1, keepdims=True)
         spread = jnp.mean(centred * centred, axis=-1, keepdims=True)
         normed = (centred * lax.rsqrt(spread + 1e-05) * gain + bias).astype(jnp.bfloat16)
-        out_ref[...] = product(order, normed).astype(jnp.bfloat16)
+        ordered = product(order, normed).astype(jnp.bfloat16)
+        blocks, _, width = out_ref.shape
+        for block in range(blocks):
+            out_ref[block] = ordered[:, block * width : (block + 1) * width]
 
 
 def group_indices():
@@ -128,13 +131,25 @@
     return [mp_index ^ apart for apart in range(n_mp)]
 
 
-def project_body(n_mp, shared, *refs):
+def project_body(blocks, *refs):
+    _, group = group_indices()
     normed_refs, refs = refs[:SHARDS], refs[SHARDS:]
-    weight_refs, (*out_refs, sent_ref, whole_ref) = refs[:n_mp], refs[n_mp:]
-    member, group = group_indices()
-    assemble(whole_ref, weight_refs, sources(n_mp, group % 2, shared))
-    for normed_ref, out_ref in zip(normed_refs, out_refs):
-        out_ref[...] = product(normed_ref[...], whole_ref[...]).astype(jnp.bfloat16)
+    n_mp, shared, some = blocks
+    weight_refs, refs = refs[: len(some)], refs[len(some) :]
+    base_refs, out_refs = refs[:-SHARDS], refs[-SHARDS:]
+    origin = sources(n_mp, group % 2, shared)
+    for shard, (normed_ref, out_ref) in enumerate(zip(normed_refs, out_refs)):
+        total = base_refs[shard][...] if base_refs else 0.0
+        for block, weight_ref in zip(some, weight_refs):
+            total = total + product(normed_ref[origin[block]], weight_ref[...])
+        out_ref[...] = total.astype(out_ref.dtype)
+
+
+def project_last_body(blocks, *refs):
+    *refs, sent_ref = refs
+    project_body(blocks, *refs)
+    out_refs = refs[-SHARDS:]
+    member, _ = group_indices()
     shard_rows = out_refs[0].shape[0]
     depth = shard_rows // WIDE
     for index in range(GROUP_HEADS):
@@ -146,12 +161,18 @@
             )
 
 
-def branch(query, key, value, bias):
-    score = product(key, query, 1, 1) * SCALE + bias
-    largest = jnp.max(score, axis=0, keepdims=True)
-    weight = jnp.exp2(score - largest)
-    total = jnp.sum(weight, axis=0, keepdims=True)
-    return largest, total, product(value, weight.astype(jnp.bfloat16), 0, 0)
+def attend(items):
+    scores = [product(key, query, 1, 1) for query, key, _, _ in items]
+    weights = []
+    for score, (_, _, _, bias) in zip(scores, items):
+        score = score * SCALE + bias
+        largest = jnp.max(score, axis=0, keepdims=True)
+        weight = jnp.exp2(score - largest)
+        weights.append((largest, jnp.sum(weight, axis=0, keepdims=True), weight.astype(jnp.bfloat16)))
+    return [
+        (largest, total, product(value, weight, 0, 0))
+        for (largest, total, weight), (_, _, value, _) in zip(weights, items)
+    ]
 
 
 def key_bias(position, valid):
@@ -165,7 +186,8 @@
     return top, left * one[1] + right * two[1], left * one[2] + right * two[2]
 
 
-def near_branches(shards, valid_ref, qkv_refs, max_ref, sum_ref, num_ref):
+def near_body(valid_ref, *refs):
+    qkv_refs, (max_ref, sum_ref, num_ref) = refs[:SHARDS], refs[SHARDS:]
     member, group = group_indices()
     valid = valid_ref[0]
     rows = qkv_refs[0].shape[0]
@@ -175,39 +197,47 @@
     place = place_of(lax.broadcasted_iota(jnp.int32, (rows, LANES), 0), rows)
     lane = lax.broadcasted_iota(jnp.int32, (1, rows), 1)
 
-    for slot, shard in enumerate(shards):
-        ref = qkv_refs[shard]
-        bias = jnp.concatenate(
-            [key_bias(place + bases[shard], valid)] * (rows // LANES), axis=1
-        )
+    def widen(bias):
+        return jnp.concatenate([bias] * (rows // LANES), axis=1)
+
+    items = []
+    for base, ref in zip(bases, qkv_refs):
+        bias = widen(key_bias(place + base, valid))
         for index in range(GROUP_HEADS):
-            stats = branch(*(ref[:, at] for at in head_slices(index)), bias)
-            max_ref[index, slot], sum_ref[index, slot], num_ref[index, slot] = stats
-    item = lax.broadcasted_iota(jnp.int32, (count, len(shards) * count), 0)
+            items.append((*(ref[:, at] for at in head_slices(index)), bias))
+    item = lax.broadcasted_iota(jnp.int32, (count, LANES), 0)
     for index in range(GROUP_HEADS):
         head = member * GROUP_HEADS + index
         taken = middle_rows(head, rows)
-        query, key, value = (
-            jnp.concatenate([qkv_refs[shard][taken, at] for shard in some], axis=0)
-            for some, at in zip((shards, range(SHARDS), range(SHARDS)), head_slices(index))
-        )
         position = item % depth * WIDE + item // depth * MID + head % MID
         bias = jnp.concatenate([key_bias(position + base, valid) for base in bases], axis=0)
-        middle = branch(query, key, value, bias)
-        inside = lane // count == head % MID
-        for slot in range(len(shards)):
+        items.append(
+            (
+                *(
+                    jnp.concatenate([ref[taken, at] for ref in qkv_refs], axis=0)
+                    for at in head_slices(index)
+                ),
+                widen(bias),
+            )
+        )
+    stats = attend(items)
+    for index in range(GROUP_HEADS):
+        middle = stats[SHARDS * GROUP_HEADS + index]
+        inside = lane // count == (member * GROUP_HEADS + index) % MID
+        for shard in range(SHARDS):
             largest, total, number = (
-                jnp.concatenate([part[:, slot * count : (slot + 1) * count]] * MID, axis=1)
+                jnp.concatenate([part[:, shard * count : (shard + 1) * count]] * MID, axis=1)
                 for part in middle
             )
-            merged = merge(
-                (max_ref[index, slot], sum_ref[index, slot], num_ref[index, slot]),
+            max_ref[index, shard], sum_ref[index, shard], num_ref[index, shard] = merge(
+                stats[shard * GROUP_HEADS + index],
                 (jnp.where(inside, largest, NEG_FILL), total, number),
             )
-            max_ref[index, slot], sum_ref[index, slot], num_ref[index, slot] = merged
-
-
-def far_branch(shards, valid_ref, qkv_refs, sent_refs, max_ref, sum_ref, num_ref, out_refs):
+
+
+def far_body(shards, valid_ref, *refs):
+    *refs, out_ref = refs
+    qkv_refs, sent_refs, (max_ref, sum_ref, num_ref) = refs[:SHARDS], refs[SHARDS:-3], refs[-3:]
     member, group = group_indices()
     valid = valid_ref[0]
     rows = qkv_refs[0].shape[0]
@@ -215,6 +245,7 @@
     count = len(shards) * depth
     item = lax.broadcasted_iota(jnp.int32, (SHARDS * depth, count), 0)
     lane = lax.broadcasted_iota(jnp.int32, (1, rows), 1)
+    items = []
     for index in range(GROUP_HEADS):
         head = member * GROUP_HEADS + index
         taken = wide_rows(head, rows)
@@ -233,9 +264,11 @@
             axis=0,
         )
         both = jnp.concatenate([ref[index] for ref in sent_refs], axis=0)
-        stats = branch(query, both[:, :HEAD_DIM], both[:, HEAD_DIM:], bias)
+        items.append((query, both[:, :HEAD_DIM], both[:, HEAD_DIM:], bias))
+    for index, (largest, total, number) in enumerate(attend(items)):
+        head = member * GROUP_HEADS + index
         stacked = jnp.concatenate(
-            [stats[2], jnp.broadcast_to(stats[0], (8, count)), jnp.broadcast_to(stats[1], (8, count))],
+            [number, jnp.broadcast_to(largest, (8, count)), jnp.broadcast_to(total, (8, count))],
             axis=0,
         )
         stacked = jnp.concatenate(
@@ -243,11 +276,11 @@
         )
         block = head % MID * STEPS + head % WIDE // MID
         inside = lane // depth == block
-        for slot, (shard, out_ref) in enumerate(zip(shards, out_refs)):
+        for slot, shard in enumerate(shards):
             shift = (block * depth - slot * depth + LANES) % LANES
             moved = jnp.concatenate([pltpu.roll(stacked, shift, 1)] * (rows // LANES), axis=1)
             _, total, number = merge(
-                (max_ref[index, slot], sum_ref[index, slot], num_ref[index, slot]),
+                (max_ref[index, shard], sum_ref[index, shard], num_ref[index, shard]),
                 (
                     jnp.where(inside, moved[HEAD_DIM : HEAD_DIM + 1], NEG_FILL),
                     moved[HEAD_DIM + 8 : HEAD_DIM + 9],
@@ -258,25 +291,9 @@
             attention = jnp.where(
                 base + place_of(lane, rows) < valid, number * (1.0 / total), 0.0
             )
-            out_ref[index * HEAD_DIM : (index + 1) * HEAD_DIM, :] = attention.astype(jnp.bfloat16)
-
-
-def near_body(shards, valid_ref, *refs):
-    near_branches(shards, valid_ref, refs[:SHARDS], *refs[SHARDS:])
-
-
-def far_body(shards, valid_ref, *refs):
-    *refs, out_ref = refs
-    sent_refs, stat_refs = refs[SHARDS:-3], refs[-3:]
-    out_refs = [out_ref.at[slot] for slot in range(len(shards))]
-    far_branch(shards, valid_ref, refs[:SHARDS], sent_refs, *stat_refs, out_refs)
-
-
-def all_body(shards, valid_ref, *refs):
-    stat_refs, out_refs = refs[-3:], refs[-len(shards) - 3 : -3]
-    sent_refs = refs[SHARDS : -len(shards) - 3]
-    near_branches(shards, valid_ref, refs[:SHARDS], *stat_refs)
-    far_branch(shards, valid_ref, refs[:SHARDS], sent_refs, *stat_refs, out_refs)
+            out_ref[slot, index * HEAD_DIM : (index + 1) * HEAD_DIM, :] = attention.astype(
+                jnp.bfloat16
+            )
 
 
 def gather_body(n_mp, shared, *refs):
@@ -291,8 +308,7 @@
     order = order_ref[...]
     update = base_ref[...].astype(jnp.float32)
     for (apart, slot), ref in zip(blocks, part_refs):
-        part = ref[...] if slot is None else ref[slot]
-        part = product(order, part, 1, 1).astype(jnp.bfloat16)
+        part = product(order, ref[slot], 1, 1).astype(jnp.bfloat16)
         start = pl.multiple_of((member ^ apart) * GROUP_WIDTH, GROUP_WIDTH)
         update = update + product(part, weight_ref[pl.ds(start, GROUP_WIDTH), :])
     out_ref[...] = update.astype(out_ref.dtype)
@@ -340,53 +356,61 @@
     gain, bias = near(norm_gain), near(norm_bias)
 
     def normalized(one, two, micros):
-        return call(norm_body, [shape((rows, width), bf16)] * 2, n_in=4, micros=micros)(
+        blocks = shape((n_mp, rows, weight_rows), bf16)
+        return call(norm_body, [blocks] * 2, n_in=4, micros=micros)(
             one, two, gain, bias
         )
 
-    normed = normalized(x_own, x_pair, 1)
+    normed = normalized(x_own, x_pair, 3)
     weights = [mine] + exchange(fetched, shared, SHARDS, normed[0])
     normed += normalized(x_far, x_last, 0.01)
 
-    out_weight = after(near(w_out), x_last)
+    out_weight = after(near(w_out), normed[2])
     out_fetched = fetch(out_weight, lambda c: c % 2, shared)
 
+    early = range(n_mp - 1)
+    partial = call(
+        lambda *refs: project_body((n_mp, shared, early), *refs),
+        [shape((rows, 3 * GROUP_WIDTH), f32)] * SHARDS,
+        n_in=SHARDS + len(early),
+        micros=1,
+    )(*normed, *weights[:-1])
     *qkv, sent = call(
-        lambda *refs: project_body(n_mp, shared, *refs),
+        lambda *refs: project_last_body((n_mp, shared, [n_mp - 1]), *refs),
         [shape((rows, 3 * GROUP_WIDTH), bf16)] * SHARDS
         + [shape((GROUP_HEADS, SHARDS * depth, 2 * HEAD_DIM), bf16)],
-        scratch=[pltpu.VMEM((width, 3 * GROUP_WIDTH), bf16)],
-        n_in=SHARDS + n_mp,
-        micros=2,
-    )(*normed, *weights)
+        n_in=2 * SHARDS + 1,
+        micros=1,
+    )(*normed, weights[-1], *partial)
     sents = [sent] + [flip(sent, "ctx", SHARDS * apart) for apart in range(1, n_groups)]
+    stats = call(
+        near_body,
+        [
+            shape((GROUP_HEADS, SHARDS, 1, rows), f32),
+            shape((GROUP_HEADS, SHARDS, 1, rows), f32),
+            shape((GROUP_HEADS, SHARDS, HEAD_DIM, rows), f32),
+        ],
+        n_scalar=1,
+        n_in=SHARDS,
+        micros=20,
+    )(valid_count, *qkv)
+
     half = SHARDS // 2
-    here, there = range(half), range(half, SHARDS)
-    stat_shapes = [
-        shape((GROUP_HEADS, half, 1, rows), f32),
-        shape((GROUP_HEADS, half, 1, rows), f32),
-        shape((GROUP_HEADS, half, HEAD_DIM, rows), f32),
-    ]
-    stats = call(
-        lambda *refs: near_body(there, *refs), stat_shapes, n_scalar=1, n_in=SHARDS, micros=3
-    )(valid_count, *qkv)
-    (sending,) = call(
-        lambda *refs: far_body(there, *refs),
-        [shape((half, GROUP_WIDTH, rows), bf16)],
-        n_scalar=1,
-        n_in=SHARDS + n_groups + 3,
-        micros=1,
-    )(valid_count, *qkv, *sents, *stats)
-    staying = call(
-        lambda *refs: all_body(here, *refs),
-        [shape((GROUP_WIDTH, rows), bf16)] * half,
-        scratch=stat_shapes,
-        n_scalar=1,
-        n_in=SHARDS + n_groups,
-        micros=2,
-    )(valid_count, *qkv, after(sents[0], sending), *sents[1:])
+
+    def finished(shards, sent_parts, micros):
+        return call(
+            lambda *refs: far_body(shards, *refs),
+            [shape((half, GROUP_WIDTH, rows), bf16)],
+            n_scalar=1,
+            n_in=SHARDS + n_groups + 3,
+            micros=micros,
+        )(valid_count, *qkv, *sent_parts, *stats)[0]
+
+    sending = finished(range(half, SHARDS), sents, 1)
+    staying = finished(range(half), [after(sents[0], sending, *out_fetched)] + sents[1:], 5)
     far_part = flip(sending, "ctx", 2)
-    out_parts = [out_weight] + exchange(out_fetched, shared, 1, staying[0])
+    pair_part = flip(staying, "ctx", 1)
+    out_parts = [out_weight] + exchange(out_fetched, shared, 1, sending)
     whole_out, order = call(
         lambda *refs: gather_body(n_mp, shared, *refs),
         [shape((width, width), bf16), shape((rows, rows), bf16)],
@@ -394,11 +418,10 @@
         micros=0.001,
     )(*out_parts)
     total = x_own
-    pair_part = flip(staying[1], "ctx", 1)
     last_part = flip(after(far_part, pair_part), "ctx", 1)
     steps = [
-        ([(0, None)], [staying[0]], shape((rows, width), f32)),
-        ([(1, None), (2, 0)], [pair_part, far_part], shape((rows, width), f32)),
+        ([(0, 0), (1, 1)], [staying, pair_part], shape((rows, width), f32)),
+        ([(2, 0)], [far_part], shape((rows, width), f32)),
         ([(3, 1)], [last_part], jax.ShapeDtypeStruct((rows, width), bf16)),
     ]
     for blocks, operands, out_shape in steps:

time: 41.3 us -> 42.2 us (1.022)
  waiting for transfers between devices: 14.4 us -> 17.3 us
  Pallas kernels: 11.7 us -> 9.07 us
  starting transfers between devices: 12.8 us -> 13.5 us
    ppermute x2, waiting for transfers between devices: 4.66 us -> 8.34 us  [fetch(): lax.ppermute(value, ('ctx', 'mp'), pairs)]
    pallas_call x6 -> x7, Pallas kernels: 9.29 us -> 6.61 us  [the longest x2 1.87 us: normalized(): call(norm_body, [blocks] * 2, n_in=4, micros=micros)(one, two, gain, bias)]
    ppermute x11, waiting for transfers between devices: 9.74 us -> 8.97 us  [flip(): return near(lax.ppermute(value, axis, pairs))]
    ppermute x11, starting transfers between devices: 7.07 us -> 7.77 us  [flip(): return near(lax.ppermute(value, axis, pairs))]
  transfers between devices with their start and end apart: 13 -> 13, of which waited for: 7 -> 8; matrix products, arithmetic and copies ran while one was open for 0% -> 0% of each run, Pallas kernels for 26% -> 19%
where the time goes in v8:
time: 42.2 us; the launch traced here: 42.1 us
  waiting for transfers between devices  17.3 us (41%)
  starting transfers between devices  13.5 us (32%)
  Pallas kernels  9.07 us (21%)
  local copies, waits for them, and re-layouts  1.27 us (3%)
  between operations  0.79 us (2%)
    ppermute x11, waiting for transfers between devices, flip(): return near(lax.ppermute(value, axis, pairs))  8.97 us
    ppermute x2, waiting for transfers between devices, fetch(): lax.ppermute(value, ('ctx', 'mp'), pairs)  8.34 us
    ppermute x11, starting transfers between devices, flip(): return near(lax.ppermute(value, axis, pairs))  7.77 us
    ppermute x2, starting transfers between devices, fetch(): lax.ppermute(value, ('ctx', 'mp'), pairs)  5.76 us
    pallas_call x3, Pallas kernels, local(): call(lambda *refs, blocks=blocks: update_body(blocks, *refs), [out_shape]...  2.36 us
    pallas_call x2, Pallas kernels, normalized(): call(norm_body, [blocks] * 2, n_in=4, micros=micros)(one, two, gain, bias)  1.87 us
    pallas_call x1, Pallas kernels, local(): call(near_body, [shape((GROUP_HEADS, SHARDS, 1, rows), f32), shape((GROUP...  1.71 us
    pallas_call x1, Pallas kernels, local(): call(lambda *refs: project_body((n_mp, shared, early), *refs), [shape((ro...  1.36 us
  transfers between devices with their start and end apart: 13, of which 8 were waited for; matrix products, arithmetic and copies ran while one was open for 0% of the time, Pallas kernels for 19%

profile of v8, /device:TPU:0, one launch (start us, length us, event | category | flops | bytes accessed | tf_op | source)
XLA Modules:
  0.0 42.1 jit_solution(7325236795237170082)
XLA Ops:
  0.0 1.3 %constant_dynamic-slice_fusion.2 = (bf16[192,192]{1,0:T(8,128)(2,1)S(1)}, bf16[192,192]{1,0:T(8,128)(2,1)S(1)}, bf16[192,192]{1,0:T(8,128)(2,1)S(1)}) fusion(bf16[192,2304]{1,0:T(8,128)(2,1)} %param.9, s32[]{:T(128)S(6)} %select_n.17, s32[]{:T(128)S(6)} %select_n.19, s32[]{:T(128)S(6)} %select_n.18), kind=kLoop, calls=%fused_computation.3 | loop fusion | bytes 442380 | tf_op jit(solution)/shard_map/dynamic_slice | solution.py:347
  1.3 0.1 pad_maximum_fusion.refs_4_
  1.4 3.0 %collective-permute-start.1 = (bf16[256,768]{1,0:T(8,128)(2,1)S(1)}, bf16[256,768]{1,0:T(8,128)(2,1)S(1)}, u32[]{:S(2)}, u32[]{:S(2)}) collective-permute-start(bf16[256,768]{1,0:T(8,128)(2,1)S(1)} %bitcast.2), channel_id=1, source_target_pairs={{0,8},{4,12},{8,0},{12,4},{16,24},{20,28},{24,16},{28,20},{1,9},{5... | collective-permute-start | bytes 1179656 | tf_op jit(solution)/shard_map/ppermute | solution.py:48
  4.4 2.6 %collective-permute-start.3 = (bf16[192,576]{1,0:T(8,128)(2,1)S(1)}, bf16[192,576]{1,0:T(8,128)(2,1)S(1)}, u32[]{:S(2)}, u32[]{:S(2)}) collective-permute-start(bf16[192,576]{1,0:T(8,128)(2,1)S(1)} %pad_maximum_fusion.refs_4_), channel_id=1, source_target_pairs={{0,2},{1,3},{2,0},{3,1},{4,6},{5,7},{6,4},{7,5},{8,10},{9,11},{10,... | collective-permute-start | bytes 663560 | tf_op jit(solution)/shard_map/ppermute | solution.py:324
  7.0 1.6 %collective-permute-start.5 = (bf16[192,576]{1,0:T(8,128)(2,1)S(1)}, bf16[192,576]{1,0:T(8,128)(2,1)S(1)}, u32[]{:S(2)}, u32[]{:S(2)}) collective-permute-start(bf16[192,576]{1,0:T(8,128)(2,1)S(1)} %pad_maximum_fusion.refs_4_), channel_id=1, source_target_pairs={{0,1},{1,0},{2,3},{3,2},{4,5},{5,4},{6,7},{7,6},{8,9},{9,8},{10,11... | collective-permute-start | bytes 663560 | tf_op jit(solution)/shard_map/ppermute | solution.py:48
  9.2 0.0 copy-start.1
  9.3 4.3 %collective-permute-done.1.refs_0_ = bf16[256,768]{1,0:T(8,128)(2,1)S(1)} collective-permute-done((bf16[256,768]{1,0:T(8,128)(2,1)S(1)}, bf16[256,768]{1,0:T(8,128)(2,1)S(1)}, u32[]{:S(2)}, u32[]{:S(2)}) %collective-permute-start.1) | collective-permute-done | bytes 393248 | tf_op jit(solution)/shard_map/ppermute | solution.py:48
  13.5 0.9 %shard_map.64 = (bf16[4,256,192]{2,1,0:T(8,128)(2,1)S(1)}, bf16[4,256,192]{2,1,0:T(8,128)(2,1)S(1)}) custom-call(bf16[256,768]{1,0:T(8,128)(2,1)S(1)} %bitcast.4, bf16[256,768]{1,0:T(8,128)(2,1)S(1)} %collective-permute-done.refs_1_, f32[768]{0:T(1024)S(1)} %copy-done.2, f32[768]{0:T(1024)S(1)} %copy-done.3), custom_call_target="tpu_custom_call" | custom-call | flops 8999999488 | bytes 27000000 | tf_op jit(solution)/shard_map/pallas_call | solution.py:360
  14.5 4.6 %collective-permute-done.3.refs_6_ = bf16[192,576]{1,0:T(8,128)(2,1)S(1)} collective-permute-done((bf16[192,576]{1,0:T(8,128)(2,1)S(1)}, bf16[192,576]{1,0:T(8,128)(2,1)S(1)}, u32[]{:S(2)}, u32[]{:S(2)}) %collective-permute-start.3) | collective-permute-done | bytes 221216 | tf_op jit(solution)/shard_map/ppermute | solution.py:324
  19.1 0.9 %shard_map.65 = (bf16[4,256,192]{2,1,0:T(8,128)(2,1)S(1)}, bf16[4,256,192]{2,1,0:T(8,128)(2,1)S(1)}) custom-call(bf16[256,768]{1,0:T(8,128)(2,1)S(1)} %collective-permute-done.1.refs_0_, bf16[256,768]{1,0:T(8,128)(2,1)S(1)} %collective-permute-done.2.refs_1_, f32[768]{0:T(1024)S(1)} %copy-done.2, f32[768]{0:T(1024)S(1)} %copy-done.3), custom_call_target="tpu_custom_call" | custom-call | flops 30000000 | bytes 90000 | tf_op jit(solution)/shard_map/pallas_call | solution.py:360
  20.0 3.2 %collective-permute-start.9 = (bf16[192,768]{1,0:T(8,128)(2,1)S(1)}, bf16[192,768]{1,0:T(8,128)(2,1)S(1)}, u32[]{:S(2)}, u32[]{:S(2)}) collective-permute-start(bf16[192,768]{1,0:T(8,128)(2,1)S(1)} %copy-done.1), channel_id=1, source_target_pairs={{0,2},{1,3},{2,0},{3,1},{4,7},{5,6},{6,5},{7,4},{8,10},{9,11},{10,... | collective-permute-start | bytes 884744 | tf_op jit(solution)/shard_map/ppermute | solution.py:324
  23.2 0.8 %collective-permute-start.8 = (bf16[192,768]{1,0:T(8,128)(2,1)S(1)}, bf16[192,768]{1,0:T(8,128)(2,1)S(1)}, u32[]{:S(2)}, u32[]{:S(2)}) collective-permute-start(bf16[192,768]{1,0:T(8,128)(2,1)S(1)} %copy-done.1), channel_id=1, source_target_pairs={{0,1},{1,0},{2,3},{3,2},{4,5},{5,4},{6,7},{7,6},{8,9},{9,8},{10,11... | collective-permute-start | bytes 884744 | tf_op jit(solution)/shard_map/ppermute | solution.py:48
  24.0 1.4 %shard_map.66 = (f32[256,576]{1,0:T(8,128)S(1)}, f32[256,576]{1,0:T(8,128)S(1)}, f32[256,576]{1,0:T(8,128)S(1)}, f32[256,576]{1,0:T(8,128)S(1)}) custom-call(bf16[4,256,192]{2,1,0:T(8,128)(2,1)S(1)} %get-tuple-element.30.refs_0_, bf16[4,256,192]{2,1,0:T(8,128)(2,1)S(1)} %get-tuple-element.31.refs_1_, bf16[4,256,192]{2,1,0:T(8,128)(2,1)S(1)} %get-tuple-element.32.refs_2_, ...), custom_call_target="tpu_custom_call" | custom-call | flops 3000000000 | bytes 9000000 | tf_op jit(solution)/shard_map/pallas_call | solution.py:372
  25.4 1.2 %collective-permute-done.4.refs_4_ = bf16[192,576]{1,0:T(8,128)(2,1)S(1)} collective-permute-done((bf16[192,576]{1,0:T(8,128)(2,1)S(1)}, bf16[192,576]{1,0:T(8,128)(2,1)S(1)}, u32[]{:S(2)}, u32[]{:S(2)}) %collective-permute-start.4) | collective-permute-done | bytes 221216 | tf_op jit(solution)/shard_map/ppermute | solution.py:48
  26.6 0.6 %shard_map.67 = (bf16[256,576]{1,0:T(8,128)(2,1)S(1)}, bf16[256,576]{1,0:T(8,128)(2,1)S(1)}, bf16[256,576]{1,0:T(8,128)(2,1)S(1)}, bf16[256,576]{1,0:T(8,128)(2,1)S(1)}, bf16[3,64,128]{2,1,0:T(8,128)(2,1)S(1)}) custom-call(bf16[4,256,192]{2,1,0:T(8,128)(2,1)S(1)} %get-tuple-element.30.refs_0_, bf16[4,256,192]{2,1,0:T(8,128)(2,1)S(1)} %get-tuple-element.31.refs_1_, ...), custom_call_target="tpu_custom_call" | custom-call | flops 3000000000 | bytes 9000000 | tf_op jit(solution)/shard_map/pallas_call | solution.py:378
  27.2 0.9 %collective-permute-start.6 = (bf16[3,64,128]{2,1,0:T(8,128)(2,1)S(1)}, bf16[3,64,128]{2,1,0:T(8,128)(2,1)S(1)}, u32[]{:S(2)}, u32[]{:S(2)}) collective-permute-start(bf16[3,64,128]{2,1,0:T(8,128)(2,1)S(1)} %get-tuple-element.48.refs_5_), channel_id=1, source_target_pairs={{0,16},{4,20},{8,24},{12,28},{16,0},{20,4},{24,8},{28,12},{1,17},{... | collective-permute-start | bytes 147464 | tf_op jit(solution)/shard_map/ppermute | solution.py:48
  28.1 1.7 %shard_map.68 = (f32[3,4,1,256]{3,2,1,0:T(1,128)S(1)}, f32[3,4,1,256]{3,2,1,0:T(1,128)S(1)}, f32[3,4,64,256]{3,2,1,0:T(8,128)S(1)}) custom-call(s32[1]{0:T(128)S(6)} %copy.7.valid_ref.refs_0_, bf16[256,576]{1,0:T(8,128)(2,1)S(1)} %get-tuple-element.39.refs_0_.refs_1_, bf16[256,576]{1,0:T(8,128)(2,1)S(1)} %get-tuple-element.40.refs_1_.refs_2_, ...), custom_call_target="tpu_custom_call" | custom-call | flops 60000002048 | bytes 180000000 | tf_op jit(solution)/shard_map/pallas_call | solution.py:386
  29.8 1.5 %collective-permute-done.6.refs_6_ = bf16[3,64,128]{2,1,0:T(8,128)(2,1)S(1)} collective-permute-done((bf16[3,64,128]{2,1,0:T(8,128)(2,1)S(1)}, bf16[3,64,128]{2,1,0:T(8,128)(2,1)S(1)}, u32[]{:S(2)}, u32[]{:S(2)}) %collective-permute-start.6) | collective-permute-done | bytes 49184 | tf_op jit(solution)/shard_map/ppermute | solution.py:48
  31.3 0.5 %shard_map.69 = bf16[2,192,256]{2,1,0:T(8,128)(2,1)S(1)} custom-call(s32[1]{0:T(128)S(6)} %copy.7.valid_ref.refs_0_, bf16[256,576]{1,0:T(8,128)(2,1)S(1)} %get-tuple-element.39.refs_0_.refs_1_, bf16[256,576]{1,0:T(8,128)(2,1)S(1)} %get-tuple-element.40.refs_1_.refs_2_, bf16[256,576]{1,0:T(8,128)(2,1)S(1)} %get-tuple-element.41.refs_2_.refs_3_, ...), custom_call_target="tpu_custom_call" | custom-call | flops 3000000000 | bytes 9000000 | tf_op jit(solution)/shard_map/pallas_call | solution.py:401
  31.9 0.7 %collective-permute-start.7 = (bf16[2,192,256]{2,1,0:T(8,128)(2,1)S(1)}, bf16[2,192,256]{2,1,0:T(8,128)(2,1)S(1)}, u32[]{:S(2)}, u32[]{:S(2)}) collective-permute-start(bf16[2,192,256]{2,1,0:T(8,128)(2,1)S(1)} %shard_map.69), channel_id=1, source_target_pairs={{0,8},{4,12},{8,0},{12,4},{16,24},{20,28},{24,16},{28,20},{1,9},{5... | collective-permute-start | bytes 589832 | tf_op jit(solution)/shard_map/ppermute | solution.py:48
  32.6 3.8 %collective-permute-done.9.refs_2_ = bf16[192,768]{1,0:T(8,128)(2,1)S(1)} collective-permute-done((bf16[192,768]{1,0:T(8,128)(2,1)S(1)}, bf16[192,768]{1,0:T(8,128)(2,1)S(1)}, u32[]{:S(2)}, u32[]{:S(2)}) %collective-permute-start.9) | collective-permute-done | bytes 294944 | tf_op jit(solution)/shard_map/ppermute | solution.py:324
  36.4 0.8 %collective-permute-done.8.refs_1_ = bf16[192,768]{1,0:T(8,128)(2,1)S(1)} collective-permute-done((bf16[192,768]{1,0:T(8,128)(2,1)S(1)}, bf16[192,768]{1,0:T(8,128)(2,1)S(1)}, u32[]{:S(2)}, u32[]{:S(2)}) %collective-permute-start.8) | collective-permute-done | bytes 294944 | tf_op jit(solution)/shard_map/ppermute | solution.py:48
  37.1 0.5 %shard_map.70.refs_0_ = bf16[2,192,256]{2,1,0:T(8,128)(2,1)S(1)} custom-call(s32[1]{0:T(128)S(6)} %copy.7.valid_ref.refs_0_, bf16[256,576]{1,0:T(8,128)(2,1)S(1)} %get-tuple-element.39.refs_0_.refs_1_, bf16[256,576]{1,0:T(8,128)(2,1)S(1)} %get-tuple-element.40.refs_1_.refs_2_, bf16[256,576]{1,0:T(8,128)(2,1)S(1)} %get-tuple-element.41.refs_2_.refs_3_, ...), custom_call_target="tpu_custom_call" | custom-call | flops 15000000512 | bytes 45000000 | tf_op jit(solution)/shard_map/pallas_call | solution.py:401
  37.7 0.1 collective-permute-start.10
  37.7 0.5 %collective-permute-start.12 = (bf16[192,768]{1,0:T(8,128)(2,1)S(1)}, bf16[192,768]{1,0:T(8,128)(2,1)S(1)}, u32[]{:S(2)}, u32[]{:S(2)}) collective-permute-start(bf16[192,768]{1,0:T(8,128)(2,1)S(1)} %collective-permute-done.9.refs_2_), channel_id=1, source_target_pairs={{0,4},{4,0},{8,12},{12,8},{16,20},{20,16},{24,28},{28,24},{1,5},{5... | collective-permute-start | bytes 884744 | tf_op jit(solution)/shard_map/ppermute | solution.py:48
  38.2 0.9 %collective-permute-done.10.refs_1_ = bf16[2,192,256]{2,1,0:T(8,128)(2,1)S(1)} collective-permute-done((bf16[2,192,256]{2,1,0:T(8,128)(2,1)S(1)}, bf16[2,192,256]{2,1,0:T(8,128)(2,1)S(1)}, u32[]{:S(2)}, u32[]{:S(2)}) %collective-permute-start.10) | collective-permute-done | bytes 196640 | tf_op jit(solution)/shard_map/ppermute | solution.py:48
  39.2 0.1 collective-permute-start.11
  39.3 0.3 collective-permute-done.12.refs_3_
  39.6 0.1 shard_map.71
  39.7 0.7 %shard_map.72.refs_3_ = f32[256,768]{1,0:T(8,128)S(1)} custom-call(bf16[2,192,256]{2,1,0:T(8,128)(2,1)S(1)} %shard_map.70.refs_0_, bf16[2,192,256]{2,1,0:T(8,128)(2,1)S(1)} %collective-permute-done.10.refs_1_, bf16[768,768]{1,0:T(8,128)(2,1)S(1)} %get-tuple-element.51.refs_2_.refs_1_, bf16[256,256]{1,0:T(8,128)(2,1)S(1)} %get-tuple-element.52.refs_3_.refs_2_, ...), custom_call_target="tpu_custom_call" | custom-call | flops 3000000 | bytes 9000 | tf_op jit(solution)/shard_map/pallas_call | solution.py:428
  40.4 0.5 %shard_map.73.refs_3_ = f32[256,768]{1,0:T(8,128)S(1)} custom-call(bf16[2,192,256]{2,1,0:T(8,128)(2,1)S(1)} %collective-permute-done.7.refs_0_, bf16[768,768]{1,0:T(8,128)(2,1)S(1)} %get-tuple-element.51.refs_2_.refs_1_, bf16[256,256]{1,0:T(8,128)(2,1)S(1)} %get-tuple-element.52.refs_3_.refs_2_, f32[256,768]{1,0:T(8,128)S(1)} %shard_map.72.refs_3_), custom_call_target="tpu_custom_call" | custom-call | flops 3000000 | bytes 9000 | tf_op jit(solution)/shard_map/pallas_call | solution.py:428
  40.9 1.2 %shard_map.74 = bf16[256,768]{1,0:T(8,128)(2,1)} custom-call(bf16[2,192,256]{2,1,0:T(8,128)(2,1)S(1)} %collective-permute-done.11.refs_0_, bf16[768,768]{1,0:T(8,128)(2,1)S(1)} %get-tuple-element.51.refs_2_.refs_1_, bf16[256,256]{1,0:T(8,128)(2,1)S(1)} %get-tuple-element.52.refs_3_.refs_2_, f32[256,768]{1,0:T(8,128)S(1)} %shard_map.73.refs_3_), custom_call_target="tpu_custom_call" | custom-call | flops 3000000 | bytes 9000 | tf_op jit(solution)/shard_map/pallas_call | solution.py:428
  (15 shorter events, 0.0 us)
Async XLA Ops:
  0.0 1.4 %copy-start = (bf16[1,256,768]{2,1,0:T(8,128)(2,1)S(1)}, bf16[1,256,768]{2,1,0:T(8,128)(2,1)}, u32[]{:S(2)}) copy-start(bf16[1,256,768]{2,1,0:T(8,128)(2,1)} %param.6) | copy-start | bytes 1179652
  0.0 13.5 %copy-start.2 = (f32[768]{0:T(1024)S(1)}, f32[768]{0:T(1024)}, u32[]{:S(2)}) copy-start(f32[768]{0:T(1024)} %refs_2_.3) | copy-start | bytes 9220
  0.0 13.5 %copy-start.3 = (f32[768]{0:T(1024)S(1)}, f32[768]{0:T(1024)}, u32[]{:S(2)}) copy-start(f32[768]{0:T(1024)} %refs_3_.3) | copy-start | bytes 9220
  1.4 12.1 %collective-permute-start.1 = (bf16[256,768]{1,0:T(8,128)(2,1)S(1)}, bf16[256,768]{1,0:T(8,128)(2,1)S(1)}, u32[]{:S(2)}, u32[]{:S(2)}) collective-permute-start(bf16[256,768]{1,0:T(8,128)(2,1)S(1)} %bitcast.2), channel_id=1, source_target_pairs={{0,8},{4,12},{8,0},{12,4},{16,24},{20,28},{24,16},{28,20},{1,9},{5... | collective-permute-start | bytes 1179656 | tf_op jit(solution)/shard_map/ppermute | solution.py:48
  4.4 9.1 %collective-permute-start = (bf16[256,768]{1,0:T(8,128)(2,1)S(1)}, bf16[256,768]{1,0:T(8,128)(2,1)S(1)}, u32[]{:S(2)}, u32[]{:S(2)}) collective-permute-start(bf16[256,768]{1,0:T(8,128)(2,1)S(1)} %bitcast.3), channel_id=1, source_target_pairs={{0,4},{4,0},{8,12},{12,8},{16,20},{20,16},{24,28},{28,24},{1,5},{5... | collective-permute-start | bytes 1179656 | tf_op jit(solution)/shard_map/ppermute | solution.py:48
  4.4 14.6 %collective-permute-start.3 = (bf16[192,576]{1,0:T(8,128)(2,1)S(1)}, bf16[192,576]{1,0:T(8,128)(2,1)S(1)}, u32[]{:S(2)}, u32[]{:S(2)}) collective-permute-start(bf16[192,576]{1,0:T(8,128)(2,1)S(1)} %pad_maximum_fusion.refs_4_), channel_id=1, source_target_pairs={{0,2},{1,3},{2,0},{3,1},{4,6},{5,7},{6,4},{7,5},{8,10},{9,11},{10,... | collective-permute-start | bytes 663560 | tf_op jit(solution)/shard_map/ppermute | solution.py:324
  7.0 17.0 %collective-permute-start.5 = (bf16[192,576]{1,0:T(8,128)(2,1)S(1)}, bf16[192,576]{1,0:T(8,128)(2,1)S(1)}, u32[]{:S(2)}, u32[]{:S(2)}) collective-permute-start(bf16[192,576]{1,0:T(8,128)(2,1)S(1)} %pad_maximum_fusion.refs_4_), channel_id=1, source_target_pairs={{0,1},{1,0},{2,3},{3,2},{4,5},{5,4},{6,7},{7,6},{8,9},{9,8},{10,11... | collective-permute-start | bytes 663560 | tf_op jit(solution)/shard_map/ppermute | solution.py:48
  9.2 10.8 %copy-start.1 = (bf16[192,768]{1,0:T(8,128)(2,1)S(1)}, bf16[192,768]{1,0:T(8,128)(2,1)}, u32[]{:S(2)}) copy-start(bf16[192,768]{1,0:T(8,128)(2,1)} %refs_0_.2) | copy-start | bytes 884740
  13.5 5.6 %collective-permute-start.2 = (bf16[256,768]{1,0:T(8,128)(2,1)S(1)}, bf16[256,768]{1,0:T(8,128)(2,1)S(1)}, u32[]{:S(2)}, u32[]{:S(2)}) collective-permute-start(bf16[256,768]{1,0:T(8,128)(2,1)S(1)} %collective-permute-done.1.refs_0_), channel_id=1, source_target_pairs={{0,4},{4,0},{8,12},{12,8},{16,20},{20,16},{24,28},{28,24},{1,5},{5... | collective-permute-start | bytes 1179656 | tf_op jit(solution)/shard_map/ppermute | solution.py:48
  19.1 7.5 %collective-permute-start.4 = (bf16[192,576]{1,0:T(8,128)(2,1)S(1)}, bf16[192,576]{1,0:T(8,128)(2,1)S(1)}, u32[]{:S(2)}, u32[]{:S(2)}) collective-permute-start(bf16[192,576]{1,0:T(8,128)(2,1)S(1)} %collective-permute-done.3.refs_6_), channel_id=1, source_target_pairs={{0,16},{4,20},{8,24},{12,28},{16,0},{20,4},{24,8},{28,12},{1,17},{... | collective-permute-start | bytes 663560 | tf_op jit(solution)/shard_map/ppermute | solution.py:48
  20.0 16.3 %collective-permute-start.9 = (bf16[192,768]{1,0:T(8,128)(2,1)S(1)}, bf16[192,768]{1,0:T(8,128)(2,1)S(1)}, u32[]{:S(2)}, u32[]{:S(2)}) collective-permute-start(bf16[192,768]{1,0:T(8,128)(2,1)S(1)} %copy-done.1), channel_id=1, source_target_pairs={{0,2},{1,3},{2,0},{3,1},{4,7},{5,6},{6,5},{7,4},{8,10},{9,11},{10,... | collective-permute-start | bytes 884744 | tf_op jit(solution)/shard_map/ppermute | solution.py:324
  23.2 13.9 %collective-permute-start.8 = (bf16[192,768]{1,0:T(8,128)(2,1)S(1)}, bf16[192,768]{1,0:T(8,128)(2,1)S(1)}, u32[]{:S(2)}, u32[]{:S(2)}) collective-permute-start(bf16[192,768]{1,0:T(8,128)(2,1)S(1)} %copy-done.1), channel_id=1, source_target_pairs={{0,1},{1,0},{2,3},{3,2},{4,5},{5,4},{6,7},{7,6},{8,9},{9,8},{10,11... | collective-permute-start | bytes 884744 | tf_op jit(solution)/shard_map/ppermute | solution.py:48
  27.2 4.1 %collective-permute-start.6 = (bf16[3,64,128]{2,1,0:T(8,128)(2,1)S(1)}, bf16[3,64,128]{2,1,0:T(8,128)(2,1)S(1)}, u32[]{:S(2)}, u32[]{:S(2)}) collective-permute-start(bf16[3,64,128]{2,1,0:T(8,128)(2,1)S(1)} %get-tuple-element.48.refs_5_), channel_id=1, source_target_pairs={{0,16},{4,20},{8,24},{12,28},{16,0},{20,4},{24,8},{28,12},{1,17},{... | collective-permute-start | bytes 147464 | tf_op jit(solution)/shard_map/ppermute | solution.py:48
  31.9 6.4 %collective-permute-start.7 = (bf16[2,192,256]{2,1,0:T(8,128)(2,1)S(1)}, bf16[2,192,256]{2,1,0:T(8,128)(2,1)S(1)}, u32[]{:S(2)}, u32[]{:S(2)}) collective-permute-start(bf16[2,192,256]{2,1,0:T(8,128)(2,1)S(1)} %shard_map.69), channel_id=1, source_target_pairs={{0,8},{4,12},{8,0},{12,4},{16,24},{20,28},{24,16},{28,20},{1,9},{5... | collective-permute-start | bytes 589832 | tf_op jit(solution)/shard_map/ppermute | solution.py:48
  37.7 1.5 %collective-permute-start.10 = (bf16[2,192,256]{2,1,0:T(8,128)(2,1)S(1)}, bf16[2,192,256]{2,1,0:T(8,128)(2,1)S(1)}, u32[]{:S(2)}, u32[]{:S(2)}) collective-permute-start(bf16[2,192,256]{2,1,0:T(8,128)(2,1)S(1)} %shard_map.70.refs_0_), channel_id=1, source_target_pairs={{0,4},{4,0},{8,12},{12,8},{16,20},{20,16},{24,28},{28,24},{1,5},{5... | collective-permute-start | bytes 589832 | tf_op jit(solution)/shard_map/ppermute | solution.py:48
  37.7 1.9 %collective-permute-start.12 = (bf16[192,768]{1,0:T(8,128)(2,1)S(1)}, bf16[192,768]{1,0:T(8,128)(2,1)S(1)}, u32[]{:S(2)}, u32[]{:S(2)}) collective-permute-start(bf16[192,768]{1,0:T(8,128)(2,1)S(1)} %collective-permute-done.9.refs_2_), channel_id=1, source_target_pairs={{0,4},{4,0},{8,12},{12,8},{16,20},{20,16},{24,28},{28,24},{1,5},{5... | collective-permute-start | bytes 884744 | tf_op jit(solution)/shard_map/ppermute | solution.py:48
  39.2 1.7 %collective-permute-start.11 = (bf16[2,192,256]{2,1,0:T(8,128)(2,1)S(1)}, bf16[2,192,256]{2,1,0:T(8,128)(2,1)S(1)}, u32[]{:S(2)}, u32[]{:S(2)}) collective-permute-start(bf16[2,192,256]{2,1,0:T(8,128)(2,1)S(1)} %collective-permute-done.7.refs_0_), channel_id=1, source_target_pairs={{0,4},{4,0},{8,12},{12,8},{16,20},{20,16},{24,28},{28,24},{1,5},{5... | collective-permute-start | bytes 589832 | tf_op jit(solution)/shard_map/ppermute | solution.py:48

commit v9 on v8

--- a/solution.py
+++ b/solution.py
@@ -299,7 +299,17 @@
 def gather_body(n_mp, shared, *refs):
     *part_refs, out_ref, order_ref = refs
     order_ref[...] = to_position(order_ref.shape[0])
-    assemble(out_ref, part_refs, sources(n_mp, lax.axis_index("ctx") % 2, shared))
+    member, group = group_indices()
+    origin = sources(n_mp, group % 2, shared)
+    rows = part_refs[0].shape[0]
+    starts = [source * rows for source in origin]
+    if shared:
+        core, half = member % 2, rows // 2
+        starts = starts[:1] + [
+            start + side * half for side in (core, 1 - core) for start in starts[1:]
+        ]
+    for ref, start in zip(part_refs, starts):
+        out_ref[pl.ds(pl.multiple_of(start, 16), ref.shape[0]), :] = ref[...]
 
 
 def update_body(blocks, *refs):
@@ -340,7 +350,7 @@
     member, _ = group_indices()
     bf16, f32 = jnp.bfloat16, jnp.float32
     shape = pltpu.VMEM
-    shared = n_mp == 4 and n_groups % 2 == 0
+    shared = n_mp == 4 and n_groups % 2 == 0 and weight_rows % 32 == 0
 
     def columns(part):
         start = part * width + member * GROUP_WIDTH
@@ -365,8 +375,13 @@
     weights = [mine] + exchange(fetched, shared, SHARDS, normed[0])
     normed += normalized(x_far, x_last, 0.01)
 
-    out_weight = after(near(w_out), normed[2])
-    out_fetched = fetch(out_weight, lambda c: c % 2, shared)
+    out_own = near(w_out)
+    out_weight = w_out
+    if shared:
+        size = weight_rows // 2
+        out_weight = lax.dynamic_slice(w_out, (member % 2 * size, 0), (size, width))
+    out_weight = after(near(out_weight), normed[2])
+    out_fetched = fetch(out_weight, lambda c: c // SHARDS % 2, shared)
 
     early = range(n_mp - 1)
     partial = call(
@@ -392,7 +407,7 @@
         ],
         n_scalar=1,
         n_in=SHARDS,
-        micros=20,
+        micros=1,
     )(valid_count, *qkv)
 
     half = SHARDS // 2
@@ -407,18 +422,22 @@
         )(valid_count, *qkv, *sent_parts, *stats)[0]
 
     sending = finished(range(half, SHARDS), sents, 1)
-    staying = finished(range(half), [after(sents[0], sending, *out_fetched)] + sents[1:], 5)
+    last_fetched = out_fetched[-1]
+    staying = finished(range(half), [after(sents[0], sending, last_fetched)] + sents[1:], 0.01)
     far_part = flip(sending, "ctx", 2)
     pair_part = flip(staying, "ctx", 1)
-    out_parts = [out_weight] + exchange(out_fetched, shared, 1, sending)
+    out_blocks = exchange(out_fetched, shared, SHARDS, stats[0])
+    out_parts = [out_own] + out_blocks
+    if shared:
+        out_parts += [flip(after(value, sending), "ctx", 1) for value in out_blocks]
     whole_out, order = call(
         lambda *refs: gather_body(n_mp, shared, *refs),
         [shape((width, width), bf16), shape((rows, rows), bf16)],
-        n_in=n_mp,
+        n_in=len(out_parts),
         micros=0.001,
     )(*out_parts)
     total = x_own
-    last_part = flip(after(far_part, pair_part), "ctx", 1)
+    last_part = flip(after(far_part, pair_part, whole_out), "ctx", 1)
     steps = [
         ([(0, 0), (1, 1)], [staying, pair_part], shape((rows, width), f32)),
         ([(2, 0)], [far_part], shape((rows, width), f32)),

time: 42.2 us -> 40.6 us (0.962)
  waiting for transfers between devices: 17.3 us -> 14.9 us
  starting transfers between devices: 13.5 us -> 14.2 us
    ppermute x2, waiting for transfers between devices: 8.34 us -> 5.26 us  [fetch(): lax.ppermute(value, ('ctx', 'mp'), pairs)]
    ppermute x11 -> x14, waiting for transfers between devices: 8.97 us -> 9.68 us  [flip(): return near(lax.ppermute(value, axis, pairs))]
    ppermute x11 -> x14, starting transfers between devices: 7.77 us -> 8.46 us  [flip(): return near(lax.ppermute(value, axis, pairs))]
  transfers between devices with their start and end apart: 13 -> 16, of which waited for: 8 -> 11; matrix products, arithmetic and copies ran while one was open for 0% -> 0% of each run, Pallas kernels for 19% -> 20%
where the time goes in v9:
time: 40.6 us; the launch traced here: 40.4 us
  waiting for transfers between devices  14.9 us (37%)
  starting transfers between devices  14.2 us (35%)
  Pallas kernels  9.09 us (22%)
  local copies, waits for them, and re-layouts  1.31 us (3%)
  between operations  0.79 us (2%)
    ppermute x14, waiting for transfers between devices, flip(): return near(lax.ppermute(value, axis, pairs))  9.68 us
    ppermute x14, starting transfers between devices, flip(): return near(lax.ppermute(value, axis, pairs))  8.46 us
    ppermute x2, starting transfers between devices, fetch(): lax.ppermute(value, ('ctx', 'mp'), pairs)  5.75 us
    ppermute x2, waiting for transfers between devices, fetch(): lax.ppermute(value, ('ctx', 'mp'), pairs)  5.26 us
    pallas_call x3, Pallas kernels, local(): call(lambda *refs, blocks=blocks: update_body(blocks, *refs), [out_shape]...  2.36 us
    pallas_call x2, Pallas kernels, normalized(): call(norm_body, [blocks] * 2, n_in=4, micros=micros)(one, two, gain, bias)  1.87 us
    pallas_call x1, Pallas kernels, local(): call(near_body, [shape((GROUP_HEADS, SHARDS, 1, rows), f32), shape((GROUP...  1.7 us
    pallas_call x1, Pallas kernels, local(): call(lambda *refs: project_body((n_mp, shared, early), *refs), [shape((ro...  1.36 us
  transfers between devices with their start and end apart: 16, of which 11 were waited for; matrix products, arithmetic and copies ran while one was open for 0% of the time, Pallas kernels for 20%

profile of v9, /device:TPU:0, one launch (start us, length us, event | category | flops | bytes accessed | tf_op | source)
XLA Modules:
  0.0 40.4 jit_solution(10231079247791560006)
XLA Ops:
  0.0 1.3 %constant_dynamic-slice_fusion.3 = (bf16[192,192]{1,0:T(8,128)(2,1)S(1)}, bf16[192,192]{1,0:T(8,128)(2,1)S(1)}, bf16[192,192]{1,0:T(8,128)(2,1)S(1)}) fusion(bf16[192,2304]{1,0:T(8,128)(2,1)} %param.9, s32[]{:T(128)S(6)} %select_n.24, s32[]{:T(128)S(6)} %select_n.26, s32[]{:T(128)S(6)} %select_n.25), kind=kLoop, calls=%fused_computation.4 | loop fusion | bytes 442380 | tf_op jit(solution)/shard_map/dynamic_slice | solution.py:357
  1.4 3.0 %collective-permute-start.1 = (bf16[256,768]{1,0:T(8,128)(2,1)S(1)}, bf16[256,768]{1,0:T(8,128)(2,1)S(1)}, u32[]{:S(2)}, u32[]{:S(2)}) collective-permute-start(bf16[256,768]{1,0:T(8,128)(2,1)S(1)} %bitcast.2), channel_id=1, source_target_pairs={{0,8},{4,12},{8,0},{12,4},{16,24},{20,28},{24,16},{28,20},{1,9},{5... | collective-permute-start | bytes 1179656 | tf_op jit(solution)/shard_map/ppermute | solution.py:48
  4.5 2.6 %collective-permute-start.3 = (bf16[192,576]{1,0:T(8,128)(2,1)S(1)}, bf16[192,576]{1,0:T(8,128)(2,1)S(1)}, u32[]{:S(2)}, u32[]{:S(2)}) collective-permute-start(bf16[192,576]{1,0:T(8,128)(2,1)S(1)} %pad_maximum_fusion.refs_4_), channel_id=1, source_target_pairs={{0,2},{1,3},{2,0},{3,1},{4,6},{5,7},{6,4},{7,5},{8,10},{9,11},{10,... | collective-permute-start | bytes 663560 | tf_op jit(solution)/shard_map/ppermute | solution.py:334
  7.0 1.6 %collective-permute-start.5 = (bf16[192,576]{1,0:T(8,128)(2,1)S(1)}, bf16[192,576]{1,0:T(8,128)(2,1)S(1)}, u32[]{:S(2)}, u32[]{:S(2)}) collective-permute-start(bf16[192,576]{1,0:T(8,128)(2,1)S(1)} %pad_maximum_fusion.refs_4_), channel_id=1, source_target_pairs={{0,1},{1,0},{2,3},{3,2},{4,5},{5,4},{6,7},{7,6},{8,9},{9,8},{10,11... | collective-permute-start | bytes 663560 | tf_op jit(solution)/shard_map/ppermute | solution.py:48
  9.3 4.2 %collective-permute-done.1.refs_0_ = bf16[256,768]{1,0:T(8,128)(2,1)S(1)} collective-permute-done((bf16[256,768]{1,0:T(8,128)(2,1)S(1)}, bf16[256,768]{1,0:T(8,128)(2,1)S(1)}, u32[]{:S(2)}, u32[]{:S(2)}) %collective-permute-start.1) | collective-permute-done | bytes 393248 | tf_op jit(solution)/shard_map/ppermute | solution.py:48
  13.6 0.9 %shard_map.64 = (bf16[4,256,192]{2,1,0:T(8,128)(2,1)S(1)}, bf16[4,256,192]{2,1,0:T(8,128)(2,1)S(1)}) custom-call(bf16[256,768]{1,0:T(8,128)(2,1)S(1)} %bitcast.4, bf16[256,768]{1,0:T(8,128)(2,1)S(1)} %collective-permute-done.refs_1_, f32[768]{0:T(1024)S(1)} %copy-done.2, f32[768]{0:T(1024)S(1)} %copy-done.3), custom_call_target="tpu_custom_call" | custom-call | flops 8999999488 | bytes 27000000 | tf_op jit(solution)/shard_map/pallas_call | solution.py:370
  14.5 4.6 %collective-permute-done.3.refs_6_ = bf16[192,576]{1,0:T(8,128)(2,1)S(1)} collective-permute-done((bf16[192,576]{1,0:T(8,128)(2,1)S(1)}, bf16[192,576]{1,0:T(8,128)(2,1)S(1)}, u32[]{:S(2)}, u32[]{:S(2)}) %collective-permute-start.3) | collective-permute-done | bytes 221216 | tf_op jit(solution)/shard_map/ppermute | solution.py:334
  19.1 0.9 %shard_map.65 = (bf16[4,256,192]{2,1,0:T(8,128)(2,1)S(1)}, bf16[4,256,192]{2,1,0:T(8,128)(2,1)S(1)}) custom-call(bf16[256,768]{1,0:T(8,128)(2,1)S(1)} %collective-permute-done.1.refs_0_, bf16[256,768]{1,0:T(8,128)(2,1)S(1)} %collective-permute-done.2.refs_1_, f32[768]{0:T(1024)S(1)} %copy-done.2, f32[768]{0:T(1024)S(1)} %copy-done.3), custom_call_target="tpu_custom_call" | custom-call | flops 30000000 | bytes 90000 | tf_op jit(solution)/shard_map/pallas_call | solution.py:370
  20.0 3.2 %collective-permute-start.8 = (bf16[96,768]{1,0:T(8,128)(2,1)S(1)}, bf16[96,768]{1,0:T(8,128)(2,1)S(1)}, u32[]{:S(2)}, u32[]{:S(2)}) collective-permute-start(bf16[96,768]{1,0:T(8,128)(2,1)S(1)} %constant_dynamic-slice_fusion), channel_id=1, source_target_pairs={{0,2},{1,3},{2,0},{3,1},{4,6},{5,7},{6,4},{7,5},{8,10},{9,11},{10,... | collective-permute-start | bytes 442376 | tf_op jit(solution)/shard_map/ppermute | solution.py:334
  23.2 0.8 %collective-permute-start.10 = (bf16[96,768]{1,0:T(8,128)(2,1)S(1)}, bf16[96,768]{1,0:T(8,128)(2,1)S(1)}, u32[]{:S(2)}, u32[]{:S(2)}) collective-permute-start(bf16[96,768]{1,0:T(8,128)(2,1)S(1)} %constant_dynamic-slice_fusion), channel_id=1, source_target_pairs={{0,1},{1,0},{2,3},{3,2},{4,5},{5,4},{6,7},{7,6},{8,9},{9,8},{10,11... | collective-permute-start | bytes 442376 | tf_op jit(solution)/shard_map/ppermute | solution.py:48
  24.1 1.4 %shard_map.66 = (f32[256,576]{1,0:T(8,128)S(1)}, f32[256,576]{1,0:T(8,128)S(1)}, f32[256,576]{1,0:T(8,128)S(1)}, f32[256,576]{1,0:T(8,128)S(1)}) custom-call(bf16[4,256,192]{2,1,0:T(8,128)(2,1)S(1)} %get-tuple-element.33.refs_0_, bf16[4,256,192]{2,1,0:T(8,128)(2,1)S(1)} %get-tuple-element.34.refs_1_, bf16[4,256,192]{2,1,0:T(8,128)(2,1)S(1)} %get-tuple-element.35.refs_2_, ...), custom_call_target="tpu_custom_call" | custom-call | flops 3000000000 | bytes 9000000 | tf_op jit(solution)/shard_map/pallas_call | solution.py:387
  25.4 1.2 %collective-permute-done.4.refs_4_ = bf16[192,576]{1,0:T(8,128)(2,1)S(1)} collective-permute-done((bf16[192,576]{1,0:T(8,128)(2,1)S(1)}, bf16[192,576]{1,0:T(8,128)(2,1)S(1)}, u32[]{:S(2)}, u32[]{:S(2)}) %collective-permute-start.4) | collective-permute-done | bytes 221216 | tf_op jit(solution)/shard_map/ppermute | solution.py:48
  26.6 0.6 %shard_map.67 = (bf16[256,576]{1,0:T(8,128)(2,1)S(1)}, bf16[256,576]{1,0:T(8,128)(2,1)S(1)}, bf16[256,576]{1,0:T(8,128)(2,1)S(1)}, bf16[256,576]{1,0:T(8,128)(2,1)S(1)}, bf16[3,64,128]{2,1,0:T(8,128)(2,1)S(1)}) custom-call(bf16[4,256,192]{2,1,0:T(8,128)(2,1)S(1)} %get-tuple-element.33.refs_0_, bf16[4,256,192]{2,1,0:T(8,128)(2,1)S(1)} %get-tuple-element.34.refs_1_, ...), custom_call_target="tpu_custom_call" | custom-call | flops 3000000000 | bytes 9000000 | tf_op jit(solution)/shard_map/pallas_call | solution.py:393
  27.3 0.3 collective-permute-start.6
  27.5 1.7 %shard_map.68 = (f32[3,4,1,256]{3,2,1,0:T(1,128)S(1)}, f32[3,4,1,256]{3,2,1,0:T(1,128)S(1)}, f32[3,4,64,256]{3,2,1,0:T(8,128)S(1)}) custom-call(s32[1]{0:T(128)S(6)} %copy.7.valid_ref.refs_0_, bf16[256,576]{1,0:T(8,128)(2,1)S(1)} %get-tuple-element.42.refs_0_.refs_1_, bf16[256,576]{1,0:T(8,128)(2,1)S(1)} %get-tuple-element.43.refs_1_.refs_2_, ...), custom_call_target="tpu_custom_call" | custom-call | flops 3000000000 | bytes 9000000 | tf_op jit(solution)/shard_map/pallas_call | solution.py:401
  29.3 0.7 %collective-permute-done.8.refs_2_ = bf16[96,768]{1,0:T(8,128)(2,1)S(1)} collective-permute-done((bf16[96,768]{1,0:T(8,128)(2,1)S(1)}, bf16[96,768]{1,0:T(8,128)(2,1)S(1)}, u32[]{:S(2)}, u32[]{:S(2)}) %collective-permute-start.8) | collective-permute-done | bytes 147488 | tf_op jit(solution)/shard_map/ppermute | solution.py:334
  29.9 1.1 %collective-permute-start.11 = (bf16[96,768]{1,0:T(8,128)(2,1)S(1)}, bf16[96,768]{1,0:T(8,128)(2,1)S(1)}, u32[]{:S(2)}, u32[]{:S(2)}) collective-permute-start(bf16[96,768]{1,0:T(8,128)(2,1)S(1)} %collective-permute-done.8.refs_2_), channel_id=1, source_target_pairs={{0,16},{4,20},{8,24},{12,28},{16,0},{20,4},{24,8},{28,12},{1,17},{... | collective-permute-start | bytes 442376 | tf_op jit(solution)/shard_map/ppermute | solution.py:48
  31.1 0.5 %collective-permute-done.6.refs_6_ = bf16[3,64,128]{2,1,0:T(8,128)(2,1)S(1)} collective-permute-done((bf16[3,64,128]{2,1,0:T(8,128)(2,1)S(1)}, bf16[3,64,128]{2,1,0:T(8,128)(2,1)S(1)}, u32[]{:S(2)}, u32[]{:S(2)}) %collective-permute-start.6) | collective-permute-done | bytes 49184 | tf_op jit(solution)/shard_map/ppermute | solution.py:48
  31.5 0.5 %shard_map.69 = bf16[2,192,256]{2,1,0:T(8,128)(2,1)S(1)} custom-call(s32[1]{0:T(128)S(6)} %copy.7.valid_ref.refs_0_, bf16[256,576]{1,0:T(8,128)(2,1)S(1)} %get-tuple-element.42.refs_0_.refs_1_, bf16[256,576]{1,0:T(8,128)(2,1)S(1)} %get-tuple-element.43.refs_1_.refs_2_, bf16[256,576]{1,0:T(8,128)(2,1)S(1)} %get-tuple-element.44.refs_2_.refs_3_, ...), custom_call_target="tpu_custom_call" | custom-call | flops 3000000000 | bytes 9000000 | tf_op jit(solution)/shard_map/pallas_call | solution.py:416
  32.1 0.9 %collective-permute-start.7 = (bf16[2,192,256]{2,1,0:T(8,128)(2,1)S(1)}, bf16[2,192,256]{2,1,0:T(8,128)(2,1)S(1)}, u32[]{:S(2)}, u32[]{:S(2)}) collective-permute-start(bf16[2,192,256]{2,1,0:T(8,128)(2,1)S(1)} %shard_map.69), channel_id=1, source_target_pairs={{0,8},{4,12},{8,0},{12,4},{16,24},{20,28},{24,16},{28,20},{1,9},{5... | collective-permute-start | bytes 589832 | tf_op jit(solution)/shard_map/ppermute | solution.py:48
  33.0 0.5 %shard_map.70.refs_0_ = bf16[2,192,256]{2,1,0:T(8,128)(2,1)S(1)} custom-call(s32[1]{0:T(128)S(6)} %copy.7.valid_ref.refs_0_, bf16[256,576]{1,0:T(8,128)(2,1)S(1)} %get-tuple-element.42.refs_0_.refs_1_, bf16[256,576]{1,0:T(8,128)(2,1)S(1)} %get-tuple-element.43.refs_1_.refs_2_, bf16[256,576]{1,0:T(8,128)(2,1)S(1)} %get-tuple-element.44.refs_2_.refs_3_, ...), custom_call_target="tpu_custom_call" | custom-call | flops 30000000 | bytes 90000 | tf_op jit(solution)/shard_map/pallas_call | solution.py:416
  33.6 0.5 %collective-permute-start.13 = (bf16[96,768]{1,0:T(8,128)(2,1)S(1)}, bf16[96,768]{1,0:T(8,128)(2,1)S(1)}, u32[]{:S(2)}, u32[]{:S(2)}) collective-permute-start(bf16[96,768]{1,0:T(8,128)(2,1)S(1)} %collective-permute-done.8.refs_2_), channel_id=1, source_target_pairs={{0,4},{4,0},{8,12},{12,8},{16,20},{20,16},{24,28},{28,24},{1,5},{5... | collective-permute-start | bytes 442376 | tf_op jit(solution)/shard_map/ppermute | solution.py:48
  34.2 0.9 %collective-permute-done.11.refs_3_ = bf16[96,768]{1,0:T(8,128)(2,1)S(1)} collective-permute-done((bf16[96,768]{1,0:T(8,128)(2,1)S(1)}, bf16[96,768]{1,0:T(8,128)(2,1)S(1)}, u32[]{:S(2)}, u32[]{:S(2)}) %collective-permute-start.11) | collective-permute-done | bytes 147488 | tf_op jit(solution)/shard_map/ppermute | solution.py:48
  35.1 0.1 collective-permute-done.13.refs_5_
  35.2 0.2 collective-permute-done.12.refs_4_
  35.5 1.0 %collective-permute-done.14.refs_6_ = bf16[96,768]{1,0:T(8,128)(2,1)S(1)} collective-permute-done((bf16[96,768]{1,0:T(8,128)(2,1)S(1)}, bf16[96,768]{1,0:T(8,128)(2,1)S(1)}, u32[]{:S(2)}, u32[]{:S(2)}) %collective-permute-start.14) | collective-permute-done | bytes 147488 | tf_op jit(solution)/shard_map/ppermute | solution.py:48
  36.5 0.1 shard_map.71
  36.6 1.2 %collective-permute-done.7.refs_0_ = bf16[2,192,256]{2,1,0:T(8,128)(2,1)S(1)} collective-permute-done((bf16[2,192,256]{2,1,0:T(8,128)(2,1)S(1)}, bf16[2,192,256]{2,1,0:T(8,128)(2,1)S(1)}, u32[]{:S(2)}, u32[]{:S(2)}) %collective-permute-start.7) | collective-permute-done | bytes 196640 | tf_op jit(solution)/shard_map/ppermute | solution.py:48
  37.8 0.7 %shard_map.72.refs_3_ = f32[256,768]{1,0:T(8,128)S(1)} custom-call(bf16[2,192,256]{2,1,0:T(8,128)(2,1)S(1)} %shard_map.70.refs_0_, bf16[2,192,256]{2,1,0:T(8,128)(2,1)S(1)} %collective-permute-done.9.refs_1_, bf16[768,768]{1,0:T(8,128)(2,1)S(1)} %get-tuple-element.56.refs_2_.refs_1_, bf16[256,256]{1,0:T(8,128)(2,1)S(1)} %get-tuple-element.58.refs_3_.refs_2_, ...), custom_call_target="tpu_custom_call" | custom-call | flops 3000000 | bytes 9000 | tf_op jit(solution)/shard_map/pallas_call | solution.py:447
  38.5 0.5 %shard_map.73.refs_3_ = f32[256,768]{1,0:T(8,128)S(1)} custom-call(bf16[2,192,256]{2,1,0:T(8,128)(2,1)S(1)} %collective-permute-done.7.refs_0_, bf16[768,768]{1,0:T(8,128)(2,1)S(1)} %get-tuple-element.56.refs_2_.refs_1_, bf16[256,256]{1,0:T(8,128)(2,1)S(1)} %get-tuple-element.58.refs_3_.refs_2_, f32[256,768]{1,0:T(8,128)S(1)} %shard_map.72.refs_3_), custom_call_target="tpu_custom_call" | custom-call | flops 3000000 | bytes 9000 | tf_op jit(solution)/shard_map/pallas_call | solution.py:447
  39.0 0.3 collective-permute-done.15.refs_0_
  39.2 1.2 %shard_map.74 = bf16[256,768]{1,0:T(8,128)(2,1)} custom-call(bf16[2,192,256]{2,1,0:T(8,128)(2,1)S(1)} %collective-permute-done.15.refs_0_, bf16[768,768]{1,0:T(8,128)(2,1)S(1)} %get-tuple-element.56.refs_2_.refs_1_, bf16[256,256]{1,0:T(8,128)(2,1)S(1)} %get-tuple-element.58.refs_3_.refs_2_, f32[256,768]{1,0:T(8,128)S(1)} %shard_map.73.refs_3_), custom_call_target="tpu_custom_call" | custom-call | flops 3000000 | bytes 9000 | tf_op jit(solution)/shard_map/pallas_call | solution.py:447
  (22 shorter events, 0.3 us)
Async XLA Ops:
  0.0 1.4 %copy-start.1 = (bf16[1,256,768]{2,1,0:T(8,128)(2,1)S(1)}, bf16[1,256,768]{2,1,0:T(8,128)(2,1)}, u32[]{:S(2)}) copy-start(bf16[1,256,768]{2,1,0:T(8,128)(2,1)} %param.6) | copy-start | bytes 1179652
  0.0 9.3 %copy-start = (bf16[192,768]{1,0:T(8,128)(2,1)S(1)}, bf16[192,768]{1,0:T(8,128)(2,1)}, u32[]{:S(2)}) copy-start(bf16[192,768]{1,0:T(8,128)(2,1)} %refs_0_.3) | copy-start | bytes 884740
  0.0 13.5 %copy-start.2 = (f32[768]{0:T(1024)S(1)}, f32[768]{0:T(1024)}, u32[]{:S(2)}) copy-start(f32[768]{0:T(1024)} %refs_2_.3) | copy-start | bytes 9220
  0.0 13.6 %copy-start.3 = (f32[768]{0:T(1024)S(1)}, f32[768]{0:T(1024)}, u32[]{:S(2)}) copy-start(f32[768]{0:T(1024)} %refs_3_.3) | copy-start | bytes 9220
  1.4 12.1 %collective-permute-start.1 = (bf16[256,768]{1,0:T(8,128)(2,1)S(1)}, bf16[256,768]{1,0:T(8,128)(2,1)S(1)}, u32[]{:S(2)}, u32[]{:S(2)}) collective-permute-start(bf16[256,768]{1,0:T(8,128)(2,1)S(1)} %bitcast.2), channel_id=1, source_target_pairs={{0,8},{4,12},{8,0},{12,4},{16,24},{20,28},{24,16},{28,20},{1,9},{5... | collective-permute-start | bytes 1179656 | tf_op jit(solution)/shard_map/ppermute | solution.py:48
  4.5 9.1 %collective-permute-start = (bf16[256,768]{1,0:T(8,128)(2,1)S(1)}, bf16[256,768]{1,0:T(8,128)(2,1)S(1)}, u32[]{:S(2)}, u32[]{:S(2)}) collective-permute-start(bf16[256,768]{1,0:T(8,128)(2,1)S(1)} %bitcast.3), channel_id=1, source_target_pairs={{0,4},{4,0},{8,12},{12,8},{16,20},{20,16},{24,28},{28,24},{1,5},{5... | collective-permute-start | bytes 1179656 | tf_op jit(solution)/shard_map/ppermute | solution.py:48
  4.5 14.6 %collective-permute-start.3 = (bf16[192,576]{1,0:T(8,128)(2,1)S(1)}, bf16[192,576]{1,0:T(8,128)(2,1)S(1)}, u32[]{:S(2)}, u32[]{:S(2)}) collective-permute-start(bf16[192,576]{1,0:T(8,128)(2,1)S(1)} %pad_maximum_fusion.refs_4_), channel_id=1, source_target_pairs={{0,2},{1,3},{2,0},{3,1},{4,6},{5,7},{6,4},{7,5},{8,10},{9,11},{10,... | collective-permute-start | bytes 663560 | tf_op jit(solution)/shard_map/ppermute | solution.py:334
  7.0 17.0 %collective-permute-start.5 = (bf16[192,576]{1,0:T(8,128)(2,1)S(1)}, bf16[192,576]{1,0:T(8,128)(2,1)S(1)}, u32[]{:S(2)}, u32[]{:S(2)}) collective-permute-start(bf16[192,576]{1,0:T(8,128)(2,1)S(1)} %pad_maximum_fusion.refs_4_), channel_id=1, source_target_pairs={{0,1},{1,0},{2,3},{3,2},{4,5},{5,4},{6,7},{7,6},{8,9},{9,8},{10,11... | collective-permute-start | bytes 663560 | tf_op jit(solution)/shard_map/ppermute | solution.py:48
  13.5 5.6 %collective-permute-start.2 = (bf16[256,768]{1,0:T(8,128)(2,1)S(1)}, bf16[256,768]{1,0:T(8,128)(2,1)S(1)}, u32[]{:S(2)}, u32[]{:S(2)}) collective-permute-start(bf16[256,768]{1,0:T(8,128)(2,1)S(1)} %collective-permute-done.1.refs_0_), channel_id=1, source_target_pairs={{0,4},{4,0},{8,12},{12,8},{16,20},{20,16},{24,28},{28,24},{1,5},{5... | collective-permute-start | bytes 1179656 | tf_op jit(solution)/shard_map/ppermute | solution.py:48
  19.1 7.5 %collective-permute-start.4 = (bf16[192,576]{1,0:T(8,128)(2,1)S(1)}, bf16[192,576]{1,0:T(8,128)(2,1)S(1)}, u32[]{:S(2)}, u32[]{:S(2)}) collective-permute-start(bf16[192,576]{1,0:T(8,128)(2,1)S(1)} %collective-permute-done.3.refs_6_), channel_id=1, source_target_pairs={{0,16},{4,20},{8,24},{12,28},{16,0},{20,4},{24,8},{28,12},{1,17},{... | collective-permute-start | bytes 663560 | tf_op jit(solution)/shard_map/ppermute | solution.py:48
  20.0 9.9 %collective-permute-start.8 = (bf16[96,768]{1,0:T(8,128)(2,1)S(1)}, bf16[96,768]{1,0:T(8,128)(2,1)S(1)}, u32[]{:S(2)}, u32[]{:S(2)}) collective-permute-start(bf16[96,768]{1,0:T(8,128)(2,1)S(1)} %constant_dynamic-slice_fusion), channel_id=1, source_target_pairs={{0,2},{1,3},{2,0},{3,1},{4,6},{5,7},{6,4},{7,5},{8,10},{9,11},{10,... | collective-permute-start | bytes 442376 | tf_op jit(solution)/shard_map/ppermute | solution.py:334
  23.2 10.9 %collective-permute-start.10 = (bf16[96,768]{1,0:T(8,128)(2,1)S(1)}, bf16[96,768]{1,0:T(8,128)(2,1)S(1)}, u32[]{:S(2)}, u32[]{:S(2)}) collective-permute-start(bf16[96,768]{1,0:T(8,128)(2,1)S(1)} %constant_dynamic-slice_fusion), channel_id=1, source_target_pairs={{0,1},{1,0},{2,3},{3,2},{4,5},{5,4},{6,7},{7,6},{8,9},{9,8},{10,11... | collective-permute-start | bytes 442376 | tf_op jit(solution)/shard_map/ppermute | solution.py:48
  27.3 4.3 %collective-permute-start.6 = (bf16[3,64,128]{2,1,0:T(8,128)(2,1)S(1)}, bf16[3,64,128]{2,1,0:T(8,128)(2,1)S(1)}, u32[]{:S(2)}, u32[]{:S(2)}) collective-permute-start(bf16[3,64,128]{2,1,0:T(8,128)(2,1)S(1)} %get-tuple-element.51.refs_5_), channel_id=1, source_target_pairs={{0,16},{4,20},{8,24},{12,28},{16,0},{20,4},{24,8},{28,12},{1,17},{... | collective-permute-start | bytes 147464 | tf_op jit(solution)/shard_map/ppermute | solution.py:48
  29.9 5.1 %collective-permute-start.11 = (bf16[96,768]{1,0:T(8,128)(2,1)S(1)}, bf16[96,768]{1,0:T(8,128)(2,1)S(1)}, u32[]{:S(2)}, u32[]{:S(2)}) collective-permute-start(bf16[96,768]{1,0:T(8,128)(2,1)S(1)} %collective-permute-done.8.refs_2_), channel_id=1, source_target_pairs={{0,16},{4,20},{8,24},{12,28},{16,0},{20,4},{24,8},{28,12},{1,17},{... | collective-permute-start | bytes 442376 | tf_op jit(solution)/shard_map/ppermute | solution.py:48
  32.1 5.7 %collective-permute-start.7 = (bf16[2,192,256]{2,1,0:T(8,128)(2,1)S(1)}, bf16[2,192,256]{2,1,0:T(8,128)(2,1)S(1)}, u32[]{:S(2)}, u32[]{:S(2)}) collective-permute-start(bf16[2,192,256]{2,1,0:T(8,128)(2,1)S(1)} %shard_map.69), channel_id=1, source_target_pairs={{0,8},{4,12},{8,0},{12,4},{16,24},{20,28},{24,16},{28,20},{1,9},{5... | collective-permute-start | bytes 589832 | tf_op jit(solution)/shard_map/ppermute | solution.py:48
  33.5 4.3 %collective-permute-start.9 = (bf16[2,192,256]{2,1,0:T(8,128)(2,1)S(1)}, bf16[2,192,256]{2,1,0:T(8,128)(2,1)S(1)}, u32[]{:S(2)}, u32[]{:S(2)}) collective-permute-start(bf16[2,192,256]{2,1,0:T(8,128)(2,1)S(1)} %shard_map.70.refs_0_), channel_id=1, source_target_pairs={{0,4},{4,0},{8,12},{12,8},{16,20},{20,16},{24,28},{28,24},{1,5},{5... | collective-permute-start | bytes 589832 | tf_op jit(solution)/shard_map/ppermute | solution.py:48
  33.6 1.6 %collective-permute-start.13 = (bf16[96,768]{1,0:T(8,128)(2,1)S(1)}, bf16[96,768]{1,0:T(8,128)(2,1)S(1)}, u32[]{:S(2)}, u32[]{:S(2)}) collective-permute-start(bf16[96,768]{1,0:T(8,128)(2,1)S(1)} %collective-permute-done.8.refs_2_), channel_id=1, source_target_pairs={{0,4},{4,0},{8,12},{12,8},{16,20},{20,16},{24,28},{28,24},{1,5},{5... | collective-permute-start | bytes 442376 | tf_op jit(solution)/shard_map/ppermute | solution.py:48
  34.1 1.4 %collective-permute-start.12 = (bf16[96,768]{1,0:T(8,128)(2,1)S(1)}, bf16[96,768]{1,0:T(8,128)(2,1)S(1)}, u32[]{:S(2)}, u32[]{:S(2)}) collective-permute-start(bf16[96,768]{1,0:T(8,128)(2,1)S(1)} %collective-permute-done.10.refs_1_), channel_id=1, source_target_pairs={{0,4},{4,0},{8,12},{12,8},{16,20},{20,16},{24,28},{28,24},{1,5},{5... | collective-permute-start | bytes 442376 | tf_op jit(solution)/shard_map/ppermute | solution.py:48
  35.1 1.4 %collective-permute-start.14 = (bf16[96,768]{1,0:T(8,128)(2,1)S(1)}, bf16[96,768]{1,0:T(8,128)(2,1)S(1)}, u32[]{:S(2)}, u32[]{:S(2)}) collective-permute-start(bf16[96,768]{1,0:T(8,128)(2,1)S(1)} %collective-permute-done.11.refs_3_), channel_id=1, source_target_pairs={{0,4},{4,0},{8,12},{12,8},{16,20},{20,16},{24,28},{28,24},{1,5},{5... | collective-permute-start | bytes 442376 | tf_op jit(solution)/shard_map/ppermute | solution.py:48
  37.8 1.4 %collective-permute-start.15 = (bf16[2,192,256]{2,1,0:T(8,128)(2,1)S(1)}, bf16[2,192,256]{2,1,0:T(8,128)(2,1)S(1)}, u32[]{:S(2)}, u32[]{:S(2)}) collective-permute-start(bf16[2,192,256]{2,1,0:T(8,128)(2,1)S(1)} %collective-permute-done.7.refs_0_), channel_id=1, source_target_pairs={{0,4},{4,0},{8,12},{12,8},{16,20},{20,16},{24,28},{28,24},{1,5},{5... | collective-permute-start | bytes 589832 | tf_op jit(solution)/shard_map/ppermute | solution.py:48

commit v10 on v9

--- a/solution.py
+++ b/solution.py
@@ -140,8 +140,9 @@
     origin = sources(n_mp, group % 2, shared)
     for shard, (normed_ref, out_ref) in enumerate(zip(normed_refs, out_refs)):
         total = base_refs[shard][...] if base_refs else 0.0
-        for block, weight_ref in zip(some, weight_refs):
-            total = total + product(normed_ref[origin[block]], weight_ref[...])
+        for (block, first), weight_ref in zip(some, weight_refs):
+            columns = slice(first, first + weight_ref.shape[0])
+            total = total + product(normed_ref[origin[block], :, columns], weight_ref[...])
         out_ref[...] = total.astype(out_ref.dtype)
 
 
@@ -324,20 +325,12 @@
     out_ref[...] = update.astype(out_ref.dtype)
 
 
-def fetch(value, turns, shared):
+def fetch_far(value, turns):
     n_mp, n_ctx = lax.axis_size("mp"), lax.axis_size("ctx")
-    if not shared:
-        return [flip(value, "mp", apart) for apart in range(1, n_mp)]
     pairs = [
         (c * n_mp + z, c * n_mp + (z ^ (2 + turns(c)))) for c in range(n_ctx) for z in range(n_mp)
     ]
-    return [flip(value, "mp", 1), near(lax.ppermute(value, ("ctx", "mp"), pairs))]
-
-
-def exchange(blocks, shared, mask, *earlier):
-    if not shared:
-        return blocks
-    return blocks + [flip(after(blocks[-1], *earlier), "ctx", mask)]
+    return near(lax.ppermute(value, ("ctx", "mp"), pairs))
 
 
 def local(tile_embeds, norm_gain, norm_bias, w_qkv, w_out, valid_count):
@@ -356,13 +349,19 @@
         start = part * width + member * GROUP_WIDTH
         return lax.dynamic_slice(w_qkv, (0, start), (weight_rows, GROUP_WIDTH))
 
-    mine = near(jnp.concatenate([columns(part) for part in range(3)], axis=1))
-    fetched = fetch(mine, lambda c: c // SHARDS % 2, shared)
+    chosen = jnp.concatenate([columns(part) for part in range(3)], axis=1)
+    mine = near(chosen)
+    parity = lambda c: c // SHARDS % 2
+    cut = weight_rows // 3
+    if shared:
+        pieces = [fetch_far(near(part), parity) for part in (chosen[:cut], chosen[cut:])]
 
     x_own = near(x)
     x_pair = flip(after(x, mine), "ctx", 1)
     x_far = flip(after(x, mine), "ctx", 2)
     x_last = flip(x_far, "ctx", 1)
+    if shared:
+        closest = flip(after(mine, x_far), "mp", 1)
     gain, bias = near(norm_gain), near(norm_bias)
 
     def normalized(one, two, micros):
@@ -371,27 +370,36 @@
             one, two, gain, bias
         )
 
-    normed = normalized(x_own, x_pair, 3)
-    weights = [mine] + exchange(fetched, shared, SHARDS, normed[0])
-    normed += normalized(x_far, x_last, 0.01)
+    normed = normalized(x_own, x_pair, 1)
+    if shared:
+        swapped = [flip(after(pieces[0]), "ctx", SHARDS)]
+        swapped.append(flip(after(pieces[1], normed[0]), "ctx", SHARDS))
+        weights = [mine, closest, *pieces, *swapped]
+        blocks = [(0, 0), (1, 0), (2, 0), (2, cut), (3, 0), (3, cut)]
+    else:
+        weights = [mine] + [flip(mine, "mp", apart) for apart in range(1, n_mp)]
+        blocks = [(apart, 0) for apart in range(n_mp)]
+    normed += normalized(x_far, x_last, 1)
 
     out_own = near(w_out)
     out_weight = w_out
     if shared:
         size = weight_rows // 2
         out_weight = lax.dynamic_slice(w_out, (member % 2 * size, 0), (size, width))
-    out_weight = after(near(out_weight), normed[2])
-    out_fetched = fetch(out_weight, lambda c: c // SHARDS % 2, shared)
-
-    early = range(n_mp - 1)
+    out_weight = after(near(out_weight), x_last)
+    if shared:
+        out_fetched = [flip(out_weight, "mp", 1), fetch_far(out_weight, parity)]
+    else:
+        out_fetched = [flip(out_weight, "mp", apart) for apart in range(1, n_mp)]
+
     partial = call(
-        lambda *refs: project_body((n_mp, shared, early), *refs),
+        lambda *refs: project_body((n_mp, shared, blocks[:-1]), *refs),
         [shape((rows, 3 * GROUP_WIDTH), f32)] * SHARDS,
-        n_in=SHARDS + len(early),
+        n_in=SHARDS + len(blocks) - 1,
         micros=1,
     )(*normed, *weights[:-1])
     *qkv, sent = call(
-        lambda *refs: project_last_body((n_mp, shared, [n_mp - 1]), *refs),
+        lambda *refs: project_last_body((n_mp, shared, blocks[-1:]), *refs),
         [shape((rows, 3 * GROUP_WIDTH), bf16)] * SHARDS
         + [shape((GROUP_HEADS, SHARDS * depth, 2 * HEAD_DIM), bf16)],
         n_in=2 * SHARDS + 1,
@@ -407,7 +415,7 @@
         ],
         n_scalar=1,
         n_in=SHARDS,
-        micros=1,
+        micros=20,
     )(valid_count, *qkv)
 
     half = SHARDS // 2
@@ -426,10 +434,12 @@
     staying = finished(range(half), [after(sents[0], sending, last_fetched)] + sents[1:], 0.01)
     far_part = flip(sending, "ctx", 2)
     pair_part = flip(staying, "ctx", 1)
-    out_blocks = exchange(out_fetched, shared, SHARDS, stats[0])
+    out_blocks = list(out_fetched)
+    if shared:
+        out_blocks.append(flip(after(out_fetched[-1], stats[0]), "ctx", SHARDS))
     out_parts = [out_own] + out_blocks
     if shared:
-        out_parts += [flip(after(value, sending), "ctx", 1) for value in out_blocks]
+        out_parts += [flip(after(value, staying), "ctx", 1) for value in out_blocks]
     whole_out, order = call(
         lambda *refs: gather_body(n_mp, shared, *refs),
         [shape((width, width), bf16), shape((rows, rows), bf16)],
@@ -448,7 +458,7 @@
             lambda *refs, blocks=blocks: update_body(blocks, *refs),
             [out_shape],
             n_in=len(operands) + 3,
-            micros=0.001,
+            micros=5 if len(operands) == 1 else 0.001,
         )(*operands, whole_out, order, total)
     return total[None]
 

time: 40.6 us -> 44.3 us (1.091)
  waiting for transfers between devices: 14.9 us -> 16.9 us
  starting transfers between devices: 14.2 us -> 15.2 us
  Pallas kernels: 9.09 us -> 9.73 us
    ppermute x14 -> x15, waiting for transfers between devices: 9.68 us -> 13.4 us  [flip(): return near(lax.ppermute(value, axis, pairs))]
    ppermute x14 -> x15, starting transfers between devices: 8.46 us -> 10.2 us  [flip(): return near(lax.ppermute(value, axis, pairs))]
    ppermute x2 -> x3, waiting for transfers between devices: 5.26 us -> 3.56 us  [fetch_far(): return near(lax.ppermute(value, ('ctx', 'mp'), pairs))]
    ppermute x2 -> x3, starting transfers between devices: 5.75 us -> 4.98 us  [fetch_far(): return near(lax.ppermute(value, ('ctx', 'mp'), pairs))]
    pallas_call x2, Pallas kernels: 2 us -> 2.64 us  [the longest x1 2 us: local(): call(lambda *refs: project_body((n_mp, shared, blocks[:-1]), *refs), [sha...]
  transfers between devices with their start and end apart: 16 -> 18, of which waited for: 11 -> 10; matrix products, arithmetic and copies ran while one was open for 0% -> 0% of each run, Pallas kernels for 20% -> 19%
where the time goes in v10:
time: 44.3 us; the launch traced here: 44.1 us
  waiting for transfers between devices  16.9 us (38%)
  starting transfers between devices  15.2 us (34%)
  Pallas kernels  9.73 us (22%)
  local copies, waits for them, and re-layouts  1.32 us (3%)
  between operations  0.81 us (2%)
    ppermute x15, waiting for transfers between devices, flip(): return near(lax.ppermute(value, axis, pairs))  13.4 us
    ppermute x15, starting transfers between devices, flip(): return near(lax.ppermute(value, axis, pairs))  10.2 us
    ppermute x3, starting transfers between devices, fetch_far(): return near(lax.ppermute(value, ('ctx', 'mp'), pairs))  4.98 us
    ppermute x3, waiting for transfers between devices, fetch_far(): return near(lax.ppermute(value, ('ctx', 'mp'), pairs))  3.56 us
    pallas_call x3, Pallas kernels, local(): call(lambda *refs, blocks=blocks: update_body(blocks, *refs), [out_shape]...  2.36 us
    pallas_call x1, Pallas kernels, local(): call(lambda *refs: project_body((n_mp, shared, blocks[:-1]), *refs), [sha...  2 us
    pallas_call x2, Pallas kernels, normalized(): call(norm_body, [blocks] * 2, n_in=4, micros=micros)(one, two, gain, bias)  1.87 us
    pallas_call x1, Pallas kernels, local(): call(near_body, [shape((GROUP_HEADS, SHARDS, 1, rows), f32), shape((GROUP...  1.71 us
  transfers between devices with their start and end apart: 18, of which 10 were waited for; matrix products, arithmetic and copies ran while one was open for 0% of the time, Pallas kernels for 19%

profile of v10, /device:TPU:0, one launch (start us, length us, event | category | flops | bytes accessed | tf_op | source)
XLA Modules:
  0.0 44.1 jit_solution(4689509005556938108)
XLA Ops:
  0.0 1.3 %constant_dynamic-slice_fusion.3 = (bf16[192,192]{1,0:T(8,128)(2,1)S(1)}, bf16[192,192]{1,0:T(8,128)(2,1)S(1)}, bf16[192,192]{1,0:T(8,128)(2,1)S(1)}) fusion(bf16[192,2304]{1,0:T(8,128)(2,1)} %param.9, s32[]{:T(128)S(6)} %select_n.24, s32[]{:T(128)S(6)} %select_n.26, s32[]{:T(128)S(6)} %select_n.25), kind=kLoop, calls=%fused_computation.4 | loop fusion | bytes 442380 | tf_op jit(solution)/shard_map/dynamic_slice | solution.py:350
  1.4 3.0 %collective-permute-start.1 = (bf16[256,768]{1,0:T(8,128)(2,1)S(1)}, bf16[256,768]{1,0:T(8,128)(2,1)S(1)}, u32[]{:S(2)}, u32[]{:S(2)}) collective-permute-start(bf16[256,768]{1,0:T(8,128)(2,1)S(1)} %bitcast.2), channel_id=1, source_target_pairs={{0,8},{4,12},{8,0},{12,4},{16,24},{20,28},{24,16},{28,20},{1,9},{5... | collective-permute-start | bytes 1179656 | tf_op jit(solution)/shard_map/ppermute | solution.py:48
  4.5 2.7 %collective-permute-start.6 = (bf16[64,576]{1,0:T(8,128)(2,1)S(1)}, bf16[64,576]{1,0:T(8,128)(2,1)S(1)}, u32[]{:S(2)}, u32[]{:S(2)}) collective-permute-start(bf16[64,576]{1,0:T(8,128)(2,1)S(1)} %slice.9), channel_id=1, source_target_pairs={{0,2},{1,3},{2,0},{3,1},{4,6},{5,7},{6,4},{7,5},{8,10},{9,11},{10,... | collective-permute-start | bytes 221192 | tf_op jit(solution)/shard_map/ppermute | solution.py:333
  7.1 0.4 collective-permute-start.3
  8.2 5.3 %collective-permute-done.1.refs_0_ = bf16[256,768]{1,0:T(8,128)(2,1)S(1)} collective-permute-done((bf16[256,768]{1,0:T(8,128)(2,1)S(1)}, bf16[256,768]{1,0:T(8,128)(2,1)S(1)}, u32[]{:S(2)}, u32[]{:S(2)}) %collective-permute-start.1) | collective-permute-done | bytes 393248 | tf_op jit(solution)/shard_map/ppermute | solution.py:48
  13.6 2.4 %collective-permute-done.6.refs_6_ = bf16[64,576]{1,0:T(8,128)(2,1)S(1)} collective-permute-done((bf16[64,576]{1,0:T(8,128)(2,1)S(1)}, bf16[64,576]{1,0:T(8,128)(2,1)S(1)}, u32[]{:S(2)}, u32[]{:S(2)}) %collective-permute-start.6) | collective-permute-done | bytes 73760 | tf_op jit(solution)/shard_map/ppermute | solution.py:333
  15.9 1.1 %collective-permute-start.5 = (bf16[192,576]{1,0:T(8,128)(2,1)S(1)}, bf16[192,576]{1,0:T(8,128)(2,1)S(1)}, u32[]{:S(2)}, u32[]{:S(2)}) collective-permute-start(bf16[192,576]{1,0:T(8,128)(2,1)S(1)} %pad_maximum_fusion.refs_4_), channel_id=1, source_target_pairs={{0,1},{1,0},{2,3},{3,2},{4,5},{5,4},{6,7},{7,6},{8,9},{9,8},{10,11... | collective-permute-start | bytes 663560 | tf_op jit(solution)/shard_map/ppermute | solution.py:48
  17.0 0.9 %shard_map.64 = (bf16[4,256,192]{2,1,0:T(8,128)(2,1)S(1)}, bf16[4,256,192]{2,1,0:T(8,128)(2,1)S(1)}) custom-call(bf16[256,768]{1,0:T(8,128)(2,1)S(1)} %bitcast.4, bf16[256,768]{1,0:T(8,128)(2,1)S(1)} %collective-permute-done.refs_1_, f32[768]{0:T(1024)S(1)} %copy-done.2, f32[768]{0:T(1024)S(1)} %copy-done.3), custom_call_target="tpu_custom_call" | custom-call | flops 3000000000 | bytes 9000000 | tf_op jit(solution)/shard_map/pallas_call | solution.py:369
  18.0 1.2 %collective-permute-done.3.refs_7_ = bf16[128,576]{1,0:T(8,128)(2,1)S(1)} collective-permute-done((bf16[128,576]{1,0:T(8,128)(2,1)S(1)}, bf16[128,576]{1,0:T(8,128)(2,1)S(1)}, u32[]{:S(2)}, u32[]{:S(2)}) %collective-permute-start.3) | collective-permute-done | bytes 147488 | tf_op jit(solution)/shard_map/ppermute | solution.py:333
  19.2 0.2 collective-permute-start.4
  19.3 1.9 %collective-permute-start.12 = (bf16[96,768]{1,0:T(8,128)(2,1)S(1)}, bf16[96,768]{1,0:T(8,128)(2,1)S(1)}, u32[]{:S(2)}, u32[]{:S(2)}) collective-permute-start(bf16[96,768]{1,0:T(8,128)(2,1)S(1)} %constant_dynamic-slice_fusion), channel_id=1, source_target_pairs={{0,1},{1,0},{2,3},{3,2},{4,5},{5,4},{6,7},{7,6},{8,9},{9,8},{10,11... | collective-permute-start | bytes 442376 | tf_op jit(solution)/shard_map/ppermute | solution.py:48
  21.3 1.9 %collective-permute-start.10 = (bf16[96,768]{1,0:T(8,128)(2,1)S(1)}, bf16[96,768]{1,0:T(8,128)(2,1)S(1)}, u32[]{:S(2)}, u32[]{:S(2)}) collective-permute-start(bf16[96,768]{1,0:T(8,128)(2,1)S(1)} %constant_dynamic-slice_fusion), channel_id=1, source_target_pairs={{0,2},{1,3},{2,0},{3,1},{4,6},{5,7},{6,4},{7,5},{8,10},{9,11},{10,... | collective-permute-start | bytes 442376 | tf_op jit(solution)/shard_map/ppermute | solution.py:333
  23.2 0.9 %shard_map.65 = (bf16[4,256,192]{2,1,0:T(8,128)(2,1)S(1)}, bf16[4,256,192]{2,1,0:T(8,128)(2,1)S(1)}) custom-call(bf16[256,768]{1,0:T(8,128)(2,1)S(1)} %collective-permute-done.1.refs_0_, bf16[256,768]{1,0:T(8,128)(2,1)S(1)} %collective-permute-done.2.refs_1_, f32[768]{0:T(1024)S(1)} %copy-done.2, f32[768]{0:T(1024)S(1)} %copy-done.3), custom_call_target="tpu_custom_call" | custom-call | flops 3000000000 | bytes 9000000 | tf_op jit(solution)/shard_map/pallas_call | solution.py:369
  24.1 3.8 %collective-permute-done.5.refs_5_ = bf16[192,576]{1,0:T(8,128)(2,1)S(1)} collective-permute-done((bf16[192,576]{1,0:T(8,128)(2,1)S(1)}, bf16[192,576]{1,0:T(8,128)(2,1)S(1)}, u32[]{:S(2)}, u32[]{:S(2)}) %collective-permute-start.5) | collective-permute-done | bytes 221216 | tf_op jit(solution)/shard_map/ppermute | solution.py:48
  28.0 2.0 %shard_map.66 = (f32[256,576]{1,0:T(8,128)S(1)}, f32[256,576]{1,0:T(8,128)S(1)}, f32[256,576]{1,0:T(8,128)S(1)}, f32[256,576]{1,0:T(8,128)S(1)}) custom-call(bf16[4,256,192]{2,1,0:T(8,128)(2,1)S(1)} %get-tuple-element.34.refs_0_, bf16[4,256,192]{2,1,0:T(8,128)(2,1)S(1)} %get-tuple-element.35.refs_1_, bf16[4,256,192]{2,1,0:T(8,128)(2,1)S(1)} %get-tuple-element.36.refs_2_, ...), custom_call_target="tpu_custom_call" | custom-call | flops 3000000000 | bytes 9000000 | tf_op jit(solution)/shard_map/pallas_call | solution.py:395
  30.0 0.6 %shard_map.67 = (bf16[256,576]{1,0:T(8,128)(2,1)S(1)}, bf16[256,576]{1,0:T(8,128)(2,1)S(1)}, bf16[256,576]{1,0:T(8,128)(2,1)S(1)}, bf16[256,576]{1,0:T(8,128)(2,1)S(1)}, bf16[3,64,128]{2,1,0:T(8,128)(2,1)S(1)}) custom-call(bf16[4,256,192]{2,1,0:T(8,128)(2,1)S(1)} %get-tuple-element.34.refs_0_, bf16[4,256,192]{2,1,0:T(8,128)(2,1)S(1)} %get-tuple-element.35.refs_1_, ...), custom_call_target="tpu_custom_call" | custom-call | flops 3000000000 | bytes 9000000 | tf_op jit(solution)/shard_map/pallas_call | solution.py:401
  30.6 1.7 %shard_map.68 = (f32[3,4,1,256]{3,2,1,0:T(1,128)S(1)}, f32[3,4,1,256]{3,2,1,0:T(1,128)S(1)}, f32[3,4,64,256]{3,2,1,0:T(8,128)S(1)}) custom-call(s32[1]{0:T(128)S(6)} %copy.7.valid_ref.refs_0_, bf16[256,576]{1,0:T(8,128)(2,1)S(1)} %get-tuple-element.44.refs_0_.refs_1_, bf16[256,576]{1,0:T(8,128)(2,1)S(1)} %get-tuple-element.45.refs_1_.refs_2_, ...), custom_call_target="tpu_custom_call" | custom-call | flops 60000002048 | bytes 180000000 | tf_op jit(solution)/shard_map/pallas_call | solution.py:409
  32.4 2.1 %collective-permute-start.13 = (bf16[96,768]{1,0:T(8,128)(2,1)S(1)}, bf16[96,768]{1,0:T(8,128)(2,1)S(1)}, u32[]{:S(2)}, u32[]{:S(2)}) collective-permute-start(bf16[96,768]{1,0:T(8,128)(2,1)S(1)} %collective-permute-done.10.refs_2_), channel_id=1, source_target_pairs={{0,16},{4,20},{8,24},{12,28},{16,0},{20,4},{24,8},{28,12},{1,17},{... | collective-permute-start | bytes 442376 | tf_op jit(solution)/shard_map/ppermute | solution.py:48
  34.4 0.8 %collective-permute-done.8.refs_6_ = bf16[3,64,128]{2,1,0:T(8,128)(2,1)S(1)} collective-permute-done((bf16[3,64,128]{2,1,0:T(8,128)(2,1)S(1)}, bf16[3,64,128]{2,1,0:T(8,128)(2,1)S(1)}, u32[]{:S(2)}, u32[]{:S(2)}) %collective-permute-start.8) | collective-permute-done | bytes 49184 | tf_op jit(solution)/shard_map/ppermute | solution.py:48
  35.2 0.5 %shard_map.69 = bf16[2,192,256]{2,1,0:T(8,128)(2,1)S(1)} custom-call(s32[1]{0:T(128)S(6)} %copy.7.valid_ref.refs_0_, bf16[256,576]{1,0:T(8,128)(2,1)S(1)} %get-tuple-element.44.refs_0_.refs_1_, bf16[256,576]{1,0:T(8,128)(2,1)S(1)} %get-tuple-element.45.refs_1_.refs_2_, bf16[256,576]{1,0:T(8,128)(2,1)S(1)} %get-tuple-element.46.refs_2_.refs_3_, ...), custom_call_target="tpu_custom_call" | custom-call | flops 3000000000 | bytes 9000000 | tf_op jit(solution)/shard_map/pallas_call | solution.py:424
  35.7 0.8 %collective-permute-start.9 = (bf16[2,192,256]{2,1,0:T(8,128)(2,1)S(1)}, bf16[2,192,256]{2,1,0:T(8,128)(2,1)S(1)}, u32[]{:S(2)}, u32[]{:S(2)}) collective-permute-start(bf16[2,192,256]{2,1,0:T(8,128)(2,1)S(1)} %shard_map.69), channel_id=1, source_target_pairs={{0,8},{4,12},{8,0},{12,4},{16,24},{20,28},{24,16},{28,20},{1,9},{5... | collective-permute-start | bytes 589832 | tf_op jit(solution)/shard_map/ppermute | solution.py:48
  36.6 0.5 %shard_map.70.refs_0_ = bf16[2,192,256]{2,1,0:T(8,128)(2,1)S(1)} custom-call(s32[1]{0:T(128)S(6)} %copy.7.valid_ref.refs_0_, bf16[256,576]{1,0:T(8,128)(2,1)S(1)} %get-tuple-element.44.refs_0_.refs_1_, bf16[256,576]{1,0:T(8,128)(2,1)S(1)} %get-tuple-element.45.refs_1_.refs_2_, bf16[256,576]{1,0:T(8,128)(2,1)S(1)} %get-tuple-element.46.refs_2_.refs_3_, ...), custom_call_target="tpu_custom_call" | custom-call | flops 30000000 | bytes 90000 | tf_op jit(solution)/shard_map/pallas_call | solution.py:424
  37.2 0.5 %collective-permute-start.14 = (bf16[96,768]{1,0:T(8,128)(2,1)S(1)}, bf16[96,768]{1,0:T(8,128)(2,1)S(1)}, u32[]{:S(2)}, u32[]{:S(2)}) collective-permute-start(bf16[96,768]{1,0:T(8,128)(2,1)S(1)} %collective-permute-done.12.refs_1_), channel_id=1, source_target_pairs={{0,4},{4,0},{8,12},{12,8},{16,20},{20,16},{24,28},{28,24},{1,5},{5... | collective-permute-start | bytes 442376 | tf_op jit(solution)/shard_map/ppermute | solution.py:48
  37.8 0.4 collective-permute-start.16
  38.2 0.6 %collective-permute-done.14.refs_4_ = bf16[96,768]{1,0:T(8,128)(2,1)S(1)} collective-permute-done((bf16[96,768]{1,0:T(8,128)(2,1)S(1)}, bf16[96,768]{1,0:T(8,128)(2,1)S(1)}, u32[]{:S(2)}, u32[]{:S(2)}) %collective-permute-start.14) | collective-permute-done | bytes 147488 | tf_op jit(solution)/shard_map/ppermute | solution.py:48
  38.8 0.2 collective-permute-done.15.refs_5_
  39.1 0.2 collective-permute-done.16.refs_6_
  39.4 2.1 %collective-permute-done.9.refs_0_ = bf16[2,192,256]{2,1,0:T(8,128)(2,1)S(1)} collective-permute-done((bf16[2,192,256]{2,1,0:T(8,128)(2,1)S(1)}, bf16[2,192,256]{2,1,0:T(8,128)(2,1)S(1)}, u32[]{:S(2)}, u32[]{:S(2)}) %collective-permute-start.9) | collective-permute-done | bytes 196640 | tf_op jit(solution)/shard_map/ppermute | solution.py:48
  41.5 0.7 %shard_map.72.refs_3_ = f32[256,768]{1,0:T(8,128)S(1)} custom-call(bf16[2,192,256]{2,1,0:T(8,128)(2,1)S(1)} %shard_map.70.refs_0_, bf16[2,192,256]{2,1,0:T(8,128)(2,1)S(1)} %collective-permute-done.11.refs_1_, bf16[768,768]{1,0:T(8,128)(2,1)S(1)} %get-tuple-element.58.refs_2_.refs_1_, bf16[256,256]{1,0:T(8,128)(2,1)S(1)} %get-tuple-element.60.refs_3_.refs_2_, ...), custom_call_target="tpu_custom_call" | custom-call | flops 3000000 | bytes 9000 | tf_op jit(solution)/shard_map/pallas_call | solution.py:457
  42.2 0.5 %shard_map.73.refs_3_ = f32[256,768]{1,0:T(8,128)S(1)} custom-call(bf16[2,192,256]{2,1,0:T(8,128)(2,1)S(1)} %collective-permute-done.9.refs_0_, bf16[768,768]{1,0:T(8,128)(2,1)S(1)} %get-tuple-element.58.refs_2_.refs_1_, bf16[256,256]{1,0:T(8,128)(2,1)S(1)} %get-tuple-element.60.refs_3_.refs_2_, f32[256,768]{1,0:T(8,128)S(1)} %shard_map.72.refs_3_), custom_call_target="tpu_custom_call" | custom-call | flops 15000000512 | bytes 45000000 | tf_op jit(solution)/shard_map/pallas_call | solution.py:457
  42.7 0.3 collective-permute-done.17.refs_0_
  42.9 1.2 %shard_map.74 = bf16[256,768]{1,0:T(8,128)(2,1)} custom-call(bf16[2,192,256]{2,1,0:T(8,128)(2,1)S(1)} %collective-permute-done.17.refs_0_, bf16[768,768]{1,0:T(8,128)(2,1)S(1)} %get-tuple-element.58.refs_2_.refs_1_, bf16[256,256]{1,0:T(8,128)(2,1)S(1)} %get-tuple-element.60.refs_3_.refs_2_, f32[256,768]{1,0:T(8,128)S(1)} %shard_map.73.refs_3_), custom_call_target="tpu_custom_call" | custom-call | flops 15000000512 | bytes 45000000 | tf_op jit(solution)/shard_map/pallas_call | solution.py:457
  (28 shorter events, 0.5 us)
Async XLA Ops:
  0.0 1.4 %copy-start.1 = (bf16[1,256,768]{2,1,0:T(8,128)(2,1)S(1)}, bf16[1,256,768]{2,1,0:T(8,128)(2,1)}, u32[]{:S(2)}) copy-start(bf16[1,256,768]{2,1,0:T(8,128)(2,1)} %param.6) | copy-start | bytes 1179652
  0.0 13.5 %copy-start = (bf16[192,768]{1,0:T(8,128)(2,1)S(1)}, bf16[192,768]{1,0:T(8,128)(2,1)}, u32[]{:S(2)}) copy-start(bf16[192,768]{1,0:T(8,128)(2,1)} %refs_0_.3) | copy-start | bytes 884740
  0.0 17.0 %copy-start.3 = (f32[768]{0:T(1024)S(1)}, f32[768]{0:T(1024)}, u32[]{:S(2)}) copy-start(f32[768]{0:T(1024)} %refs_3_.3) | copy-start | bytes 9220
  0.0 17.0 %copy-start.2 = (f32[768]{0:T(1024)S(1)}, f32[768]{0:T(1024)}, u32[]{:S(2)}) copy-start(f32[768]{0:T(1024)} %refs_2_.3) | copy-start | bytes 9220
  1.4 12.1 %collective-permute-start.1 = (bf16[256,768]{1,0:T(8,128)(2,1)S(1)}, bf16[256,768]{1,0:T(8,128)(2,1)S(1)}, u32[]{:S(2)}, u32[]{:S(2)}) collective-permute-start(bf16[256,768]{1,0:T(8,128)(2,1)S(1)} %bitcast.2), channel_id=1, source_target_pairs={{0,8},{4,12},{8,0},{12,4},{16,24},{20,28},{24,16},{28,20},{1,9},{5... | collective-permute-start | bytes 1179656 | tf_op jit(solution)/shard_map/ppermute | solution.py:48
  4.5 12.6 %collective-permute-start = (bf16[256,768]{1,0:T(8,128)(2,1)S(1)}, bf16[256,768]{1,0:T(8,128)(2,1)S(1)}, u32[]{:S(2)}, u32[]{:S(2)}) collective-permute-start(bf16[256,768]{1,0:T(8,128)(2,1)S(1)} %bitcast.3), channel_id=1, source_target_pairs={{0,4},{4,0},{8,12},{12,8},{16,20},{20,16},{24,28},{28,24},{1,5},{5... | collective-permute-start | bytes 1179656 | tf_op jit(solution)/shard_map/ppermute | solution.py:48
  4.5 11.5 %collective-permute-start.6 = (bf16[64,576]{1,0:T(8,128)(2,1)S(1)}, bf16[64,576]{1,0:T(8,128)(2,1)S(1)}, u32[]{:S(2)}, u32[]{:S(2)}) collective-permute-start(bf16[64,576]{1,0:T(8,128)(2,1)S(1)} %slice.9), channel_id=1, source_target_pairs={{0,2},{1,3},{2,0},{3,1},{4,6},{5,7},{6,4},{7,5},{8,10},{9,11},{10,... | collective-permute-start | bytes 221192 | tf_op jit(solution)/shard_map/ppermute | solution.py:333
  7.1 12.0 %collective-permute-start.3 = (bf16[128,576]{1,0:T(8,128)(2,1)S(1)}, bf16[128,576]{1,0:T(8,128)(2,1)S(1)}, u32[]{:S(2)}, u32[]{:S(2)}) collective-permute-start(bf16[128,576]{1,0:T(8,128)(2,1)S(1)} %slice.8), channel_id=1, source_target_pairs={{0,2},{1,3},{2,0},{3,1},{4,6},{5,7},{6,4},{7,5},{8,10},{9,11},{10,... | collective-permute-start | bytes 442376 | tf_op jit(solution)/shard_map/ppermute | solution.py:333
  13.5 5.8 %collective-permute-start.2 = (bf16[256,768]{1,0:T(8,128)(2,1)S(1)}, bf16[256,768]{1,0:T(8,128)(2,1)S(1)}, u32[]{:S(2)}, u32[]{:S(2)}) collective-permute-start(bf16[256,768]{1,0:T(8,128)(2,1)S(1)} %collective-permute-done.1.refs_0_), channel_id=1, source_target_pairs={{0,4},{4,0},{8,12},{12,8},{16,20},{20,16},{24,28},{28,24},{1,5},{5... | collective-permute-start | bytes 1179656 | tf_op jit(solution)/shard_map/ppermute | solution.py:48
  15.9 8.2 %collective-permute-start.7 = (bf16[64,576]{1,0:T(8,128)(2,1)S(1)}, bf16[64,576]{1,0:T(8,128)(2,1)S(1)}, u32[]{:S(2)}, u32[]{:S(2)}) collective-permute-start(bf16[64,576]{1,0:T(8,128)(2,1)S(1)} %collective-permute-done.6.refs_6_), channel_id=1, source_target_pairs={{0,16},{4,20},{8,24},{12,28},{16,0},{20,4},{24,8},{28,12},{1,17},{... | collective-permute-start | bytes 221192 | tf_op jit(solution)/shard_map/ppermute | solution.py:48
  15.9 12.0 %collective-permute-start.5 = (bf16[192,576]{1,0:T(8,128)(2,1)S(1)}, bf16[192,576]{1,0:T(8,128)(2,1)S(1)}, u32[]{:S(2)}, u32[]{:S(2)}) collective-permute-start(bf16[192,576]{1,0:T(8,128)(2,1)S(1)} %pad_maximum_fusion.refs_4_), channel_id=1, source_target_pairs={{0,1},{1,0},{2,3},{3,2},{4,5},{5,4},{6,7},{7,6},{8,9},{9,8},{10,11... | collective-permute-start | bytes 663560 | tf_op jit(solution)/shard_map/ppermute | solution.py:48
  19.2 10.8 %collective-permute-start.4 = (bf16[128,576]{1,0:T(8,128)(2,1)S(1)}, bf16[128,576]{1,0:T(8,128)(2,1)S(1)}, u32[]{:S(2)}, u32[]{:S(2)}) collective-permute-start(bf16[128,576]{1,0:T(8,128)(2,1)S(1)} %collective-permute-done.3.refs_7_), channel_id=1, source_target_pairs={{0,16},{4,20},{8,24},{12,28},{16,0},{20,4},{24,8},{28,12},{1,17},{... | collective-permute-start | bytes 442376 | tf_op jit(solution)/shard_map/ppermute | solution.py:48
  19.3 17.9 %collective-permute-start.12 = (bf16[96,768]{1,0:T(8,128)(2,1)S(1)}, bf16[96,768]{1,0:T(8,128)(2,1)S(1)}, u32[]{:S(2)}, u32[]{:S(2)}) collective-permute-start(bf16[96,768]{1,0:T(8,128)(2,1)S(1)} %constant_dynamic-slice_fusion), channel_id=1, source_target_pairs={{0,1},{1,0},{2,3},{3,2},{4,5},{5,4},{6,7},{7,6},{8,9},{9,8},{10,11... | collective-permute-start | bytes 442376 | tf_op jit(solution)/shard_map/ppermute | solution.py:48
  21.3 11.1 %collective-permute-start.10 = (bf16[96,768]{1,0:T(8,128)(2,1)S(1)}, bf16[96,768]{1,0:T(8,128)(2,1)S(1)}, u32[]{:S(2)}, u32[]{:S(2)}) collective-permute-start(bf16[96,768]{1,0:T(8,128)(2,1)S(1)} %constant_dynamic-slice_fusion), channel_id=1, source_target_pairs={{0,2},{1,3},{2,0},{3,1},{4,6},{5,7},{6,4},{7,5},{8,10},{9,11},{10,... | collective-permute-start | bytes 442376 | tf_op jit(solution)/shard_map/ppermute | solution.py:333
  30.6 4.6 %collective-permute-start.8 = (bf16[3,64,128]{2,1,0:T(8,128)(2,1)S(1)}, bf16[3,64,128]{2,1,0:T(8,128)(2,1)S(1)}, u32[]{:S(2)}, u32[]{:S(2)}) collective-permute-start(bf16[3,64,128]{2,1,0:T(8,128)(2,1)S(1)} %get-tuple-element.53.refs_5_), channel_id=1, source_target_pairs={{0,16},{4,20},{8,24},{12,28},{16,0},{20,4},{24,8},{28,12},{1,17},{... | collective-permute-start | bytes 147464 | tf_op jit(solution)/shard_map/ppermute | solution.py:48
  32.4 5.4 %collective-permute-start.13 = (bf16[96,768]{1,0:T(8,128)(2,1)S(1)}, bf16[96,768]{1,0:T(8,128)(2,1)S(1)}, u32[]{:S(2)}, u32[]{:S(2)}) collective-permute-start(bf16[96,768]{1,0:T(8,128)(2,1)S(1)} %collective-permute-done.10.refs_2_), channel_id=1, source_target_pairs={{0,16},{4,20},{8,24},{12,28},{16,0},{20,4},{24,8},{28,12},{1,17},{... | collective-permute-start | bytes 442376 | tf_op jit(solution)/shard_map/ppermute | solution.py:48
  35.7 5.7 %collective-permute-start.9 = (bf16[2,192,256]{2,1,0:T(8,128)(2,1)S(1)}, bf16[2,192,256]{2,1,0:T(8,128)(2,1)S(1)}, u32[]{:S(2)}, u32[]{:S(2)}) collective-permute-start(bf16[2,192,256]{2,1,0:T(8,128)(2,1)S(1)} %shard_map.69), channel_id=1, source_target_pairs={{0,8},{4,12},{8,0},{12,4},{16,24},{20,28},{24,16},{28,20},{1,9},{5... | collective-permute-start | bytes 589832 | tf_op jit(solution)/shard_map/ppermute | solution.py:48
  37.1 4.4 %collective-permute-start.11 = (bf16[2,192,256]{2,1,0:T(8,128)(2,1)S(1)}, bf16[2,192,256]{2,1,0:T(8,128)(2,1)S(1)}, u32[]{:S(2)}, u32[]{:S(2)}) collective-permute-start(bf16[2,192,256]{2,1,0:T(8,128)(2,1)S(1)} %shard_map.70.refs_0_), channel_id=1, source_target_pairs={{0,4},{4,0},{8,12},{12,8},{16,20},{20,16},{24,28},{28,24},{1,5},{5... | collective-permute-start | bytes 589832 | tf_op jit(solution)/shard_map/ppermute | solution.py:48
  37.2 1.6 %collective-permute-start.14 = (bf16[96,768]{1,0:T(8,128)(2,1)S(1)}, bf16[96,768]{1,0:T(8,128)(2,1)S(1)}, u32[]{:S(2)}, u32[]{:S(2)}) collective-permute-start(bf16[96,768]{1,0:T(8,128)(2,1)S(1)} %collective-permute-done.12.refs_1_), channel_id=1, source_target_pairs={{0,4},{4,0},{8,12},{12,8},{16,20},{20,16},{24,28},{28,24},{1,5},{5... | collective-permute-start | bytes 442376 | tf_op jit(solution)/shard_map/ppermute | solution.py:48
  37.7 1.4 %collective-permute-start.15 = (bf16[96,768]{1,0:T(8,128)(2,1)S(1)}, bf16[96,768]{1,0:T(8,128)(2,1)S(1)}, u32[]{:S(2)}, u32[]{:S(2)}) collective-permute-start(bf16[96,768]{1,0:T(8,128)(2,1)S(1)} %collective-permute-done.10.refs_2_), channel_id=1, source_target_pairs={{0,4},{4,0},{8,12},{12,8},{16,20},{20,16},{24,28},{28,24},{1,5},{5... | collective-permute-start | bytes 442376 | tf_op jit(solution)/shard_map/ppermute | solution.py:48
  37.8 1.5 %collective-permute-start.16 = (bf16[96,768]{1,0:T(8,128)(2,1)S(1)}, bf16[96,768]{1,0:T(8,128)(2,1)S(1)}, u32[]{:S(2)}, u32[]{:S(2)}) collective-permute-start(bf16[96,768]{1,0:T(8,128)(2,1)S(1)} %collective-permute-done.13.refs_3_), channel_id=1, source_target_pairs={{0,4},{4,0},{8,12},{12,8},{16,20},{20,16},{24,28},{28,24},{1,5},{5... | collective-permute-start | bytes 442376 | tf_op jit(solution)/shard_map/ppermute | solution.py:48
  41.5 1.4 %collective-permute-start.17 = (bf16[2,192,256]{2,1,0:T(8,128)(2,1)S(1)}, bf16[2,192,256]{2,1,0:T(8,128)(2,1)S(1)}, u32[]{:S(2)}, u32[]{:S(2)}) collective-permute-start(bf16[2,192,256]{2,1,0:T(8,128)(2,1)S(1)} %collective-permute-done.9.refs_0_), channel_id=1, source_target_pairs={{0,4},{4,0},{8,12},{12,8},{16,20},{20,16},{24,28},{28,24},{1,5},{5... | collective-permute-start | bytes 589832 | tf_op jit(solution)/shard_map/ppermute | solution.py:48

commit v11 on v10

--- a/solution.py
+++ b/solution.py
@@ -140,9 +140,11 @@
     origin = sources(n_mp, group % 2, shared)
     for shard, (normed_ref, out_ref) in enumerate(zip(normed_refs, out_refs)):
         total = base_refs[shard][...] if base_refs else 0.0
-        for (block, first), weight_ref in zip(some, weight_refs):
-            columns = slice(first, first + weight_ref.shape[0])
-            total = total + product(normed_ref[origin[block], :, columns], weight_ref[...])
+        for block in sorted({block for block, _ in some}):
+            pieces = [(first, ref) for (at, first), ref in zip(some, weight_refs) if at == block]
+            weight = jnp.concatenate([ref[...] for _, ref in pieces], axis=0)
+            columns = slice(pieces[0][0], pieces[0][0] + weight.shape[0])
+            total = total + product(normed_ref[origin[block], :, columns], weight)
         out_ref[...] = total.astype(out_ref.dtype)
 
 
@@ -361,7 +363,7 @@
     x_far = flip(after(x, mine), "ctx", 2)
     x_last = flip(x_far, "ctx", 1)
     if shared:
-        closest = flip(after(mine, x_far), "mp", 1)
+        closest = flip(after(mine, x_pair), "mp", 1)
     gain, bias = near(norm_gain), near(norm_bias)
 
     def normalized(one, two, micros):
@@ -372,21 +374,21 @@
 
     normed = normalized(x_own, x_pair, 1)
     if shared:
-        swapped = [flip(after(pieces[0]), "ctx", SHARDS)]
-        swapped.append(flip(after(pieces[1], normed[0]), "ctx", SHARDS))
+        swapped = [flip(after(pieces[0], normed[0]), "ctx", SHARDS)]
+        swapped.append(flip(after(pieces[1], pieces[0]), "ctx", SHARDS))
         weights = [mine, closest, *pieces, *swapped]
         blocks = [(0, 0), (1, 0), (2, 0), (2, cut), (3, 0), (3, cut)]
     else:
         weights = [mine] + [flip(mine, "mp", apart) for apart in range(1, n_mp)]
         blocks = [(apart, 0) for apart in range(n_mp)]
-    normed += normalized(x_far, x_last, 1)
+    normed += normalized(x_far, x_last, 0.01)
 
     out_own = near(w_out)
     out_weight = w_out
     if shared:
         size = weight_rows // 2
         out_weight = lax.dynamic_slice(w_out, (member % 2 * size, 0), (size, width))
-    out_weight = after(near(out_weight), x_last)
+    out_weight = after(near(out_weight), normed[2])
     if shared:
         out_fetched = [flip(out_weight, "mp", 1), fetch_far(out_weight, parity)]
     else:
@@ -415,7 +417,7 @@
         ],
         n_scalar=1,
         n_in=SHARDS,
-        micros=20,
+        micros=5,
     )(valid_count, *qkv)
 
     half = SHARDS // 2
@@ -429,14 +431,13 @@
             micros=micros,
         )(valid_count, *qkv, *sent_parts, *stats)[0]
 
-    sending = finished(range(half, SHARDS), sents, 1)
-    last_fetched = out_fetched[-1]
-    staying = finished(range(half), [after(sents[0], sending, last_fetched)] + sents[1:], 0.01)
+    sending = finished(range(half, SHARDS), sents, 5)
+    out_blocks = list(out_fetched)
+    if shared:
+        out_blocks.append(flip(after(out_fetched[-1], stats[0]), "ctx", SHARDS))
+    staying = finished(range(half), [after(sents[0], sending, *out_blocks)] + sents[1:], 5)
     far_part = flip(sending, "ctx", 2)
     pair_part = flip(staying, "ctx", 1)
-    out_blocks = list(out_fetched)
-    if shared:
-        out_blocks.append(flip(after(out_fetched[-1], stats[0]), "ctx", SHARDS))
     out_parts = [out_own] + out_blocks
     if shared:
         out_parts += [flip(after(value, staying), "ctx", 1) for value in out_blocks]

time: 44.3 us -> 40.5 us (0.914)
  waiting for transfers between devices: 16.9 us -> 10.8 us
  starting transfers between devices: 15.2 us -> 17.8 us
    ppermute x15, waiting for transfers between devices: 13.4 us -> 8.59 us  [flip(): return near(lax.ppermute(value, axis, pairs))]
    ppermute x15, starting transfers between devices: 10.2 us -> 11.6 us  [flip(): return near(lax.ppermute(value, axis, pairs))]
    ppermute x3, waiting for transfers between devices: 3.56 us -> 2.23 us  [fetch_far(): return near(lax.ppermute(value, ('ctx', 'mp'), pairs))]
    ppermute x3, starting transfers between devices: 4.98 us -> 6.22 us  [fetch_far(): return near(lax.ppermute(value, ('ctx', 'mp'), pairs))]
  transfers between devices with their start and end apart: 18 -> 18, of which waited for: 10 -> 7; matrix products, arithmetic and copies ran while one was open for 0% -> 0% of each run, Pallas kernels for 19% -> 20%
where the time goes in v11:
time: 40.5 us; the launch traced here: 40.3 us
  starting transfers between devices  17.8 us (44%)
  waiting for transfers between devices  10.8 us (27%)
  Pallas kernels  9.45 us (23%)
  local copies, waits for them, and re-layouts  1.3 us (3%)
  between operations  0.82 us (2%)
    ppermute x15, starting transfers between devices, flip(): return near(lax.ppermute(value, axis, pairs))  11.6 us
    ppermute x15, waiting for transfers between devices, flip(): return near(lax.ppermute(value, axis, pairs))  8.59 us
    ppermute x3, starting transfers between devices, fetch_far(): return near(lax.ppermute(value, ('ctx', 'mp'), pairs))  6.22 us
    pallas_call x3, Pallas kernels, local(): call(lambda *refs, blocks=blocks: update_body(blocks, *refs), [out_shape]...  2.35 us
    ppermute x3, waiting for transfers between devices, fetch_far(): return near(lax.ppermute(value, ('ctx', 'mp'), pairs))  2.23 us
    pallas_call x2, Pallas kernels, normalized(): call(norm_body, [blocks] * 2, n_in=4, micros=micros)(one, two, gain, bias)  1.87 us
    pallas_call x1, Pallas kernels, local(): call(lambda *refs: project_body((n_mp, shared, blocks[:-1]), *refs), [sha...  1.72 us
    pallas_call x1, Pallas kernels, local(): call(near_body, [shape((GROUP_HEADS, SHARDS, 1, rows), f32), shape((GROUP...  1.71 us
  transfers between devices with their start and end apart: 18, of which 7 were waited for; matrix products, arithmetic and copies ran while one was open for 0% of the time, Pallas kernels for 20%

profile of v11, /device:TPU:0, one launch (start us, length us, event | category | flops | bytes accessed | tf_op | source)
XLA Modules:
  0.0 40.3 jit_solution(3197333097074996384)
XLA Ops:
  0.0 1.3 %constant_dynamic-slice_fusion.3 = (bf16[192,192]{1,0:T(8,128)(2,1)S(1)}, bf16[192,192]{1,0:T(8,128)(2,1)S(1)}, bf16[192,192]{1,0:T(8,128)(2,1)S(1)}) fusion(bf16[192,2304]{1,0:T(8,128)(2,1)} %param.9, s32[]{:T(128)S(6)} %select_n.24, s32[]{:T(128)S(6)} %select_n.26, s32[]{:T(128)S(6)} %select_n.25), kind=kLoop, calls=%fused_computation.4 | loop fusion | bytes 442380 | tf_op jit(solution)/shard_map/dynamic_slice | solution.py:352
  1.4 0.5 %collective-permute-start = (bf16[256,768]{1,0:T(8,128)(2,1)S(1)}, bf16[256,768]{1,0:T(8,128)(2,1)S(1)}, u32[]{:S(2)}, u32[]{:S(2)}) collective-permute-start(bf16[256,768]{1,0:T(8,128)(2,1)S(1)} %bitcast.2), channel_id=1, source_target_pairs={{0,4},{4,0},{8,12},{12,8},{16,20},{20,16},{24,28},{28,24},{1,5},{5... | collective-permute-start | bytes 1179656 | tf_op jit(solution)/shard_map/ppermute | solution.py:48
  1.9 2.6 %collective-permute-start.1 = (bf16[256,768]{1,0:T(8,128)(2,1)S(1)}, bf16[256,768]{1,0:T(8,128)(2,1)S(1)}, u32[]{:S(2)}, u32[]{:S(2)}) collective-permute-start(bf16[256,768]{1,0:T(8,128)(2,1)S(1)} %bitcast.3), channel_id=1, source_target_pairs={{0,8},{4,12},{8,0},{12,4},{16,24},{20,28},{24,16},{28,20},{1,9},{5... | collective-permute-start | bytes 1179656 | tf_op jit(solution)/shard_map/ppermute | solution.py:48
  4.5 2.7 %collective-permute-start.4 = (bf16[64,576]{1,0:T(8,128)(2,1)S(1)}, bf16[64,576]{1,0:T(8,128)(2,1)S(1)}, u32[]{:S(2)}, u32[]{:S(2)}) collective-permute-start(bf16[64,576]{1,0:T(8,128)(2,1)S(1)} %slice.9), channel_id=1, source_target_pairs={{0,2},{1,3},{2,0},{3,1},{4,6},{5,7},{6,4},{7,5},{8,10},{9,11},{10,... | collective-permute-start | bytes 221192 | tf_op jit(solution)/shard_map/ppermute | solution.py:335
  7.2 0.4 collective-permute-start.3
  8.3 1.6 %collective-permute-start.6 = (bf16[192,576]{1,0:T(8,128)(2,1)S(1)}, bf16[192,576]{1,0:T(8,128)(2,1)S(1)}, u32[]{:S(2)}, u32[]{:S(2)}) collective-permute-start(bf16[192,576]{1,0:T(8,128)(2,1)S(1)} %pad_maximum_fusion.refs_4_), channel_id=1, source_target_pairs={{0,1},{1,0},{2,3},{3,2},{4,5},{5,4},{6,7},{7,6},{8,9},{9,8},{10,11... | collective-permute-start | bytes 663560 | tf_op jit(solution)/shard_map/ppermute | solution.py:48
  9.9 4.3 %collective-permute-done.1.refs_0_ = bf16[256,768]{1,0:T(8,128)(2,1)S(1)} collective-permute-done((bf16[256,768]{1,0:T(8,128)(2,1)S(1)}, bf16[256,768]{1,0:T(8,128)(2,1)S(1)}, u32[]{:S(2)}, u32[]{:S(2)}) %collective-permute-start.1) | collective-permute-done | bytes 393248 | tf_op jit(solution)/shard_map/ppermute | solution.py:48
  14.2 0.9 %shard_map.64 = (bf16[4,256,192]{2,1,0:T(8,128)(2,1)S(1)}, bf16[4,256,192]{2,1,0:T(8,128)(2,1)S(1)}) custom-call(bf16[256,768]{1,0:T(8,128)(2,1)S(1)} %bitcast.4, bf16[256,768]{1,0:T(8,128)(2,1)S(1)} %collective-permute-done.refs_1_, f32[768]{0:T(1024)S(1)} %copy-done.2, f32[768]{0:T(1024)S(1)} %copy-done.3), custom_call_target="tpu_custom_call" | custom-call | flops 3000000000 | bytes 9000000 | tf_op jit(solution)/shard_map/pallas_call | solution.py:371
  15.2 0.4 collective-permute-done.4.refs_6_
  15.6 1.5 %collective-permute-start.7 = (bf16[64,576]{1,0:T(8,128)(2,1)S(1)}, bf16[64,576]{1,0:T(8,128)(2,1)S(1)}, u32[]{:S(2)}, u32[]{:S(2)}) collective-permute-start(bf16[64,576]{1,0:T(8,128)(2,1)S(1)} %collective-permute-done.4.refs_6_), channel_id=1, source_target_pairs={{0,16},{4,20},{8,24},{12,28},{16,0},{20,4},{24,8},{28,12},{1,17},{... | collective-permute-start | bytes 221192 | tf_op jit(solution)/shard_map/ppermute | solution.py:48
  17.0 1.8 %collective-permute-done.3.refs_7_ = bf16[128,576]{1,0:T(8,128)(2,1)S(1)} collective-permute-done((bf16[128,576]{1,0:T(8,128)(2,1)S(1)}, bf16[128,576]{1,0:T(8,128)(2,1)S(1)}, u32[]{:S(2)}, u32[]{:S(2)}) %collective-permute-start.3) | collective-permute-done | bytes 147488 | tf_op jit(solution)/shard_map/ppermute | solution.py:335
  18.9 0.9 %shard_map.65 = (bf16[4,256,192]{2,1,0:T(8,128)(2,1)S(1)}, bf16[4,256,192]{2,1,0:T(8,128)(2,1)S(1)}) custom-call(bf16[256,768]{1,0:T(8,128)(2,1)S(1)} %collective-permute-done.1.refs_0_, bf16[256,768]{1,0:T(8,128)(2,1)S(1)} %collective-permute-done.2.refs_1_, f32[768]{0:T(1024)S(1)} %copy-done.2, f32[768]{0:T(1024)S(1)} %copy-done.3), custom_call_target="tpu_custom_call" | custom-call | flops 30000000 | bytes 90000 | tf_op jit(solution)/shard_map/pallas_call | solution.py:371
  19.8 3.2 %collective-permute-start.11 = (bf16[96,768]{1,0:T(8,128)(2,1)S(1)}, bf16[96,768]{1,0:T(8,128)(2,1)S(1)}, u32[]{:S(2)}, u32[]{:S(2)}) collective-permute-start(bf16[96,768]{1,0:T(8,128)(2,1)S(1)} %constant_dynamic-slice_fusion), channel_id=1, source_target_pairs={{0,2},{1,3},{2,0},{3,1},{4,6},{5,7},{6,4},{7,5},{8,10},{9,11},{10,... | collective-permute-start | bytes 442376 | tf_op jit(solution)/shard_map/ppermute | solution.py:335
  23.0 1.0 %collective-permute-start.10 = (bf16[96,768]{1,0:T(8,128)(2,1)S(1)}, bf16[96,768]{1,0:T(8,128)(2,1)S(1)}, u32[]{:S(2)}, u32[]{:S(2)}) collective-permute-start(bf16[96,768]{1,0:T(8,128)(2,1)S(1)} %constant_dynamic-slice_fusion), channel_id=1, source_target_pairs={{0,1},{1,0},{2,3},{3,2},{4,5},{5,4},{6,7},{7,6},{8,9},{9,8},{10,11... | collective-permute-start | bytes 442376 | tf_op jit(solution)/shard_map/ppermute | solution.py:48
  24.0 1.7 %shard_map.66 = (f32[256,576]{1,0:T(8,128)S(1)}, f32[256,576]{1,0:T(8,128)S(1)}, f32[256,576]{1,0:T(8,128)S(1)}, f32[256,576]{1,0:T(8,128)S(1)}) custom-call(bf16[4,256,192]{2,1,0:T(8,128)(2,1)S(1)} %get-tuple-element.35.refs_0_, bf16[4,256,192]{2,1,0:T(8,128)(2,1)S(1)} %get-tuple-element.36.refs_1_, bf16[4,256,192]{2,1,0:T(8,128)(2,1)S(1)} %get-tuple-element.37.refs_2_, ...), custom_call_target="tpu_custom_call" | custom-call | flops 3000000000 | bytes 9000000 | tf_op jit(solution)/shard_map/pallas_call | solution.py:397
  25.7 0.6 %shard_map.67 = (bf16[256,576]{1,0:T(8,128)(2,1)S(1)}, bf16[256,576]{1,0:T(8,128)(2,1)S(1)}, bf16[256,576]{1,0:T(8,128)(2,1)S(1)}, bf16[256,576]{1,0:T(8,128)(2,1)S(1)}, bf16[3,64,128]{2,1,0:T(8,128)(2,1)S(1)}) custom-call(bf16[4,256,192]{2,1,0:T(8,128)(2,1)S(1)} %get-tuple-element.35.refs_0_, bf16[4,256,192]{2,1,0:T(8,128)(2,1)S(1)} %get-tuple-element.36.refs_1_, ...), custom_call_target="tpu_custom_call" | custom-call | flops 3000000000 | bytes 9000000 | tf_op jit(solution)/shard_map/pallas_call | solution.py:403
  26.3 1.5 %collective-permute-start.8 = (bf16[3,64,128]{2,1,0:T(8,128)(2,1)S(1)}, bf16[3,64,128]{2,1,0:T(8,128)(2,1)S(1)}, u32[]{:S(2)}, u32[]{:S(2)}) collective-permute-start(bf16[3,64,128]{2,1,0:T(8,128)(2,1)S(1)} %get-tuple-element.56.refs_5_), channel_id=1, source_target_pairs={{0,16},{4,20},{8,24},{12,28},{16,0},{20,4},{24,8},{28,12},{1,17},{... | collective-permute-start | bytes 147464 | tf_op jit(solution)/shard_map/ppermute | solution.py:48
  27.8 1.7 %shard_map.68 = (f32[3,4,1,256]{3,2,1,0:T(1,128)S(1)}, f32[3,4,1,256]{3,2,1,0:T(1,128)S(1)}, f32[3,4,64,256]{3,2,1,0:T(8,128)S(1)}) custom-call(s32[1]{0:T(128)S(6)} %copy.7.valid_ref.refs_0_, bf16[256,576]{1,0:T(8,128)(2,1)S(1)} %get-tuple-element.46.refs_0_.refs_1_, bf16[256,576]{1,0:T(8,128)(2,1)S(1)} %get-tuple-element.47.refs_1_.refs_2_, ...), custom_call_target="tpu_custom_call" | custom-call | flops 15000000512 | bytes 45000000 | tf_op jit(solution)/shard_map/pallas_call | solution.py:411
  29.5 1.0 %collective-permute-start.12 = (bf16[96,768]{1,0:T(8,128)(2,1)S(1)}, bf16[96,768]{1,0:T(8,128)(2,1)S(1)}, u32[]{:S(2)}, u32[]{:S(2)}) collective-permute-start(bf16[96,768]{1,0:T(8,128)(2,1)S(1)} %collective-permute-done.11.refs_2_), channel_id=1, source_target_pairs={{0,16},{4,20},{8,24},{12,28},{16,0},{20,4},{24,8},{28,12},{1,17},{... | collective-permute-start | bytes 442376 | tf_op jit(solution)/shard_map/ppermute | solution.py:48
  30.5 0.5 %shard_map.69 = bf16[2,192,256]{2,1,0:T(8,128)(2,1)S(1)} custom-call(s32[1]{0:T(128)S(6)} %copy.7.valid_ref.refs_0_, bf16[256,576]{1,0:T(8,128)(2,1)S(1)} %get-tuple-element.46.refs_0_.refs_1_, bf16[256,576]{1,0:T(8,128)(2,1)S(1)} %get-tuple-element.47.refs_1_.refs_2_, bf16[256,576]{1,0:T(8,128)(2,1)S(1)} %get-tuple-element.48.refs_2_.refs_3_, ...), custom_call_target="tpu_custom_call" | custom-call | flops 15000000512 | bytes 45000000 | tf_op jit(solution)/shard_map/pallas_call | solution.py:426
  31.0 0.5 %collective-permute-start.9 = (bf16[2,192,256]{2,1,0:T(8,128)(2,1)S(1)}, bf16[2,192,256]{2,1,0:T(8,128)(2,1)S(1)}, u32[]{:S(2)}, u32[]{:S(2)}) collective-permute-start(bf16[2,192,256]{2,1,0:T(8,128)(2,1)S(1)} %shard_map.69), channel_id=1, source_target_pairs={{0,8},{4,12},{8,0},{12,4},{16,24},{20,28},{24,16},{28,20},{1,9},{5... | collective-permute-start | bytes 589832 | tf_op jit(solution)/shard_map/ppermute | solution.py:48
  31.6 3.2 %collective-permute-done.12.refs_3_ = bf16[96,768]{1,0:T(8,128)(2,1)S(1)} collective-permute-done((bf16[96,768]{1,0:T(8,128)(2,1)S(1)}, bf16[96,768]{1,0:T(8,128)(2,1)S(1)}, u32[]{:S(2)}, u32[]{:S(2)}) %collective-permute-start.12) | collective-permute-done | bytes 147488 | tf_op jit(solution)/shard_map/ppermute | solution.py:48
  34.7 0.5 %shard_map.70.refs_0_ = bf16[2,192,256]{2,1,0:T(8,128)(2,1)S(1)} custom-call(s32[1]{0:T(128)S(6)} %copy.7.valid_ref.refs_0_, bf16[256,576]{1,0:T(8,128)(2,1)S(1)} %get-tuple-element.46.refs_0_.refs_1_, bf16[256,576]{1,0:T(8,128)(2,1)S(1)} %get-tuple-element.47.refs_1_.refs_2_, bf16[256,576]{1,0:T(8,128)(2,1)S(1)} %get-tuple-element.48.refs_2_.refs_3_, ...), custom_call_target="tpu_custom_call" | custom-call | flops 15000000512 | bytes 45000000 | tf_op jit(solution)/shard_map/pallas_call | solution.py:426
  35.3 0.5 %collective-permute-start.16 = (bf16[96,768]{1,0:T(8,128)(2,1)S(1)}, bf16[96,768]{1,0:T(8,128)(2,1)S(1)}, u32[]{:S(2)}, u32[]{:S(2)}) collective-permute-start(bf16[96,768]{1,0:T(8,128)(2,1)S(1)} %collective-permute-done.12.refs_3_), channel_id=1, source_target_pairs={{0,4},{4,0},{8,12},{12,8},{16,20},{20,16},{24,28},{28,24},{1,5},{5... | collective-permute-start | bytes 442376 | tf_op jit(solution)/shard_map/ppermute | solution.py:48
  35.9 0.4 %collective-permute-start.14 = (bf16[96,768]{1,0:T(8,128)(2,1)S(1)}, bf16[96,768]{1,0:T(8,128)(2,1)S(1)}, u32[]{:S(2)}, u32[]{:S(2)}) collective-permute-start(bf16[96,768]{1,0:T(8,128)(2,1)S(1)} %collective-permute-done.10.refs_1_), channel_id=1, source_target_pairs={{0,4},{4,0},{8,12},{12,8},{16,20},{20,16},{24,28},{28,24},{1,5},{5... | collective-permute-start | bytes 442376 | tf_op jit(solution)/shard_map/ppermute | solution.py:48
  36.3 0.6 %collective-permute-done.16.refs_6_ = bf16[96,768]{1,0:T(8,128)(2,1)S(1)} collective-permute-done((bf16[96,768]{1,0:T(8,128)(2,1)S(1)}, bf16[96,768]{1,0:T(8,128)(2,1)S(1)}, u32[]{:S(2)}, u32[]{:S(2)}) %collective-permute-start.16) | collective-permute-done | bytes 147488 | tf_op jit(solution)/shard_map/ppermute | solution.py:48
  37.0 0.2 collective-permute-done.15.refs_5_
  37.2 0.2 collective-permute-done.14.refs_4_
  37.6 0.4 collective-permute-start.17
  37.9 0.7 %shard_map.72.refs_3_ = f32[256,768]{1,0:T(8,128)S(1)} custom-call(bf16[2,192,256]{2,1,0:T(8,128)(2,1)S(1)} %shard_map.70.refs_0_, bf16[2,192,256]{2,1,0:T(8,128)(2,1)S(1)} %collective-permute-done.13.refs_1_, bf16[768,768]{1,0:T(8,128)(2,1)S(1)} %get-tuple-element.60.refs_2_.refs_1_, bf16[256,256]{1,0:T(8,128)(2,1)S(1)} %get-tuple-element.62.refs_3_.refs_2_, ...), custom_call_target="tpu_custom_call" | custom-call | flops 3000000 | bytes 9000 | tf_op jit(solution)/shard_map/pallas_call | solution.py:458
  38.6 0.5 %shard_map.73.refs_3_ = f32[256,768]{1,0:T(8,128)S(1)} custom-call(bf16[2,192,256]{2,1,0:T(8,128)(2,1)S(1)} %collective-permute-done.9.refs_0_, bf16[768,768]{1,0:T(8,128)(2,1)S(1)} %get-tuple-element.60.refs_2_.refs_1_, bf16[256,256]{1,0:T(8,128)(2,1)S(1)} %get-tuple-element.62.refs_3_.refs_2_, f32[256,768]{1,0:T(8,128)S(1)} %shard_map.72.refs_3_), custom_call_target="tpu_custom_call" | custom-call | flops 15000000512 | bytes 45000000 | tf_op jit(solution)/shard_map/pallas_call | solution.py:458
  39.1 1.2 %shard_map.74 = bf16[256,768]{1,0:T(8,128)(2,1)} custom-call(bf16[2,192,256]{2,1,0:T(8,128)(2,1)S(1)} %collective-permute-done.17.refs_0_, bf16[768,768]{1,0:T(8,128)(2,1)S(1)} %get-tuple-element.60.refs_2_.refs_1_, bf16[256,256]{1,0:T(8,128)(2,1)S(1)} %get-tuple-element.62.refs_3_.refs_2_, f32[256,768]{1,0:T(8,128)S(1)} %shard_map.73.refs_3_), custom_call_target="tpu_custom_call" | custom-call | flops 15000000512 | bytes 45000000 | tf_op jit(solution)/shard_map/pallas_call | solution.py:458
  (28 shorter events, 0.5 us)
Async XLA Ops:
  0.0 1.4 %copy-start.1 = (bf16[1,256,768]{2,1,0:T(8,128)(2,1)S(1)}, bf16[1,256,768]{2,1,0:T(8,128)(2,1)}, u32[]{:S(2)}) copy-start(bf16[1,256,768]{2,1,0:T(8,128)(2,1)} %param.6) | copy-start | bytes 1179652
  0.0 14.2 %copy-start.2 = (f32[768]{0:T(1024)S(1)}, f32[768]{0:T(1024)}, u32[]{:S(2)}) copy-start(f32[768]{0:T(1024)} %refs_2_.3) | copy-start | bytes 9220
  0.0 14.2 %copy-start.3 = (f32[768]{0:T(1024)S(1)}, f32[768]{0:T(1024)}, u32[]{:S(2)}) copy-start(f32[768]{0:T(1024)} %refs_3_.3) | copy-start | bytes 9220
  1.4 6.9 %collective-permute-start = (bf16[256,768]{1,0:T(8,128)(2,1)S(1)}, bf16[256,768]{1,0:T(8,128)(2,1)S(1)}, u32[]{:S(2)}, u32[]{:S(2)}) collective-permute-start(bf16[256,768]{1,0:T(8,128)(2,1)S(1)} %bitcast.2), channel_id=1, source_target_pairs={{0,4},{4,0},{8,12},{12,8},{16,20},{20,16},{24,28},{28,24},{1,5},{5... | collective-permute-start | bytes 1179656 | tf_op jit(solution)/shard_map/ppermute | solution.py:48
  1.9 12.3 %collective-permute-start.1 = (bf16[256,768]{1,0:T(8,128)(2,1)S(1)}, bf16[256,768]{1,0:T(8,128)(2,1)S(1)}, u32[]{:S(2)}, u32[]{:S(2)}) collective-permute-start(bf16[256,768]{1,0:T(8,128)(2,1)S(1)} %bitcast.3), channel_id=1, source_target_pairs={{0,8},{4,12},{8,0},{12,4},{16,24},{20,28},{24,16},{28,20},{1,9},{5... | collective-permute-start | bytes 1179656 | tf_op jit(solution)/shard_map/ppermute | solution.py:48
  4.5 11.0 %collective-permute-start.4 = (bf16[64,576]{1,0:T(8,128)(2,1)S(1)}, bf16[64,576]{1,0:T(8,128)(2,1)S(1)}, u32[]{:S(2)}, u32[]{:S(2)}) collective-permute-start(bf16[64,576]{1,0:T(8,128)(2,1)S(1)} %slice.9), channel_id=1, source_target_pairs={{0,2},{1,3},{2,0},{3,1},{4,6},{5,7},{6,4},{7,5},{8,10},{9,11},{10,... | collective-permute-start | bytes 221192 | tf_op jit(solution)/shard_map/ppermute | solution.py:335
  7.2 11.7 %collective-permute-start.3 = (bf16[128,576]{1,0:T(8,128)(2,1)S(1)}, bf16[128,576]{1,0:T(8,128)(2,1)S(1)}, u32[]{:S(2)}, u32[]{:S(2)}) collective-permute-start(bf16[128,576]{1,0:T(8,128)(2,1)S(1)} %slice.8), channel_id=1, source_target_pairs={{0,2},{1,3},{2,0},{3,1},{4,6},{5,7},{6,4},{7,5},{8,10},{9,11},{10,... | collective-permute-start | bytes 442376 | tf_op jit(solution)/shard_map/ppermute | solution.py:335
  8.2 8.8 %copy-start = (bf16[192,768]{1,0:T(8,128)(2,1)S(1)}, bf16[192,768]{1,0:T(8,128)(2,1)}, u32[]{:S(2)}) copy-start(bf16[192,768]{1,0:T(8,128)(2,1)} %refs_0_.3) | copy-start | bytes 884740
  8.3 15.7 %collective-permute-start.6 = (bf16[192,576]{1,0:T(8,128)(2,1)S(1)}, bf16[192,576]{1,0:T(8,128)(2,1)S(1)}, u32[]{:S(2)}, u32[]{:S(2)}) collective-permute-start(bf16[192,576]{1,0:T(8,128)(2,1)S(1)} %pad_maximum_fusion.refs_4_), channel_id=1, source_target_pairs={{0,1},{1,0},{2,3},{3,2},{4,5},{5,4},{6,7},{7,6},{8,9},{9,8},{10,11... | collective-permute-start | bytes 663560 | tf_op jit(solution)/shard_map/ppermute | solution.py:48
  14.2 4.7 %collective-permute-start.2 = (bf16[256,768]{1,0:T(8,128)(2,1)S(1)}, bf16[256,768]{1,0:T(8,128)(2,1)S(1)}, u32[]{:S(2)}, u32[]{:S(2)}) collective-permute-start(bf16[256,768]{1,0:T(8,128)(2,1)S(1)} %collective-permute-done.1.refs_0_), channel_id=1, source_target_pairs={{0,4},{4,0},{8,12},{12,8},{16,20},{20,16},{24,28},{28,24},{1,5},{5... | collective-permute-start | bytes 1179656 | tf_op jit(solution)/shard_map/ppermute | solution.py:48
  15.6 8.4 %collective-permute-start.7 = (bf16[64,576]{1,0:T(8,128)(2,1)S(1)}, bf16[64,576]{1,0:T(8,128)(2,1)S(1)}, u32[]{:S(2)}, u32[]{:S(2)}) collective-permute-start(bf16[64,576]{1,0:T(8,128)(2,1)S(1)} %collective-permute-done.4.refs_6_), channel_id=1, source_target_pairs={{0,16},{4,20},{8,24},{12,28},{16,0},{20,4},{24,8},{28,12},{1,17},{... | collective-permute-start | bytes 221192 | tf_op jit(solution)/shard_map/ppermute | solution.py:48
  18.9 6.8 %collective-permute-start.5 = (bf16[128,576]{1,0:T(8,128)(2,1)S(1)}, bf16[128,576]{1,0:T(8,128)(2,1)S(1)}, u32[]{:S(2)}, u32[]{:S(2)}) collective-permute-start(bf16[128,576]{1,0:T(8,128)(2,1)S(1)} %collective-permute-done.3.refs_7_), channel_id=1, source_target_pairs={{0,16},{4,20},{8,24},{12,28},{16,0},{20,4},{24,8},{28,12},{1,17},{... | collective-permute-start | bytes 442376 | tf_op jit(solution)/shard_map/ppermute | solution.py:48
  19.8 9.7 %collective-permute-start.11 = (bf16[96,768]{1,0:T(8,128)(2,1)S(1)}, bf16[96,768]{1,0:T(8,128)(2,1)S(1)}, u32[]{:S(2)}, u32[]{:S(2)}) collective-permute-start(bf16[96,768]{1,0:T(8,128)(2,1)S(1)} %constant_dynamic-slice_fusion), channel_id=1, source_target_pairs={{0,2},{1,3},{2,0},{3,1},{4,6},{5,7},{6,4},{7,5},{8,10},{9,11},{10,... | collective-permute-start | bytes 442376 | tf_op jit(solution)/shard_map/ppermute | solution.py:335
  23.0 8.6 %collective-permute-start.10 = (bf16[96,768]{1,0:T(8,128)(2,1)S(1)}, bf16[96,768]{1,0:T(8,128)(2,1)S(1)}, u32[]{:S(2)}, u32[]{:S(2)}) collective-permute-start(bf16[96,768]{1,0:T(8,128)(2,1)S(1)} %constant_dynamic-slice_fusion), channel_id=1, source_target_pairs={{0,1},{1,0},{2,3},{3,2},{4,5},{5,4},{6,7},{7,6},{8,9},{9,8},{10,11... | collective-permute-start | bytes 442376 | tf_op jit(solution)/shard_map/ppermute | solution.py:48
  26.3 4.2 %collective-permute-start.8 = (bf16[3,64,128]{2,1,0:T(8,128)(2,1)S(1)}, bf16[3,64,128]{2,1,0:T(8,128)(2,1)S(1)}, u32[]{:S(2)}, u32[]{:S(2)}) collective-permute-start(bf16[3,64,128]{2,1,0:T(8,128)(2,1)S(1)} %get-tuple-element.56.refs_5_), channel_id=1, source_target_pairs={{0,16},{4,20},{8,24},{12,28},{16,0},{20,4},{24,8},{28,12},{1,17},{... | collective-permute-start | bytes 147464 | tf_op jit(solution)/shard_map/ppermute | solution.py:48
  29.5 5.2 %collective-permute-start.12 = (bf16[96,768]{1,0:T(8,128)(2,1)S(1)}, bf16[96,768]{1,0:T(8,128)(2,1)S(1)}, u32[]{:S(2)}, u32[]{:S(2)}) collective-permute-start(bf16[96,768]{1,0:T(8,128)(2,1)S(1)} %collective-permute-done.11.refs_2_), channel_id=1, source_target_pairs={{0,16},{4,20},{8,24},{12,28},{16,0},{20,4},{24,8},{28,12},{1,17},{... | collective-permute-start | bytes 442376 | tf_op jit(solution)/shard_map/ppermute | solution.py:48
  31.0 6.5 %collective-permute-start.9 = (bf16[2,192,256]{2,1,0:T(8,128)(2,1)S(1)}, bf16[2,192,256]{2,1,0:T(8,128)(2,1)S(1)}, u32[]{:S(2)}, u32[]{:S(2)}) collective-permute-start(bf16[2,192,256]{2,1,0:T(8,128)(2,1)S(1)} %shard_map.69), channel_id=1, source_target_pairs={{0,8},{4,12},{8,0},{12,4},{16,24},{20,28},{24,16},{28,20},{1,9},{5... | collective-permute-start | bytes 589832 | tf_op jit(solution)/shard_map/ppermute | solution.py:48
  35.3 2.3 %collective-permute-start.13 = (bf16[2,192,256]{2,1,0:T(8,128)(2,1)S(1)}, bf16[2,192,256]{2,1,0:T(8,128)(2,1)S(1)}, u32[]{:S(2)}, u32[]{:S(2)}) collective-permute-start(bf16[2,192,256]{2,1,0:T(8,128)(2,1)S(1)} %shard_map.70.refs_0_), channel_id=1, source_target_pairs={{0,4},{4,0},{8,12},{12,8},{16,20},{20,16},{24,28},{28,24},{1,5},{5... | collective-permute-start | bytes 589832 | tf_op jit(solution)/shard_map/ppermute | solution.py:48
  35.3 1.6 %collective-permute-start.16 = (bf16[96,768]{1,0:T(8,128)(2,1)S(1)}, bf16[96,768]{1,0:T(8,128)(2,1)S(1)}, u32[]{:S(2)}, u32[]{:S(2)}) collective-permute-start(bf16[96,768]{1,0:T(8,128)(2,1)S(1)} %collective-permute-done.12.refs_3_), channel_id=1, source_target_pairs={{0,4},{4,0},{8,12},{12,8},{16,20},{20,16},{24,28},{28,24},{1,5},{5... | collective-permute-start | bytes 442376 | tf_op jit(solution)/shard_map/ppermute | solution.py:48
  35.8 1.4 %collective-permute-start.15 = (bf16[96,768]{1,0:T(8,128)(2,1)S(1)}, bf16[96,768]{1,0:T(8,128)(2,1)S(1)}, u32[]{:S(2)}, u32[]{:S(2)}) collective-permute-start(bf16[96,768]{1,0:T(8,128)(2,1)S(1)} %collective-permute-done.11.refs_2_), channel_id=1, source_target_pairs={{0,4},{4,0},{8,12},{12,8},{16,20},{20,16},{24,28},{28,24},{1,5},{5... | collective-permute-start | bytes 442376 | tf_op jit(solution)/shard_map/ppermute | solution.py:48
  35.9 1.5 %collective-permute-start.14 = (bf16[96,768]{1,0:T(8,128)(2,1)S(1)}, bf16[96,768]{1,0:T(8,128)(2,1)S(1)}, u32[]{:S(2)}, u32[]{:S(2)}) collective-permute-start(bf16[96,768]{1,0:T(8,128)(2,1)S(1)} %collective-permute-done.10.refs_1_), channel_id=1, source_target_pairs={{0,4},{4,0},{8,12},{12,8},{16,20},{20,16},{24,28},{28,24},{1,5},{5... | collective-permute-start | bytes 442376 | tf_op jit(solution)/shard_map/ppermute | solution.py:48
  37.6 1.5 %collective-permute-start.17 = (bf16[2,192,256]{2,1,0:T(8,128)(2,1)S(1)}, bf16[2,192,256]{2,1,0:T(8,128)(2,1)S(1)}, u32[]{:S(2)}, u32[]{:S(2)}) collective-permute-start(bf16[2,192,256]{2,1,0:T(8,128)(2,1)S(1)} %collective-permute-done.9.refs_0_), channel_id=1, source_target_pairs={{0,4},{4,0},{8,12},{12,8},{16,20},{20,16},{24,28},{28,24},{1,5},{5... | collective-permute-start | bytes 589832 | tf_op jit(solution)/shard_map/ppermute | solution.py:48

commit v12 on v11

--- a/solution.py
+++ b/solution.py
@@ -417,7 +417,7 @@
         ],
         n_scalar=1,
         n_in=SHARDS,
-        micros=5,
+        micros=1,
     )(valid_count, *qkv)
 
     half = SHARDS // 2
@@ -431,16 +431,16 @@
             micros=micros,
         )(valid_count, *qkv, *sent_parts, *stats)[0]
 
-    sending = finished(range(half, SHARDS), sents, 5)
-    out_blocks = list(out_fetched)
-    if shared:
-        out_blocks.append(flip(after(out_fetched[-1], stats[0]), "ctx", SHARDS))
-    staying = finished(range(half), [after(sents[0], sending, *out_blocks)] + sents[1:], 5)
+    sending = finished(range(half, SHARDS), sents, 1)
+    staying = finished(range(half), [after(sents[0], sending, out_fetched[-1])] + sents[1:], 0.01)
     far_part = flip(sending, "ctx", 2)
     pair_part = flip(staying, "ctx", 1)
+    out_blocks = list(out_fetched)
+    if shared:
+        out_blocks.append(flip(after(out_fetched[-1], stats[0]), "ctx", SHARDS))
     out_parts = [out_own] + out_blocks
     if shared:
-        out_parts += [flip(after(value, staying), "ctx", 1) for value in out_blocks]
+        out_parts += [flip(after(value, sending), "ctx", 1) for value in out_blocks]
     whole_out, order = call(
         lambda *refs: gather_body(n_mp, shared, *refs),
         [shape((width, width), bf16), shape((rows, rows), bf16)],
@@ -459,7 +459,7 @@
             lambda *refs, blocks=blocks: update_body(blocks, *refs),
             [out_shape],
             n_in=len(operands) + 3,
-            micros=5 if len(operands) == 1 else 0.001,
+            micros=0.001 if len(operands) == 1 else 0.001,
         )(*operands, whole_out, order, total)
     return total[None]
 

time: 40.5 us -> 39.5 us (0.975)
  starting transfers between devices: 17.8 us -> 17 us
    ppermute x15, starting transfers between devices: 11.6 us -> 10.8 us  [flip(): return near(lax.ppermute(value, axis, pairs))]
  transfers between devices with their start and end apart: 18 -> 18, of which waited for: 7 -> 7; matrix products, arithmetic and copies ran while one was open for 0% -> 0% of each run, Pallas kernels for 20% -> 21%
where the time goes in v12:
time: 39.5 us; the launch traced here: 39.4 us
  starting transfers between devices  17 us (43%)
  waiting for transfers between devices  10.7 us (27%)
  Pallas kernels  9.45 us (24%)
  local copies, waits for them, and re-layouts  1.3 us (3%)
  between operations  0.8 us (2%)
    ppermute x15, starting transfers between devices, flip(): return near(lax.ppermute(value, axis, pairs))  10.8 us
    ppermute x15, waiting for transfers between devices, flip(): return near(lax.ppermute(value, axis, pairs))  8.47 us
    ppermute x3, starting transfers between devices, fetch_far(): return near(lax.ppermute(value, ('ctx', 'mp'), pairs))  6.22 us
    pallas_call x3, Pallas kernels, local(): call(lambda *refs, blocks=blocks: update_body(blocks, *refs), [out_shape]...  2.36 us
    ppermute x3, waiting for transfers between devices, fetch_far(): return near(lax.ppermute(value, ('ctx', 'mp'), pairs))  2.23 us
    pallas_call x2, Pallas kernels, normalized(): call(norm_body, [blocks] * 2, n_in=4, micros=micros)(one, two, gain, bias)  1.87 us
    pallas_call x1, Pallas kernels, local(): call(lambda *refs: project_body((n_mp, shared, blocks[:-1]), *refs), [sha...  1.72 us
    pallas_call x1, Pallas kernels, local(): call(near_body, [shape((GROUP_HEADS, SHARDS, 1, rows), f32), shape((GROUP...  1.71 us
  transfers between devices with their start and end apart: 18, of which 7 were waited for; matrix products, arithmetic and copies ran while one was open for 0% of the time, Pallas kernels for 21%

profile of v12, /device:TPU:0, one launch (start us, length us, event | category | flops | bytes accessed | tf_op | source)
XLA Modules:
  0.0 39.4 jit_solution(8506353243927371057)
XLA Ops:
  0.0 1.3 %constant_dynamic-slice_fusion.3 = (bf16[192,192]{1,0:T(8,128)(2,1)S(1)}, bf16[192,192]{1,0:T(8,128)(2,1)S(1)}, bf16[192,192]{1,0:T(8,128)(2,1)S(1)}) fusion(bf16[192,2304]{1,0:T(8,128)(2,1)} %param.9, s32[]{:T(128)S(6)} %select_n.24, s32[]{:T(128)S(6)} %select_n.26, s32[]{:T(128)S(6)} %select_n.25), kind=kLoop, calls=%fused_computation.4 | loop fusion | bytes 442380 | tf_op jit(solution)/shard_map/dynamic_slice | solution.py:352
  1.3 0.1 pad_maximum_fusion.refs_4_
  1.4 0.5 %collective-permute-start = (bf16[256,768]{1,0:T(8,128)(2,1)S(1)}, bf16[256,768]{1,0:T(8,128)(2,1)S(1)}, u32[]{:S(2)}, u32[]{:S(2)}) collective-permute-start(bf16[256,768]{1,0:T(8,128)(2,1)S(1)} %bitcast.2), channel_id=1, source_target_pairs={{0,4},{4,0},{8,12},{12,8},{16,20},{20,16},{24,28},{28,24},{1,5},{5... | collective-permute-start | bytes 1179656 | tf_op jit(solution)/shard_map/ppermute | solution.py:48
  1.9 2.6 %collective-permute-start.1 = (bf16[256,768]{1,0:T(8,128)(2,1)S(1)}, bf16[256,768]{1,0:T(8,128)(2,1)S(1)}, u32[]{:S(2)}, u32[]{:S(2)}) collective-permute-start(bf16[256,768]{1,0:T(8,128)(2,1)S(1)} %bitcast.3), channel_id=1, source_target_pairs={{0,8},{4,12},{8,0},{12,4},{16,24},{20,28},{24,16},{28,20},{1,9},{5... | collective-permute-start | bytes 1179656 | tf_op jit(solution)/shard_map/ppermute | solution.py:48
  4.5 2.7 %collective-permute-start.4 = (bf16[64,576]{1,0:T(8,128)(2,1)S(1)}, bf16[64,576]{1,0:T(8,128)(2,1)S(1)}, u32[]{:S(2)}, u32[]{:S(2)}) collective-permute-start(bf16[64,576]{1,0:T(8,128)(2,1)S(1)} %slice.9), channel_id=1, source_target_pairs={{0,2},{1,3},{2,0},{3,1},{4,6},{5,7},{6,4},{7,5},{8,10},{9,11},{10,... | collective-permute-start | bytes 221192 | tf_op jit(solution)/shard_map/ppermute | solution.py:335
  7.2 0.4 %collective-permute-start.3 = (bf16[128,576]{1,0:T(8,128)(2,1)S(1)}, bf16[128,576]{1,0:T(8,128)(2,1)S(1)}, u32[]{:S(2)}, u32[]{:S(2)}) collective-permute-start(bf16[128,576]{1,0:T(8,128)(2,1)S(1)} %slice.8), channel_id=1, source_target_pairs={{0,2},{1,3},{2,0},{3,1},{4,6},{5,7},{6,4},{7,5},{8,10},{9,11},{10,... | collective-permute-start | bytes 442376 | tf_op jit(solution)/shard_map/ppermute | solution.py:335
  8.3 1.6 %collective-permute-start.6 = (bf16[192,576]{1,0:T(8,128)(2,1)S(1)}, bf16[192,576]{1,0:T(8,128)(2,1)S(1)}, u32[]{:S(2)}, u32[]{:S(2)}) collective-permute-start(bf16[192,576]{1,0:T(8,128)(2,1)S(1)} %pad_maximum_fusion.refs_4_), channel_id=1, source_target_pairs={{0,1},{1,0},{2,3},{3,2},{4,5},{5,4},{6,7},{7,6},{8,9},{9,8},{10,11... | collective-permute-start | bytes 663560 | tf_op jit(solution)/shard_map/ppermute | solution.py:48
  9.9 4.3 %collective-permute-done.1.refs_0_ = bf16[256,768]{1,0:T(8,128)(2,1)S(1)} collective-permute-done((bf16[256,768]{1,0:T(8,128)(2,1)S(1)}, bf16[256,768]{1,0:T(8,128)(2,1)S(1)}, u32[]{:S(2)}, u32[]{:S(2)}) %collective-permute-start.1) | collective-permute-done | bytes 393248 | tf_op jit(solution)/shard_map/ppermute | solution.py:48
  14.2 0.9 %shard_map.64 = (bf16[4,256,192]{2,1,0:T(8,128)(2,1)S(1)}, bf16[4,256,192]{2,1,0:T(8,128)(2,1)S(1)}) custom-call(bf16[256,768]{1,0:T(8,128)(2,1)S(1)} %bitcast.4, bf16[256,768]{1,0:T(8,128)(2,1)S(1)} %collective-permute-done.refs_1_, f32[768]{0:T(1024)S(1)} %copy-done.2, f32[768]{0:T(1024)S(1)} %copy-done.3), custom_call_target="tpu_custom_call" | custom-call | flops 3000000000 | bytes 9000000 | tf_op jit(solution)/shard_map/pallas_call | solution.py:371
  15.2 0.4 collective-permute-done.4.refs_6_
  15.6 1.5 %collective-permute-start.7 = (bf16[64,576]{1,0:T(8,128)(2,1)S(1)}, bf16[64,576]{1,0:T(8,128)(2,1)S(1)}, u32[]{:S(2)}, u32[]{:S(2)}) collective-permute-start(bf16[64,576]{1,0:T(8,128)(2,1)S(1)} %collective-permute-done.4.refs_6_), channel_id=1, source_target_pairs={{0,16},{4,20},{8,24},{12,28},{16,0},{20,4},{24,8},{28,12},{1,17},{... | collective-permute-start | bytes 221192 | tf_op jit(solution)/shard_map/ppermute | solution.py:48
  17.0 1.8 %collective-permute-done.3.refs_7_ = bf16[128,576]{1,0:T(8,128)(2,1)S(1)} collective-permute-done((bf16[128,576]{1,0:T(8,128)(2,1)S(1)}, bf16[128,576]{1,0:T(8,128)(2,1)S(1)}, u32[]{:S(2)}, u32[]{:S(2)}) %collective-permute-start.3) | collective-permute-done | bytes 147488 | tf_op jit(solution)/shard_map/ppermute | solution.py:335
  18.9 0.9 %shard_map.65 = (bf16[4,256,192]{2,1,0:T(8,128)(2,1)S(1)}, bf16[4,256,192]{2,1,0:T(8,128)(2,1)S(1)}) custom-call(bf16[256,768]{1,0:T(8,128)(2,1)S(1)} %collective-permute-done.1.refs_0_, bf16[256,768]{1,0:T(8,128)(2,1)S(1)} %collective-permute-done.2.refs_1_, f32[768]{0:T(1024)S(1)} %copy-done.2, f32[768]{0:T(1024)S(1)} %copy-done.3), custom_call_target="tpu_custom_call" | custom-call | flops 30000000 | bytes 90000 | tf_op jit(solution)/shard_map/pallas_call | solution.py:371
  19.8 3.2 %collective-permute-start.10 = (bf16[96,768]{1,0:T(8,128)(2,1)S(1)}, bf16[96,768]{1,0:T(8,128)(2,1)S(1)}, u32[]{:S(2)}, u32[]{:S(2)}) collective-permute-start(bf16[96,768]{1,0:T(8,128)(2,1)S(1)} %constant_dynamic-slice_fusion), channel_id=1, source_target_pairs={{0,2},{1,3},{2,0},{3,1},{4,6},{5,7},{6,4},{7,5},{8,10},{9,11},{10,... | collective-permute-start | bytes 442376 | tf_op jit(solution)/shard_map/ppermute | solution.py:335
  23.0 1.0 %collective-permute-start.12 = (bf16[96,768]{1,0:T(8,128)(2,1)S(1)}, bf16[96,768]{1,0:T(8,128)(2,1)S(1)}, u32[]{:S(2)}, u32[]{:S(2)}) collective-permute-start(bf16[96,768]{1,0:T(8,128)(2,1)S(1)} %constant_dynamic-slice_fusion), channel_id=1, source_target_pairs={{0,1},{1,0},{2,3},{3,2},{4,5},{5,4},{6,7},{7,6},{8,9},{9,8},{10,11... | collective-permute-start | bytes 442376 | tf_op jit(solution)/shard_map/ppermute | solution.py:48
  24.0 1.7 %shard_map.66 = (f32[256,576]{1,0:T(8,128)S(1)}, f32[256,576]{1,0:T(8,128)S(1)}, f32[256,576]{1,0:T(8,128)S(1)}, f32[256,576]{1,0:T(8,128)S(1)}) custom-call(bf16[4,256,192]{2,1,0:T(8,128)(2,1)S(1)} %get-tuple-element.35.refs_0_, bf16[4,256,192]{2,1,0:T(8,128)(2,1)S(1)} %get-tuple-element.36.refs_1_, bf16[4,256,192]{2,1,0:T(8,128)(2,1)S(1)} %get-tuple-element.37.refs_2_, ...), custom_call_target="tpu_custom_call" | custom-call | flops 3000000000 | bytes 9000000 | tf_op jit(solution)/shard_map/pallas_call | solution.py:397
  25.7 0.6 %shard_map.67 = (bf16[256,576]{1,0:T(8,128)(2,1)S(1)}, bf16[256,576]{1,0:T(8,128)(2,1)S(1)}, bf16[256,576]{1,0:T(8,128)(2,1)S(1)}, bf16[256,576]{1,0:T(8,128)(2,1)S(1)}, bf16[3,64,128]{2,1,0:T(8,128)(2,1)S(1)}) custom-call(bf16[4,256,192]{2,1,0:T(8,128)(2,1)S(1)} %get-tuple-element.35.refs_0_, bf16[4,256,192]{2,1,0:T(8,128)(2,1)S(1)} %get-tuple-element.36.refs_1_, ...), custom_call_target="tpu_custom_call" | custom-call | flops 3000000000 | bytes 9000000 | tf_op jit(solution)/shard_map/pallas_call | solution.py:403
  26.3 1.5 %collective-permute-start.8 = (bf16[3,64,128]{2,1,0:T(8,128)(2,1)S(1)}, bf16[3,64,128]{2,1,0:T(8,128)(2,1)S(1)}, u32[]{:S(2)}, u32[]{:S(2)}) collective-permute-start(bf16[3,64,128]{2,1,0:T(8,128)(2,1)S(1)} %get-tuple-element.55.refs_5_), channel_id=1, source_target_pairs={{0,16},{4,20},{8,24},{12,28},{16,0},{20,4},{24,8},{28,12},{1,17},{... | collective-permute-start | bytes 147464 | tf_op jit(solution)/shard_map/ppermute | solution.py:48
  27.8 1.7 %shard_map.68 = (f32[3,4,1,256]{3,2,1,0:T(1,128)S(1)}, f32[3,4,1,256]{3,2,1,0:T(1,128)S(1)}, f32[3,4,64,256]{3,2,1,0:T(8,128)S(1)}) custom-call(s32[1]{0:T(128)S(6)} %copy.7.valid_ref.refs_0_, bf16[256,576]{1,0:T(8,128)(2,1)S(1)} %get-tuple-element.46.refs_0_.refs_1_, bf16[256,576]{1,0:T(8,128)(2,1)S(1)} %get-tuple-element.47.refs_1_.refs_2_, ...), custom_call_target="tpu_custom_call" | custom-call | flops 3000000000 | bytes 9000000 | tf_op jit(solution)/shard_map/pallas_call | solution.py:411
  29.5 1.0 %collective-permute-start.13 = (bf16[96,768]{1,0:T(8,128)(2,1)S(1)}, bf16[96,768]{1,0:T(8,128)(2,1)S(1)}, u32[]{:S(2)}, u32[]{:S(2)}) collective-permute-start(bf16[96,768]{1,0:T(8,128)(2,1)S(1)} %collective-permute-done.10.refs_2_), channel_id=1, source_target_pairs={{0,16},{4,20},{8,24},{12,28},{16,0},{20,4},{24,8},{28,12},{1,17},{... | collective-permute-start | bytes 442376 | tf_op jit(solution)/shard_map/ppermute | solution.py:48
  30.5 0.5 %shard_map.69 = bf16[2,192,256]{2,1,0:T(8,128)(2,1)S(1)} custom-call(s32[1]{0:T(128)S(6)} %copy.7.valid_ref.refs_0_, bf16[256,576]{1,0:T(8,128)(2,1)S(1)} %get-tuple-element.46.refs_0_.refs_1_, bf16[256,576]{1,0:T(8,128)(2,1)S(1)} %get-tuple-element.47.refs_1_.refs_2_, bf16[256,576]{1,0:T(8,128)(2,1)S(1)} %get-tuple-element.48.refs_2_.refs_3_, ...), custom_call_target="tpu_custom_call" | custom-call | flops 3000000000 | bytes 9000000 | tf_op jit(solution)/shard_map/pallas_call | solution.py:426
  31.0 0.5 %collective-permute-start.9 = (bf16[2,192,256]{2,1,0:T(8,128)(2,1)S(1)}, bf16[2,192,256]{2,1,0:T(8,128)(2,1)S(1)}, u32[]{:S(2)}, u32[]{:S(2)}) collective-permute-start(bf16[2,192,256]{2,1,0:T(8,128)(2,1)S(1)} %shard_map.69), channel_id=1, source_target_pairs={{0,8},{4,12},{8,0},{12,4},{16,24},{20,28},{24,16},{28,20},{1,9},{5... | collective-permute-start | bytes 589832 | tf_op jit(solution)/shard_map/ppermute | solution.py:48
  31.5 0.5 %shard_map.70.refs_0_ = bf16[2,192,256]{2,1,0:T(8,128)(2,1)S(1)} custom-call(s32[1]{0:T(128)S(6)} %copy.7.valid_ref.refs_0_, bf16[256,576]{1,0:T(8,128)(2,1)S(1)} %get-tuple-element.46.refs_0_.refs_1_, bf16[256,576]{1,0:T(8,128)(2,1)S(1)} %get-tuple-element.47.refs_1_.refs_2_, bf16[256,576]{1,0:T(8,128)(2,1)S(1)} %get-tuple-element.48.refs_2_.refs_3_, ...), custom_call_target="tpu_custom_call" | custom-call | flops 30000000 | bytes 90000 | tf_op jit(solution)/shard_map/pallas_call | solution.py:426
  32.1 0.5 %collective-permute-start.15 = (bf16[96,768]{1,0:T(8,128)(2,1)S(1)}, bf16[96,768]{1,0:T(8,128)(2,1)S(1)}, u32[]{:S(2)}, u32[]{:S(2)}) collective-permute-start(bf16[96,768]{1,0:T(8,128)(2,1)S(1)} %collective-permute-done.10.refs_2_), channel_id=1, source_target_pairs={{0,4},{4,0},{8,12},{12,8},{16,20},{20,16},{24,28},{28,24},{1,5},{5... | collective-permute-start | bytes 442376 | tf_op jit(solution)/shard_map/ppermute | solution.py:48
  32.7 2.0 %collective-permute-done.13.refs_3_ = bf16[96,768]{1,0:T(8,128)(2,1)S(1)} collective-permute-done((bf16[96,768]{1,0:T(8,128)(2,1)S(1)}, bf16[96,768]{1,0:T(8,128)(2,1)S(1)}, u32[]{:S(2)}, u32[]{:S(2)}) %collective-permute-start.13) | collective-permute-done | bytes 147488 | tf_op jit(solution)/shard_map/ppermute | solution.py:48
  34.8 1.4 %collective-permute-done.16.refs_6_ = bf16[96,768]{1,0:T(8,128)(2,1)S(1)} collective-permute-done((bf16[96,768]{1,0:T(8,128)(2,1)S(1)}, bf16[96,768]{1,0:T(8,128)(2,1)S(1)}, u32[]{:S(2)}, u32[]{:S(2)}) %collective-permute-start.16) | collective-permute-done | bytes 147488 | tf_op jit(solution)/shard_map/ppermute | solution.py:48
  36.1 0.1 shard_map.71
  36.2 0.5 %collective-permute-done.9.refs_0_ = bf16[2,192,256]{2,1,0:T(8,128)(2,1)S(1)} collective-permute-done((bf16[2,192,256]{2,1,0:T(8,128)(2,1)S(1)}, bf16[2,192,256]{2,1,0:T(8,128)(2,1)S(1)}, u32[]{:S(2)}, u32[]{:S(2)}) %collective-permute-start.9) | collective-permute-done | bytes 196640 | tf_op jit(solution)/shard_map/ppermute | solution.py:48
  36.7 0.7 %shard_map.72.refs_3_ = f32[256,768]{1,0:T(8,128)S(1)} custom-call(bf16[2,192,256]{2,1,0:T(8,128)(2,1)S(1)} %shard_map.70.refs_0_, bf16[2,192,256]{2,1,0:T(8,128)(2,1)S(1)} %collective-permute-done.11.refs_1_, bf16[768,768]{1,0:T(8,128)(2,1)S(1)} %get-tuple-element.60.refs_2_.refs_1_, bf16[256,256]{1,0:T(8,128)(2,1)S(1)} %get-tuple-element.62.refs_3_.refs_2_, ...), custom_call_target="tpu_custom_call" | custom-call | flops 3000000 | bytes 9000 | tf_op jit(solution)/shard_map/pallas_call | solution.py:458
  37.5 0.5 %shard_map.73.refs_3_ = f32[256,768]{1,0:T(8,128)S(1)} custom-call(bf16[2,192,256]{2,1,0:T(8,128)(2,1)S(1)} %collective-permute-done.9.refs_0_, bf16[768,768]{1,0:T(8,128)(2,1)S(1)} %get-tuple-element.60.refs_2_.refs_1_, bf16[256,256]{1,0:T(8,128)(2,1)S(1)} %get-tuple-element.62.refs_3_.refs_2_, f32[256,768]{1,0:T(8,128)S(1)} %shard_map.72.refs_3_), custom_call_target="tpu_custom_call" | custom-call | flops 3000000 | bytes 9000 | tf_op jit(solution)/shard_map/pallas_call | solution.py:458
  37.9 0.3 collective-permute-done.17.refs_0_
  38.2 1.2 %shard_map.74 = bf16[256,768]{1,0:T(8,128)(2,1)} custom-call(bf16[2,192,256]{2,1,0:T(8,128)(2,1)S(1)} %collective-permute-done.17.refs_0_, bf16[768,768]{1,0:T(8,128)(2,1)S(1)} %get-tuple-element.60.refs_2_.refs_1_, bf16[256,256]{1,0:T(8,128)(2,1)S(1)} %get-tuple-element.62.refs_3_.refs_2_, f32[256,768]{1,0:T(8,128)S(1)} %shard_map.73.refs_3_), custom_call_target="tpu_custom_call" | custom-call | flops 3000000 | bytes 9000 | tf_op jit(solution)/shard_map/pallas_call | solution.py:458
  (28 shorter events, 0.2 us)
Async XLA Ops:
  0.0 1.4 %copy-start.1 = (bf16[1,256,768]{2,1,0:T(8,128)(2,1)S(1)}, bf16[1,256,768]{2,1,0:T(8,128)(2,1)}, u32[]{:S(2)}) copy-start(bf16[1,256,768]{2,1,0:T(8,128)(2,1)} %param.6) | copy-start | bytes 1179652
  0.0 14.2 %copy-start.2 = (f32[768]{0:T(1024)S(1)}, f32[768]{0:T(1024)}, u32[]{:S(2)}) copy-start(f32[768]{0:T(1024)} %refs_2_.3) | copy-start | bytes 9220
  0.0 14.2 %copy-start.3 = (f32[768]{0:T(1024)S(1)}, f32[768]{0:T(1024)}, u32[]{:S(2)}) copy-start(f32[768]{0:T(1024)} %refs_3_.3) | copy-start | bytes 9220
  1.4 6.9 %collective-permute-start = (bf16[256,768]{1,0:T(8,128)(2,1)S(1)}, bf16[256,768]{1,0:T(8,128)(2,1)S(1)}, u32[]{:S(2)}, u32[]{:S(2)}) collective-permute-start(bf16[256,768]{1,0:T(8,128)(2,1)S(1)} %bitcast.2), channel_id=1, source_target_pairs={{0,4},{4,0},{8,12},{12,8},{16,20},{20,16},{24,28},{28,24},{1,5},{5... | collective-permute-start | bytes 1179656 | tf_op jit(solution)/shard_map/ppermute | solution.py:48
  1.9 12.3 %collective-permute-start.1 = (bf16[256,768]{1,0:T(8,128)(2,1)S(1)}, bf16[256,768]{1,0:T(8,128)(2,1)S(1)}, u32[]{:S(2)}, u32[]{:S(2)}) collective-permute-start(bf16[256,768]{1,0:T(8,128)(2,1)S(1)} %bitcast.3), channel_id=1, source_target_pairs={{0,8},{4,12},{8,0},{12,4},{16,24},{20,28},{24,16},{28,20},{1,9},{5... | collective-permute-start | bytes 1179656 | tf_op jit(solution)/shard_map/ppermute | solution.py:48
  4.5 11.0 %collective-permute-start.4 = (bf16[64,576]{1,0:T(8,128)(2,1)S(1)}, bf16[64,576]{1,0:T(8,128)(2,1)S(1)}, u32[]{:S(2)}, u32[]{:S(2)}) collective-permute-start(bf16[64,576]{1,0:T(8,128)(2,1)S(1)} %slice.9), channel_id=1, source_target_pairs={{0,2},{1,3},{2,0},{3,1},{4,6},{5,7},{6,4},{7,5},{8,10},{9,11},{10,... | collective-permute-start | bytes 221192 | tf_op jit(solution)/shard_map/ppermute | solution.py:335
  7.2 11.7 %collective-permute-start.3 = (bf16[128,576]{1,0:T(8,128)(2,1)S(1)}, bf16[128,576]{1,0:T(8,128)(2,1)S(1)}, u32[]{:S(2)}, u32[]{:S(2)}) collective-permute-start(bf16[128,576]{1,0:T(8,128)(2,1)S(1)} %slice.8), channel_id=1, source_target_pairs={{0,2},{1,3},{2,0},{3,1},{4,6},{5,7},{6,4},{7,5},{8,10},{9,11},{10,... | collective-permute-start | bytes 442376 | tf_op jit(solution)/shard_map/ppermute | solution.py:335
  8.2 8.8 %copy-start = (bf16[192,768]{1,0:T(8,128)(2,1)S(1)}, bf16[192,768]{1,0:T(8,128)(2,1)}, u32[]{:S(2)}) copy-start(bf16[192,768]{1,0:T(8,128)(2,1)} %refs_0_.3) | copy-start | bytes 884740
  8.3 15.7 %collective-permute-start.6 = (bf16[192,576]{1,0:T(8,128)(2,1)S(1)}, bf16[192,576]{1,0:T(8,128)(2,1)S(1)}, u32[]{:S(2)}, u32[]{:S(2)}) collective-permute-start(bf16[192,576]{1,0:T(8,128)(2,1)S(1)} %pad_maximum_fusion.refs_4_), channel_id=1, source_target_pairs={{0,1},{1,0},{2,3},{3,2},{4,5},{5,4},{6,7},{7,6},{8,9},{9,8},{10,11... | collective-permute-start | bytes 663560 | tf_op jit(solution)/shard_map/ppermute | solution.py:48
  14.2 4.7 %collective-permute-start.2 = (bf16[256,768]{1,0:T(8,128)(2,1)S(1)}, bf16[256,768]{1,0:T(8,128)(2,1)S(1)}, u32[]{:S(2)}, u32[]{:S(2)}) collective-permute-start(bf16[256,768]{1,0:T(8,128)(2,1)S(1)} %collective-permute-done.1.refs_0_), channel_id=1, source_target_pairs={{0,4},{4,0},{8,12},{12,8},{16,20},{20,16},{24,28},{28,24},{1,5},{5... | collective-permute-start | bytes 1179656 | tf_op jit(solution)/shard_map/ppermute | solution.py:48
  15.6 8.4 %collective-permute-start.7 = (bf16[64,576]{1,0:T(8,128)(2,1)S(1)}, bf16[64,576]{1,0:T(8,128)(2,1)S(1)}, u32[]{:S(2)}, u32[]{:S(2)}) collective-permute-start(bf16[64,576]{1,0:T(8,128)(2,1)S(1)} %collective-permute-done.4.refs_6_), channel_id=1, source_target_pairs={{0,16},{4,20},{8,24},{12,28},{16,0},{20,4},{24,8},{28,12},{1,17},{... | collective-permute-start | bytes 221192 | tf_op jit(solution)/shard_map/ppermute | solution.py:48
  18.9 6.8 %collective-permute-start.5 = (bf16[128,576]{1,0:T(8,128)(2,1)S(1)}, bf16[128,576]{1,0:T(8,128)(2,1)S(1)}, u32[]{:S(2)}, u32[]{:S(2)}) collective-permute-start(bf16[128,576]{1,0:T(8,128)(2,1)S(1)} %collective-permute-done.3.refs_7_), channel_id=1, source_target_pairs={{0,16},{4,20},{8,24},{12,28},{16,0},{20,4},{24,8},{28,12},{1,17},{... | collective-permute-start | bytes 442376 | tf_op jit(solution)/shard_map/ppermute | solution.py:48
  19.8 9.7 %collective-permute-start.10 = (bf16[96,768]{1,0:T(8,128)(2,1)S(1)}, bf16[96,768]{1,0:T(8,128)(2,1)S(1)}, u32[]{:S(2)}, u32[]{:S(2)}) collective-permute-start(bf16[96,768]{1,0:T(8,128)(2,1)S(1)} %constant_dynamic-slice_fusion), channel_id=1, source_target_pairs={{0,2},{1,3},{2,0},{3,1},{4,6},{5,7},{6,4},{7,5},{8,10},{9,11},{10,... | collective-permute-start | bytes 442376 | tf_op jit(solution)/shard_map/ppermute | solution.py:335
  23.0 9.7 %collective-permute-start.12 = (bf16[96,768]{1,0:T(8,128)(2,1)S(1)}, bf16[96,768]{1,0:T(8,128)(2,1)S(1)}, u32[]{:S(2)}, u32[]{:S(2)}) collective-permute-start(bf16[96,768]{1,0:T(8,128)(2,1)S(1)} %constant_dynamic-slice_fusion), channel_id=1, source_target_pairs={{0,1},{1,0},{2,3},{3,2},{4,5},{5,4},{6,7},{7,6},{8,9},{9,8},{10,11... | collective-permute-start | bytes 442376 | tf_op jit(solution)/shard_map/ppermute | solution.py:48
  26.3 4.2 %collective-permute-start.8 = (bf16[3,64,128]{2,1,0:T(8,128)(2,1)S(1)}, bf16[3,64,128]{2,1,0:T(8,128)(2,1)S(1)}, u32[]{:S(2)}, u32[]{:S(2)}) collective-permute-start(bf16[3,64,128]{2,1,0:T(8,128)(2,1)S(1)} %get-tuple-element.55.refs_5_), channel_id=1, source_target_pairs={{0,16},{4,20},{8,24},{12,28},{16,0},{20,4},{24,8},{28,12},{1,17},{... | collective-permute-start | bytes 147464 | tf_op jit(solution)/shard_map/ppermute | solution.py:48
  29.5 5.2 %collective-permute-start.13 = (bf16[96,768]{1,0:T(8,128)(2,1)S(1)}, bf16[96,768]{1,0:T(8,128)(2,1)S(1)}, u32[]{:S(2)}, u32[]{:S(2)}) collective-permute-start(bf16[96,768]{1,0:T(8,128)(2,1)S(1)} %collective-permute-done.10.refs_2_), channel_id=1, source_target_pairs={{0,16},{4,20},{8,24},{12,28},{16,0},{20,4},{24,8},{28,12},{1,17},{... | collective-permute-start | bytes 442376 | tf_op jit(solution)/shard_map/ppermute | solution.py:48
  31.0 5.7 %collective-permute-start.9 = (bf16[2,192,256]{2,1,0:T(8,128)(2,1)S(1)}, bf16[2,192,256]{2,1,0:T(8,128)(2,1)S(1)}, u32[]{:S(2)}, u32[]{:S(2)}) collective-permute-start(bf16[2,192,256]{2,1,0:T(8,128)(2,1)S(1)} %shard_map.69), channel_id=1, source_target_pairs={{0,8},{4,12},{8,0},{12,4},{16,24},{20,28},{24,16},{28,20},{1,9},{5... | collective-permute-start | bytes 589832 | tf_op jit(solution)/shard_map/ppermute | solution.py:48
  32.1 4.7 %collective-permute-start.11 = (bf16[2,192,256]{2,1,0:T(8,128)(2,1)S(1)}, bf16[2,192,256]{2,1,0:T(8,128)(2,1)S(1)}, u32[]{:S(2)}, u32[]{:S(2)}) collective-permute-start(bf16[2,192,256]{2,1,0:T(8,128)(2,1)S(1)} %shard_map.70.refs_0_), channel_id=1, source_target_pairs={{0,4},{4,0},{8,12},{12,8},{16,20},{20,16},{24,28},{28,24},{1,5},{5... | collective-permute-start | bytes 589832 | tf_op jit(solution)/shard_map/ppermute | solution.py:48
  32.1 2.6 %collective-permute-start.15 = (bf16[96,768]{1,0:T(8,128)(2,1)S(1)}, bf16[96,768]{1,0:T(8,128)(2,1)S(1)}, u32[]{:S(2)}, u32[]{:S(2)}) collective-permute-start(bf16[96,768]{1,0:T(8,128)(2,1)S(1)} %collective-permute-done.10.refs_2_), channel_id=1, source_target_pairs={{0,4},{4,0},{8,12},{12,8},{16,20},{20,16},{24,28},{28,24},{1,5},{5... | collective-permute-start | bytes 442376 | tf_op jit(solution)/shard_map/ppermute | solution.py:48
  32.6 2.1 %collective-permute-start.14 = (bf16[96,768]{1,0:T(8,128)(2,1)S(1)}, bf16[96,768]{1,0:T(8,128)(2,1)S(1)}, u32[]{:S(2)}, u32[]{:S(2)}) collective-permute-start(bf16[96,768]{1,0:T(8,128)(2,1)S(1)} %collective-permute-done.12.refs_1_), channel_id=1, source_target_pairs={{0,4},{4,0},{8,12},{12,8},{16,20},{20,16},{24,28},{28,24},{1,5},{5... | collective-permute-start | bytes 442376 | tf_op jit(solution)/shard_map/ppermute | solution.py:48
  34.7 1.4 %collective-permute-start.16 = (bf16[96,768]{1,0:T(8,128)(2,1)S(1)}, bf16[96,768]{1,0:T(8,128)(2,1)S(1)}, u32[]{:S(2)}, u32[]{:S(2)}) collective-permute-start(bf16[96,768]{1,0:T(8,128)(2,1)S(1)} %collective-permute-done.13.refs_3_), channel_id=1, source_target_pairs={{0,4},{4,0},{8,12},{12,8},{16,20},{20,16},{24,28},{28,24},{1,5},{5... | collective-permute-start | bytes 442376 | tf_op jit(solution)/shard_map/ppermute | solution.py:48
  36.7 1.4 %collective-permute-start.17 = (bf16[2,192,256]{2,1,0:T(8,128)(2,1)S(1)}, bf16[2,192,256]{2,1,0:T(8,128)(2,1)S(1)}, u32[]{:S(2)}, u32[]{:S(2)}) collective-permute-start(bf16[2,192,256]{2,1,0:T(8,128)(2,1)S(1)} %collective-permute-done.9.refs_0_), channel_id=1, source_target_pairs={{0,4},{4,0},{8,12},{12,8},{16,20},{20,16},{24,28},{28,24},{1,5},{5... | collective-permute-start | bytes 589832 | tf_op jit(solution)/shard_map/ppermute | solution.py:48

commit v13 on v12

--- a/solution.py
+++ b/solution.py
@@ -305,14 +305,27 @@
     member, group = group_indices()
     origin = sources(n_mp, group % 2, shared)
     rows = part_refs[0].shape[0]
-    starts = [source * rows for source in origin]
-    if shared:
-        core, half = member % 2, rows // 2
-        starts = starts[:1] + [
-            start + side * half for side in (core, 1 - core) for start in starts[1:]
-        ]
-    for ref, start in zip(part_refs, starts):
-        out_ref[pl.ds(pl.multiple_of(start, 16), ref.shape[0]), :] = ref[...]
+
+    def put(ref, source):
+        out_ref[pl.ds(pl.multiple_of(source * rows, 16), rows), :] = ref[...]
+
+    if shared:
+        own_ref, fetched_ref, paired_ref, swapped_ref, passed_ref = part_refs
+        even = member % 2 == 0
+        put(own_ref, origin[0])
+        put(fetched_ref, jnp.where(even, origin[1], origin[2]))
+        put(paired_ref, jnp.where(even, origin[2], origin[1]))
+
+        @pl.when(even)
+        def _():
+            put(passed_ref, origin[3])
+
+        @pl.when(jnp.logical_not(even))
+        def _():
+            put(swapped_ref, origin[3])
+    else:
+        for ref, source in zip(part_refs, origin):
+            put(ref, source)
 
 
 def update_body(blocks, *refs):
@@ -327,12 +340,15 @@
     out_ref[...] = update.astype(out_ref.dtype)
 
 
-def fetch_far(value, turns):
+def fetch_from(value, apart):
     n_mp, n_ctx = lax.axis_size("mp"), lax.axis_size("ctx")
-    pairs = [
-        (c * n_mp + z, c * n_mp + (z ^ (2 + turns(c)))) for c in range(n_ctx) for z in range(n_mp)
-    ]
+    pairs = [(c * n_mp + z, c * n_mp + (z ^ apart(c))) for c in range(n_ctx) for z in range(n_mp)]
     return near(lax.ppermute(value, ("ctx", "mp"), pairs))
+
+
+def odd_flip(value, mask):
+    pairs = [(c, c ^ mask) for c in range(lax.axis_size("ctx")) if c % 2]
+    return near(lax.ppermute(value, "ctx", pairs))
 
 
 def local(tile_embeds, norm_gain, norm_bias, w_qkv, w_out, valid_count):
@@ -353,10 +369,10 @@
 
     chosen = jnp.concatenate([columns(part) for part in range(3)], axis=1)
     mine = near(chosen)
-    parity = lambda c: c // SHARDS % 2
+    far = lambda c: 2 + c // SHARDS % 2
     cut = weight_rows // 3
     if shared:
-        pieces = [fetch_far(near(part), parity) for part in (chosen[:cut], chosen[cut:])]
+        pieces = [fetch_from(near(part), far) for part in (chosen[:cut], chosen[cut:])]
 
     x_own = near(x)
     x_pair = flip(after(x, mine), "ctx", 1)
@@ -384,15 +400,12 @@
     normed += normalized(x_far, x_last, 0.01)
 
     out_own = near(w_out)
-    out_weight = w_out
-    if shared:
-        size = weight_rows // 2
-        out_weight = lax.dynamic_slice(w_out, (member % 2 * size, 0), (size, width))
-    out_weight = after(near(out_weight), normed[2])
-    if shared:
-        out_fetched = [flip(out_weight, "mp", 1), fetch_far(out_weight, parity)]
+    out_weight = after(out_own, normed[2])
+    if shared:
+        fetched = fetch_from(out_weight, lambda c: far(c) if c % 2 else 1)
+        out_parts = [out_own, fetched]
     else:
-        out_fetched = [flip(out_weight, "mp", apart) for apart in range(1, n_mp)]
+        out_parts = [out_own] + [flip(out_weight, "mp", apart) for apart in range(1, n_mp)]
 
     partial = call(
         lambda *refs: project_body((n_mp, shared, blocks[:-1]), *refs),
@@ -432,15 +445,13 @@
         )(valid_count, *qkv, *sent_parts, *stats)[0]
 
     sending = finished(range(half, SHARDS), sents, 1)
-    staying = finished(range(half), [after(sents[0], sending, out_fetched[-1])] + sents[1:], 0.01)
+    staying = finished(range(half), [after(sents[0], sending, out_parts[1])] + sents[1:], 0.01)
     far_part = flip(sending, "ctx", 2)
     pair_part = flip(staying, "ctx", 1)
-    out_blocks = list(out_fetched)
-    if shared:
-        out_blocks.append(flip(after(out_fetched[-1], stats[0]), "ctx", SHARDS))
-    out_parts = [out_own] + out_blocks
-    if shared:
-        out_parts += [flip(after(value, sending), "ctx", 1) for value in out_blocks]
+    if shared:
+        swapped = odd_flip(after(fetched, stats[0]), SHARDS)
+        paired = flip(after(fetched, sending), "ctx", 1)
+        out_parts += [paired, swapped, odd_flip(after(swapped, sending), 1)]
     whole_out, order = call(
         lambda *refs: gather_body(n_mp, shared, *refs),
         [shape((width, width), bf16), shape((rows, rows), bf16)],

time: 39.5 us -> 55 us (1.39)
  waiting for transfers between devices: 10.7 us -> 21.1 us
  starting transfers between devices: 17 us -> 22.1 us
    ppermute x3 -> x5, waiting for transfers between devices: 2.23 us -> 10.1 us  [the longest x3 10.1 us: fetch_from(): return near(lax.ppermute(value, ('ctx', 'mp'), pairs))]
    ppermute x15 -> x11, starting transfers between devices: 10.8 us -> 14.8 us  [flip(): return near(lax.ppermute(value, axis, pairs))]
    ppermute x15 -> x11, waiting for transfers between devices: 8.47 us -> 11.1 us  [flip(): return near(lax.ppermute(value, axis, pairs))]
    ppermute x3 -> x5, starting transfers between devices: 6.22 us -> 7.2 us  [the longest x3 5.25 us: fetch_from(): return near(lax.ppermute(value, ('ctx', 'mp'), pairs))]
  transfers between devices with their start and end apart: 18 -> 16, of which waited for: 7 -> 7; matrix products, arithmetic and copies ran while one was open for 0% -> 0% of each run, Pallas kernels for 21% -> 15%
where the time goes in v13:
time: 55 us; the launch traced here: 54.8 us
  starting transfers between devices  22.1 us (40%)
  waiting for transfers between devices  21.1 us (38%)
  Pallas kernels  9.44 us (17%)
  local copies, waits for them, and re-layouts  1.29 us (2%)
  between operations  0.8 us (1%)
    ppermute x11, starting transfers between devices, flip(): return near(lax.ppermute(value, axis, pairs))  14.8 us
    ppermute x11, waiting for transfers between devices, flip(): return near(lax.ppermute(value, axis, pairs))  11.1 us
    ppermute x3, waiting for transfers between devices, fetch_from(): return near(lax.ppermute(value, ('ctx', 'mp'), pairs))  10.1 us
    ppermute x3, starting transfers between devices, fetch_from(): return near(lax.ppermute(value, ('ctx', 'mp'), pairs))  5.25 us
    pallas_call x3, Pallas kernels, local(): call(lambda *refs, blocks=blocks: update_body(blocks, *refs), [out_shape]...  2.35 us
    ppermute x2, starting transfers between devices, odd_flip(): return near(lax.ppermute(value, 'ctx', pairs))  1.95 us
    pallas_call x2, Pallas kernels, normalized(): call(norm_body, [blocks] * 2, n_in=4, micros=micros)(one, two, gain, bias)  1.87 us
    pallas_call x1, Pallas kernels, local(): call(lambda *refs: project_body((n_mp, shared, blocks[:-1]), *refs), [sha...  1.72 us
  transfers between devices with their start and end apart: 16, of which 7 were waited for; matrix products, arithmetic and copies ran while one was open for 0% of the time, Pallas kernels for 15%

profile of v13, /device:TPU:0, one launch (start us, length us, event | category | flops | bytes accessed | tf_op | source)
XLA Modules:
  0.0 54.8 jit_solution(6012616188025943430)
XLA Ops:
  0.0 1.3 %constant_dynamic-slice_fusion.2 = (bf16[192,192]{1,0:T(8,128)(2,1)S(1)}, bf16[192,192]{1,0:T(8,128)(2,1)S(1)}, bf16[192,192]{1,0:T(8,128)(2,1)S(1)}) fusion(bf16[192,2304]{1,0:T(8,128)(2,1)} %param.9, s32[]{:T(128)S(6)} %select_n.17, s32[]{:T(128)S(6)} %select_n.19, s32[]{:T(128)S(6)} %select_n.18), kind=kLoop, calls=%fused_computation.3 | loop fusion | bytes 442380 | tf_op jit(solution)/shard_map/dynamic_slice | solution.py:368
  1.3 0.1 pad_maximum_fusion.refs_4_
  1.4 3.0 %collective-permute-start.1 = (bf16[256,768]{1,0:T(8,128)(2,1)S(1)}, bf16[256,768]{1,0:T(8,128)(2,1)S(1)}, u32[]{:S(2)}, u32[]{:S(2)}) collective-permute-start(bf16[256,768]{1,0:T(8,128)(2,1)S(1)} %bitcast.2), channel_id=1, source_target_pairs={{0,8},{4,12},{8,0},{12,4},{16,24},{20,28},{24,16},{28,20},{1,9},{5... | collective-permute-start | bytes 1179656 | tf_op jit(solution)/shard_map/ppermute | solution.py:48
  4.4 9.1 %collective-permute-done.1.refs_0_ = bf16[256,768]{1,0:T(8,128)(2,1)S(1)} collective-permute-done((bf16[256,768]{1,0:T(8,128)(2,1)S(1)}, bf16[256,768]{1,0:T(8,128)(2,1)S(1)}, u32[]{:S(2)}, u32[]{:S(2)}) %collective-permute-start.1) | collective-permute-done | bytes 393248 | tf_op jit(solution)/shard_map/ppermute | solution.py:48
  13.5 2.9 %collective-permute-start.4 = (bf16[64,576]{1,0:T(8,128)(2,1)S(1)}, bf16[64,576]{1,0:T(8,128)(2,1)S(1)}, u32[]{:S(2)}, u32[]{:S(2)}) collective-permute-start(bf16[64,576]{1,0:T(8,128)(2,1)S(1)} %slice.9), channel_id=1, source_target_pairs={{0,2},{1,3},{2,0},{3,1},{4,6},{5,7},{6,4},{7,5},{8,10},{9,11},{10,... | collective-permute-start | bytes 221192 | tf_op jit(solution)/shard_map/ppermute | solution.py:346
  16.5 0.1 collective-permute-start.3
  16.6 1.8 %collective-permute-start.6 = (bf16[192,576]{1,0:T(8,128)(2,1)S(1)}, bf16[192,576]{1,0:T(8,128)(2,1)S(1)}, u32[]{:S(2)}, u32[]{:S(2)}) collective-permute-start(bf16[192,576]{1,0:T(8,128)(2,1)S(1)} %pad_maximum_fusion.refs_4_), channel_id=1, source_target_pairs={{0,1},{1,0},{2,3},{3,2},{4,5},{5,4},{6,7},{7,6},{8,9},{9,8},{10,11... | collective-permute-start | bytes 663560 | tf_op jit(solution)/shard_map/ppermute | solution.py:48
  18.5 0.9 %shard_map.64 = (bf16[4,256,192]{2,1,0:T(8,128)(2,1)S(1)}, bf16[4,256,192]{2,1,0:T(8,128)(2,1)S(1)}) custom-call(bf16[256,768]{1,0:T(8,128)(2,1)S(1)} %bitcast.4, bf16[256,768]{1,0:T(8,128)(2,1)S(1)} %collective-permute-done.refs_1_, f32[768]{0:T(1024)S(1)} %copy-done.2, f32[768]{0:T(1024)S(1)} %copy-done.3), custom_call_target="tpu_custom_call" | custom-call | flops 3000000000 | bytes 9000000 | tf_op jit(solution)/shard_map/pallas_call | solution.py:387
  19.4 5.2 %collective-permute-done.4.refs_6_ = bf16[64,576]{1,0:T(8,128)(2,1)S(1)} collective-permute-done((bf16[64,576]{1,0:T(8,128)(2,1)S(1)}, bf16[64,576]{1,0:T(8,128)(2,1)S(1)}, u32[]{:S(2)}, u32[]{:S(2)}) %collective-permute-start.4) | collective-permute-done | bytes 73760 | tf_op jit(solution)/shard_map/ppermute | solution.py:346
  25.3 3.2 %collective-permute-done.3.refs_7_ = bf16[128,576]{1,0:T(8,128)(2,1)S(1)} collective-permute-done((bf16[128,576]{1,0:T(8,128)(2,1)S(1)}, bf16[128,576]{1,0:T(8,128)(2,1)S(1)}, u32[]{:S(2)}, u32[]{:S(2)}) %collective-permute-start.3) | collective-permute-done | bytes 147488 | tf_op jit(solution)/shard_map/ppermute | solution.py:346
  28.5 0.9 %shard_map.65 = (bf16[4,256,192]{2,1,0:T(8,128)(2,1)S(1)}, bf16[4,256,192]{2,1,0:T(8,128)(2,1)S(1)}) custom-call(bf16[256,768]{1,0:T(8,128)(2,1)S(1)} %collective-permute-done.1.refs_0_, bf16[256,768]{1,0:T(8,128)(2,1)S(1)} %collective-permute-done.2.refs_1_, f32[768]{0:T(1024)S(1)} %copy-done.2, f32[768]{0:T(1024)S(1)} %copy-done.3), custom_call_target="tpu_custom_call" | custom-call | flops 30000000 | bytes 90000 | tf_op jit(solution)/shard_map/pallas_call | solution.py:387
  29.4 2.2 %collective-permute-start.10 = (bf16[192,768]{1,0:T(8,128)(2,1)S(1)}, bf16[192,768]{1,0:T(8,128)(2,1)S(1)}, u32[]{:S(2)}, u32[]{:S(2)}) collective-permute-start(bf16[192,768]{1,0:T(8,128)(2,1)S(1)} %copy-done.1), channel_id=1, source_target_pairs={{0,1},{1,0},{2,3},{3,2},{4,6},{5,7},{6,4},{7,5},{8,9},{9,8},{10,11... | collective-permute-start | bytes 884744 | tf_op jit(solution)/shard_map/ppermute | solution.py:346
  31.6 1.7 %shard_map.66 = (f32[256,576]{1,0:T(8,128)S(1)}, f32[256,576]{1,0:T(8,128)S(1)}, f32[256,576]{1,0:T(8,128)S(1)}, f32[256,576]{1,0:T(8,128)S(1)}) custom-call(bf16[4,256,192]{2,1,0:T(8,128)(2,1)S(1)} %get-tuple-element.34.refs_0_, bf16[4,256,192]{2,1,0:T(8,128)(2,1)S(1)} %get-tuple-element.35.refs_1_, bf16[4,256,192]{2,1,0:T(8,128)(2,1)S(1)} %get-tuple-element.36.refs_2_, ...), custom_call_target="tpu_custom_call" | custom-call | flops 3000000000 | bytes 9000000 | tf_op jit(solution)/shard_map/pallas_call | solution.py:410
  33.3 1.0 %collective-permute-done.5.refs_4_ = bf16[128,576]{1,0:T(8,128)(2,1)S(1)} collective-permute-done((bf16[128,576]{1,0:T(8,128)(2,1)S(1)}, bf16[128,576]{1,0:T(8,128)(2,1)S(1)}, u32[]{:S(2)}, u32[]{:S(2)}) %collective-permute-start.5) | collective-permute-done | bytes 147488 | tf_op jit(solution)/shard_map/ppermute | solution.py:48
  34.4 0.6 %shard_map.67 = (bf16[256,576]{1,0:T(8,128)(2,1)S(1)}, bf16[256,576]{1,0:T(8,128)(2,1)S(1)}, bf16[256,576]{1,0:T(8,128)(2,1)S(1)}, bf16[256,576]{1,0:T(8,128)(2,1)S(1)}, bf16[3,64,128]{2,1,0:T(8,128)(2,1)S(1)}) custom-call(bf16[4,256,192]{2,1,0:T(8,128)(2,1)S(1)} %get-tuple-element.34.refs_0_, bf16[4,256,192]{2,1,0:T(8,128)(2,1)S(1)} %get-tuple-element.35.refs_1_, ...), custom_call_target="tpu_custom_call" | custom-call | flops 3000000000 | bytes 9000000 | tf_op jit(solution)/shard_map/pallas_call | solution.py:416
  35.0 0.3 collective-permute-start.8
  35.3 1.7 %shard_map.68 = (f32[3,4,1,256]{3,2,1,0:T(1,128)S(1)}, f32[3,4,1,256]{3,2,1,0:T(1,128)S(1)}, f32[3,4,64,256]{3,2,1,0:T(8,128)S(1)}) custom-call(s32[1]{0:T(128)S(6)} %copy.7.valid_ref.refs_0_, bf16[256,576]{1,0:T(8,128)(2,1)S(1)} %get-tuple-element.45.refs_0_.refs_1_, bf16[256,576]{1,0:T(8,128)(2,1)S(1)} %get-tuple-element.46.refs_1_.refs_2_, ...), custom_call_target="tpu_custom_call" | custom-call | flops 3000000000 | bytes 9000000 | tf_op jit(solution)/shard_map/pallas_call | solution.py:424
  37.0 1.7 %collective-permute-done.10.refs_1_ = bf16[192,768]{1,0:T(8,128)(2,1)S(1)} collective-permute-done((bf16[192,768]{1,0:T(8,128)(2,1)S(1)}, bf16[192,768]{1,0:T(8,128)(2,1)S(1)}, u32[]{:S(2)}, u32[]{:S(2)}) %collective-permute-start.10) | collective-permute-done | bytes 294944 | tf_op jit(solution)/shard_map/ppermute | solution.py:346
  38.7 0.7 %collective-permute-start.13 = (bf16[192,768]{1,0:T(8,128)(2,1)S(1)}, bf16[192,768]{1,0:T(8,128)(2,1)S(1)}, u32[]{:S(2)}, u32[]{:S(2)}) collective-permute-start(bf16[192,768]{1,0:T(8,128)(2,1)S(1)} %collective-permute-done.10.refs_1_), channel_id=1, source_target_pairs={{4,20},{12,28},{20,4},{28,12},{5,21},{13,29},{21,5},{29,13},{6,22}... | collective-permute-start | bytes 884744 | tf_op jit(solution)/shard_map/ppermute | solution.py:351
  39.4 0.5 shard_map.69
  39.9 3.2 %collective-permute-start.12 = (bf16[192,768]{1,0:T(8,128)(2,1)S(1)}, bf16[192,768]{1,0:T(8,128)(2,1)S(1)}, u32[]{:S(2)}, u32[]{:S(2)}) collective-permute-start(bf16[192,768]{1,0:T(8,128)(2,1)S(1)} %collective-permute-done.10.refs_1_), channel_id=1, source_target_pairs={{0,4},{4,0},{8,12},{12,8},{16,20},{20,16},{24,28},{28,24},{1,5},{5... | collective-permute-start | bytes 884744 | tf_op jit(solution)/shard_map/ppermute | solution.py:48
  43.1 1.3 %collective-permute-start.14 = (bf16[192,768]{1,0:T(8,128)(2,1)S(1)}, bf16[192,768]{1,0:T(8,128)(2,1)S(1)}, u32[]{:S(2)}, u32[]{:S(2)}) collective-permute-start(bf16[192,768]{1,0:T(8,128)(2,1)S(1)} %collective-permute-done.13.refs_3_), channel_id=1, source_target_pairs={{4,0},{12,8},{20,16},{28,24},{5,1},{13,9},{21,17},{29,25},{6,2},{1... | collective-permute-start | bytes 884744 | tf_op jit(solution)/shard_map/ppermute | solution.py:351
  44.4 1.5 %collective-permute-start.9 = (bf16[2,192,256]{2,1,0:T(8,128)(2,1)S(1)}, bf16[2,192,256]{2,1,0:T(8,128)(2,1)S(1)}, u32[]{:S(2)}, u32[]{:S(2)}) collective-permute-start(bf16[2,192,256]{2,1,0:T(8,128)(2,1)S(1)} %shard_map.69), channel_id=1, source_target_pairs={{0,8},{4,12},{8,0},{12,4},{16,24},{20,28},{24,16},{28,20},{1,9},{5... | collective-permute-start | bytes 589832 | tf_op jit(solution)/shard_map/ppermute | solution.py:48
  45.9 0.5 shard_map.70.refs_0_
  46.4 3.3 %collective-permute-start.11 = (bf16[2,192,256]{2,1,0:T(8,128)(2,1)S(1)}, bf16[2,192,256]{2,1,0:T(8,128)(2,1)S(1)}, u32[]{:S(2)}, u32[]{:S(2)}) collective-permute-start(bf16[2,192,256]{2,1,0:T(8,128)(2,1)S(1)} %shard_map.70.refs_0_), channel_id=1, source_target_pairs={{0,4},{4,0},{8,12},{12,8},{16,20},{20,16},{24,28},{28,24},{1,5},{5... | collective-permute-start | bytes 589832 | tf_op jit(solution)/shard_map/ppermute | solution.py:48
  49.7 0.1 shard_map.71
  49.8 0.2 collective-permute-done.9.refs_0_
  50.1 0.7 %collective-permute-done.11.refs_1_ = bf16[2,192,256]{2,1,0:T(8,128)(2,1)S(1)} collective-permute-done((bf16[2,192,256]{2,1,0:T(8,128)(2,1)S(1)}, bf16[2,192,256]{2,1,0:T(8,128)(2,1)S(1)}, u32[]{:S(2)}, u32[]{:S(2)}) %collective-permute-start.11) | collective-permute-done | bytes 196640 | tf_op jit(solution)/shard_map/ppermute | solution.py:48
  50.8 1.7 %collective-permute-start.15 = (bf16[2,192,256]{2,1,0:T(8,128)(2,1)S(1)}, bf16[2,192,256]{2,1,0:T(8,128)(2,1)S(1)}, u32[]{:S(2)}, u32[]{:S(2)}) collective-permute-start(bf16[2,192,256]{2,1,0:T(8,128)(2,1)S(1)} %collective-permute-done.9.refs_0_), channel_id=1, source_target_pairs={{0,4},{4,0},{8,12},{12,8},{16,20},{20,16},{24,28},{28,24},{1,5},{5... | collective-permute-start | bytes 589832 | tf_op jit(solution)/shard_map/ppermute | solution.py:48
  52.5 0.7 %shard_map.72.refs_3_ = f32[256,768]{1,0:T(8,128)S(1)} custom-call(bf16[2,192,256]{2,1,0:T(8,128)(2,1)S(1)} %shard_map.70.refs_0_, bf16[2,192,256]{2,1,0:T(8,128)(2,1)S(1)} %collective-permute-done.11.refs_1_, bf16[768,768]{1,0:T(8,128)(2,1)S(1)} %get-tuple-element.58.refs_2_.refs_1_, bf16[256,256]{1,0:T(8,128)(2,1)S(1)} %get-tuple-element.60.refs_3_.refs_2_, ...), custom_call_target="tpu_custom_call" | custom-call | flops 3000000 | bytes 9000 | tf_op jit(solution)/shard_map/pallas_call | solution.py:469
  53.2 0.5 shard_map.73.refs_3_
  53.6 1.2 %shard_map.74 = bf16[256,768]{1,0:T(8,128)(2,1)} custom-call(bf16[2,192,256]{2,1,0:T(8,128)(2,1)S(1)} %collective-permute-done.15.refs_0_, bf16[768,768]{1,0:T(8,128)(2,1)S(1)} %get-tuple-element.58.refs_2_.refs_1_, bf16[256,256]{1,0:T(8,128)(2,1)S(1)} %get-tuple-element.60.refs_3_.refs_2_, f32[256,768]{1,0:T(8,128)S(1)} %shard_map.73.refs_3_), custom_call_target="tpu_custom_call" | custom-call | flops 3000000 | bytes 9000 | tf_op jit(solution)/shard_map/pallas_call | solution.py:469
  (23 shorter events, 0.1 us)
Async XLA Ops:
  0.0 1.4 %copy-start = (bf16[1,256,768]{2,1,0:T(8,128)(2,1)S(1)}, bf16[1,256,768]{2,1,0:T(8,128)(2,1)}, u32[]{:S(2)}) copy-start(bf16[1,256,768]{2,1,0:T(8,128)(2,1)} %param.6) | copy-start | bytes 1179652
  0.0 18.5 %copy-start.2 = (f32[768]{0:T(1024)S(1)}, f32[768]{0:T(1024)}, u32[]{:S(2)}) copy-start(f32[768]{0:T(1024)} %refs_2_.3) | copy-start | bytes 9220
  0.0 18.5 %copy-start.3 = (f32[768]{0:T(1024)S(1)}, f32[768]{0:T(1024)}, u32[]{:S(2)}) copy-start(f32[768]{0:T(1024)} %refs_3_.3) | copy-start | bytes 9220
  1.4 12.1 %collective-permute-start.1 = (bf16[256,768]{1,0:T(8,128)(2,1)S(1)}, bf16[256,768]{1,0:T(8,128)(2,1)S(1)}, u32[]{:S(2)}, u32[]{:S(2)}) collective-permute-start(bf16[256,768]{1,0:T(8,128)(2,1)S(1)} %bitcast.2), channel_id=1, source_target_pairs={{0,8},{4,12},{8,0},{12,4},{16,24},{20,28},{24,16},{28,20},{1,9},{5... | collective-permute-start | bytes 1179656 | tf_op jit(solution)/shard_map/ppermute | solution.py:48
  4.4 12.2 %collective-permute-start = (bf16[256,768]{1,0:T(8,128)(2,1)S(1)}, bf16[256,768]{1,0:T(8,128)(2,1)S(1)}, u32[]{:S(2)}, u32[]{:S(2)}) collective-permute-start(bf16[256,768]{1,0:T(8,128)(2,1)S(1)} %bitcast.3), channel_id=1, source_target_pairs={{0,4},{4,0},{8,12},{12,8},{16,20},{20,16},{24,28},{28,24},{1,5},{5... | collective-permute-start | bytes 1179656 | tf_op jit(solution)/shard_map/ppermute | solution.py:48
  13.5 15.0 %collective-permute-start.2 = (bf16[256,768]{1,0:T(8,128)(2,1)S(1)}, bf16[256,768]{1,0:T(8,128)(2,1)S(1)}, u32[]{:S(2)}, u32[]{:S(2)}) collective-permute-start(bf16[256,768]{1,0:T(8,128)(2,1)S(1)} %collective-permute-done.1.refs_0_), channel_id=1, source_target_pairs={{0,4},{4,0},{8,12},{12,8},{16,20},{20,16},{24,28},{28,24},{1,5},{5... | collective-permute-start | bytes 1179656 | tf_op jit(solution)/shard_map/ppermute | solution.py:48
  13.5 11.1 %collective-permute-start.4 = (bf16[64,576]{1,0:T(8,128)(2,1)S(1)}, bf16[64,576]{1,0:T(8,128)(2,1)S(1)}, u32[]{:S(2)}, u32[]{:S(2)}) collective-permute-start(bf16[64,576]{1,0:T(8,128)(2,1)S(1)} %slice.9), channel_id=1, source_target_pairs={{0,2},{1,3},{2,0},{3,1},{4,6},{5,7},{6,4},{7,5},{8,10},{9,11},{10,... | collective-permute-start | bytes 221192 | tf_op jit(solution)/shard_map/ppermute | solution.py:346
  16.5 12.9 %copy-start.1 = (bf16[192,768]{1,0:T(8,128)(2,1)S(1)}, bf16[192,768]{1,0:T(8,128)(2,1)}, u32[]{:S(2)}) copy-start(bf16[192,768]{1,0:T(8,128)(2,1)} %refs_0_.3) | copy-start | bytes 884740
  16.5 12.0 %collective-permute-start.3 = (bf16[128,576]{1,0:T(8,128)(2,1)S(1)}, bf16[128,576]{1,0:T(8,128)(2,1)S(1)}, u32[]{:S(2)}, u32[]{:S(2)}) collective-permute-start(bf16[128,576]{1,0:T(8,128)(2,1)S(1)} %slice.8), channel_id=1, source_target_pairs={{0,2},{1,3},{2,0},{3,1},{4,6},{5,7},{6,4},{7,5},{8,10},{9,11},{10,... | collective-permute-start | bytes 442376 | tf_op jit(solution)/shard_map/ppermute | solution.py:346
  16.6 15.0 %collective-permute-start.6 = (bf16[192,576]{1,0:T(8,128)(2,1)S(1)}, bf16[192,576]{1,0:T(8,128)(2,1)S(1)}, u32[]{:S(2)}, u32[]{:S(2)}) collective-permute-start(bf16[192,576]{1,0:T(8,128)(2,1)S(1)} %pad_maximum_fusion.refs_4_), channel_id=1, source_target_pairs={{0,1},{1,0},{2,3},{3,2},{4,5},{5,4},{6,7},{7,6},{8,9},{9,8},{10,11... | collective-permute-start | bytes 663560 | tf_op jit(solution)/shard_map/ppermute | solution.py:48
  24.6 7.0 %collective-permute-start.7 = (bf16[64,576]{1,0:T(8,128)(2,1)S(1)}, bf16[64,576]{1,0:T(8,128)(2,1)S(1)}, u32[]{:S(2)}, u32[]{:S(2)}) collective-permute-start(bf16[64,576]{1,0:T(8,128)(2,1)S(1)} %collective-permute-done.4.refs_6_), channel_id=1, source_target_pairs={{0,16},{4,20},{8,24},{12,28},{16,0},{20,4},{24,8},{28,12},{1,17},{... | collective-permute-start | bytes 221192 | tf_op jit(solution)/shard_map/ppermute | solution.py:48
  28.5 5.9 %collective-permute-start.5 = (bf16[128,576]{1,0:T(8,128)(2,1)S(1)}, bf16[128,576]{1,0:T(8,128)(2,1)S(1)}, u32[]{:S(2)}, u32[]{:S(2)}) collective-permute-start(bf16[128,576]{1,0:T(8,128)(2,1)S(1)} %collective-permute-done.3.refs_7_), channel_id=1, source_target_pairs={{0,16},{4,20},{8,24},{12,28},{16,0},{20,4},{24,8},{28,12},{1,17},{... | collective-permute-start | bytes 442376 | tf_op jit(solution)/shard_map/ppermute | solution.py:48
  29.4 9.3 %collective-permute-start.10 = (bf16[192,768]{1,0:T(8,128)(2,1)S(1)}, bf16[192,768]{1,0:T(8,128)(2,1)S(1)}, u32[]{:S(2)}, u32[]{:S(2)}) collective-permute-start(bf16[192,768]{1,0:T(8,128)(2,1)S(1)} %copy-done.1), channel_id=1, source_target_pairs={{0,1},{1,0},{2,3},{3,2},{4,6},{5,7},{6,4},{7,5},{8,9},{9,8},{10,11... | collective-permute-start | bytes 884744 | tf_op jit(solution)/shard_map/ppermute | solution.py:346
  35.0 4.4 %collective-permute-start.8 = (bf16[3,64,128]{2,1,0:T(8,128)(2,1)S(1)}, bf16[3,64,128]{2,1,0:T(8,128)(2,1)S(1)}, u32[]{:S(2)}, u32[]{:S(2)}) collective-permute-start(bf16[3,64,128]{2,1,0:T(8,128)(2,1)S(1)} %get-tuple-element.54.refs_5_), channel_id=1, source_target_pairs={{0,16},{4,20},{8,24},{12,28},{16,0},{20,4},{24,8},{28,12},{1,17},{... | collective-permute-start | bytes 147464 | tf_op jit(solution)/shard_map/ppermute | solution.py:48
  38.7 4.4 %collective-permute-start.13 = (bf16[192,768]{1,0:T(8,128)(2,1)S(1)}, bf16[192,768]{1,0:T(8,128)(2,1)S(1)}, u32[]{:S(2)}, u32[]{:S(2)}) collective-permute-start(bf16[192,768]{1,0:T(8,128)(2,1)S(1)} %collective-permute-done.10.refs_1_), channel_id=1, source_target_pairs={{4,20},{12,28},{20,4},{28,12},{5,21},{13,29},{21,5},{29,13},{6,22}... | collective-permute-start | bytes 884744 | tf_op jit(solution)/shard_map/ppermute | solution.py:351
  39.9 9.8 %collective-permute-start.12 = (bf16[192,768]{1,0:T(8,128)(2,1)S(1)}, bf16[192,768]{1,0:T(8,128)(2,1)S(1)}, u32[]{:S(2)}, u32[]{:S(2)}) collective-permute-start(bf16[192,768]{1,0:T(8,128)(2,1)S(1)} %collective-permute-done.10.refs_1_), channel_id=1, source_target_pairs={{0,4},{4,0},{8,12},{12,8},{16,20},{20,16},{24,28},{28,24},{1,5},{5... | collective-permute-start | bytes 884744 | tf_op jit(solution)/shard_map/ppermute | solution.py:48
  43.1 6.6 %collective-permute-start.14 = (bf16[192,768]{1,0:T(8,128)(2,1)S(1)}, bf16[192,768]{1,0:T(8,128)(2,1)S(1)}, u32[]{:S(2)}, u32[]{:S(2)}) collective-permute-start(bf16[192,768]{1,0:T(8,128)(2,1)S(1)} %collective-permute-done.13.refs_3_), channel_id=1, source_target_pairs={{4,0},{12,8},{20,16},{28,24},{5,1},{13,9},{21,17},{29,25},{6,2},{1... | collective-permute-start | bytes 884744 | tf_op jit(solution)/shard_map/ppermute | solution.py:351
  44.4 5.7 %collective-permute-start.9 = (bf16[2,192,256]{2,1,0:T(8,128)(2,1)S(1)}, bf16[2,192,256]{2,1,0:T(8,128)(2,1)S(1)}, u32[]{:S(2)}, u32[]{:S(2)}) collective-permute-start(bf16[2,192,256]{2,1,0:T(8,128)(2,1)S(1)} %shard_map.69), channel_id=1, source_target_pairs={{0,8},{4,12},{8,0},{12,4},{16,24},{20,28},{24,16},{28,20},{1,9},{5... | collective-permute-start | bytes 589832 | tf_op jit(solution)/shard_map/ppermute | solution.py:48
  46.4 4.4 %collective-permute-start.11 = (bf16[2,192,256]{2,1,0:T(8,128)(2,1)S(1)}, bf16[2,192,256]{2,1,0:T(8,128)(2,1)S(1)}, u32[]{:S(2)}, u32[]{:S(2)}) collective-permute-start(bf16[2,192,256]{2,1,0:T(8,128)(2,1)S(1)} %shard_map.70.refs_0_), channel_id=1, source_target_pairs={{0,4},{4,0},{8,12},{12,8},{16,20},{20,16},{24,28},{28,24},{1,5},{5... | collective-permute-start | bytes 589832 | tf_op jit(solution)/shard_map/ppermute | solution.py:48
  50.8 2.9 %collective-permute-start.15 = (bf16[2,192,256]{2,1,0:T(8,128)(2,1)S(1)}, bf16[2,192,256]{2,1,0:T(8,128)(2,1)S(1)}, u32[]{:S(2)}, u32[]{:S(2)}) collective-permute-start(bf16[2,192,256]{2,1,0:T(8,128)(2,1)S(1)} %collective-permute-done.9.refs_0_), channel_id=1, source_target_pairs={{0,4},{4,0},{8,12},{12,8},{16,20},{20,16},{24,28},{28,24},{1,5},{5... | collective-permute-start | bytes 589832 | tf_op jit(solution)/shard_map/ppermute | solution.py:48

commit v14 on v12

--- a/solution.py
+++ b/solution.py
@@ -84,15 +84,18 @@
     order = to_order(x_refs[0].shape[0])
     gain = gain_ref[...][None, :]
     bias = bias_ref[...][None, :]
-    for x_ref, out_ref in zip(x_refs, out_refs):
-        floats = x_ref[...].astype(jnp.float32)
-        centred = floats - jnp.mean(floats, axis=-1, keepdims=True)
-        spread = jnp.mean(centred * centred, axis=-1, keepdims=True)
-        normed = (centred * lax.rsqrt(spread + 1e-05) * gain + bias).astype(jnp.bfloat16)
-        ordered = product(order, normed).astype(jnp.bfloat16)
+    floats = [x_ref[...].astype(jnp.float32) for x_ref in x_refs]
+    centred = [value - jnp.mean(value, axis=-1, keepdims=True) for value in floats]
+    spreads = [jnp.mean(value * value, axis=-1, keepdims=True) for value in centred]
+    normed = [
+        (value * lax.rsqrt(spread + 1e-05) * gain + bias).astype(jnp.bfloat16)
+        for value, spread in zip(centred, spreads)
+    ]
+    ordered = [product(order, value).astype(jnp.bfloat16) for value in normed]
+    for value, out_ref in zip(ordered, out_refs):
         blocks, _, width = out_ref.shape
         for block in range(blocks):
-            out_ref[block] = ordered[:, block * width : (block + 1) * width]
+            out_ref[block] = value[:, block * width : (block + 1) * width]
 
 
 def group_indices():
@@ -139,12 +142,13 @@
     base_refs, out_refs = refs[:-SHARDS], refs[-SHARDS:]
     origin = sources(n_mp, group % 2, shared)
     for shard, (normed_ref, out_ref) in enumerate(zip(normed_refs, out_refs)):
-        total = base_refs[shard][...] if base_refs else 0.0
+        total = base_refs[shard][...] if base_refs else None
         for block in sorted({block for block, _ in some}):
             pieces = [(first, ref) for (at, first), ref in zip(some, weight_refs) if at == block]
             weight = jnp.concatenate([ref[...] for _, ref in pieces], axis=0)
             columns = slice(pieces[0][0], pieces[0][0] + weight.shape[0])
-            total = total + product(normed_ref[origin[block], :, columns], weight)
+            part = product(normed_ref[origin[block], :, columns], weight)
+            total = part if total is None else total + part
         out_ref[...] = total.astype(out_ref.dtype)
 
 

time: 39.5 us -> 39.5 us (level)
  no operation moved by 1% of the time
where the time goes in v14:
time: 39.5 us; the launch traced here: 39.4 us
  starting transfers between devices  17 us (43%)
  waiting for transfers between devices  10.7 us (27%)
  Pallas kernels  9.45 us (24%)
  local copies, waits for them, and re-layouts  1.3 us (3%)
  between operations  0.8 us (2%)
    ppermute x15, starting transfers between devices, flip(): return near(lax.ppermute(value, axis, pairs))  10.8 us
    ppermute x15, waiting for transfers between devices, flip(): return near(lax.ppermute(value, axis, pairs))  8.47 us
    ppermute x3, starting transfers between devices, fetch_far(): return near(lax.ppermute(value, ('ctx', 'mp'), pairs))  6.22 us
    pallas_call x3, Pallas kernels, local(): call(lambda *refs, blocks=blocks: update_body(blocks, *refs), [out_shape]...  2.36 us
    ppermute x3, waiting for transfers between devices, fetch_far(): return near(lax.ppermute(value, ('ctx', 'mp'), pairs))  2.23 us
    pallas_call x2, Pallas kernels, normalized(): call(norm_body, [blocks] * 2, n_in=4, micros=micros)(one, two, gain, bias)  1.87 us
    pallas_call x1, Pallas kernels, local(): call(lambda *refs: project_body((n_mp, shared, blocks[:-1]), *refs), [sha...  1.72 us
    pallas_call x1, Pallas kernels, local(): call(near_body, [shape((GROUP_HEADS, SHARDS, 1, rows), f32), shape((GROUP...  1.71 us
  transfers between devices with their start and end apart: 18, of which 7 were waited for; matrix products, arithmetic and copies ran while one was open for 0% of the time, Pallas kernels for 21%

profile of v14, /device:TPU:0, one launch (start us, length us, event | category | flops | bytes accessed | tf_op | source)
XLA Modules:
  0.0 39.4 jit_solution(8506353243927371057)
XLA Ops:
  0.0 1.3 %constant_dynamic-slice_fusion.3 = (bf16[192,192]{1,0:T(8,128)(2,1)S(1)}, bf16[192,192]{1,0:T(8,128)(2,1)S(1)}, bf16[192,192]{1,0:T(8,128)(2,1)S(1)}) fusion(bf16[192,2304]{1,0:T(8,128)(2,1)} %param.9, s32[]{:T(128)S(6)} %select_n.24, s32[]{:T(128)S(6)} %select_n.26, s32[]{:T(128)S(6)} %select_n.25), kind=kLoop, calls=%fused_computation.4 | loop fusion | bytes 442380 | tf_op jit(solution)/shard_map/dynamic_slice | solution.py:356
  1.3 0.1 pad_maximum_fusion.refs_4_
  1.4 0.5 %collective-permute-start = (bf16[256,768]{1,0:T(8,128)(2,1)S(1)}, bf16[256,768]{1,0:T(8,128)(2,1)S(1)}, u32[]{:S(2)}, u32[]{:S(2)}) collective-permute-start(bf16[256,768]{1,0:T(8,128)(2,1)S(1)} %bitcast.2), channel_id=1, source_target_pairs={{0,4},{4,0},{8,12},{12,8},{16,20},{20,16},{24,28},{28,24},{1,5},{5... | collective-permute-start | bytes 1179656 | tf_op jit(solution)/shard_map/ppermute | solution.py:48
  1.9 2.6 %collective-permute-start.1 = (bf16[256,768]{1,0:T(8,128)(2,1)S(1)}, bf16[256,768]{1,0:T(8,128)(2,1)S(1)}, u32[]{:S(2)}, u32[]{:S(2)}) collective-permute-start(bf16[256,768]{1,0:T(8,128)(2,1)S(1)} %bitcast.3), channel_id=1, source_target_pairs={{0,8},{4,12},{8,0},{12,4},{16,24},{20,28},{24,16},{28,20},{1,9},{5... | collective-permute-start | bytes 1179656 | tf_op jit(solution)/shard_map/ppermute | solution.py:48
  4.5 2.7 %collective-permute-start.4 = (bf16[64,576]{1,0:T(8,128)(2,1)S(1)}, bf16[64,576]{1,0:T(8,128)(2,1)S(1)}, u32[]{:S(2)}, u32[]{:S(2)}) collective-permute-start(bf16[64,576]{1,0:T(8,128)(2,1)S(1)} %slice.9), channel_id=1, source_target_pairs={{0,2},{1,3},{2,0},{3,1},{4,6},{5,7},{6,4},{7,5},{8,10},{9,11},{10,... | collective-permute-start | bytes 221192 | tf_op jit(solution)/shard_map/ppermute | solution.py:339
  7.2 0.4 %collective-permute-start.3 = (bf16[128,576]{1,0:T(8,128)(2,1)S(1)}, bf16[128,576]{1,0:T(8,128)(2,1)S(1)}, u32[]{:S(2)}, u32[]{:S(2)}) collective-permute-start(bf16[128,576]{1,0:T(8,128)(2,1)S(1)} %slice.8), channel_id=1, source_target_pairs={{0,2},{1,3},{2,0},{3,1},{4,6},{5,7},{6,4},{7,5},{8,10},{9,11},{10,... | collective-permute-start | bytes 442376 | tf_op jit(solution)/shard_map/ppermute | solution.py:339
  8.3 1.6 %collective-permute-start.6 = (bf16[192,576]{1,0:T(8,128)(2,1)S(1)}, bf16[192,576]{1,0:T(8,128)(2,1)S(1)}, u32[]{:S(2)}, u32[]{:S(2)}) collective-permute-start(bf16[192,576]{1,0:T(8,128)(2,1)S(1)} %pad_maximum_fusion.refs_4_), channel_id=1, source_target_pairs={{0,1},{1,0},{2,3},{3,2},{4,5},{5,4},{6,7},{7,6},{8,9},{9,8},{10,11... | collective-permute-start | bytes 663560 | tf_op jit(solution)/shard_map/ppermute | solution.py:48
  9.9 4.3 %collective-permute-done.1.refs_0_ = bf16[256,768]{1,0:T(8,128)(2,1)S(1)} collective-permute-done((bf16[256,768]{1,0:T(8,128)(2,1)S(1)}, bf16[256,768]{1,0:T(8,128)(2,1)S(1)}, u32[]{:S(2)}, u32[]{:S(2)}) %collective-permute-start.1) | collective-permute-done | bytes 393248 | tf_op jit(solution)/shard_map/ppermute | solution.py:48
  14.2 0.9 %shard_map.64 = (bf16[4,256,192]{2,1,0:T(8,128)(2,1)S(1)}, bf16[4,256,192]{2,1,0:T(8,128)(2,1)S(1)}) custom-call(bf16[256,768]{1,0:T(8,128)(2,1)S(1)} %bitcast.4, bf16[256,768]{1,0:T(8,128)(2,1)S(1)} %collective-permute-done.refs_1_, f32[768]{0:T(1024)S(1)} %copy-done.2, f32[768]{0:T(1024)S(1)} %copy-done.3), custom_call_target="tpu_custom_call" | custom-call | flops 3000000000 | bytes 9000000 | tf_op jit(solution)/shard_map/pallas_call | solution.py:375
  15.2 0.4 collective-permute-done.4.refs_6_
  15.6 1.5 %collective-permute-start.7 = (bf16[64,576]{1,0:T(8,128)(2,1)S(1)}, bf16[64,576]{1,0:T(8,128)(2,1)S(1)}, u32[]{:S(2)}, u32[]{:S(2)}) collective-permute-start(bf16[64,576]{1,0:T(8,128)(2,1)S(1)} %collective-permute-done.4.refs_6_), channel_id=1, source_target_pairs={{0,16},{4,20},{8,24},{12,28},{16,0},{20,4},{24,8},{28,12},{1,17},{... | collective-permute-start | bytes 221192 | tf_op jit(solution)/shard_map/ppermute | solution.py:48
  17.0 1.8 %collective-permute-done.3.refs_7_ = bf16[128,576]{1,0:T(8,128)(2,1)S(1)} collective-permute-done((bf16[128,576]{1,0:T(8,128)(2,1)S(1)}, bf16[128,576]{1,0:T(8,128)(2,1)S(1)}, u32[]{:S(2)}, u32[]{:S(2)}) %collective-permute-start.3) | collective-permute-done | bytes 147488 | tf_op jit(solution)/shard_map/ppermute | solution.py:339
  18.9 0.9 %shard_map.65 = (bf16[4,256,192]{2,1,0:T(8,128)(2,1)S(1)}, bf16[4,256,192]{2,1,0:T(8,128)(2,1)S(1)}) custom-call(bf16[256,768]{1,0:T(8,128)(2,1)S(1)} %collective-permute-done.1.refs_0_, bf16[256,768]{1,0:T(8,128)(2,1)S(1)} %collective-permute-done.2.refs_1_, f32[768]{0:T(1024)S(1)} %copy-done.2, f32[768]{0:T(1024)S(1)} %copy-done.3), custom_call_target="tpu_custom_call" | custom-call | flops 30000000 | bytes 90000 | tf_op jit(solution)/shard_map/pallas_call | solution.py:375
  19.8 3.2 %collective-permute-start.10 = (bf16[96,768]{1,0:T(8,128)(2,1)S(1)}, bf16[96,768]{1,0:T(8,128)(2,1)S(1)}, u32[]{:S(2)}, u32[]{:S(2)}) collective-permute-start(bf16[96,768]{1,0:T(8,128)(2,1)S(1)} %constant_dynamic-slice_fusion), channel_id=1, source_target_pairs={{0,2},{1,3},{2,0},{3,1},{4,6},{5,7},{6,4},{7,5},{8,10},{9,11},{10,... | collective-permute-start | bytes 442376 | tf_op jit(solution)/shard_map/ppermute | solution.py:339
  23.0 1.0 %collective-permute-start.12 = (bf16[96,768]{1,0:T(8,128)(2,1)S(1)}, bf16[96,768]{1,0:T(8,128)(2,1)S(1)}, u32[]{:S(2)}, u32[]{:S(2)}) collective-permute-start(bf16[96,768]{1,0:T(8,128)(2,1)S(1)} %constant_dynamic-slice_fusion), channel_id=1, source_target_pairs={{0,1},{1,0},{2,3},{3,2},{4,5},{5,4},{6,7},{7,6},{8,9},{9,8},{10,11... | collective-permute-start | bytes 442376 | tf_op jit(solution)/shard_map/ppermute | solution.py:48
  24.0 1.7 %shard_map.66 = (f32[256,576]{1,0:T(8,128)S(1)}, f32[256,576]{1,0:T(8,128)S(1)}, f32[256,576]{1,0:T(8,128)S(1)}, f32[256,576]{1,0:T(8,128)S(1)}) custom-call(bf16[4,256,192]{2,1,0:T(8,128)(2,1)S(1)} %get-tuple-element.35.refs_0_, bf16[4,256,192]{2,1,0:T(8,128)(2,1)S(1)} %get-tuple-element.36.refs_1_, bf16[4,256,192]{2,1,0:T(8,128)(2,1)S(1)} %get-tuple-element.37.refs_2_, ...), custom_call_target="tpu_custom_call" | custom-call | flops 3000000000 | bytes 9000000 | tf_op jit(solution)/shard_map/pallas_call | solution.py:401
  25.7 0.6 %shard_map.67 = (bf16[256,576]{1,0:T(8,128)(2,1)S(1)}, bf16[256,576]{1,0:T(8,128)(2,1)S(1)}, bf16[256,576]{1,0:T(8,128)(2,1)S(1)}, bf16[256,576]{1,0:T(8,128)(2,1)S(1)}, bf16[3,64,128]{2,1,0:T(8,128)(2,1)S(1)}) custom-call(bf16[4,256,192]{2,1,0:T(8,128)(2,1)S(1)} %get-tuple-element.35.refs_0_, bf16[4,256,192]{2,1,0:T(8,128)(2,1)S(1)} %get-tuple-element.36.refs_1_, ...), custom_call_target="tpu_custom_call" | custom-call | flops 3000000000 | bytes 9000000 | tf_op jit(solution)/shard_map/pallas_call | solution.py:407
  26.3 1.5 %collective-permute-start.8 = (bf16[3,64,128]{2,1,0:T(8,128)(2,1)S(1)}, bf16[3,64,128]{2,1,0:T(8,128)(2,1)S(1)}, u32[]{:S(2)}, u32[]{:S(2)}) collective-permute-start(bf16[3,64,128]{2,1,0:T(8,128)(2,1)S(1)} %get-tuple-element.55.refs_5_), channel_id=1, source_target_pairs={{0,16},{4,20},{8,24},{12,28},{16,0},{20,4},{24,8},{28,12},{1,17},{... | collective-permute-start | bytes 147464 | tf_op jit(solution)/shard_map/ppermute | solution.py:48
  27.8 1.7 %shard_map.68 = (f32[3,4,1,256]{3,2,1,0:T(1,128)S(1)}, f32[3,4,1,256]{3,2,1,0:T(1,128)S(1)}, f32[3,4,64,256]{3,2,1,0:T(8,128)S(1)}) custom-call(s32[1]{0:T(128)S(6)} %copy.7.valid_ref.refs_0_, bf16[256,576]{1,0:T(8,128)(2,1)S(1)} %get-tuple-element.46.refs_0_.refs_1_, bf16[256,576]{1,0:T(8,128)(2,1)S(1)} %get-tuple-element.47.refs_1_.refs_2_, ...), custom_call_target="tpu_custom_call" | custom-call | flops 3000000000 | bytes 9000000 | tf_op jit(solution)/shard_map/pallas_call | solution.py:415
  29.5 1.0 %collective-permute-start.13 = (bf16[96,768]{1,0:T(8,128)(2,1)S(1)}, bf16[96,768]{1,0:T(8,128)(2,1)S(1)}, u32[]{:S(2)}, u32[]{:S(2)}) collective-permute-start(bf16[96,768]{1,0:T(8,128)(2,1)S(1)} %collective-permute-done.10.refs_2_), channel_id=1, source_target_pairs={{0,16},{4,20},{8,24},{12,28},{16,0},{20,4},{24,8},{28,12},{1,17},{... | collective-permute-start | bytes 442376 | tf_op jit(solution)/shard_map/ppermute | solution.py:48
  30.5 0.5 %shard_map.69 = bf16[2,192,256]{2,1,0:T(8,128)(2,1)S(1)} custom-call(s32[1]{0:T(128)S(6)} %copy.7.valid_ref.refs_0_, bf16[256,576]{1,0:T(8,128)(2,1)S(1)} %get-tuple-element.46.refs_0_.refs_1_, bf16[256,576]{1,0:T(8,128)(2,1)S(1)} %get-tuple-element.47.refs_1_.refs_2_, bf16[256,576]{1,0:T(8,128)(2,1)S(1)} %get-tuple-element.48.refs_2_.refs_3_, ...), custom_call_target="tpu_custom_call" | custom-call | flops 3000000000 | bytes 9000000 | tf_op jit(solution)/shard_map/pallas_call | solution.py:430
  31.0 0.5 %collective-permute-start.9 = (bf16[2,192,256]{2,1,0:T(8,128)(2,1)S(1)}, bf16[2,192,256]{2,1,0:T(8,128)(2,1)S(1)}, u32[]{:S(2)}, u32[]{:S(2)}) collective-permute-start(bf16[2,192,256]{2,1,0:T(8,128)(2,1)S(1)} %shard_map.69), channel_id=1, source_target_pairs={{0,8},{4,12},{8,0},{12,4},{16,24},{20,28},{24,16},{28,20},{1,9},{5... | collective-permute-start | bytes 589832 | tf_op jit(solution)/shard_map/ppermute | solution.py:48
  31.5 0.5 %shard_map.70.refs_0_ = bf16[2,192,256]{2,1,0:T(8,128)(2,1)S(1)} custom-call(s32[1]{0:T(128)S(6)} %copy.7.valid_ref.refs_0_, bf16[256,576]{1,0:T(8,128)(2,1)S(1)} %get-tuple-element.46.refs_0_.refs_1_, bf16[256,576]{1,0:T(8,128)(2,1)S(1)} %get-tuple-element.47.refs_1_.refs_2_, bf16[256,576]{1,0:T(8,128)(2,1)S(1)} %get-tuple-element.48.refs_2_.refs_3_, ...), custom_call_target="tpu_custom_call" | custom-call | flops 30000000 | bytes 90000 | tf_op jit(solution)/shard_map/pallas_call | solution.py:430
  32.1 0.5 %collective-permute-start.15 = (bf16[96,768]{1,0:T(8,128)(2,1)S(1)}, bf16[96,768]{1,0:T(8,128)(2,1)S(1)}, u32[]{:S(2)}, u32[]{:S(2)}) collective-permute-start(bf16[96,768]{1,0:T(8,128)(2,1)S(1)} %collective-permute-done.10.refs_2_), channel_id=1, source_target_pairs={{0,4},{4,0},{8,12},{12,8},{16,20},{20,16},{24,28},{28,24},{1,5},{5... | collective-permute-start | bytes 442376 | tf_op jit(solution)/shard_map/ppermute | solution.py:48
  32.7 2.0 %collective-permute-done.13.refs_3_ = bf16[96,768]{1,0:T(8,128)(2,1)S(1)} collective-permute-done((bf16[96,768]{1,0:T(8,128)(2,1)S(1)}, bf16[96,768]{1,0:T(8,128)(2,1)S(1)}, u32[]{:S(2)}, u32[]{:S(2)}) %collective-permute-start.13) | collective-permute-done | bytes 147488 | tf_op jit(solution)/shard_map/ppermute | solution.py:48
  34.8 1.4 %collective-permute-done.16.refs_6_ = bf16[96,768]{1,0:T(8,128)(2,1)S(1)} collective-permute-done((bf16[96,768]{1,0:T(8,128)(2,1)S(1)}, bf16[96,768]{1,0:T(8,128)(2,1)S(1)}, u32[]{:S(2)}, u32[]{:S(2)}) %collective-permute-start.16) | collective-permute-done | bytes 147488 | tf_op jit(solution)/shard_map/ppermute | solution.py:48
  36.1 0.1 shard_map.71
  36.2 0.5 %collective-permute-done.9.refs_0_ = bf16[2,192,256]{2,1,0:T(8,128)(2,1)S(1)} collective-permute-done((bf16[2,192,256]{2,1,0:T(8,128)(2,1)S(1)}, bf16[2,192,256]{2,1,0:T(8,128)(2,1)S(1)}, u32[]{:S(2)}, u32[]{:S(2)}) %collective-permute-start.9) | collective-permute-done | bytes 196640 | tf_op jit(solution)/shard_map/ppermute | solution.py:48
  36.7 0.7 %shard_map.72.refs_3_ = f32[256,768]{1,0:T(8,128)S(1)} custom-call(bf16[2,192,256]{2,1,0:T(8,128)(2,1)S(1)} %shard_map.70.refs_0_, bf16[2,192,256]{2,1,0:T(8,128)(2,1)S(1)} %collective-permute-done.11.refs_1_, bf16[768,768]{1,0:T(8,128)(2,1)S(1)} %get-tuple-element.60.refs_2_.refs_1_, bf16[256,256]{1,0:T(8,128)(2,1)S(1)} %get-tuple-element.62.refs_3_.refs_2_, ...), custom_call_target="tpu_custom_call" | custom-call | flops 3000000 | bytes 9000 | tf_op jit(solution)/shard_map/pallas_call | solution.py:462
  37.5 0.5 %shard_map.73.refs_3_ = f32[256,768]{1,0:T(8,128)S(1)} custom-call(bf16[2,192,256]{2,1,0:T(8,128)(2,1)S(1)} %collective-permute-done.9.refs_0_, bf16[768,768]{1,0:T(8,128)(2,1)S(1)} %get-tuple-element.60.refs_2_.refs_1_, bf16[256,256]{1,0:T(8,128)(2,1)S(1)} %get-tuple-element.62.refs_3_.refs_2_, f32[256,768]{1,0:T(8,128)S(1)} %shard_map.72.refs_3_), custom_call_target="tpu_custom_call" | custom-call | flops 3000000 | bytes 9000 | tf_op jit(solution)/shard_map/pallas_call | solution.py:462
  37.9 0.3 collective-permute-done.17.refs_0_
  38.2 1.2 %shard_map.74 = bf16[256,768]{1,0:T(8,128)(2,1)} custom-call(bf16[2,192,256]{2,1,0:T(8,128)(2,1)S(1)} %collective-permute-done.17.refs_0_, bf16[768,768]{1,0:T(8,128)(2,1)S(1)} %get-tuple-element.60.refs_2_.refs_1_, bf16[256,256]{1,0:T(8,128)(2,1)S(1)} %get-tuple-element.62.refs_3_.refs_2_, f32[256,768]{1,0:T(8,128)S(1)} %shard_map.73.refs_3_), custom_call_target="tpu_custom_call" | custom-call | flops 3000000 | bytes 9000 | tf_op jit(solution)/shard_map/pallas_call | solution.py:462
  (28 shorter events, 0.2 us)
Async XLA Ops:
  0.0 1.4 %copy-start.1 = (bf16[1,256,768]{2,1,0:T(8,128)(2,1)S(1)}, bf16[1,256,768]{2,1,0:T(8,128)(2,1)}, u32[]{:S(2)}) copy-start(bf16[1,256,768]{2,1,0:T(8,128)(2,1)} %param.6) | copy-start | bytes 1179652
  0.0 14.2 %copy-start.2 = (f32[768]{0:T(1024)S(1)}, f32[768]{0:T(1024)}, u32[]{:S(2)}) copy-start(f32[768]{0:T(1024)} %refs_2_.3) | copy-start | bytes 9220
  0.0 14.2 %copy-start.3 = (f32[768]{0:T(1024)S(1)}, f32[768]{0:T(1024)}, u32[]{:S(2)}) copy-start(f32[768]{0:T(1024)} %refs_3_.3) | copy-start | bytes 9220
  1.4 6.9 %collective-permute-start = (bf16[256,768]{1,0:T(8,128)(2,1)S(1)}, bf16[256,768]{1,0:T(8,128)(2,1)S(1)}, u32[]{:S(2)}, u32[]{:S(2)}) collective-permute-start(bf16[256,768]{1,0:T(8,128)(2,1)S(1)} %bitcast.2), channel_id=1, source_target_pairs={{0,4},{4,0},{8,12},{12,8},{16,20},{20,16},{24,28},{28,24},{1,5},{5... | collective-permute-start | bytes 1179656 | tf_op jit(solution)/shard_map/ppermute | solution.py:48
  1.9 12.3 %collective-permute-start.1 = (bf16[256,768]{1,0:T(8,128)(2,1)S(1)}, bf16[256,768]{1,0:T(8,128)(2,1)S(1)}, u32[]{:S(2)}, u32[]{:S(2)}) collective-permute-start(bf16[256,768]{1,0:T(8,128)(2,1)S(1)} %bitcast.3), channel_id=1, source_target_pairs={{0,8},{4,12},{8,0},{12,4},{16,24},{20,28},{24,16},{28,20},{1,9},{5... | collective-permute-start | bytes 1179656 | tf_op jit(solution)/shard_map/ppermute | solution.py:48
  4.5 11.0 %collective-permute-start.4 = (bf16[64,576]{1,0:T(8,128)(2,1)S(1)}, bf16[64,576]{1,0:T(8,128)(2,1)S(1)}, u32[]{:S(2)}, u32[]{:S(2)}) collective-permute-start(bf16[64,576]{1,0:T(8,128)(2,1)S(1)} %slice.9), channel_id=1, source_target_pairs={{0,2},{1,3},{2,0},{3,1},{4,6},{5,7},{6,4},{7,5},{8,10},{9,11},{10,... | collective-permute-start | bytes 221192 | tf_op jit(solution)/shard_map/ppermute | solution.py:339
  7.2 11.7 %collective-permute-start.3 = (bf16[128,576]{1,0:T(8,128)(2,1)S(1)}, bf16[128,576]{1,0:T(8,128)(2,1)S(1)}, u32[]{:S(2)}, u32[]{:S(2)}) collective-permute-start(bf16[128,576]{1,0:T(8,128)(2,1)S(1)} %slice.8), channel_id=1, source_target_pairs={{0,2},{1,3},{2,0},{3,1},{4,6},{5,7},{6,4},{7,5},{8,10},{9,11},{10,... | collective-permute-start | bytes 442376 | tf_op jit(solution)/shard_map/ppermute | solution.py:339
  8.2 8.8 %copy-start = (bf16[192,768]{1,0:T(8,128)(2,1)S(1)}, bf16[192,768]{1,0:T(8,128)(2,1)}, u32[]{:S(2)}) copy-start(bf16[192,768]{1,0:T(8,128)(2,1)} %refs_0_.3) | copy-start | bytes 884740
  8.3 15.7 %collective-permute-start.6 = (bf16[192,576]{1,0:T(8,128)(2,1)S(1)}, bf16[192,576]{1,0:T(8,128)(2,1)S(1)}, u32[]{:S(2)}, u32[]{:S(2)}) collective-permute-start(bf16[192,576]{1,0:T(8,128)(2,1)S(1)} %pad_maximum_fusion.refs_4_), channel_id=1, source_target_pairs={{0,1},{1,0},{2,3},{3,2},{4,5},{5,4},{6,7},{7,6},{8,9},{9,8},{10,11... | collective-permute-start | bytes 663560 | tf_op jit(solution)/shard_map/ppermute | solution.py:48
  14.2 4.7 %collective-permute-start.2 = (bf16[256,768]{1,0:T(8,128)(2,1)S(1)}, bf16[256,768]{1,0:T(8,128)(2,1)S(1)}, u32[]{:S(2)}, u32[]{:S(2)}) collective-permute-start(bf16[256,768]{1,0:T(8,128)(2,1)S(1)} %collective-permute-done.1.refs_0_), channel_id=1, source_target_pairs={{0,4},{4,0},{8,12},{12,8},{16,20},{20,16},{24,28},{28,24},{1,5},{5... | collective-permute-start | bytes 1179656 | tf_op jit(solution)/shard_map/ppermute | solution.py:48
  15.6 8.4 %collective-permute-start.7 = (bf16[64,576]{1,0:T(8,128)(2,1)S(1)}, bf16[64,576]{1,0:T(8,128)(2,1)S(1)}, u32[]{:S(2)}, u32[]{:S(2)}) collective-permute-start(bf16[64,576]{1,0:T(8,128)(2,1)S(1)} %collective-permute-done.4.refs_6_), channel_id=1, source_target_pairs={{0,16},{4,20},{8,24},{12,28},{16,0},{20,4},{24,8},{28,12},{1,17},{... | collective-permute-start | bytes 221192 | tf_op jit(solution)/shard_map/ppermute | solution.py:48
  18.9 6.8 %collective-permute-start.5 = (bf16[128,576]{1,0:T(8,128)(2,1)S(1)}, bf16[128,576]{1,0:T(8,128)(2,1)S(1)}, u32[]{:S(2)}, u32[]{:S(2)}) collective-permute-start(bf16[128,576]{1,0:T(8,128)(2,1)S(1)} %collective-permute-done.3.refs_7_), channel_id=1, source_target_pairs={{0,16},{4,20},{8,24},{12,28},{16,0},{20,4},{24,8},{28,12},{1,17},{... | collective-permute-start | bytes 442376 | tf_op jit(solution)/shard_map/ppermute | solution.py:48
  19.8 9.7 %collective-permute-start.10 = (bf16[96,768]{1,0:T(8,128)(2,1)S(1)}, bf16[96,768]{1,0:T(8,128)(2,1)S(1)}, u32[]{:S(2)}, u32[]{:S(2)}) collective-permute-start(bf16[96,768]{1,0:T(8,128)(2,1)S(1)} %constant_dynamic-slice_fusion), channel_id=1, source_target_pairs={{0,2},{1,3},{2,0},{3,1},{4,6},{5,7},{6,4},{7,5},{8,10},{9,11},{10,... | collective-permute-start | bytes 442376 | tf_op jit(solution)/shard_map/ppermute | solution.py:339
  23.0 9.7 %collective-permute-start.12 = (bf16[96,768]{1,0:T(8,128)(2,1)S(1)}, bf16[96,768]{1,0:T(8,128)(2,1)S(1)}, u32[]{:S(2)}, u32[]{:S(2)}) collective-permute-start(bf16[96,768]{1,0:T(8,128)(2,1)S(1)} %constant_dynamic-slice_fusion), channel_id=1, source_target_pairs={{0,1},{1,0},{2,3},{3,2},{4,5},{5,4},{6,7},{7,6},{8,9},{9,8},{10,11... | collective-permute-start | bytes 442376 | tf_op jit(solution)/shard_map/ppermute | solution.py:48
  26.3 4.2 %collective-permute-start.8 = (bf16[3,64,128]{2,1,0:T(8,128)(2,1)S(1)}, bf16[3,64,128]{2,1,0:T(8,128)(2,1)S(1)}, u32[]{:S(2)}, u32[]{:S(2)}) collective-permute-start(bf16[3,64,128]{2,1,0:T(8,128)(2,1)S(1)} %get-tuple-element.55.refs_5_), channel_id=1, source_target_pairs={{0,16},{4,20},{8,24},{12,28},{16,0},{20,4},{24,8},{28,12},{1,17},{... | collective-permute-start | bytes 147464 | tf_op jit(solution)/shard_map/ppermute | solution.py:48
  29.5 5.2 %collective-permute-start.13 = (bf16[96,768]{1,0:T(8,128)(2,1)S(1)}, bf16[96,768]{1,0:T(8,128)(2,1)S(1)}, u32[]{:S(2)}, u32[]{:S(2)}) collective-permute-start(bf16[96,768]{1,0:T(8,128)(2,1)S(1)} %collective-permute-done.10.refs_2_), channel_id=1, source_target_pairs={{0,16},{4,20},{8,24},{12,28},{16,0},{20,4},{24,8},{28,12},{1,17},{... | collective-permute-start | bytes 442376 | tf_op jit(solution)/shard_map/ppermute | solution.py:48
  31.0 5.7 %collective-permute-start.9 = (bf16[2,192,256]{2,1,0:T(8,128)(2,1)S(1)}, bf16[2,192,256]{2,1,0:T(8,128)(2,1)S(1)}, u32[]{:S(2)}, u32[]{:S(2)}) collective-permute-start(bf16[2,192,256]{2,1,0:T(8,128)(2,1)S(1)} %shard_map.69), channel_id=1, source_target_pairs={{0,8},{4,12},{8,0},{12,4},{16,24},{20,28},{24,16},{28,20},{1,9},{5... | collective-permute-start | bytes 589832 | tf_op jit(solution)/shard_map/ppermute | solution.py:48
  32.1 4.7 %collective-permute-start.11 = (bf16[2,192,256]{2,1,0:T(8,128)(2,1)S(1)}, bf16[2,192,256]{2,1,0:T(8,128)(2,1)S(1)}, u32[]{:S(2)}, u32[]{:S(2)}) collective-permute-start(bf16[2,192,256]{2,1,0:T(8,128)(2,1)S(1)} %shard_map.70.refs_0_), channel_id=1, source_target_pairs={{0,4},{4,0},{8,12},{12,8},{16,20},{20,16},{24,28},{28,24},{1,5},{5... | collective-permute-start | bytes 589832 | tf_op jit(solution)/shard_map/ppermute | solution.py:48
  32.1 2.6 %collective-permute-start.15 = (bf16[96,768]{1,0:T(8,128)(2,1)S(1)}, bf16[96,768]{1,0:T(8,128)(2,1)S(1)}, u32[]{:S(2)}, u32[]{:S(2)}) collective-permute-start(bf16[96,768]{1,0:T(8,128)(2,1)S(1)} %collective-permute-done.10.refs_2_), channel_id=1, source_target_pairs={{0,4},{4,0},{8,12},{12,8},{16,20},{20,16},{24,28},{28,24},{1,5},{5... | collective-permute-start | bytes 442376 | tf_op jit(solution)/shard_map/ppermute | solution.py:48
  32.6 2.1 %collective-permute-start.14 = (bf16[96,768]{1,0:T(8,128)(2,1)S(1)}, bf16[96,768]{1,0:T(8,128)(2,1)S(1)}, u32[]{:S(2)}, u32[]{:S(2)}) collective-permute-start(bf16[96,768]{1,0:T(8,128)(2,1)S(1)} %collective-permute-done.12.refs_1_), channel_id=1, source_target_pairs={{0,4},{4,0},{8,12},{12,8},{16,20},{20,16},{24,28},{28,24},{1,5},{5... | collective-permute-start | bytes 442376 | tf_op jit(solution)/shard_map/ppermute | solution.py:48
  34.7 1.4 %collective-permute-start.16 = (bf16[96,768]{1,0:T(8,128)(2,1)S(1)}, bf16[96,768]{1,0:T(8,128)(2,1)S(1)}, u32[]{:S(2)}, u32[]{:S(2)}) collective-permute-start(bf16[96,768]{1,0:T(8,128)(2,1)S(1)} %collective-permute-done.13.refs_3_), channel_id=1, source_target_pairs={{0,4},{4,0},{8,12},{12,8},{16,20},{20,16},{24,28},{28,24},{1,5},{5... | collective-permute-start | bytes 442376 | tf_op jit(solution)/shard_map/ppermute | solution.py:48
  36.7 1.4 %collective-permute-start.17 = (bf16[2,192,256]{2,1,0:T(8,128)(2,1)S(1)}, bf16[2,192,256]{2,1,0:T(8,128)(2,1)S(1)}, u32[]{:S(2)}, u32[]{:S(2)}) collective-permute-start(bf16[2,192,256]{2,1,0:T(8,128)(2,1)S(1)} %collective-permute-done.9.refs_0_), channel_id=1, source_target_pairs={{0,4},{4,0},{8,12},{12,8},{16,20},{20,16},{24,28},{28,24},{1,5},{5... | collective-permute-start | bytes 589832 | tf_op jit(solution)/shard_map/ppermute | solution.py:48

commit v15 on v14

--- a/solution.py
+++ b/solution.py
@@ -454,8 +454,11 @@
     total = x_own
     last_part = flip(after(far_part, pair_part, whole_out), "ctx", 1)
     steps = [
-        ([(0, 0), (1, 1)], [staying, pair_part], shape((rows, width), f32)),
-        ([(2, 0)], [far_part], shape((rows, width), f32)),
+        (
+            [(0, 0), (1, 1), (2, 0)],
+            [staying, pair_part, far_part],
+            shape((rows, width), f32),
+        ),
         ([(3, 1)], [last_part], jax.ShapeDtypeStruct((rows, width), bf16)),
     ]
     for blocks, operands, out_shape in steps:

time: 39.5 us -> 39.5 us (level)
    pallas_call x3 -> x2, Pallas kernels: 2.36 us -> 2.12 us  [local(): call(lambda *refs, blocks=blocks: update_body(blocks, *refs), [out_shape]...]
  transfers between devices with their start and end apart: 18 -> 18, of which waited for: 7 -> 7; matrix products, arithmetic and copies ran while one was open for 0% -> 0% of each run, Pallas kernels for 21% -> 20%
where the time goes in v15:
time: 39.5 us; the launch traced here: 39.4 us
  starting transfers between devices  17 us (43%)
  waiting for transfers between devices  10.9 us (28%)
  Pallas kernels  9.21 us (23%)
  local copies, waits for them, and re-layouts  1.3 us (3%)
  between operations  0.8 us (2%)
    ppermute x15, starting transfers between devices, flip(): return near(lax.ppermute(value, axis, pairs))  10.8 us
    ppermute x15, waiting for transfers between devices, flip(): return near(lax.ppermute(value, axis, pairs))  8.71 us
    ppermute x3, starting transfers between devices, fetch_far(): return near(lax.ppermute(value, ('ctx', 'mp'), pairs))  6.22 us
    ppermute x3, waiting for transfers between devices, fetch_far(): return near(lax.ppermute(value, ('ctx', 'mp'), pairs))  2.23 us
    pallas_call x2, Pallas kernels, local(): call(lambda *refs, blocks=blocks: update_body(blocks, *refs), [out_shape]...  2.12 us
    pallas_call x2, Pallas kernels, normalized(): call(norm_body, [blocks] * 2, n_in=4, micros=micros)(one, two, gain, bias)  1.87 us
    pallas_call x1, Pallas kernels, local(): call(lambda *refs: project_body((n_mp, shared, blocks[:-1]), *refs), [sha...  1.72 us
    pallas_call x1, Pallas kernels, local(): call(near_body, [shape((GROUP_HEADS, SHARDS, 1, rows), f32), shape((GROUP...  1.71 us
  transfers between devices with their start and end apart: 18, of which 7 were waited for; matrix products, arithmetic and copies ran while one was open for 0% of the time, Pallas kernels for 20%

profile of v15, /device:TPU:0, one launch (start us, length us, event | category | flops | bytes accessed | tf_op | source)
XLA Modules:
  0.0 39.4 jit_solution(763706797349786669)
XLA Ops:
  0.0 1.3 %constant_dynamic-slice_fusion.3 = (bf16[192,192]{1,0:T(8,128)(2,1)S(1)}, bf16[192,192]{1,0:T(8,128)(2,1)S(1)}, bf16[192,192]{1,0:T(8,128)(2,1)S(1)}) fusion(bf16[192,2304]{1,0:T(8,128)(2,1)} %param.9, s32[]{:T(128)S(6)} %select_n.24, s32[]{:T(128)S(6)} %select_n.26, s32[]{:T(128)S(6)} %select_n.25), kind=kLoop, calls=%fused_computation.4 | loop fusion | bytes 442380 | tf_op jit(solution)/shard_map/dynamic_slice | solution.py:356
  1.3 0.1 pad_maximum_fusion.refs_4_
  1.4 0.5 %collective-permute-start = (bf16[256,768]{1,0:T(8,128)(2,1)S(1)}, bf16[256,768]{1,0:T(8,128)(2,1)S(1)}, u32[]{:S(2)}, u32[]{:S(2)}) collective-permute-start(bf16[256,768]{1,0:T(8,128)(2,1)S(1)} %bitcast.2), channel_id=1, source_target_pairs={{0,4},{4,0},{8,12},{12,8},{16,20},{20,16},{24,28},{28,24},{1,5},{5... | collective-permute-start | bytes 1179656 | tf_op jit(solution)/shard_map/ppermute | solution.py:48
  1.9 2.6 %collective-permute-start.1 = (bf16[256,768]{1,0:T(8,128)(2,1)S(1)}, bf16[256,768]{1,0:T(8,128)(2,1)S(1)}, u32[]{:S(2)}, u32[]{:S(2)}) collective-permute-start(bf16[256,768]{1,0:T(8,128)(2,1)S(1)} %bitcast.3), channel_id=1, source_target_pairs={{0,8},{4,12},{8,0},{12,4},{16,24},{20,28},{24,16},{28,20},{1,9},{5... | collective-permute-start | bytes 1179656 | tf_op jit(solution)/shard_map/ppermute | solution.py:48
  4.5 2.7 %collective-permute-start.4 = (bf16[64,576]{1,0:T(8,128)(2,1)S(1)}, bf16[64,576]{1,0:T(8,128)(2,1)S(1)}, u32[]{:S(2)}, u32[]{:S(2)}) collective-permute-start(bf16[64,576]{1,0:T(8,128)(2,1)S(1)} %slice.9), channel_id=1, source_target_pairs={{0,2},{1,3},{2,0},{3,1},{4,6},{5,7},{6,4},{7,5},{8,10},{9,11},{10,... | collective-permute-start | bytes 221192 | tf_op jit(solution)/shard_map/ppermute | solution.py:339
  7.2 0.4 %collective-permute-start.3 = (bf16[128,576]{1,0:T(8,128)(2,1)S(1)}, bf16[128,576]{1,0:T(8,128)(2,1)S(1)}, u32[]{:S(2)}, u32[]{:S(2)}) collective-permute-start(bf16[128,576]{1,0:T(8,128)(2,1)S(1)} %slice.8), channel_id=1, source_target_pairs={{0,2},{1,3},{2,0},{3,1},{4,6},{5,7},{6,4},{7,5},{8,10},{9,11},{10,... | collective-permute-start | bytes 442376 | tf_op jit(solution)/shard_map/ppermute | solution.py:339
  8.3 1.6 %collective-permute-start.6 = (bf16[192,576]{1,0:T(8,128)(2,1)S(1)}, bf16[192,576]{1,0:T(8,128)(2,1)S(1)}, u32[]{:S(2)}, u32[]{:S(2)}) collective-permute-start(bf16[192,576]{1,0:T(8,128)(2,1)S(1)} %pad_maximum_fusion.refs_4_), channel_id=1, source_target_pairs={{0,1},{1,0},{2,3},{3,2},{4,5},{5,4},{6,7},{7,6},{8,9},{9,8},{10,11... | collective-permute-start | bytes 663560 | tf_op jit(solution)/shard_map/ppermute | solution.py:48
  9.9 4.3 %collective-permute-done.1.refs_0_ = bf16[256,768]{1,0:T(8,128)(2,1)S(1)} collective-permute-done((bf16[256,768]{1,0:T(8,128)(2,1)S(1)}, bf16[256,768]{1,0:T(8,128)(2,1)S(1)}, u32[]{:S(2)}, u32[]{:S(2)}) %collective-permute-start.1) | collective-permute-done | bytes 393248 | tf_op jit(solution)/shard_map/ppermute | solution.py:48
  14.2 0.9 %shard_map.64 = (bf16[4,256,192]{2,1,0:T(8,128)(2,1)S(1)}, bf16[4,256,192]{2,1,0:T(8,128)(2,1)S(1)}) custom-call(bf16[256,768]{1,0:T(8,128)(2,1)S(1)} %bitcast.4, bf16[256,768]{1,0:T(8,128)(2,1)S(1)} %collective-permute-done.refs_1_, f32[768]{0:T(1024)S(1)} %copy-done.2, f32[768]{0:T(1024)S(1)} %copy-done.3), custom_call_target="tpu_custom_call" | custom-call | flops 3000000000 | bytes 9000000 | tf_op jit(solution)/shard_map/pallas_call | solution.py:375
  15.2 0.4 collective-permute-done.4.refs_6_
  15.6 1.5 %collective-permute-start.7 = (bf16[64,576]{1,0:T(8,128)(2,1)S(1)}, bf16[64,576]{1,0:T(8,128)(2,1)S(1)}, u32[]{:S(2)}, u32[]{:S(2)}) collective-permute-start(bf16[64,576]{1,0:T(8,128)(2,1)S(1)} %collective-permute-done.4.refs_6_), channel_id=1, source_target_pairs={{0,16},{4,20},{8,24},{12,28},{16,0},{20,4},{24,8},{28,12},{1,17},{... | collective-permute-start | bytes 221192 | tf_op jit(solution)/shard_map/ppermute | solution.py:48
  17.0 1.8 %collective-permute-done.3.refs_7_ = bf16[128,576]{1,0:T(8,128)(2,1)S(1)} collective-permute-done((bf16[128,576]{1,0:T(8,128)(2,1)S(1)}, bf16[128,576]{1,0:T(8,128)(2,1)S(1)}, u32[]{:S(2)}, u32[]{:S(2)}) %collective-permute-start.3) | collective-permute-done | bytes 147488 | tf_op jit(solution)/shard_map/ppermute | solution.py:339
  18.9 0.9 %shard_map.65 = (bf16[4,256,192]{2,1,0:T(8,128)(2,1)S(1)}, bf16[4,256,192]{2,1,0:T(8,128)(2,1)S(1)}) custom-call(bf16[256,768]{1,0:T(8,128)(2,1)S(1)} %collective-permute-done.1.refs_0_, bf16[256,768]{1,0:T(8,128)(2,1)S(1)} %collective-permute-done.2.refs_1_, f32[768]{0:T(1024)S(1)} %copy-done.2, f32[768]{0:T(1024)S(1)} %copy-done.3), custom_call_target="tpu_custom_call" | custom-call | flops 30000000 | bytes 90000 | tf_op jit(solution)/shard_map/pallas_call | solution.py:375
  19.8 3.2 %collective-permute-start.10 = (bf16[96,768]{1,0:T(8,128)(2,1)S(1)}, bf16[96,768]{1,0:T(8,128)(2,1)S(1)}, u32[]{:S(2)}, u32[]{:S(2)}) collective-permute-start(bf16[96,768]{1,0:T(8,128)(2,1)S(1)} %constant_dynamic-slice_fusion), channel_id=1, source_target_pairs={{0,2},{1,3},{2,0},{3,1},{4,6},{5,7},{6,4},{7,5},{8,10},{9,11},{10,... | collective-permute-start | bytes 442376 | tf_op jit(solution)/shard_map/ppermute | solution.py:339
  23.0 1.0 %collective-permute-start.12 = (bf16[96,768]{1,0:T(8,128)(2,1)S(1)}, bf16[96,768]{1,0:T(8,128)(2,1)S(1)}, u32[]{:S(2)}, u32[]{:S(2)}) collective-permute-start(bf16[96,768]{1,0:T(8,128)(2,1)S(1)} %constant_dynamic-slice_fusion), channel_id=1, source_target_pairs={{0,1},{1,0},{2,3},{3,2},{4,5},{5,4},{6,7},{7,6},{8,9},{9,8},{10,11... | collective-permute-start | bytes 442376 | tf_op jit(solution)/shard_map/ppermute | solution.py:48
  24.0 1.7 %shard_map.66 = (f32[256,576]{1,0:T(8,128)S(1)}, f32[256,576]{1,0:T(8,128)S(1)}, f32[256,576]{1,0:T(8,128)S(1)}, f32[256,576]{1,0:T(8,128)S(1)}) custom-call(bf16[4,256,192]{2,1,0:T(8,128)(2,1)S(1)} %get-tuple-element.35.refs_0_, bf16[4,256,192]{2,1,0:T(8,128)(2,1)S(1)} %get-tuple-element.36.refs_1_, bf16[4,256,192]{2,1,0:T(8,128)(2,1)S(1)} %get-tuple-element.37.refs_2_, ...), custom_call_target="tpu_custom_call" | custom-call | flops 3000000000 | bytes 9000000 | tf_op jit(solution)/shard_map/pallas_call | solution.py:401
  25.7 0.6 %shard_map.67 = (bf16[256,576]{1,0:T(8,128)(2,1)S(1)}, bf16[256,576]{1,0:T(8,128)(2,1)S(1)}, bf16[256,576]{1,0:T(8,128)(2,1)S(1)}, bf16[256,576]{1,0:T(8,128)(2,1)S(1)}, bf16[3,64,128]{2,1,0:T(8,128)(2,1)S(1)}) custom-call(bf16[4,256,192]{2,1,0:T(8,128)(2,1)S(1)} %get-tuple-element.35.refs_0_, bf16[4,256,192]{2,1,0:T(8,128)(2,1)S(1)} %get-tuple-element.36.refs_1_, ...), custom_call_target="tpu_custom_call" | custom-call | flops 3000000000 | bytes 9000000 | tf_op jit(solution)/shard_map/pallas_call | solution.py:407
  26.3 1.5 %collective-permute-start.8 = (bf16[3,64,128]{2,1,0:T(8,128)(2,1)S(1)}, bf16[3,64,128]{2,1,0:T(8,128)(2,1)S(1)}, u32[]{:S(2)}, u32[]{:S(2)}) collective-permute-start(bf16[3,64,128]{2,1,0:T(8,128)(2,1)S(1)} %get-tuple-element.55.refs_5_), channel_id=1, source_target_pairs={{0,16},{4,20},{8,24},{12,28},{16,0},{20,4},{24,8},{28,12},{1,17},{... | collective-permute-start | bytes 147464 | tf_op jit(solution)/shard_map/ppermute | solution.py:48
  27.8 1.7 %shard_map.68 = (f32[3,4,1,256]{3,2,1,0:T(1,128)S(1)}, f32[3,4,1,256]{3,2,1,0:T(1,128)S(1)}, f32[3,4,64,256]{3,2,1,0:T(8,128)S(1)}) custom-call(s32[1]{0:T(128)S(6)} %copy.7.valid_ref.refs_0_, bf16[256,576]{1,0:T(8,128)(2,1)S(1)} %get-tuple-element.46.refs_0_.refs_1_, bf16[256,576]{1,0:T(8,128)(2,1)S(1)} %get-tuple-element.47.refs_1_.refs_2_, ...), custom_call_target="tpu_custom_call" | custom-call | flops 3000000000 | bytes 9000000 | tf_op jit(solution)/shard_map/pallas_call | solution.py:415
  29.5 1.0 %collective-permute-start.13 = (bf16[96,768]{1,0:T(8,128)(2,1)S(1)}, bf16[96,768]{1,0:T(8,128)(2,1)S(1)}, u32[]{:S(2)}, u32[]{:S(2)}) collective-permute-start(bf16[96,768]{1,0:T(8,128)(2,1)S(1)} %collective-permute-done.10.refs_2_), channel_id=1, source_target_pairs={{0,16},{4,20},{8,24},{12,28},{16,0},{20,4},{24,8},{28,12},{1,17},{... | collective-permute-start | bytes 442376 | tf_op jit(solution)/shard_map/ppermute | solution.py:48
  30.5 0.5 %shard_map.69 = bf16[2,192,256]{2,1,0:T(8,128)(2,1)S(1)} custom-call(s32[1]{0:T(128)S(6)} %copy.7.valid_ref.refs_0_, bf16[256,576]{1,0:T(8,128)(2,1)S(1)} %get-tuple-element.46.refs_0_.refs_1_, bf16[256,576]{1,0:T(8,128)(2,1)S(1)} %get-tuple-element.47.refs_1_.refs_2_, bf16[256,576]{1,0:T(8,128)(2,1)S(1)} %get-tuple-element.48.refs_2_.refs_3_, ...), custom_call_target="tpu_custom_call" | custom-call | flops 3000000000 | bytes 9000000 | tf_op jit(solution)/shard_map/pallas_call | solution.py:430
  31.0 0.5 %collective-permute-start.9 = (bf16[2,192,256]{2,1,0:T(8,128)(2,1)S(1)}, bf16[2,192,256]{2,1,0:T(8,128)(2,1)S(1)}, u32[]{:S(2)}, u32[]{:S(2)}) collective-permute-start(bf16[2,192,256]{2,1,0:T(8,128)(2,1)S(1)} %shard_map.69), channel_id=1, source_target_pairs={{0,8},{4,12},{8,0},{12,4},{16,24},{20,28},{24,16},{28,20},{1,9},{5... | collective-permute-start | bytes 589832 | tf_op jit(solution)/shard_map/ppermute | solution.py:48
  31.5 0.5 %shard_map.70.refs_0_ = bf16[2,192,256]{2,1,0:T(8,128)(2,1)S(1)} custom-call(s32[1]{0:T(128)S(6)} %copy.7.valid_ref.refs_0_, bf16[256,576]{1,0:T(8,128)(2,1)S(1)} %get-tuple-element.46.refs_0_.refs_1_, bf16[256,576]{1,0:T(8,128)(2,1)S(1)} %get-tuple-element.47.refs_1_.refs_2_, bf16[256,576]{1,0:T(8,128)(2,1)S(1)} %get-tuple-element.48.refs_2_.refs_3_, ...), custom_call_target="tpu_custom_call" | custom-call | flops 30000000 | bytes 90000 | tf_op jit(solution)/shard_map/pallas_call | solution.py:430
  32.1 0.5 %collective-permute-start.15 = (bf16[96,768]{1,0:T(8,128)(2,1)S(1)}, bf16[96,768]{1,0:T(8,128)(2,1)S(1)}, u32[]{:S(2)}, u32[]{:S(2)}) collective-permute-start(bf16[96,768]{1,0:T(8,128)(2,1)S(1)} %collective-permute-done.10.refs_2_), channel_id=1, source_target_pairs={{0,4},{4,0},{8,12},{12,8},{16,20},{20,16},{24,28},{28,24},{1,5},{5... | collective-permute-start | bytes 442376 | tf_op jit(solution)/shard_map/ppermute | solution.py:48
  32.6 0.1 collective-permute-start.14
  32.7 2.0 %collective-permute-done.13.refs_3_ = bf16[96,768]{1,0:T(8,128)(2,1)S(1)} collective-permute-done((bf16[96,768]{1,0:T(8,128)(2,1)S(1)}, bf16[96,768]{1,0:T(8,128)(2,1)S(1)}, u32[]{:S(2)}, u32[]{:S(2)}) %collective-permute-start.13) | collective-permute-done | bytes 147488 | tf_op jit(solution)/shard_map/ppermute | solution.py:48
  34.8 1.4 %collective-permute-done.16.refs_6_ = bf16[96,768]{1,0:T(8,128)(2,1)S(1)} collective-permute-done((bf16[96,768]{1,0:T(8,128)(2,1)S(1)}, bf16[96,768]{1,0:T(8,128)(2,1)S(1)}, u32[]{:S(2)}, u32[]{:S(2)}) %collective-permute-start.16) | collective-permute-done | bytes 147488 | tf_op jit(solution)/shard_map/ppermute | solution.py:48
  36.1 0.1 shard_map.71
  36.2 0.5 %collective-permute-done.9.refs_2_ = bf16[2,192,256]{2,1,0:T(8,128)(2,1)S(1)} collective-permute-done((bf16[2,192,256]{2,1,0:T(8,128)(2,1)S(1)}, bf16[2,192,256]{2,1,0:T(8,128)(2,1)S(1)}, u32[]{:S(2)}, u32[]{:S(2)}) %collective-permute-start.9) | collective-permute-done | bytes 196640 | tf_op jit(solution)/shard_map/ppermute | solution.py:48
  36.7 0.9 %shard_map.72.refs_3_ = f32[256,768]{1,0:T(8,128)S(1)} custom-call(bf16[2,192,256]{2,1,0:T(8,128)(2,1)S(1)} %shard_map.70.refs_0_, bf16[2,192,256]{2,1,0:T(8,128)(2,1)S(1)} %collective-permute-done.11.refs_1_, bf16[2,192,256]{2,1,0:T(8,128)(2,1)S(1)} %collective-permute-done.9.refs_2_, bf16[768,768]{1,0:T(8,128)(2,1)S(1)} %get-tuple-element.60.refs_3_.refs_1_, ...), custom_call_target="tpu_custom_call" | custom-call | flops 3000000 | bytes 9000 | tf_op jit(solution)/shard_map/pallas_call | solution.py:465
  37.7 0.5 %collective-permute-done.17.refs_0_ = bf16[2,192,256]{2,1,0:T(8,128)(2,1)S(1)} collective-permute-done((bf16[2,192,256]{2,1,0:T(8,128)(2,1)S(1)}, bf16[2,192,256]{2,1,0:T(8,128)(2,1)S(1)}, u32[]{:S(2)}, u32[]{:S(2)}) %collective-permute-start.17) | collective-permute-done | bytes 196640 | tf_op jit(solution)/shard_map/ppermute | solution.py:48
  38.2 1.2 %shard_map.73 = bf16[256,768]{1,0:T(8,128)(2,1)} custom-call(bf16[2,192,256]{2,1,0:T(8,128)(2,1)S(1)} %collective-permute-done.17.refs_0_, bf16[768,768]{1,0:T(8,128)(2,1)S(1)} %get-tuple-element.60.refs_3_.refs_1_, bf16[256,256]{1,0:T(8,128)(2,1)S(1)} %get-tuple-element.62.refs_4_.refs_2_, f32[256,768]{1,0:T(8,128)S(1)} %shard_map.72.refs_3_), custom_call_target="tpu_custom_call" | custom-call | flops 3000000 | bytes 9000 | tf_op jit(solution)/shard_map/pallas_call | solution.py:465
  (27 shorter events, 0.2 us)
Async XLA Ops:
  0.0 1.4 %copy-start.1 = (bf16[1,256,768]{2,1,0:T(8,128)(2,1)S(1)}, bf16[1,256,768]{2,1,0:T(8,128)(2,1)}, u32[]{:S(2)}) copy-start(bf16[1,256,768]{2,1,0:T(8,128)(2,1)} %param.6) | copy-start | bytes 1179652
  0.0 14.2 %copy-start.2 = (f32[768]{0:T(1024)S(1)}, f32[768]{0:T(1024)}, u32[]{:S(2)}) copy-start(f32[768]{0:T(1024)} %refs_2_.3) | copy-start | bytes 9220
  0.0 14.2 %copy-start.3 = (f32[768]{0:T(1024)S(1)}, f32[768]{0:T(1024)}, u32[]{:S(2)}) copy-start(f32[768]{0:T(1024)} %refs_3_.3) | copy-start | bytes 9220
  1.4 6.9 %collective-permute-start = (bf16[256,768]{1,0:T(8,128)(2,1)S(1)}, bf16[256,768]{1,0:T(8,128)(2,1)S(1)}, u32[]{:S(2)}, u32[]{:S(2)}) collective-permute-start(bf16[256,768]{1,0:T(8,128)(2,1)S(1)} %bitcast.2), channel_id=1, source_target_pairs={{0,4},{4,0},{8,12},{12,8},{16,20},{20,16},{24,28},{28,24},{1,5},{5... | collective-permute-start | bytes 1179656 | tf_op jit(solution)/shard_map/ppermute | solution.py:48
  1.9 12.3 %collective-permute-start.1 = (bf16[256,768]{1,0:T(8,128)(2,1)S(1)}, bf16[256,768]{1,0:T(8,128)(2,1)S(1)}, u32[]{:S(2)}, u32[]{:S(2)}) collective-permute-start(bf16[256,768]{1,0:T(8,128)(2,1)S(1)} %bitcast.3), channel_id=1, source_target_pairs={{0,8},{4,12},{8,0},{12,4},{16,24},{20,28},{24,16},{28,20},{1,9},{5... | collective-permute-start | bytes 1179656 | tf_op jit(solution)/shard_map/ppermute | solution.py:48
  4.5 11.0 %collective-permute-start.4 = (bf16[64,576]{1,0:T(8,128)(2,1)S(1)}, bf16[64,576]{1,0:T(8,128)(2,1)S(1)}, u32[]{:S(2)}, u32[]{:S(2)}) collective-permute-start(bf16[64,576]{1,0:T(8,128)(2,1)S(1)} %slice.9), channel_id=1, source_target_pairs={{0,2},{1,3},{2,0},{3,1},{4,6},{5,7},{6,4},{7,5},{8,10},{9,11},{10,... | collective-permute-start | bytes 221192 | tf_op jit(solution)/shard_map/ppermute | solution.py:339
  7.2 11.7 %collective-permute-start.3 = (bf16[128,576]{1,0:T(8,128)(2,1)S(1)}, bf16[128,576]{1,0:T(8,128)(2,1)S(1)}, u32[]{:S(2)}, u32[]{:S(2)}) collective-permute-start(bf16[128,576]{1,0:T(8,128)(2,1)S(1)} %slice.8), channel_id=1, source_target_pairs={{0,2},{1,3},{2,0},{3,1},{4,6},{5,7},{6,4},{7,5},{8,10},{9,11},{10,... | collective-permute-start | bytes 442376 | tf_op jit(solution)/shard_map/ppermute | solution.py:339
  8.2 8.8 %copy-start = (bf16[192,768]{1,0:T(8,128)(2,1)S(1)}, bf16[192,768]{1,0:T(8,128)(2,1)}, u32[]{:S(2)}) copy-start(bf16[192,768]{1,0:T(8,128)(2,1)} %refs_0_.3) | copy-start | bytes 884740
  8.3 15.7 %collective-permute-start.6 = (bf16[192,576]{1,0:T(8,128)(2,1)S(1)}, bf16[192,576]{1,0:T(8,128)(2,1)S(1)}, u32[]{:S(2)}, u32[]{:S(2)}) collective-permute-start(bf16[192,576]{1,0:T(8,128)(2,1)S(1)} %pad_maximum_fusion.refs_4_), channel_id=1, source_target_pairs={{0,1},{1,0},{2,3},{3,2},{4,5},{5,4},{6,7},{7,6},{8,9},{9,8},{10,11... | collective-permute-start | bytes 663560 | tf_op jit(solution)/shard_map/ppermute | solution.py:48
  14.2 4.7 %collective-permute-start.2 = (bf16[256,768]{1,0:T(8,128)(2,1)S(1)}, bf16[256,768]{1,0:T(8,128)(2,1)S(1)}, u32[]{:S(2)}, u32[]{:S(2)}) collective-permute-start(bf16[256,768]{1,0:T(8,128)(2,1)S(1)} %collective-permute-done.1.refs_0_), channel_id=1, source_target_pairs={{0,4},{4,0},{8,12},{12,8},{16,20},{20,16},{24,28},{28,24},{1,5},{5... | collective-permute-start | bytes 1179656 | tf_op jit(solution)/shard_map/ppermute | solution.py:48
  15.6 8.4 %collective-permute-start.7 = (bf16[64,576]{1,0:T(8,128)(2,1)S(1)}, bf16[64,576]{1,0:T(8,128)(2,1)S(1)}, u32[]{:S(2)}, u32[]{:S(2)}) collective-permute-start(bf16[64,576]{1,0:T(8,128)(2,1)S(1)} %collective-permute-done.4.refs_6_), channel_id=1, source_target_pairs={{0,16},{4,20},{8,24},{12,28},{16,0},{20,4},{24,8},{28,12},{1,17},{... | collective-permute-start | bytes 221192 | tf_op jit(solution)/shard_map/ppermute | solution.py:48
  18.9 6.8 %collective-permute-start.5 = (bf16[128,576]{1,0:T(8,128)(2,1)S(1)}, bf16[128,576]{1,0:T(8,128)(2,1)S(1)}, u32[]{:S(2)}, u32[]{:S(2)}) collective-permute-start(bf16[128,576]{1,0:T(8,128)(2,1)S(1)} %collective-permute-done.3.refs_7_), channel_id=1, source_target_pairs={{0,16},{4,20},{8,24},{12,28},{16,0},{20,4},{24,8},{28,12},{1,17},{... | collective-permute-start | bytes 442376 | tf_op jit(solution)/shard_map/ppermute | solution.py:48
  19.8 9.7 %collective-permute-start.10 = (bf16[96,768]{1,0:T(8,128)(2,1)S(1)}, bf16[96,768]{1,0:T(8,128)(2,1)S(1)}, u32[]{:S(2)}, u32[]{:S(2)}) collective-permute-start(bf16[96,768]{1,0:T(8,128)(2,1)S(1)} %constant_dynamic-slice_fusion), channel_id=1, source_target_pairs={{0,2},{1,3},{2,0},{3,1},{4,6},{5,7},{6,4},{7,5},{8,10},{9,11},{10,... | collective-permute-start | bytes 442376 | tf_op jit(solution)/shard_map/ppermute | solution.py:339
  23.0 9.7 %collective-permute-start.12 = (bf16[96,768]{1,0:T(8,128)(2,1)S(1)}, bf16[96,768]{1,0:T(8,128)(2,1)S(1)}, u32[]{:S(2)}, u32[]{:S(2)}) collective-permute-start(bf16[96,768]{1,0:T(8,128)(2,1)S(1)} %constant_dynamic-slice_fusion), channel_id=1, source_target_pairs={{0,1},{1,0},{2,3},{3,2},{4,5},{5,4},{6,7},{7,6},{8,9},{9,8},{10,11... | collective-permute-start | bytes 442376 | tf_op jit(solution)/shard_map/ppermute | solution.py:48
  26.3 4.2 %collective-permute-start.8 = (bf16[3,64,128]{2,1,0:T(8,128)(2,1)S(1)}, bf16[3,64,128]{2,1,0:T(8,128)(2,1)S(1)}, u32[]{:S(2)}, u32[]{:S(2)}) collective-permute-start(bf16[3,64,128]{2,1,0:T(8,128)(2,1)S(1)} %get-tuple-element.55.refs_5_), channel_id=1, source_target_pairs={{0,16},{4,20},{8,24},{12,28},{16,0},{20,4},{24,8},{28,12},{1,17},{... | collective-permute-start | bytes 147464 | tf_op jit(solution)/shard_map/ppermute | solution.py:48
  29.5 5.2 %collective-permute-start.13 = (bf16[96,768]{1,0:T(8,128)(2,1)S(1)}, bf16[96,768]{1,0:T(8,128)(2,1)S(1)}, u32[]{:S(2)}, u32[]{:S(2)}) collective-permute-start(bf16[96,768]{1,0:T(8,128)(2,1)S(1)} %collective-permute-done.10.refs_2_), channel_id=1, source_target_pairs={{0,16},{4,20},{8,24},{12,28},{16,0},{20,4},{24,8},{28,12},{1,17},{... | collective-permute-start | bytes 442376 | tf_op jit(solution)/shard_map/ppermute | solution.py:48
  31.0 5.7 %collective-permute-start.9 = (bf16[2,192,256]{2,1,0:T(8,128)(2,1)S(1)}, bf16[2,192,256]{2,1,0:T(8,128)(2,1)S(1)}, u32[]{:S(2)}, u32[]{:S(2)}) collective-permute-start(bf16[2,192,256]{2,1,0:T(8,128)(2,1)S(1)} %shard_map.69), channel_id=1, source_target_pairs={{0,8},{4,12},{8,0},{12,4},{16,24},{20,28},{24,16},{28,20},{1,9},{5... | collective-permute-start | bytes 589832 | tf_op jit(solution)/shard_map/ppermute | solution.py:48
  32.1 4.7 %collective-permute-start.11 = (bf16[2,192,256]{2,1,0:T(8,128)(2,1)S(1)}, bf16[2,192,256]{2,1,0:T(8,128)(2,1)S(1)}, u32[]{:S(2)}, u32[]{:S(2)}) collective-permute-start(bf16[2,192,256]{2,1,0:T(8,128)(2,1)S(1)} %shard_map.70.refs_0_), channel_id=1, source_target_pairs={{0,4},{4,0},{8,12},{12,8},{16,20},{20,16},{24,28},{28,24},{1,5},{5... | collective-permute-start | bytes 589832 | tf_op jit(solution)/shard_map/ppermute | solution.py:48
  32.1 2.6 %collective-permute-start.15 = (bf16[96,768]{1,0:T(8,128)(2,1)S(1)}, bf16[96,768]{1,0:T(8,128)(2,1)S(1)}, u32[]{:S(2)}, u32[]{:S(2)}) collective-permute-start(bf16[96,768]{1,0:T(8,128)(2,1)S(1)} %collective-permute-done.10.refs_2_), channel_id=1, source_target_pairs={{0,4},{4,0},{8,12},{12,8},{16,20},{20,16},{24,28},{28,24},{1,5},{5... | collective-permute-start | bytes 442376 | tf_op jit(solution)/shard_map/ppermute | solution.py:48
  32.6 2.1 %collective-permute-start.14 = (bf16[96,768]{1,0:T(8,128)(2,1)S(1)}, bf16[96,768]{1,0:T(8,128)(2,1)S(1)}, u32[]{:S(2)}, u32[]{:S(2)}) collective-permute-start(bf16[96,768]{1,0:T(8,128)(2,1)S(1)} %collective-permute-done.12.refs_1_), channel_id=1, source_target_pairs={{0,4},{4,0},{8,12},{12,8},{16,20},{20,16},{24,28},{28,24},{1,5},{5... | collective-permute-start | bytes 442376 | tf_op jit(solution)/shard_map/ppermute | solution.py:48
  34.7 1.4 %collective-permute-start.16 = (bf16[96,768]{1,0:T(8,128)(2,1)S(1)}, bf16[96,768]{1,0:T(8,128)(2,1)S(1)}, u32[]{:S(2)}, u32[]{:S(2)}) collective-permute-start(bf16[96,768]{1,0:T(8,128)(2,1)S(1)} %collective-permute-done.13.refs_3_), channel_id=1, source_target_pairs={{0,4},{4,0},{8,12},{12,8},{16,20},{20,16},{24,28},{28,24},{1,5},{5... | collective-permute-start | bytes 442376 | tf_op jit(solution)/shard_map/ppermute | solution.py:48
  36.7 1.4 %collective-permute-start.17 = (bf16[2,192,256]{2,1,0:T(8,128)(2,1)S(1)}, bf16[2,192,256]{2,1,0:T(8,128)(2,1)S(1)}, u32[]{:S(2)}, u32[]{:S(2)}) collective-permute-start(bf16[2,192,256]{2,1,0:T(8,128)(2,1)S(1)} %collective-permute-done.9.refs_2_), channel_id=1, source_target_pairs={{0,4},{4,0},{8,12},{12,8},{16,20},{20,16},{24,28},{28,24},{1,5},{5... | collective-permute-start | bytes 589832 | tf_op jit(solution)/shard_map/ppermute | solution.py:48
